TPU v7x, 128 devices: a whole 4x4x4 slice. The times are simulated.
128 devices in a mesh: blk: 16 (over y, x), win: 8 (over z, core).
Axes of the slice: x: 4, y: 4, z: 4, core: 2. Of those that a mesh axis runs over, the one named last changes fastest.
Arguments:
- record: bfloat16 [16384, 8192], P('blk', 'win'), may hold values from -6 to 6
- deck_ids: int32 [128], replicated, may hold values from 0 to 1, as said below
- partners: int32 [128, 4], replicated, may hold values from 0 to 127, as said below
Outputs:
- correlations: bfloat16 [512, 64, 16384], P(('blk', 'win'))
Inputs may be any that keep to these rules, and one draw needn't show every extreme that they name: `deck_ids`: 0 on the first deck and 1 on the second; non-decreasing in the block id (a single switch from 0 to 1), and both decks occur. Row b lists the partner blocks of block b. Take the blocks in groups of 8 consecutive ids: the partners of the blocks of one group are all different, and they name exactly 2 blocks of every group.
All inputs are finite; a program needn't handle non-finite values.
Results may differ from a plain program's by a relative error of at most 0.0075.
Values may be sent and summed in bfloat16 or wider, within the bound.
No kernel may reach another device: no remote copies, remote signals or barrier semaphores. Data moves between devices by JAX's collectives and lax.ppermute only.
A program may use at most 128 MiB of HBM per device.

v0:
```python
import math

import jax
import jax.numpy as jnp
from jax import lax
from jax.sharding import PartitionSpec as P

WS = 512
BINS = 128
LAGS = 64


def forward_table():
    samples = jnp.arange(WS, dtype=jnp.int32)
    frequency = jnp.arange(1, BINS + 1, dtype=jnp.int32)
    phases = samples[:, None] * frequency[None, :] % WS
    angles = phases.astype(jnp.float32) * (2.0 * math.pi / WS)
    return jnp.concatenate([jnp.cos(angles), -jnp.sin(angles)], axis=1).astype(jnp.bfloat16)


def lag_table():
    frequency = jnp.arange(1, BINS + 1, dtype=jnp.int32)
    shifts = jnp.arange(LAGS, dtype=jnp.int32) - LAGS // 2
    phases = shifts[:, None] * frequency[None, :] % WS
    angles = phases.astype(jnp.float32) * (2.0 * math.pi / WS)
    return (
        jnp.stack([jnp.cos(angles), -jnp.sin(angles)], axis=2)
        .reshape(LAGS, 2 * BINS)
        .astype(jnp.bfloat16)
    )


def whiten(windowed, polarity):
    spectra = jnp.dot(windowed, forward_table(), preferred_element_type=jnp.float32)
    power_mean = jnp.sum(spectra * spectra, axis=1) / BINS
    factor = polarity / jnp.sqrt(power_mean + 1e-06)
    return (spectra * factor[:, None]).astype(jnp.bfloat16)


def shards(record, deck_ids, partners):
    groups = lax.axis_size("blk")
    members = lax.axis_size("win")
    group_index = lax.axis_index("blk")
    member_index = lax.axis_index("win")
    block_rows = record.shape[0] // members
    slab_windows = record.shape[1] // WS
    windows = slab_windows * members
    pair_count = partners.shape[1]
    capacity = members * pair_count // groups
    all_blocks = groups * members
    listed = jnp.any(
        partners[:, :, None] == jnp.arange(all_blocks, dtype=jnp.int32)[None, None, :], axis=1
    )
    needed = jnp.any(listed.reshape(groups, members, groups, members), axis=1)
    ranked = jnp.cumsum(needed.astype(jnp.int32), axis=2) - 1
    needed_here = lax.dynamic_index_in_dim(needed, group_index, 1, keepdims=False)
    ranked_here = lax.dynamic_index_in_dim(ranked, group_index, 1, keepdims=False)
    chosen = needed_here[:, None, :] & (
        ranked_here[:, None, :] == jnp.arange(capacity, dtype=jnp.int32)[None, :, None]
    )
    slot_member = jnp.sum(
        jnp.where(chosen, jnp.arange(members, dtype=jnp.int32)[None, None, :], 0), axis=2
    )
    group_rows = lax.dynamic_slice_in_dim(partners, group_index * members, members, 0)
    source = group_rows // members
    ranked_mine = lax.dynamic_index_in_dim(ranked, group_index, 0, keepdims=False)
    slot_rank = jnp.take(
        ranked_mine.reshape(-1), (source * members + group_rows % members).reshape(-1)
    )
    flat_index = source.reshape(-1) * capacity + slot_rank
    payload = record.reshape(members, block_rows, slab_windows, WS)
    value_width = payload.shape[3]
    outgoing = jnp.take(payload, slot_member.reshape(-1), axis=0)
    outgoing = outgoing.reshape(groups, capacity, block_rows, slab_windows, value_width)
    incoming = lax.all_to_all(outgoing, "blk", split_axis=0, concat_axis=0, tiled=True)
    pieces = jnp.take(
        incoming.reshape(groups * capacity, block_rows, slab_windows, value_width),
        flat_index,
        axis=0,
    )
    pieces = pieces.reshape(members, pair_count, block_rows, slab_windows, value_width)
    bundle = jnp.concatenate([payload[:, None], pieces], axis=1)
    pair_items = lax.all_to_all(bundle, "win", split_axis=0, concat_axis=3, tiled=True)
    pair_items = pair_items.reshape(1 + pair_count, block_rows, windows, value_width)
    own_id = group_index * members + member_index
    own_row = lax.dynamic_index_in_dim(partners, own_id, 0, keepdims=False)
    item_ids = jnp.concatenate([own_id.reshape(1), own_row])
    polarity = jnp.repeat(
        1.0 - 2.0 * jnp.take(deck_ids, item_ids).astype(jnp.float32), block_rows * windows
    )
    spectra = whiten(pair_items.reshape(-1, WS), polarity).reshape(
        1 + pair_count, block_rows, windows, 2 * BINS
    )
    by_bins = jnp.transpose(
        spectra.reshape(1 + pair_count, block_rows, windows, 2, BINS), (0, 4, 2, 3, 1)
    )
    own_spectra = by_bins[0]
    rotated = jnp.stack([own_spectra[:, :, 1], -own_spectra[:, :, 0]], axis=2)
    left_side = jnp.concatenate([own_spectra, rotated], axis=3)
    lags = lag_table()
    lag_scale = 1.0 / math.sqrt(windows * BINS)

    def one_pair(partner):
        cross_spec = lax.dot_general(
            left_side, partner, (((1, 2), (1, 2)), ((0,), (0,))), preferred_element_type=jnp.float32
        )
        cross_spec = cross_spec.astype(jnp.bfloat16).reshape(BINS * 2, block_rows * block_rows)
        lagged = jnp.dot(lags, cross_spec, preferred_element_type=jnp.float32)
        return (lagged * lag_scale).astype(jnp.bfloat16)

    return lax.map(one_pair, by_bins[1:])


def solution(mesh):
    return jax.shard_map(
        shards,
        mesh=mesh,
        in_specs=(P("blk", "win"), P(), P()),
        out_specs=P(("blk", "win"), None, None),
        check_vma=False,
    )
```

profile of v0, /device:TPU:1, one launch (start us, length us, event | category | flops | bytes accessed | tf_op | source)
XLA Modules:
  0.0 572.8 jit_solution(12981537645367244706)
XLA Ops:
  1.6 2.6 reduce_window_sum.11
  5.6 3.3 reshape.414
  8.9 18.3 %gather_fusion.1 = bf16[32,128,2,512]{3,2,1,0:T(2,128)(2,1)} fusion(bf16[8,128,2,512]{3,2,1,0:T(2,128)(2,1)S(1)} %reshape.414, s32[1024]{0:T(1024)S(1)} %pad_clamp_fusion.2), kind=kCustom, calls=%fused_computation.1 | custom fusion | bytes 16777344 | tf_op jit(solution)/shard_map/jit(_take)/gather | solution.py:73
  27.2 8.7 %copy.80 = bf16[32,128,2,512]{3,1,2,0:T(8,128)(2,1)} copy(bf16[32,128,2,512]{3,2,1,0:T(2,128)(2,1)} %gather_fusion.1) | data formatting | bytes 16777216 | tf_op jit(solution)/shard_map/jit(_take)/gather | solution.py:73
  36.0 7.6 %broadcast_select_fusion = bf16[16,2,128,2,512]{4,2,3,1,0:T(8,128)(2,1)} fusion(bf16[16,2,128,2,512]{4,2,3,1,0:T(8,128)(2,1)} %bitcast.62, pred[16,2]{1,0:T(8,128)(4,1)S(1)} %copy.78), kind=kLoop, calls=%fused_computation.15 | loop fusion | flops 4194304 | bytes 16777248 | tf_op jit(solution)/shard_map/jit(_take)/select_n | solution.py:73
  43.6 7.8 %all-to-all-start = ((bf16[16,2,128,2,512]{4,2,3,1,0:T(8,128)(2,1)}), bf16[16,2,128,2,512]{4,2,3,1,0:T(8,128)(2,1)}, u32[]{:S(2)}, u32[]{:S(2)}) async-start(bf16[16,2,128,2,512]{4,2,3,1,0:T(8,128)(2,1)} %broadcast_select_fusion), calls=%async_computation | async-start | bytes 16777216 | tf_op jit(solution)/shard_map/all_to_all | solution.py:75
  51.5 2.8 reshape.451
  55.2 2.0 copy.81
  57.3 117.3 %all-to-all-done = bf16[16,2,128,2,512]{4,2,3,1,0:T(8,128)(2,1)} async-done(((bf16[16,2,128,2,512]{4,2,3,1,0:T(8,128)(2,1)}), bf16[16,2,128,2,512]{4,2,3,1,0:T(8,128)(2,1)}, u32[]{:S(2)}, u32[]{:S(2)}) %all-to-all-start) | async-done | bytes 8388640 | tf_op jit(solution)/shard_map/all_to_all | solution.py:75
  174.6 8.6 %gather_fusion.2 = bf16[32,128,2,512]{3,1,2,0:T(8,128)(2,1)} fusion(bf16[32,128,2,512]{3,1,2,0:T(8,128)(2,1)} %bitcast.11, s32[1024]{0:T(1024)S(1)} %pad_clamp_fusion.1), kind=kCustom, calls=%fused_computation.2 | custom fusion | bytes 16777344 | tf_op jit(solution)/shard_map/jit(_take)/gather | solution.py:76
  183.2 7.6 %broadcast_select_fusion.1 = bf16[8,4,128,2,512]{4,2,3,1,0:T(8,128)(2,1)} fusion(bf16[8,4,128,2,512]{4,2,3,1,0:T(8,128)(2,1)} %bitcast.61, pred[8,4]{1,0:T(8,128)(4,1)S(1)} %compare_and_fusion), kind=kLoop, calls=%fused_computation.16 | loop fusion | flops 4194304 | bytes 16777248 | tf_op jit(solution)/shard_map/jit(_take)/select_n | solution.py:76
  190.8 8.9 %pad_maximum_fusion = bf16[8,5,128,2,512]{4,2,3,1,0:T(8,128)(2,1)} fusion(bf16[8,4,128,2,512]{4,2,3,1,0:T(8,128)(2,1)} %broadcast_select_fusion.1, bf16[8,1,128,2,512]{4,2,3,1,0:T(8,128)(2,1)S(1)} %copy.81), kind=kLoop, calls=%fused_computation.12 | loop fusion | flops 5242880 | bytes 20971520 | tf_op jit(solution)/shard_map/concatenate | solution.py:82
  199.7 7.3 %all-to-all-start.1 = ((bf16[8,5,128,2,512]{4,2,3,1,0:T(8,128)(2,1)}), bf16[8,5,128,2,512]{4,2,3,1,0:T(8,128)(2,1)}, u32[]{:S(2)}, u32[]{:S(2)}) async-start(bf16[8,5,128,2,512]{4,2,3,1,0:T(8,128)(2,1)} %pad_maximum_fusion), calls=%async_computation.1 | async-start | bytes 20971520 | tf_op jit(solution)/shard_map/all_to_all | solution.py:83
  209.7 113.3 %all-to-all-done.1 = bf16[8,5,128,2,512]{4,2,3,1,0:T(8,128)(2,1)} async-done(((bf16[8,5,128,2,512]{4,2,3,1,0:T(8,128)(2,1)}), bf16[8,5,128,2,512]{4,2,3,1,0:T(8,128)(2,1)}, u32[]{:S(2)}, u32[]{:S(2)}) %all-to-all-start.1) | async-done | bytes 10485792 | tf_op jit(solution)/shard_map/all_to_all | solution.py:83
  323.0 20.1 %copy.82 = bf16[1,5,128,8,2,512]{5,4,3,2,1,0:T(2,128)(2,1)} copy(bf16[1,5,128,8,2,512]{5,2,4,1,3,0:T(8,128)(2,1)} %bitcast.16) | data formatting | bytes 20971520 | tf_op jit(solution)/shard_map/all_to_all | solution.py:83
  343.1 16.0 %reshape_reshape.6 = bf16[10240,512]{1,0:T(8,128)(2,1)} reshape(bf16[1,5,128,8,2,512]{5,4,3,2,1,0:T(2,128)(2,1)} %copy.82) | data formatting | bytes 20971520 | tf_op jit(solution)/shard_map/reshape;reshape | solution.py:91
  359.1 5.9 %multiply_reduce_fusion = (f32[10240]{0:T(1024)S(1)}, f32[10240,256]{0,1:T(8,128)S(1)}) fusion(bf16[10240,512]{1,0:T(8,128)(2,1)} %reshape_reshape.6, bf16[512,128]{1,0:T(8,128)(2,1)S(1)} %get-tuple-element.80, bf16[512,128]{1,0:T(8,128)(2,1)S(1)} %get-tuple-element.79), kind=kOutput, calls=%fused_computation.14 | convolution fusion | flops 2690111488 | bytes 21274624 | tf_op jit(solution)/shard_map/dot_general | solution.py:34
  365.1 3.3 multiply_convert_fusion
  368.3 7.9 %copy.83 = bf16[10240,256]{1,0:T(8,128)(2,1)} copy(bf16[10240,256]{0,1:T(8,128)(2,1)} %multiply_convert_fusion) | data formatting | bytes 10485760 | tf_op jit(solution)/shard_map/convert_element_type | solution.py:37
  376.3 8.3 %reshape_reshape.7 = bf16[5,128,16,2,128]{4,3,2,1,0:T(2,128)(2,1)} reshape(bf16[10240,256]{1,0:T(8,128)(2,1)} %copy.83) | data formatting | bytes 10485760 | tf_op jit(solution)/shard_map/reshape;reshape | solution.py:95
  384.6 1.9 slice_bitcast_fusion
  386.6 7.2 %slice.24 = bf16[4,128,16,2,128]{1,3,2,4,0:T(2,128)(2,1)} slice(bf16[5,128,16,2,128]{1,3,2,4,0:T(2,128)(2,1)} %bitcast.64), slice={[1:5], [0:128], [0:16], [0:2], [0:128]} | slice | bytes 8388608 | tf_op jit(solution)/shard_map/slice | solution.py:111
  393.7 1.9 fusion.29
  395.7 3.5 maximum_maximum_fusion
  399.1 3.8 copy.86
  402.9 169.2 %while.10 = (s32[]{:T(128)}, bf16[4,64,16384]{2,1,0:T(8,128)(2,1)}, bf16[4,128,16,2,128]{1,3,2,4,0:T(2,128)(2,1)}, bf16[128,16,2,256]{3,1,2,0:T(8,128)(2,1)}, bf16[64,256]{1,0:T(8,128)(2,1)S(1)}, /*index=5*/s32[]{:T(128)}) while((s32[]{:T(128)}, bf16[4,64,16384]{2,1,0:T(8,128)(2,1)}, bf16[4,128,16,2,128]{1,3,2,4,0:T(2,128)(2,1)}, ...), condition=%wide.region_6.7_spmd, body=%wide.region_5.6_spmd.sunk | while | flops 811597824 | bytes 59802184 | solution.py:111
  402.9 1.9 constant_dynamic-slice_fusion.6
  404.9 1.6 copy.95
  406.5 7.2 %fusion.44 = bf16[128,256,128]{1,2,0:T(8,128)(2,1)} fusion(bf16[128,16,2,256]{3,1,2,0:T(8,128)(2,1)} %get-tuple-element.131, bf16[1,128,16,2,128]{4,2,3,1,0:T(8,128)(2,1)S(1)} %copy.95), kind=kOutput, calls=%fused_computation.9.clone.1 | convolution fusion | flops 272629760 | bytes 11534336 | tf_op jit(solution)/shard_map/while/body/eval_jaxpr/dot_general | solution.py:104
  413.7 11.9 %copy.96 = bf16[128,256,128]{2,1,0:T(8,128)(2,1)} copy(bf16[128,256,128]{1,2,0:T(8,128)(2,1)} %fusion.44) | data formatting | bytes 16777216 | tf_op jit(solution)/shard_map/while/body/eval_jaxpr/convert_element_type | solution.py:107
  425.6 13.3 %reshape.455 = bf16[256,16384]{1,0:T(8,128)(2,1)} reshape(bf16[128,256,128]{2,1,0:T(8,128)(2,1)} %copy.96) | data formatting | bytes 16777216 | tf_op jit(solution)/shard_map/while/body/eval_jaxpr/reshape | solution.py:107
  439.0 6.3 %fusion.45 = bf16[4,64,16384]{2,1,0:T(8,128)(2,1)} fusion(bf16[4,64,16384]{2,1,0:T(8,128)(2,1)} %get-tuple-element.123, s32[]{:T(128)} %get-tuple-element.122, bf16[64,256]{1,0:T(8,128)(2,1)S(1)} %get-tuple-element.132, bf16[256,16384]{1,0:T(8,128)(2,1)} %reshape.455), kind=kOutput, calls=%fused_computation.7.clone.1 | convolution fusion | flops 538968064 | bytes 10519040 | tf_op jit(solution)/shard_map/while/body/eval_jaxpr/dot_general | solution.py:108
  445.2 1.9 constant_dynamic-slice_fusion.6
  447.2 1.6 copy.95
  448.8 7.2 %fusion.44 = bf16[128,256,128]{1,2,0:T(8,128)(2,1)} fusion(bf16[128,16,2,256]{3,1,2,0:T(8,128)(2,1)} %get-tuple-element.131, bf16[1,128,16,2,128]{4,2,3,1,0:T(8,128)(2,1)S(1)} %copy.95), kind=kOutput, calls=%fused_computation.9.clone.1 | convolution fusion | flops 272629760 | bytes 11534336 | tf_op jit(solution)/shard_map/while/body/eval_jaxpr/dot_general | solution.py:104
  456.0 11.9 %copy.96 = bf16[128,256,128]{2,1,0:T(8,128)(2,1)} copy(bf16[128,256,128]{1,2,0:T(8,128)(2,1)} %fusion.44) | data formatting | bytes 16777216 | tf_op jit(solution)/shard_map/while/body/eval_jaxpr/convert_element_type | solution.py:107
  467.9 13.3 %reshape.455 = bf16[256,16384]{1,0:T(8,128)(2,1)} reshape(bf16[128,256,128]{2,1,0:T(8,128)(2,1)} %copy.96) | data formatting | bytes 16777216 | tf_op jit(solution)/shard_map/while/body/eval_jaxpr/reshape | solution.py:107
  481.2 6.3 %fusion.45 = bf16[4,64,16384]{2,1,0:T(8,128)(2,1)} fusion(bf16[4,64,16384]{2,1,0:T(8,128)(2,1)} %get-tuple-element.123, s32[]{:T(128)} %get-tuple-element.122, bf16[64,256]{1,0:T(8,128)(2,1)S(1)} %get-tuple-element.132, bf16[256,16384]{1,0:T(8,128)(2,1)} %reshape.455), kind=kOutput, calls=%fused_computation.7.clone.1 | convolution fusion | flops 538968064 | bytes 10519040 | tf_op jit(solution)/shard_map/while/body/eval_jaxpr/dot_general | solution.py:108
  487.5 1.9 constant_dynamic-slice_fusion.6
  491.1 7.2 %fusion.44 = bf16[128,256,128]{1,2,0:T(8,128)(2,1)} fusion(bf16[128,16,2,256]{3,1,2,0:T(8,128)(2,1)} %get-tuple-element.131, bf16[1,128,16,2,128]{4,2,3,1,0:T(8,128)(2,1)S(1)} %copy.95), kind=kOutput, calls=%fused_computation.9.clone.1 | convolution fusion | flops 272629760 | bytes 11534336 | tf_op jit(solution)/shard_map/while/body/eval_jaxpr/dot_general | solution.py:104
  498.3 11.9 %copy.96 = bf16[128,256,128]{2,1,0:T(8,128)(2,1)} copy(bf16[128,256,128]{1,2,0:T(8,128)(2,1)} %fusion.44) | data formatting | bytes 16777216 | tf_op jit(solution)/shard_map/while/body/eval_jaxpr/convert_element_type | solution.py:107
  510.2 13.3 %reshape.455 = bf16[256,16384]{1,0:T(8,128)(2,1)} reshape(bf16[128,256,128]{2,1,0:T(8,128)(2,1)} %copy.96) | data formatting | bytes 16777216 | tf_op jit(solution)/shard_map/while/body/eval_jaxpr/reshape | solution.py:107
  523.5 6.3 %fusion.45 = bf16[4,64,16384]{2,1,0:T(8,128)(2,1)} fusion(bf16[4,64,16384]{2,1,0:T(8,128)(2,1)} %get-tuple-element.123, s32[]{:T(128)} %get-tuple-element.122, bf16[64,256]{1,0:T(8,128)(2,1)S(1)} %get-tuple-element.132, bf16[256,16384]{1,0:T(8,128)(2,1)} %reshape.455), kind=kOutput, calls=%fused_computation.7.clone.1 | convolution fusion | flops 538968064 | bytes 10519040 | tf_op jit(solution)/shard_map/while/body/eval_jaxpr/dot_general | solution.py:108
  529.8 1.9 constant_dynamic-slice_fusion.6
  533.4 7.2 %fusion.44 = bf16[128,256,128]{1,2,0:T(8,128)(2,1)} fusion(bf16[128,16,2,256]{3,1,2,0:T(8,128)(2,1)} %get-tuple-element.131, bf16[1,128,16,2,128]{4,2,3,1,0:T(8,128)(2,1)S(1)} %copy.95), kind=kOutput, calls=%fused_computation.9.clone.1 | convolution fusion | flops 272629760 | bytes 11534336 | tf_op jit(solution)/shard_map/while/body/eval_jaxpr/dot_general | solution.py:104
  540.6 11.9 %copy.96 = bf16[128,256,128]{2,1,0:T(8,128)(2,1)} copy(bf16[128,256,128]{1,2,0:T(8,128)(2,1)} %fusion.44) | data formatting | bytes 16777216 | tf_op jit(solution)/shard_map/while/body/eval_jaxpr/convert_element_type | solution.py:107
  552.5 13.3 %reshape.455 = bf16[256,16384]{1,0:T(8,128)(2,1)} reshape(bf16[128,256,128]{2,1,0:T(8,128)(2,1)} %copy.96) | data formatting | bytes 16777216 | tf_op jit(solution)/shard_map/while/body/eval_jaxpr/reshape | solution.py:107
  565.8 6.3 %fusion.45 = bf16[4,64,16384]{2,1,0:T(8,128)(2,1)} fusion(bf16[4,64,16384]{2,1,0:T(8,128)(2,1)} %get-tuple-element.123, s32[]{:T(128)} %get-tuple-element.122, bf16[64,256]{1,0:T(8,128)(2,1)S(1)} %get-tuple-element.132, bf16[256,16384]{1,0:T(8,128)(2,1)} %reshape.455), kind=kOutput, calls=%fused_computation.7.clone.1 | convolution fusion | flops 538968064 | bytes 10519040 | tf_op jit(solution)/shard_map/while/body/eval_jaxpr/dot_general | solution.py:108
  (55 shorter events, 10.7 us)
Async XLA Ops:
  0.0 207.2 %copy-start = (s32[128]{0:T(128)S(1)}, s32[128]{0:T(128)}, u32[]{:S(2)}) copy-start(s32[128]{0:T(128)} %param.6) | copy-start | bytes 1540
  43.6 7.8 %copy-start.2 = (bf16[1024,1024]{1,0:T(8,128)(2,1)S(1)}, bf16[1024,1024]{1,0:T(8,128)(2,1)}, u32[]{:S(2)}) copy-start(bf16[1024,1024]{1,0:T(8,128)(2,1)} %param.5) | copy-start | bytes 6291460
  43.6 130.9 %all-to-all-start = ((bf16[16,2,128,2,512]{4,2,3,1,0:T(8,128)(2,1)}), bf16[16,2,128,2,512]{4,2,3,1,0:T(8,128)(2,1)}, u32[]{:S(2)}, u32[]{:S(2)}) async-start(bf16[16,2,128,2,512]{4,2,3,1,0:T(8,128)(2,1)} %broadcast_select_fusion), calls=%async_computation | async-start | bytes 16777216 | tf_op jit(solution)/shard_map/all_to_all | solution.py:75
  199.7 7.3 %copy-start.3 = (s32[128,4]{0,1:T(4,128)S(1)}, s32[128,4]{0,1:T(4,128)}, u32[]{:S(2)}) copy-start(s32[128,4]{0,1:T(4,128)} %param.7) | copy-start | bytes 6148
  199.7 123.3 %all-to-all-start.1 = ((bf16[8,5,128,2,512]{4,2,3,1,0:T(8,128)(2,1)}), bf16[8,5,128,2,512]{4,2,3,1,0:T(8,128)(2,1)}, u32[]{:S(2)}, u32[]{:S(2)}) async-start(bf16[8,5,128,2,512]{4,2,3,1,0:T(8,128)(2,1)} %pad_maximum_fusion), calls=%async_computation.1 | async-start | bytes 20971520 | tf_op jit(solution)/shard_map/all_to_all | solution.py:83
  572.1 0.7 copy-start.1
where the time goes:
time: 577 us; the launch traced here: 573 us
  waiting for transfers between devices  231 us (40%)
  local copies, waits for them, and re-layouts  229 us (40%)
  matrix products  59.8 us (10%)
  other arithmetic  38 us (7%)
  starting transfers between devices  15.1 us (3%)
    all_to_all x1, waiting for transfers between devices, shards(): lax.all_to_all(outgoing, 'blk', split_axis=0, concat_axis=0, tiled=True)  117 us
    all_to_all x1, waiting for transfers between devices, shards(): lax.all_to_all(bundle, 'win', split_axis=0, concat_axis=3, tiled=True)  113 us
    reshape x4, local copies, waits for them, and re-layouts, one_pair(): cross_spec.astype(jnp.bfloat16).reshape(BINS * 2, block_rows * block_rows)  53.2 us
    convert_element_type x4, local copies, waits for them, and re-layouts, one_pair(): cross_spec.astype(jnp.bfloat16).reshape(BINS * 2, block_rows * block_rows)  47.7 us
    dot_general x4, matrix products, one_pair(): lax.dot_general(left_side, partner, (((1, 2), (1, 2)), ((0,), (0,))), pre...  28.8 us
    gather x2, local copies, waits for them, and re-layouts, shards(): outgoing = jnp.take(payload, slot_member.reshape(-1), axis=0)  27 us
    dot_general x4, matrix products, one_pair(): lagged = jnp.dot(lags, cross_spec, preferred_element_type=jnp.float32)  25.2 us
    all_to_all x1, local copies, waits for them, and re-layouts, shards(): lax.all_to_all(bundle, 'win', split_axis=0, concat_axis=3, tiled=True)  20.1 us
  transfers between devices with their start and end apart: 2, of which 2 were waited for; matrix products, arithmetic and copies ran while one was open for 1% of the time, Pallas kernels for 0%

commit v1 on v0

v1 whole, which is shorter than its diff:
```python
import functools
import math

import jax
import jax.numpy as jnp
import ml_dtypes
import numpy as np
from jax import lax
from jax.experimental import pallas as pl
from jax.experimental.pallas import tpu as pltpu
from jax.sharding import PartitionSpec as P

WS = 512
BINS = 128
LAGS = 64
BCH = 128
OCT = BINS // 8
ROWS = OCT * 32
CHUNKS = 1
VMEM_LIMIT = 56 * 1024 * 1024


def forward_table():
    t = np.arange(WS)
    f = np.arange(1, BINS + 1)
    angle = (f[:, None] * t[None, :] % WS) * (2.0 * math.pi / WS)
    return np.concatenate([np.cos(angle), -np.sin(angle)], 0).astype(ml_dtypes.bfloat16)


def lag_table():
    f = np.arange(1, BINS + 1)
    s = np.arange(LAGS) - LAGS // 2
    angle = (s[:, None] * f[None, :] % WS) * (2.0 * math.pi / WS)
    both = np.stack([np.cos(angle), -np.sin(angle)], 1).reshape(LAGS, 2, OCT, 8)
    return both.transpose(0, 2, 1, 3).reshape(LAGS, 2 * BINS).astype(ml_dtypes.bfloat16)


def spread_table():
    i = np.arange(BCH)
    table = np.zeros((BCH, 2, 8, 2, BCH), np.float32)
    for v in range(2):
        table[i, v, :, v, i] = 1.0
    return table.reshape(16 * BCH, 2 * BCH).astype(ml_dtypes.bfloat16)


def spectra_kernel(members, groups, meta, x_ref, table_ref, *rest):
    own_refs = rest[:members]
    send_refs = rest[members : members + CHUNKS]
    held, own_sem, send_sem = rest[members + CHUNKS :]
    step = pl.program_id(0)
    polarity = 1.0 - 2.0 * meta[2 * groups + step].astype(jnp.float32)
    for w in range(2):
        spectra = lax.dot_general(
            table_ref[...],
            x_ref[:, w * WS : (w + 1) * WS],
            (((1,), (1,)), ((), ())),
            preferred_element_type=jnp.float32,
        )
        power = jnp.sum(spectra * spectra, axis=0, keepdims=True) / BINS
        white = spectra * (polarity / jnp.sqrt(power + 1e-06))
        for o in range(OCT):
            tile = jnp.concatenate(
                [white[o * 8 : o * 8 + 8], white[BINS + o * 8 : BINS + o * 8 + 8]], 0
            )
            held[step, o * 32 + w * 16 : o * 32 + w * 16 + 16, :] = tile.astype(jnp.bfloat16)

    @pl.when(step == members - 1)
    def _():
        copies = []
        me = meta[2 * groups + members]
        for k in range(members):
            src = held.at[lax.rem(me + k, members)]
            copies.append(pltpu.make_async_copy(src, own_refs[k], own_sem.at[k]))
        rows = ROWS // CHUNKS
        for c in range(CHUNKS):
            for j in range(2 * groups):
                src = held.at[meta[j], pl.ds(c * rows, rows), :]
                copies.append(
                    pltpu.make_async_copy(src, send_refs[c].at[j], send_sem.at[c, j])
                )
        for copy in copies:
            copy.start()
        for copy in copies:
            copy.wait()


def pack_kernel(members, pairs, meta, in_ref, *rest):
    out_refs, sem = rest[:members], rest[members]
    me = meta[members * pairs]
    copies = []
    for k in range(members):
        target = lax.rem(me + k, members)
        for q in range(pairs):
            src = in_ref.at[meta[target * pairs + q]]
            copies.append(
                pltpu.make_async_copy(src, out_refs[k].at[q], sem.at[k * pairs + q])
            )
    for copy in copies:
        copy.start()
    for copy in copies:
        copy.wait()


def pair_kernel(members, pairs, spread_ref, lag_ref, *rest):
    own_refs = rest[:members]
    part_refs = rest[members : 2 * members]
    out_ref = rest[2 * members]
    cross_ref = rest[2 * members + 1]
    step = pl.program_id(0)
    depth = members * 32

    @pl.when(step < OCT)
    def _():
        rows = pl.ds(pl.multiple_of(step * 32, 32), 32)
        own = jnp.concatenate([r[rows, :] for r in own_refs], 0)
        halves = own.astype(jnp.float32).reshape(depth // 16, 2, 8, BCH)
        turned = jnp.stack([halves[:, 1], -halves[:, 0]], axis=1)
        turned = turned.reshape(depth, BCH).astype(jnp.bfloat16)
        both = jnp.concatenate([own, turned], 1)
        right = jnp.concatenate(
            [jnp.concatenate([r[q, rows, :] for r in part_refs], 0) for q in range(pairs)], 1
        )
        same = (
            lax.broadcasted_iota(jnp.int32, (256, depth), 0) % 8
            == lax.broadcasted_iota(jnp.int32, (256, depth), 1) % 8
        )

        def body(ib, _):
            at = pl.ds(pl.multiple_of(ib * 256, 256), 256)
            left = lax.dot_general(
                spread_ref[at, :],
                both,
                (((1,), (1,)), ((), ())),
                preferred_element_type=jnp.float32,
            )
            left = jnp.where(same, left, 0.0).astype(jnp.bfloat16)
            cross = jnp.dot(left, right, preferred_element_type=jnp.float32)
            cross_ref[step, pl.ds(ib * 16, 16)] = cross.astype(jnp.bfloat16).reshape(
                16, 16, pairs * BCH
            )
            return 0

        lax.fori_loop(0, BCH // 16, body, 0)

    @pl.when(step >= OCT)
    def _():
        scale = 1.0 / math.sqrt(members * 2 * BINS)
        for ii in range(8):
            i = (step - OCT) * 8 + ii
            right = cross_ref[:, i].reshape(2 * BINS, pairs * BCH)
            lagged = jnp.dot(lag_ref[...], right, preferred_element_type=jnp.float32)
            lagged = (lagged * scale).astype(jnp.bfloat16)
            for q in range(pairs):
                out_ref[q, :, ii * BCH : (ii + 1) * BCH] = lagged[:, q * BCH : (q + 1) * BCH]


def shards(record, deck_ids, partners):
    groups = lax.axis_size("blk")
    members = lax.axis_size("win")
    group = lax.axis_index("blk")
    member = lax.axis_index("win")
    pairs = partners.shape[1]
    any_space = pl.BlockSpec(memory_space=pl.ANY)

    listed = partners.reshape(groups, members * pairs)
    here = listed // members == group
    first = jnp.min(jnp.where(here, listed % members, members), axis=1)
    second = jnp.max(jnp.where(here, listed % members, -1), axis=1)
    slots = jnp.stack([first, second], axis=1).reshape(-1)
    decks = lax.dynamic_slice_in_dim(deck_ids, group * members, members, 0)
    meta = jnp.concatenate([slots, decks, member.reshape(1)]).astype(jnp.int32)
    wanted = lax.dynamic_slice_in_dim(listed, group, 1, 0).reshape(-1)
    lower = (wanted[None, :] // members == wanted[:, None] // members) & (
        wanted[None, :] < wanted[:, None]
    )
    place = 2 * (wanted // members) + jnp.any(lower, axis=1).astype(jnp.int32)
    place = jnp.concatenate([place, member.reshape(1)]).astype(jnp.int32)

    rows = ROWS // CHUNKS
    outs = pl.pallas_call(
        functools.partial(spectra_kernel, members, groups),
        grid_spec=pltpu.PrefetchScalarGridSpec(
            num_scalar_prefetch=1,
            grid=(members,),
            in_specs=[
                pl.BlockSpec((BCH, 2 * WS), lambda b, meta: (b, 0)),
                pl.BlockSpec((2 * BINS, WS), lambda b, meta: (0, 0)),
            ],
            out_specs=[any_space] * (members + CHUNKS),
            scratch_shapes=[
                pltpu.VMEM((members, ROWS, BCH), jnp.bfloat16),
                pltpu.SemaphoreType.DMA((members,)),
                pltpu.SemaphoreType.DMA((CHUNKS, 2 * groups)),
            ],
        ),
        out_shape=[jax.ShapeDtypeStruct((ROWS, BCH), jnp.bfloat16)] * members
        + [jax.ShapeDtypeStruct((2 * groups, rows, BCH), jnp.bfloat16)] * CHUNKS,
        compiler_params=pltpu.CompilerParams(vmem_limit_bytes=VMEM_LIMIT),
        name="spectra",
    )(meta, record, jnp.asarray(forward_table()))
    own, sends = list(outs[:members]), outs[members:]

    def shift(k):
        return [(m, (m + k) % members) for m in range(members)]

    own = [own[0]] + [lax.ppermute(own[k], "win", shift(k)) for k in range(1, members)]
    got = lax.all_to_all(
        sends[0].reshape(groups, 2 * rows, BCH), "blk", split_axis=0, concat_axis=0, tiled=True
    )
    parts = pl.pallas_call(
        functools.partial(pack_kernel, members, pairs),
        grid_spec=pltpu.PrefetchScalarGridSpec(
            num_scalar_prefetch=1,
            grid=(),
            in_specs=[any_space],
            out_specs=[any_space] * members,
            scratch_shapes=[pltpu.SemaphoreType.DMA((members * pairs,))],
        ),
        out_shape=[jax.ShapeDtypeStruct((pairs, rows, BCH), jnp.bfloat16)] * members,
        name="pack",
    )(place, got.reshape(2 * groups, rows, BCH))
    parts = [parts[0]] + [lax.ppermute(parts[k], "win", shift(k)) for k in range(1, members)]

    def whole(shape):
        return pl.BlockSpec(shape, lambda s: (0,) * len(shape))

    return pl.pallas_call(
        functools.partial(pair_kernel, members, pairs),
        grid=(2 * OCT,),
        in_specs=[whole((16 * BCH, 2 * BCH)), whole((LAGS, 2 * BINS))]
        + [whole((ROWS, BCH))] * members
        + [whole((pairs, rows, BCH))] * members,
        out_specs=pl.BlockSpec(
            (pairs, LAGS, 8 * BCH), lambda s: (0, 0, jnp.maximum(s - OCT, 0))
        ),
        out_shape=jax.ShapeDtypeStruct((pairs, LAGS, BCH * BCH), jnp.bfloat16),
        scratch_shapes=[pltpu.VMEM((OCT, BCH, 16, pairs * BCH), jnp.bfloat16)],
        compiler_params=pltpu.CompilerParams(vmem_limit_bytes=VMEM_LIMIT),
        name="correlate",
    )(jnp.asarray(spread_table()), jnp.asarray(lag_table()), *own, *parts)


def solution(mesh):
    return jax.shard_map(
        shards,
        mesh=mesh,
        in_specs=(P("blk", "win"), P(), P()),
        out_specs=P(("blk", "win"), None, None),
        check_vma=False,
    )
```

time: 577 us -> 370 us (0.64)
  local copies, waits for them, and re-layouts: 229 us -> 2.03 us
  Pallas kernels: 0 us -> 210 us
  waiting for transfers between devices: 231 us -> 126 us
  matrix products: 59.8 us -> 0 us
  other arithmetic: 38 us -> 2.45 us
  starting transfers between devices: 15.1 us -> 27.7 us
    pallas_call x0 -> x3, Pallas kernels: none -> 210 us  [the longest x1 129 us: shards(): pl.pallas_call(functools.partial(pack_kernel, members, pairs), grid_spec=...]
    all_to_all x2 -> x1, waiting for transfers between devices: 231 us -> 61.2 us  [shards(): lax.all_to_all(sends[0].reshape(groups, 2 * rows, BCH), 'blk', split_axis...]
    ppermute x0 -> x14, waiting for transfers between devices: none -> 65.2 us  [the longest x7 40.4 us: shards(): lax.ppermute(parts[k], 'win', shift(k))]
    dot_general x9 -> x0, matrix products: 59.8 us -> none  [the longest x4 28.8 us: one_pair(): lax.dot_general(left_side, partner, (((1, 2), (1, 2)), ((0,), (0,))), pre...]
    reshape x10 -> x2, local copies, waits for them, and re-layouts: 57.4 us -> 0.17 us  [the longest x1 0.09 us: shards(): slots = jnp.stack([first, second], axis=1).reshape(-1)]
    convert_element_type x5 -> x0, local copies, waits for them, and re-layouts: 55.6 us -> none  [the longest x4 47.7 us: one_pair(): cross_spec.astype(jnp.bfloat16).reshape(BINS * 2, block_rows * block_rows)]
    gather x6 -> x0, local copies, waits for them, and re-layouts: 37 us -> none  [the longest x2 27 us: shards(): outgoing = jnp.take(payload, slot_member.reshape(-1), axis=0)]
    another operation x5 -> x1, local copies, waits for them, and re-layouts: 29.3 us -> 0.08 us  [shards(): slots = jnp.stack([first, second], axis=1).reshape(-1)]
  transfers between devices with their start and end apart: 2 -> 15, of which waited for: 2 -> 11; matrix products, arithmetic and copies ran while one was open for 1% -> 0% of each run, Pallas kernels for 0% -> 0%
where the time goes in v1:
time: 370 us; the launch traced here: 369 us
  Pallas kernels  210 us (57%)
  waiting for transfers between devices  126 us (34%)
  starting transfers between devices  27.7 us (7%)
    pallas_call x1, Pallas kernels, shards(): pl.pallas_call(functools.partial(pack_kernel, members, pairs), grid_spec=...  129 us
    pallas_call x1, Pallas kernels, shards(): pl.pallas_call(functools.partial(pair_kernel, members, pairs), grid=(2 *...  72.3 us
    all_to_all x1, waiting for transfers between devices, shards(): lax.all_to_all(sends[0].reshape(groups, 2 * rows, BCH), 'blk', split_axis...  61.2 us
    ppermute x7, waiting for transfers between devices, shards(): lax.ppermute(parts[k], 'win', shift(k))  40.4 us
    ppermute x7, waiting for transfers between devices, shards(): lax.ppermute(own[k], 'win', shift(k))  24.8 us
    ppermute x7, starting transfers between devices, shards(): lax.ppermute(parts[k], 'win', shift(k))  10.9 us
    ppermute x7, starting transfers between devices, shards(): lax.ppermute(own[k], 'win', shift(k))  9.1 us
    pallas_call x1, Pallas kernels, shards(): pl.pallas_call(functools.partial(spectra_kernel, members, groups), grid_s...  9.03 us
  transfers between devices with their start and end apart: 15, of which 11 were waited for; matrix products, arithmetic and copies ran while one was open for 0% of the time, Pallas kernels for 0%

profile of v1, /device:TPU:1, one launch (start us, length us, event | category | flops | bytes accessed | tf_op | source)
XLA Modules:
  0.0 369.2 jit_solution(16947492562051792634)
XLA Ops:
  0.0 0.7 select_reduce_fusion.1
  0.7 0.1 reduce_min.14
  0.8 0.1 reduce_max.14
  0.9 0.1 reduce_min.18
  1.0 0.1 reduce_max.18
  1.1 0.1 copy.10
  1.2 0.1 reshape.81
  1.3 0.7 dynamic_slice.6
  2.0 0.6 pad_add_fusion.1.meta
  2.7 9.0 %spectra.1 = (bf16[512,128]{1,0:T(8,128)(2,1)}, bf16[512,128]{1,0:T(8,128)(2,1)}, bf16[512,128]{1,0:T(8,128)(2,1)}, bf16[512,128]{1,0:T(8,128)(2,1)}, bf16[512,1...) custom-call(s32[41]{0:T(128)} %pad_add_fusion.1.meta, ...), custom_call_target="tpu_custom_call" | custom-call | tf_op jit(solution)/shard_map/spectra/pallas_call | solution.py:180
  11.7 0.0 copy-start.14
  11.7 7.6 %all-to-all-start = ((bf16[16,1024,128]{2,1,0:T(8,128)(2,1)}), bf16[16,1024,128]{2,1,0:T(8,128)(2,1)}, u32[]{:S(2)}, u32[]{:S(2)}) async-start(bf16[16,1024,128]{2,1,0:T(8,128)(2,1)} %bitcast.10), calls=%async_computation | async-start | bytes 8388608 | tf_op jit(solution)/shard_map/all_to_all | solution.py:207
  19.4 0.1 copy.11
  19.6 0.1 reshape.83
  19.7 0.2 and_reduce_fusion
  19.9 0.7 pad_add_fusion.2.meta
  20.5 61.2 %all-to-all-done = bf16[16,1024,128]{2,1,0:T(8,128)(2,1)} async-done(((bf16[16,1024,128]{2,1,0:T(8,128)(2,1)}), bf16[16,1024,128]{2,1,0:T(8,128)(2,1)}, u32[]{:S(2)}, u32[]{:S(2)}) %all-to-all-start) | async-done | bytes 4194336 | tf_op jit(solution)/shard_map/all_to_all | solution.py:207
  81.7 129.1 %pack.1 = (bf16[4,512,128]{2,1,0:T(8,128)(2,1)}, bf16[4,512,128]{2,1,0:T(8,128)(2,1)}, bf16[4,512,128]{2,1,0:T(8,128)(2,1)}, bf16[4,512,128]{2,1,0:T(8,128)(2,1)...) custom-call(s32[33]{0:T(128)} %pad_add_fusion.2.meta, ...), custom_call_target="tpu_custom_call" | custom-call | tf_op jit(solution)/shard_map/pack/pallas_call | solution.py:210
  210.9 3.4 collective-permute-start.7
  214.2 1.6 collective-permute-start.8
  215.9 0.4 collective-permute-start
  216.2 1.4 collective-permute-start.1
  217.6 1.2 collective-permute-start.2
  218.8 17.2 %collective-permute-done.rest_1_ = bf16[512,128]{1,0:T(8,128)(2,1)S(1)} collective-permute-done((bf16[512,128]{1,0:T(8,128)(2,1)S(1)}, bf16[512,128]{1,0:T(8,128)(2,1)S(1)}, u32[]{:S(2)}, u32[]{:S(2)}) %collective-permute-start) | collective-permute-done | bytes 131104 | tf_op jit(solution)/shard_map/ppermute | solution.py:206
  236.0 3.3 collective-permute-start.3
  239.3 0.0 collective-permute-done.1.rest_2_
  239.3 1.9 collective-permute-start.4
  241.3 0.0 collective-permute-done.2.rest_3_
  241.3 0.5 collective-permute-start.5
  241.8 3.8 %collective-permute-done.3.rest_4_ = bf16[512,128]{1,0:T(8,128)(2,1)S(1)} collective-permute-done((bf16[512,128]{1,0:T(8,128)(2,1)S(1)}, bf16[512,128]{1,0:T(8,128)(2,1)S(1)}, u32[]{:S(2)}, u32[]{:S(2)}) %collective-permute-start.3) | collective-permute-done | bytes 131104 | tf_op jit(solution)/shard_map/ppermute | solution.py:206
  245.6 0.5 collective-permute-start.6
  246.1 0.7 collective-permute-done.4.rest_5_
  246.8 0.4 collective-permute-start.9
  247.2 1.9 collective-permute-done.5.rest_6_
  249.1 1.9 collective-permute-start.10
  250.9 1.1 collective-permute-done.6.rest_7_
  252.0 1.0 collective-permute-start.11
  253.0 0.0 collective-permute-done.7.rest_9_
  253.0 1.0 collective-permute-start.12
  254.0 0.0 collective-permute-done.8.rest_10_
  254.0 1.7 collective-permute-start.13
  255.7 8.7 %collective-permute-done.9.rest_11_ = bf16[4,512,128]{2,1,0:T(8,128)(2,1)S(1)} collective-permute-done((bf16[4,512,128]{2,1,0:T(8,128)(2,1)}, bf16[4,512,128]{2,1,0:T(8,128)(2,1)S(1)}, u32[]{:S(2)}, u32[]{:S(2)}) %collective-permute-start.9) | collective-permute-done | bytes 524320 | tf_op jit(solution)/shard_map/ppermute | solution.py:222
  264.4 6.4 %collective-permute-done.10.rest_12_ = bf16[4,512,128]{2,1,0:T(8,128)(2,1)S(1)} collective-permute-done((bf16[4,512,128]{2,1,0:T(8,128)(2,1)}, bf16[4,512,128]{2,1,0:T(8,128)(2,1)S(1)}, u32[]{:S(2)}, u32[]{:S(2)}) %collective-permute-start.10) | collective-permute-done | bytes 524320 | tf_op jit(solution)/shard_map/ppermute | solution.py:222
  270.9 13.3 %collective-permute-done.11.rest_13_ = bf16[4,512,128]{2,1,0:T(8,128)(2,1)S(1)} collective-permute-done((bf16[4,512,128]{2,1,0:T(8,128)(2,1)}, bf16[4,512,128]{2,1,0:T(8,128)(2,1)S(1)}, u32[]{:S(2)}, u32[]{:S(2)}) %collective-permute-start.11) | collective-permute-done | bytes 524320 | tf_op jit(solution)/shard_map/ppermute | solution.py:222
  284.1 11.2 %collective-permute-done.12.rest_14_ = bf16[4,512,128]{2,1,0:T(8,128)(2,1)S(1)} collective-permute-done((bf16[4,512,128]{2,1,0:T(8,128)(2,1)}, bf16[4,512,128]{2,1,0:T(8,128)(2,1)S(1)}, u32[]{:S(2)}, u32[]{:S(2)}) %collective-permute-start.12) | collective-permute-done | bytes 524320 | tf_op jit(solution)/shard_map/ppermute | solution.py:222
  295.4 0.8 collective-permute-done.13.rest_15_
  296.3 0.7 copy-done.6
  296.9 72.3 %correlate.1 = bf16[4,64,16384]{2,1,0:T(8,128)(2,1)} custom-call(bf16[2048,256]{1,0:T(8,128)(2,1)} %constant.88.clone.spread_ref, bf16[64,256]{1,0:T(8,128)(2,1)} %constant.89.clone.lag_ref, bf16[512,128]{1,0:T(8,128)(2,1)} %get-tuple-element.22.rest_0_, bf16[512,128]{1,0:T(8,128)(2,1)} %copy-done.7, bf16[512,128]{1,0:T(8,128)(2,1)} %copy-done.8, ...), custom_call_target="tpu_custom_call" | custom-call | tf_op jit(solution)/shard_map/correlate/pallas_call | solution.py:227
  (46 shorter events, 0.1 us)
Async XLA Ops:
  11.7 7.7 %copy-start.14 = (s32[128,4]{0,1:T(4,128)S(1)}, s32[128,4]{0,1:T(4,128)}, u32[]{:S(2)}) copy-start(s32[128,4]{0,1:T(4,128)} %param.8) | copy-start | bytes 6148
  11.7 70.0 %all-to-all-start = ((bf16[16,1024,128]{2,1,0:T(8,128)(2,1)}), bf16[16,1024,128]{2,1,0:T(8,128)(2,1)}, u32[]{:S(2)}, u32[]{:S(2)}) async-start(bf16[16,1024,128]{2,1,0:T(8,128)(2,1)} %bitcast.10), calls=%async_computation | async-start | bytes 8388608 | tf_op jit(solution)/shard_map/all_to_all | solution.py:207
  19.4 196.5 %copy-start.21 = (bf16[512,128]{1,0:T(8,128)(2,1)S(1)}, bf16[512,128]{1,0:T(8,128)(2,1)}, u32[]{:S(2)}) copy-start(bf16[512,128]{1,0:T(8,128)(2,1)} %get-tuple-element.23) | copy-start | bytes 393220
  19.4 196.9 %copy-start.20 = (bf16[512,128]{1,0:T(8,128)(2,1)S(1)}, bf16[512,128]{1,0:T(8,128)(2,1)}, u32[]{:S(2)}) copy-start(bf16[512,128]{1,0:T(8,128)(2,1)} %get-tuple-element.24) | copy-start | bytes 393220
  19.4 198.2 %copy-start.19 = (bf16[512,128]{1,0:T(8,128)(2,1)S(1)}, bf16[512,128]{1,0:T(8,128)(2,1)}, u32[]{:S(2)}) copy-start(bf16[512,128]{1,0:T(8,128)(2,1)} %get-tuple-element.25) | copy-start | bytes 393220
  19.4 216.6 %copy-start.18 = (bf16[512,128]{1,0:T(8,128)(2,1)S(1)}, bf16[512,128]{1,0:T(8,128)(2,1)}, u32[]{:S(2)}) copy-start(bf16[512,128]{1,0:T(8,128)(2,1)} %get-tuple-element.26) | copy-start | bytes 393220
  19.4 219.9 %copy-start.17 = (bf16[512,128]{1,0:T(8,128)(2,1)S(1)}, bf16[512,128]{1,0:T(8,128)(2,1)}, u32[]{:S(2)}) copy-start(bf16[512,128]{1,0:T(8,128)(2,1)} %get-tuple-element.27) | copy-start | bytes 393220
  19.4 221.8 %copy-start.16 = (bf16[512,128]{1,0:T(8,128)(2,1)S(1)}, bf16[512,128]{1,0:T(8,128)(2,1)}, u32[]{:S(2)}) copy-start(bf16[512,128]{1,0:T(8,128)(2,1)} %get-tuple-element.28) | copy-start | bytes 393220
  19.4 226.2 %copy-start.15 = (bf16[512,128]{1,0:T(8,128)(2,1)S(1)}, bf16[512,128]{1,0:T(8,128)(2,1)}, u32[]{:S(2)}) copy-start(bf16[512,128]{1,0:T(8,128)(2,1)} %get-tuple-element.29) | copy-start | bytes 393220
  210.9 42.1 %collective-permute-start.7 = (bf16[4,512,128]{2,1,0:T(8,128)(2,1)}, bf16[4,512,128]{2,1,0:T(8,128)(2,1)S(1)}, u32[]{:S(2)}, u32[]{:S(2)}) collective-permute-start(bf16[4,512,128]{2,1,0:T(8,128)(2,1)} %get-tuple-element.32), channel_id=1, source_target_pairs={{0,1},{1,2},{2,3},{3,4},{4,5},{5,6},{6,7},{7,0},{8,9},{9,10},{10,1... | collective-permute-start | bytes 1572872 | tf_op jit(solution)/shard_map/ppermute | solution.py:222
  214.2 39.8 %collective-permute-start.8 = (bf16[4,512,128]{2,1,0:T(8,128)(2,1)}, bf16[4,512,128]{2,1,0:T(8,128)(2,1)S(1)}, u32[]{:S(2)}, u32[]{:S(2)}) collective-permute-start(bf16[4,512,128]{2,1,0:T(8,128)(2,1)} %get-tuple-element.33), channel_id=1, source_target_pairs={{0,2},{1,3},{2,4},{3,5},{4,6},{5,7},{6,0},{7,1},{8,10},{9,11},{10,... | collective-permute-start | bytes 1572872 | tf_op jit(solution)/shard_map/ppermute | solution.py:222
  215.9 20.2 %collective-permute-start = (bf16[512,128]{1,0:T(8,128)(2,1)S(1)}, bf16[512,128]{1,0:T(8,128)(2,1)S(1)}, u32[]{:S(2)}, u32[]{:S(2)}) collective-permute-start(bf16[512,128]{1,0:T(8,128)(2,1)S(1)} %copy-done.21), channel_id=1, source_target_pairs={{0,1},{1,2},{2,3},{3,4},{4,5},{5,6},{6,7},{7,0},{8,9},{9,10},{10,1... | collective-permute-start | bytes 393224 | tf_op jit(solution)/shard_map/ppermute | solution.py:206
  216.2 23.1 %collective-permute-start.1 = (bf16[512,128]{1,0:T(8,128)(2,1)S(1)}, bf16[512,128]{1,0:T(8,128)(2,1)S(1)}, u32[]{:S(2)}, u32[]{:S(2)}) collective-permute-start(bf16[512,128]{1,0:T(8,128)(2,1)S(1)} %copy-done.20), channel_id=1, source_target_pairs={{0,2},{1,3},{2,4},{3,5},{4,6},{5,7},{6,0},{7,1},{8,10},{9,11},{10,... | collective-permute-start | bytes 393224 | tf_op jit(solution)/shard_map/ppermute | solution.py:206
  217.6 23.7 %collective-permute-start.2 = (bf16[512,128]{1,0:T(8,128)(2,1)S(1)}, bf16[512,128]{1,0:T(8,128)(2,1)S(1)}, u32[]{:S(2)}, u32[]{:S(2)}) collective-permute-start(bf16[512,128]{1,0:T(8,128)(2,1)S(1)} %copy-done.19), channel_id=1, source_target_pairs={{0,3},{1,4},{2,5},{3,6},{4,7},{5,0},{6,1},{7,2},{8,11},{9,12},{10,... | collective-permute-start | bytes 393224 | tf_op jit(solution)/shard_map/ppermute | solution.py:206
  236.0 60.1 %copy-start.7 = (bf16[512,128]{1,0:T(8,128)(2,1)}, bf16[512,128]{1,0:T(8,128)(2,1)S(1)}, u32[]{:S(2)}) copy-start(bf16[512,128]{1,0:T(8,128)(2,1)S(1)} %collective-permute-done.rest_1_) | copy-start | bytes 393220
  236.0 9.6 %collective-permute-start.3 = (bf16[512,128]{1,0:T(8,128)(2,1)S(1)}, bf16[512,128]{1,0:T(8,128)(2,1)S(1)}, u32[]{:S(2)}, u32[]{:S(2)}) collective-permute-start(bf16[512,128]{1,0:T(8,128)(2,1)S(1)} %copy-done.18), channel_id=1, source_target_pairs={{0,4},{1,5},{2,6},{3,7},{4,0},{5,1},{6,2},{7,3},{8,12},{9,13},{10,... | collective-permute-start | bytes 393224 | tf_op jit(solution)/shard_map/ppermute | solution.py:206
  239.3 56.8 %copy-start.8 = (bf16[512,128]{1,0:T(8,128)(2,1)}, bf16[512,128]{1,0:T(8,128)(2,1)S(1)}, u32[]{:S(2)}) copy-start(bf16[512,128]{1,0:T(8,128)(2,1)S(1)} %collective-permute-done.1.rest_2_) | copy-start | bytes 393220
  239.3 7.4 %collective-permute-start.4 = (bf16[512,128]{1,0:T(8,128)(2,1)S(1)}, bf16[512,128]{1,0:T(8,128)(2,1)S(1)}, u32[]{:S(2)}, u32[]{:S(2)}) collective-permute-start(bf16[512,128]{1,0:T(8,128)(2,1)S(1)} %copy-done.17), channel_id=1, source_target_pairs={{0,5},{1,6},{2,7},{3,0},{4,1},{5,2},{6,3},{7,4},{8,13},{9,14},{10,... | collective-permute-start | bytes 393224 | tf_op jit(solution)/shard_map/ppermute | solution.py:206
  241.3 54.9 %copy-start.9 = (bf16[512,128]{1,0:T(8,128)(2,1)}, bf16[512,128]{1,0:T(8,128)(2,1)S(1)}, u32[]{:S(2)}) copy-start(bf16[512,128]{1,0:T(8,128)(2,1)S(1)} %collective-permute-done.2.rest_3_) | copy-start | bytes 393220
  241.3 7.8 %collective-permute-start.5 = (bf16[512,128]{1,0:T(8,128)(2,1)S(1)}, bf16[512,128]{1,0:T(8,128)(2,1)S(1)}, u32[]{:S(2)}, u32[]{:S(2)}) collective-permute-start(bf16[512,128]{1,0:T(8,128)(2,1)S(1)} %copy-done.16), channel_id=1, source_target_pairs={{0,6},{1,7},{2,0},{3,1},{4,2},{5,3},{6,4},{7,5},{8,14},{9,15},{10,... | collective-permute-start | bytes 393224 | tf_op jit(solution)/shard_map/ppermute | solution.py:206
  245.6 50.5 %copy-start.10 = (bf16[512,128]{1,0:T(8,128)(2,1)}, bf16[512,128]{1,0:T(8,128)(2,1)S(1)}, u32[]{:S(2)}) copy-start(bf16[512,128]{1,0:T(8,128)(2,1)S(1)} %collective-permute-done.3.rest_4_) | copy-start | bytes 393220
  245.6 6.4 %collective-permute-start.6 = (bf16[512,128]{1,0:T(8,128)(2,1)S(1)}, bf16[512,128]{1,0:T(8,128)(2,1)S(1)}, u32[]{:S(2)}, u32[]{:S(2)}) collective-permute-start(bf16[512,128]{1,0:T(8,128)(2,1)S(1)} %copy-done.15), channel_id=1, source_target_pairs={{0,7},{1,0},{2,1},{3,2},{4,3},{5,4},{6,5},{7,6},{8,15},{9,8},{10,9... | collective-permute-start | bytes 393224 | tf_op jit(solution)/shard_map/ppermute | solution.py:206
  246.8 49.4 %copy-start.11 = (bf16[512,128]{1,0:T(8,128)(2,1)}, bf16[512,128]{1,0:T(8,128)(2,1)S(1)}, u32[]{:S(2)}) copy-start(bf16[512,128]{1,0:T(8,128)(2,1)S(1)} %collective-permute-done.4.rest_5_) | copy-start | bytes 393220
  246.8 17.7 %collective-permute-start.9 = (bf16[4,512,128]{2,1,0:T(8,128)(2,1)}, bf16[4,512,128]{2,1,0:T(8,128)(2,1)S(1)}, u32[]{:S(2)}, u32[]{:S(2)}) collective-permute-start(bf16[4,512,128]{2,1,0:T(8,128)(2,1)} %get-tuple-element.34), channel_id=1, source_target_pairs={{0,3},{1,4},{2,5},{3,6},{4,7},{5,0},{6,1},{7,2},{8,11},{9,12},{10,... | collective-permute-start | bytes 1572872 | tf_op jit(solution)/shard_map/ppermute | solution.py:222
  249.1 47.1 %copy-start.12 = (bf16[512,128]{1,0:T(8,128)(2,1)}, bf16[512,128]{1,0:T(8,128)(2,1)S(1)}, u32[]{:S(2)}) copy-start(bf16[512,128]{1,0:T(8,128)(2,1)S(1)} %collective-permute-done.5.rest_6_) | copy-start | bytes 393220
  249.1 21.8 %collective-permute-start.10 = (bf16[4,512,128]{2,1,0:T(8,128)(2,1)}, bf16[4,512,128]{2,1,0:T(8,128)(2,1)S(1)}, u32[]{:S(2)}, u32[]{:S(2)}) collective-permute-start(bf16[4,512,128]{2,1,0:T(8,128)(2,1)} %get-tuple-element.35), channel_id=1, source_target_pairs={{0,4},{1,5},{2,6},{3,7},{4,0},{5,1},{6,2},{7,3},{8,12},{9,13},{10,... | collective-permute-start | bytes 1572872 | tf_op jit(solution)/shard_map/ppermute | solution.py:222
  252.0 44.1 %copy-start.13 = (bf16[512,128]{1,0:T(8,128)(2,1)}, bf16[512,128]{1,0:T(8,128)(2,1)S(1)}, u32[]{:S(2)}) copy-start(bf16[512,128]{1,0:T(8,128)(2,1)S(1)} %collective-permute-done.6.rest_7_) | copy-start | bytes 393220
  252.0 32.1 %collective-permute-start.11 = (bf16[4,512,128]{2,1,0:T(8,128)(2,1)}, bf16[4,512,128]{2,1,0:T(8,128)(2,1)S(1)}, u32[]{:S(2)}, u32[]{:S(2)}) collective-permute-start(bf16[4,512,128]{2,1,0:T(8,128)(2,1)} %get-tuple-element.36), channel_id=1, source_target_pairs={{0,5},{1,6},{2,7},{3,0},{4,1},{5,2},{6,3},{7,4},{8,13},{9,14},{10,... | collective-permute-start | bytes 1572872 | tf_op jit(solution)/shard_map/ppermute | solution.py:222
  253.0 43.2 %copy-start = (bf16[4,512,128]{2,1,0:T(8,128)(2,1)}, bf16[4,512,128]{2,1,0:T(8,128)(2,1)S(1)}, u32[]{:S(2)}) copy-start(bf16[4,512,128]{2,1,0:T(8,128)(2,1)S(1)} %collective-permute-done.7.rest_9_) | copy-start | bytes 1572868
  253.0 42.4 %collective-permute-start.12 = (bf16[4,512,128]{2,1,0:T(8,128)(2,1)}, bf16[4,512,128]{2,1,0:T(8,128)(2,1)S(1)}, u32[]{:S(2)}, u32[]{:S(2)}) collective-permute-start(bf16[4,512,128]{2,1,0:T(8,128)(2,1)} %get-tuple-element.37), channel_id=1, source_target_pairs={{0,6},{1,7},{2,0},{3,1},{4,2},{5,3},{6,4},{7,5},{8,14},{9,15},{10,... | collective-permute-start | bytes 1572872 | tf_op jit(solution)/shard_map/ppermute | solution.py:222
  254.0 42.2 %copy-start.1 = (bf16[4,512,128]{2,1,0:T(8,128)(2,1)}, bf16[4,512,128]{2,1,0:T(8,128)(2,1)S(1)}, u32[]{:S(2)}) copy-start(bf16[4,512,128]{2,1,0:T(8,128)(2,1)S(1)} %collective-permute-done.8.rest_10_) | copy-start | bytes 1572868
  254.0 42.1 %collective-permute-start.13 = (bf16[4,512,128]{2,1,0:T(8,128)(2,1)}, bf16[4,512,128]{2,1,0:T(8,128)(2,1)S(1)}, u32[]{:S(2)}, u32[]{:S(2)}) collective-permute-start(bf16[4,512,128]{2,1,0:T(8,128)(2,1)} %get-tuple-element.38), channel_id=1, source_target_pairs={{0,7},{1,0},{2,1},{3,2},{4,3},{5,4},{6,5},{7,6},{8,15},{9,8},{10,9... | collective-permute-start | bytes 1572872 | tf_op jit(solution)/shard_map/ppermute | solution.py:222
  264.4 31.8 %copy-start.2 = (bf16[4,512,128]{2,1,0:T(8,128)(2,1)}, bf16[4,512,128]{2,1,0:T(8,128)(2,1)S(1)}, u32[]{:S(2)}) copy-start(bf16[4,512,128]{2,1,0:T(8,128)(2,1)S(1)} %collective-permute-done.9.rest_11_) | copy-start | bytes 1572868
  270.9 25.3 %copy-start.3 = (bf16[4,512,128]{2,1,0:T(8,128)(2,1)}, bf16[4,512,128]{2,1,0:T(8,128)(2,1)S(1)}, u32[]{:S(2)}) copy-start(bf16[4,512,128]{2,1,0:T(8,128)(2,1)S(1)} %collective-permute-done.10.rest_12_) | copy-start | bytes 1572868
  284.1 12.1 %copy-start.4 = (bf16[4,512,128]{2,1,0:T(8,128)(2,1)}, bf16[4,512,128]{2,1,0:T(8,128)(2,1)S(1)}, u32[]{:S(2)}) copy-start(bf16[4,512,128]{2,1,0:T(8,128)(2,1)S(1)} %collective-permute-done.11.rest_13_) | copy-start | bytes 1572868
  295.4 0.9 copy-start.5
  296.1 0.8 copy-start.6

commit v2 on v1

--- a/solution.py
+++ b/solution.py
@@ -16,7 +16,7 @@
 BCH = 128
 OCT = BINS // 8
 ROWS = OCT * 32
-CHUNKS = 1
+CHUNKS = 2
 VMEM_LIMIT = 56 * 1024 * 1024
 
 
@@ -84,70 +84,74 @@
             copy.wait()
 
 
-def pack_kernel(members, pairs, meta, in_ref, *rest):
-    out_refs, sem = rest[:members], rest[members]
+def pack_kernel(members, pairs, meta, in_ref, *out_refs):
     me = meta[members * pairs]
-    copies = []
     for k in range(members):
         target = lax.rem(me + k, members)
         for q in range(pairs):
-            src = in_ref.at[meta[target * pairs + q]]
-            copies.append(
-                pltpu.make_async_copy(src, out_refs[k].at[q], sem.at[k * pairs + q])
-            )
-    for copy in copies:
-        copy.start()
-    for copy in copies:
-        copy.wait()
-
-
-def pair_kernel(members, pairs, spread_ref, lag_ref, *rest):
-    own_refs = rest[:members]
-    part_refs = rest[members : 2 * members]
-    out_ref = rest[2 * members]
-    cross_ref = rest[2 * members + 1]
+            out_refs[k][q] = in_ref[meta[target * pairs + q]]
+
+
+def left_kernel(members, spread_ref, *rest):
+    own_refs, left_ref = rest[:members], rest[members]
+    depth = members * 32
+    rows = pl.ds(pl.multiple_of(pl.program_id(0) * 32, 32), 32)
+    own = jnp.concatenate([r[rows, :] for r in own_refs], 0)
+    halves = own.astype(jnp.float32).reshape(depth // 16, 2, 8, BCH)
+    turned = jnp.stack([halves[:, 1], -halves[:, 0]], axis=1)
+    turned = turned.reshape(depth, BCH).astype(jnp.bfloat16)
+    both = jnp.concatenate([own, turned], 1)
+    same = (
+        lax.broadcasted_iota(jnp.int32, (256, depth), 0) % 8
+        == lax.broadcasted_iota(jnp.int32, (256, depth), 1) % 8
+    )
+    for ib in range(BCH // 16):
+        at = slice(ib * 256, (ib + 1) * 256)
+        left = lax.dot_general(
+            spread_ref[at, :],
+            both,
+            (((1,), (1,)), ((), ())),
+            preferred_element_type=jnp.float32,
+        )
+        left_ref[0, at, :] = jnp.where(same, left, 0.0).astype(jnp.bfloat16)
+
+
+def cross_octet(members, pairs, octet, left_ref, part_refs):
+    rows = pl.ds(pl.multiple_of(octet * 32, 32), 32)
+    right = jnp.concatenate(
+        [jnp.concatenate([r[q, rows, :] for r in part_refs], 0) for q in range(pairs)], 1
+    )
+    for ib in range(BCH // 16):
+        left = left_ref[0, ib * 256 : (ib + 1) * 256, :]
+        cross = jnp.dot(left, right, preferred_element_type=jnp.float32)
+        yield ib * 16, cross.astype(jnp.bfloat16).reshape(16, 16, pairs * BCH)
+
+
+def cross_kernel(members, pairs, left_ref, *rest):
+    part_refs, cross_ref = rest[:members], rest[members]
+    for i, cross in cross_octet(members, pairs, pl.program_id(0), left_ref, part_refs):
+        cross_ref[0, i : i + 16] = cross
+
+
+def pair_kernel(members, pairs, octets, left_ref, lag_ref, *rest):
+    part_refs = rest[:members]
+    early_refs = rest[members : members + CHUNKS - 1]
+    out_ref = rest[members + CHUNKS - 1]
+    last_ref = rest[members + CHUNKS]
     step = pl.program_id(0)
-    depth = members * 32
-
-    @pl.when(step < OCT)
+
+    @pl.when(step < octets)
     def _():
-        rows = pl.ds(pl.multiple_of(step * 32, 32), 32)
-        own = jnp.concatenate([r[rows, :] for r in own_refs], 0)
-        halves = own.astype(jnp.float32).reshape(depth // 16, 2, 8, BCH)
-        turned = jnp.stack([halves[:, 1], -halves[:, 0]], axis=1)
-        turned = turned.reshape(depth, BCH).astype(jnp.bfloat16)
-        both = jnp.concatenate([own, turned], 1)
-        right = jnp.concatenate(
-            [jnp.concatenate([r[q, rows, :] for r in part_refs], 0) for q in range(pairs)], 1
-        )
-        same = (
-            lax.broadcasted_iota(jnp.int32, (256, depth), 0) % 8
-            == lax.broadcasted_iota(jnp.int32, (256, depth), 1) % 8
-        )
-
-        def body(ib, _):
-            at = pl.ds(pl.multiple_of(ib * 256, 256), 256)
-            left = lax.dot_general(
-                spread_ref[at, :],
-                both,
-                (((1,), (1,)), ((), ())),
-                preferred_element_type=jnp.float32,
-            )
-            left = jnp.where(same, left, 0.0).astype(jnp.bfloat16)
-            cross = jnp.dot(left, right, preferred_element_type=jnp.float32)
-            cross_ref[step, pl.ds(ib * 16, 16)] = cross.astype(jnp.bfloat16).reshape(
-                16, 16, pairs * BCH
-            )
-            return 0
-
-        lax.fori_loop(0, BCH // 16, body, 0)
-
-    @pl.when(step >= OCT)
+        for i, cross in cross_octet(members, pairs, step, left_ref, part_refs):
+            last_ref[step, i : i + 16] = cross
+
+    @pl.when(step >= octets)
     def _():
         scale = 1.0 / math.sqrt(members * 2 * BINS)
         for ii in range(8):
-            i = (step - OCT) * 8 + ii
-            right = cross_ref[:, i].reshape(2 * BINS, pairs * BCH)
+            i = (step - octets) * 8 + ii
+            right = jnp.concatenate([r[:, ii] for r in early_refs] + [last_ref[:, i]], 0)
+            right = right.reshape(2 * BINS, pairs * BCH)
             lagged = jnp.dot(lag_ref[...], right, preferred_element_type=jnp.float32)
             lagged = (lagged * scale).astype(jnp.bfloat16)
             for q in range(pairs):
@@ -161,6 +165,12 @@
     member = lax.axis_index("win")
     pairs = partners.shape[1]
     any_space = pl.BlockSpec(memory_space=pl.ANY)
+
+    def whole(shape):
+        return pl.BlockSpec(shape, lambda *_: (0,) * len(shape))
+
+    def shift(k):
+        return [(m, (m + k) % members) for m in range(members)]
 
     listed = partners.reshape(groups, members * pairs)
     here = listed // members == group
@@ -198,46 +208,97 @@
         compiler_params=pltpu.CompilerParams(vmem_limit_bytes=VMEM_LIMIT),
         name="spectra",
     )(meta, record, jnp.asarray(forward_table()))
-    own, sends = list(outs[:members]), outs[members:]
-
-    def shift(k):
-        return [(m, (m + k) % members) for m in range(members)]
+    own, sends = list(outs[:members]), list(outs[members:])
 
     own = [own[0]] + [lax.ppermute(own[k], "win", shift(k)) for k in range(1, members)]
-    got = lax.all_to_all(
-        sends[0].reshape(groups, 2 * rows, BCH), "blk", split_axis=0, concat_axis=0, tiled=True
-    )
-    parts = pl.pallas_call(
-        functools.partial(pack_kernel, members, pairs),
-        grid_spec=pltpu.PrefetchScalarGridSpec(
-            num_scalar_prefetch=1,
-            grid=(),
-            in_specs=[any_space],
-            out_specs=[any_space] * members,
-            scratch_shapes=[pltpu.SemaphoreType.DMA((members * pairs,))],
+    octets = OCT // CHUNKS
+    left = pl.pallas_call(
+        functools.partial(left_kernel, members),
+        grid=(OCT,),
+        in_specs=[whole((16 * BCH, 2 * BCH))] + [whole((ROWS, BCH))] * members,
+        out_specs=pl.BlockSpec((1, 16 * BCH, 32 * members), lambda s: (s, 0, 0)),
+        out_shape=jax.ShapeDtypeStruct((OCT, 16 * BCH, 32 * members), jnp.bfloat16),
+        compiler_params=pltpu.CompilerParams(vmem_limit_bytes=VMEM_LIMIT),
+        cost_estimate=pl.CostEstimate(
+            flops=10_000_000_000, bytes_accessed=2**24, transcendentals=0
         ),
-        out_shape=[jax.ShapeDtypeStruct((pairs, rows, BCH), jnp.bfloat16)] * members,
-        name="pack",
-    )(place, got.reshape(2 * groups, rows, BCH))
-    parts = [parts[0]] + [lax.ppermute(parts[k], "win", shift(k)) for k in range(1, members)]
-
-    def whole(shape):
-        return pl.BlockSpec(shape, lambda s: (0,) * len(shape))
+        name="left",
+    )(jnp.asarray(spread_table()), *own)
+
+    def exchange(send):
+        return lax.all_to_all(
+            send.reshape(groups, 2 * rows, BCH), "blk", split_axis=0, concat_axis=0, tiled=True
+        )
+
+    def deliver(got):
+        parts = pl.pallas_call(
+            functools.partial(pack_kernel, members, pairs),
+            grid_spec=pltpu.PrefetchScalarGridSpec(
+                num_scalar_prefetch=1,
+                grid=(1,),
+                in_specs=[whole((2 * groups, rows, BCH))],
+                out_specs=[whole((pairs, rows, BCH))] * members,
+            ),
+            out_shape=[jax.ShapeDtypeStruct((pairs, rows, BCH), jnp.bfloat16)] * members,
+            compiler_params=pltpu.CompilerParams(vmem_limit_bytes=VMEM_LIMIT),
+            name="pack",
+        )(place, got.reshape(2 * groups, rows, BCH))
+        return [parts[0]] + [lax.ppermute(parts[k], "win", shift(k)) for k in range(1, members)]
+
+    def crossed(c, parts):
+        return pl.pallas_call(
+            functools.partial(cross_kernel, members, pairs),
+            grid=(octets,),
+            in_specs=[
+                pl.BlockSpec(
+                    (1, 16 * BCH, 32 * members), lambda s: (c * octets + s, 0, 0)
+                )
+            ]
+            + [whole((pairs, rows, BCH))] * members,
+            out_specs=pl.BlockSpec((1, BCH, 16, pairs * BCH), lambda s: (s, 0, 0, 0)),
+            out_shape=jax.ShapeDtypeStruct((octets, BCH, 16, pairs * BCH), jnp.bfloat16),
+            compiler_params=pltpu.CompilerParams(vmem_limit_bytes=VMEM_LIMIT),
+            cost_estimate=pl.CostEstimate(
+                flops=20_000_000_000 // CHUNKS, bytes_accessed=2**25, transcendentals=0
+            ),
+            name="cross",
+        )(left, *parts)
+
+    early = []
+    for c in range(CHUNKS):
+        got = exchange(sends[c])
+        if c == 0:
+            got, left = lax.optimization_barrier((got, left))
+        else:
+            got, parts = lax.optimization_barrier((got, parts))
+        if c < CHUNKS - 1:
+            got, sends[c + 1] = lax.optimization_barrier((got, sends[c + 1]))
+        if c > 0:
+            early.append(crossed(c - 1, parts))
+        parts = deliver(got)
+
+    def after(s):
+        return jnp.maximum(s - octets, 0)
 
     return pl.pallas_call(
-        functools.partial(pair_kernel, members, pairs),
-        grid=(2 * OCT,),
-        in_specs=[whole((16 * BCH, 2 * BCH)), whole((LAGS, 2 * BINS))]
-        + [whole((ROWS, BCH))] * members
-        + [whole((pairs, rows, BCH))] * members,
-        out_specs=pl.BlockSpec(
-            (pairs, LAGS, 8 * BCH), lambda s: (0, 0, jnp.maximum(s - OCT, 0))
-        ),
+        functools.partial(pair_kernel, members, pairs, octets),
+        grid=(octets + OCT,),
+        in_specs=[
+            pl.BlockSpec(
+                (1, 16 * BCH, 32 * members),
+                lambda s: (jnp.minimum(OCT - octets + s, OCT - 1), 0, 0),
+            ),
+            whole((LAGS, 2 * BINS)),
+        ]
+        + [whole((pairs, rows, BCH))] * members
+        + [pl.BlockSpec((octets, 8, 16, pairs * BCH), lambda s: (0, after(s), 0, 0))]
+        * (CHUNKS - 1),
+        out_specs=pl.BlockSpec((pairs, LAGS, 8 * BCH), lambda s: (0, 0, after(s))),
         out_shape=jax.ShapeDtypeStruct((pairs, LAGS, BCH * BCH), jnp.bfloat16),
-        scratch_shapes=[pltpu.VMEM((OCT, BCH, 16, pairs * BCH), jnp.bfloat16)],
+        scratch_shapes=[pltpu.VMEM((octets, BCH, 16, pairs * BCH), jnp.bfloat16)],
         compiler_params=pltpu.CompilerParams(vmem_limit_bytes=VMEM_LIMIT),
         name="correlate",
-    )(jnp.asarray(spread_table()), jnp.asarray(lag_table()), *own, *parts)
+    )(left, jnp.asarray(lag_table()), *parts, *early)
 
 
 def solution(mesh):

time: 370 us -> 168 us (0.45)
  Pallas kernels: 210 us -> 70.4 us
  waiting for transfers between devices: 126 us -> 47.3 us
  starting transfers between devices: 27.7 us -> 41.8 us
    pallas_call x2 -> x5, Pallas kernels: 201 us -> 61 us  [the longest x1 26.5 us: shards(): pl.pallas_call(functools.partial(pair_kernel, members, pairs, octets), gr...]
    all_to_all x1 -> x2, waiting for transfers between devices: 61.2 us -> 1.75 us  [exchange(): lax.all_to_all(send.reshape(groups, 2 * rows, BCH), 'blk', split_axis=0,...]
    ppermute x7, waiting for transfers between devices: 24.8 us -> 7.94 us  [shards(): lax.ppermute(own[k], 'win', shift(k))]
    all_to_all x1 -> x2, starting transfers between devices: 7.65 us -> 14.7 us  [exchange(): lax.all_to_all(send.reshape(groups, 2 * rows, BCH), 'blk', split_axis=0,...]
    ppermute x7 -> x14, starting transfers between devices: 10.9 us -> 16.5 us  [deliver(): lax.ppermute(parts[k], 'win', shift(k))]
    ppermute x7 -> x14, waiting for transfers between devices: 40.4 us -> 37.6 us  [deliver(): lax.ppermute(parts[k], 'win', shift(k))]
  transfers between devices with their start and end apart: 15 -> 23, of which waited for: 11 -> 9; matrix products, arithmetic and copies ran while one was open for 0% -> 1% of each run, Pallas kernels for 0% -> 19%
where the time goes in v2:
time: 168 us; the launch traced here: 167 us
  Pallas kernels  70.4 us (42%)
  waiting for transfers between devices  47.3 us (28%)
  starting transfers between devices  41.8 us (25%)
  local copies, waits for them, and re-layouts  4.26 us (3%)
  other arithmetic  2.41 us (1%)
    ppermute x14, waiting for transfers between devices, deliver(): lax.ppermute(parts[k], 'win', shift(k))  37.6 us
    pallas_call x1, Pallas kernels, shards(): pl.pallas_call(functools.partial(pair_kernel, members, pairs, octets), gr...  26.5 us
    ppermute x14, starting transfers between devices, deliver(): lax.ppermute(parts[k], 'win', shift(k))  16.5 us
    all_to_all x2, starting transfers between devices, exchange(): lax.all_to_all(send.reshape(groups, 2 * rows, BCH), 'blk', split_axis=0,...  14.7 us
    pallas_call x1, Pallas kernels, shards(): pl.pallas_call(functools.partial(left_kernel, members), grid=(OCT,), in_s...  13.9 us
    pallas_call x1, Pallas kernels, crossed(): pl.pallas_call(functools.partial(cross_kernel, members, pairs), grid=(oct...  13.3 us
    ppermute x7, starting transfers between devices, shards(): lax.ppermute(own[k], 'win', shift(k))  10.6 us
    pallas_call x1, Pallas kernels, shards(): pl.pallas_call(functools.partial(spectra_kernel, members, groups), grid_s...  9.36 us
  transfers between devices with their start and end apart: 23, of which 9 were waited for; matrix products, arithmetic and copies ran while one was open for 1% of the time, Pallas kernels for 19%

profile of v2, /device:TPU:1, one launch (start us, length us, event | category | flops | bytes accessed | tf_op | source)
XLA Modules:
  0.0 166.5 jit_solution(14967163653826761072)
XLA Ops:
  0.0 0.7 select_reduce_fusion.1
  0.9 0.1 reduce_min.18
  1.0 0.1 reduce_max.18
  1.3 0.7 dynamic_slice.6
  2.0 0.6 pad_add_fusion.1.meta
  2.6 9.4 %spectra.1 = (bf16[512,128]{1,0:T(8,128)(2,1)}, bf16[512,128]{1,0:T(8,128)(2,1)}, bf16[512,128]{1,0:T(8,128)(2,1)}, bf16[512,128]{1,0:T(8,128)(2,1)}, bf16[512,1...) custom-call(s32[41]{0:T(128)} %pad_add_fusion.1.meta, ...), custom_call_target="tpu_custom_call" | custom-call | tf_op jit(solution)/shard_map/spectra/pallas_call | solution.py:190
  12.1 7.7 %all-to-all-start = ((bf16[16,512,128]{2,1,0:T(8,128)(2,1)}), bf16[16,512,128]{2,1,0:T(8,128)(2,1)S(1)}, u32[]{:S(2)}, u32[]{:S(2)}) async-start(bf16[16,512,128]{2,1,0:T(8,128)(2,1)} %bitcast.14), calls=%async_computation | async-start | bytes 4194304 | tf_op jit(solution)/shard_map/all_to_all | solution.py:229
  19.8 2.5 %collective-permute-start = (bf16[512,128]{1,0:T(8,128)(2,1)S(1)}, bf16[512,128]{1,0:T(8,128)(2,1)S(1)}, u32[]{:S(2)}, u32[]{:S(2)}) collective-permute-start(bf16[512,128]{1,0:T(8,128)(2,1)S(1)} %copy-done.27), channel_id=1, source_target_pairs={{0,1},{1,2},{2,3},{3,4},{4,5},{5,6},{6,7},{7,0},{8,9},{9,10},{10,1... | collective-permute-start | bytes 393224 | tf_op jit(solution)/shard_map/ppermute | solution.py:213
  22.3 1.7 collective-permute-start.1
  24.0 2.0 %collective-permute-start.2 = (bf16[512,128]{1,0:T(8,128)(2,1)S(1)}, bf16[512,128]{1,0:T(8,128)(2,1)S(1)}, u32[]{:S(2)}, u32[]{:S(2)}) collective-permute-start(bf16[512,128]{1,0:T(8,128)(2,1)S(1)} %copy-done.22), channel_id=1, source_target_pairs={{0,3},{1,4},{2,5},{3,6},{4,7},{5,0},{6,1},{7,2},{8,11},{9,12},{10,... | collective-permute-start | bytes 393224 | tf_op jit(solution)/shard_map/ppermute | solution.py:213
  26.0 2.3 %collective-permute-start.4 = (bf16[512,128]{1,0:T(8,128)(2,1)S(1)}, bf16[512,128]{1,0:T(8,128)(2,1)S(1)}, u32[]{:S(2)}, u32[]{:S(2)}) collective-permute-start(bf16[512,128]{1,0:T(8,128)(2,1)S(1)} %copy-done.18), channel_id=1, source_target_pairs={{0,5},{1,6},{2,7},{3,0},{4,1},{5,2},{6,3},{7,4},{8,13},{9,14},{10,... | collective-permute-start | bytes 393224 | tf_op jit(solution)/shard_map/ppermute | solution.py:213
  28.3 0.8 collective-permute-start.5
  29.2 1.2 collective-permute-start.6
  30.5 7.0 %collective-permute-done.3.rest_4_ = bf16[512,128]{1,0:T(8,128)(2,1)S(1)} collective-permute-done((bf16[512,128]{1,0:T(8,128)(2,1)S(1)}, bf16[512,128]{1,0:T(8,128)(2,1)S(1)}, u32[]{:S(2)}, u32[]{:S(2)}) %collective-permute-start.3) | collective-permute-done | bytes 131104 | tf_op jit(solution)/shard_map/ppermute | solution.py:213
  37.5 0.6 collective-permute-done.4.rest_5_
  38.1 0.3 collective-permute-done.6.rest_7_
  38.4 0.3 copy-done.26
  38.8 0.2 copy-done.29
  39.0 13.9 %left.1.left_ref = bf16[16,2048,256]{2,1,0:T(8,128)(2,1)} custom-call(bf16[2048,256]{1,0:T(8,128)(2,1)} %constant.88.clone.spread_ref, bf16[512,128]{1,0:T(8,128)(2,1)} %get-tuple-element.45.rest_0_, bf16[512,128]{1,0:T(8,128)(2,1)} %copy-done.19, bf16[512,128]{1,0:T(8,128)(2,1)} %copy-done.21, bf16[512,128]{1,0:T(8,128)(2,1)} %copy-done.23, ...), custom_call_target="tpu_custom_call" | custom-call | flops 10000000000 | bytes 16777216 | tf_op jit(solution)/shard_map/left/pallas_call | solution.py:215
  52.9 1.3 copy-done
  54.2 7.0 %all-to-all-start.1 = ((bf16[16,512,128]{2,1,0:T(8,128)(2,1)}), bf16[16,512,128]{2,1,0:T(8,128)(2,1)}, u32[]{:S(2)}, u32[]{:S(2)}) async-start(bf16[16,512,128]{2,1,0:T(8,128)(2,1)} %bitcast.13), calls=%async_computation.1 | async-start | bytes 4194304 | tf_op jit(solution)/shard_map/all_to_all | solution.py:229
  61.2 0.1 copy.11
  61.5 0.2 and_reduce_fusion
  61.6 0.6 pad_add_fusion.2.meta
  62.3 3.7 %pack.2 = (bf16[4,256,128]{2,1,0:T(8,128)(2,1)}, bf16[4,256,128]{2,1,0:T(8,128)(2,1)}, bf16[4,256,128]{2,1,0:T(8,128)(2,1)}, bf16[4,256,128]{2,1,0:T(8,128)(2,1)...) custom-call(s32[33]{0:T(128)} %pad_add_fusion.2.meta, ...), custom_call_target="tpu_custom_call" | custom-call | tf_op jit(solution)/shard_map/pack/pallas_call | solution.py:234
  66.0 1.4 collective-permute-start.8
  67.4 2.8 %collective-permute-start.9 = (bf16[4,256,128]{2,1,0:T(8,128)(2,1)}, bf16[4,256,128]{2,1,0:T(8,128)(2,1)S(1)}, u32[]{:S(2)}, u32[]{:S(2)}) collective-permute-start(bf16[4,256,128]{2,1,0:T(8,128)(2,1)} %get-tuple-element.61), channel_id=1, source_target_pairs={{0,3},{1,4},{2,5},{3,6},{4,7},{5,0},{6,1},{7,2},{8,11},{9,12},{10,... | collective-permute-start | bytes 786440 | tf_op jit(solution)/shard_map/ppermute | solution.py:246
  70.2 0.8 collective-permute-start.10
  71.0 1.2 collective-permute-start.11
  72.2 1.3 collective-permute-start.12
  73.5 7.6 %collective-permute-done.8.rest_2_ = bf16[4,256,128]{2,1,0:T(8,128)(2,1)S(1)} collective-permute-done((bf16[4,256,128]{2,1,0:T(8,128)(2,1)}, bf16[4,256,128]{2,1,0:T(8,128)(2,1)S(1)}, u32[]{:S(2)}, u32[]{:S(2)}) %collective-permute-start.8) | collective-permute-done | bytes 262176 | tf_op jit(solution)/shard_map/ppermute | solution.py:246
  81.2 10.8 %collective-permute-done.9.rest_3_ = bf16[4,256,128]{2,1,0:T(8,128)(2,1)S(1)} collective-permute-done((bf16[4,256,128]{2,1,0:T(8,128)(2,1)}, bf16[4,256,128]{2,1,0:T(8,128)(2,1)S(1)}, u32[]{:S(2)}, u32[]{:S(2)}) %collective-permute-start.9) | collective-permute-done | bytes 262176 | tf_op jit(solution)/shard_map/ppermute | solution.py:246
  92.0 0.8 collective-permute-done.12.rest_6_
  92.8 1.2 collective-permute-done.13.rest_7_
  94.0 1.7 %all-to-all-done.1 = bf16[16,512,128]{2,1,0:T(8,128)(2,1)} async-done(((bf16[16,512,128]{2,1,0:T(8,128)(2,1)}), bf16[16,512,128]{2,1,0:T(8,128)(2,1)}, u32[]{:S(2)}, u32[]{:S(2)}) %all-to-all-start.1) | async-done | bytes 2097184 | tf_op jit(solution)/shard_map/all_to_all | solution.py:229
  95.7 3.7 %pack.3 = (bf16[4,256,128]{2,1,0:T(8,128)(2,1)}, bf16[4,256,128]{2,1,0:T(8,128)(2,1)}, bf16[4,256,128]{2,1,0:T(8,128)(2,1)}, bf16[4,256,128]{2,1,0:T(8,128)(2,1)...) custom-call(s32[33]{0:T(128)} %pad_add_fusion.2.meta, ...), custom_call_target="tpu_custom_call" | custom-call | tf_op jit(solution)/shard_map/pack/pallas_call | solution.py:234
  99.4 2.1 %collective-permute-start.15 = (bf16[4,256,128]{2,1,0:T(8,128)(2,1)}, bf16[4,256,128]{2,1,0:T(8,128)(2,1)S(1)}, u32[]{:S(2)}, u32[]{:S(2)}) collective-permute-start(bf16[4,256,128]{2,1,0:T(8,128)(2,1)} %get-tuple-element.69), channel_id=1, source_target_pairs={{0,2},{1,3},{2,4},{3,5},{4,6},{5,7},{6,0},{7,1},{8,10},{9,11},{10,... | collective-permute-start | bytes 786440 | tf_op jit(solution)/shard_map/ppermute | solution.py:246
  101.6 0.6 collective-permute-start.16
  102.2 1.5 collective-permute-start.17
  103.7 2.6 %collective-permute-start.18 = (bf16[4,256,128]{2,1,0:T(8,128)(2,1)}, bf16[4,256,128]{2,1,0:T(8,128)(2,1)S(1)}, u32[]{:S(2)}, u32[]{:S(2)}) collective-permute-start(bf16[4,256,128]{2,1,0:T(8,128)(2,1)} %get-tuple-element.72), channel_id=1, source_target_pairs={{0,5},{1,6},{2,7},{3,0},{4,1},{5,2},{6,3},{7,4},{8,13},{9,14},{10,... | collective-permute-start | bytes 786440 | tf_op jit(solution)/shard_map/ppermute | solution.py:246
  106.3 2.1 %collective-permute-start.19 = (bf16[4,256,128]{2,1,0:T(8,128)(2,1)}, bf16[4,256,128]{2,1,0:T(8,128)(2,1)S(1)}, u32[]{:S(2)}, u32[]{:S(2)}) collective-permute-start(bf16[4,256,128]{2,1,0:T(8,128)(2,1)} %get-tuple-element.73), channel_id=1, source_target_pairs={{0,6},{1,7},{2,0},{3,1},{4,2},{5,3},{6,4},{7,5},{8,14},{9,15},{10,... | collective-permute-start | bytes 786440 | tf_op jit(solution)/shard_map/ppermute | solution.py:246
  108.4 17.2 %collective-permute-done.15.rest_2_ = bf16[4,256,128]{2,1,0:T(8,128)(2,1)S(1)} collective-permute-done((bf16[4,256,128]{2,1,0:T(8,128)(2,1)}, bf16[4,256,128]{2,1,0:T(8,128)(2,1)S(1)}, u32[]{:S(2)}, u32[]{:S(2)}) %collective-permute-start.15) | collective-permute-done | bytes 262176 | tf_op jit(solution)/shard_map/ppermute | solution.py:246
  125.7 13.3 %cross.1.rest_8_ = bf16[8,128,16,512]{3,2,1,0:T(8,128)(2,1)} custom-call(bf16[16,2048,256]{2,1,0:T(8,128)(2,1)} %left.1.left_ref, bf16[4,256,128]{2,1,0:T(8,128)(2,1)} %get-tuple-element.75.rest_0_, bf16[4,256,128]{2,1,0:T(8,128)(2,1)} %copy-done.9, bf16[4,256,128]{2,1,0:T(8,128)(2,1)} %copy-done.10, bf16[4,256,128]{2,1,0:T(8,128)(2,1)} %copy-done.11, ...), custom_call_target="tpu_custom_call" | custom-call | flops 10000000000 | bytes 33554432 | tf_op jit(solution)/shard_map/cross/pallas_call | solution.py:249
  139.1 0.6 copy-done.3
  139.7 0.1 copy-done.4
  139.8 0.1 copy-done.5
  140.0 0.1 copy-done.7
  140.0 26.5 %correlate.1 = bf16[4,64,16384]{2,1,0:T(8,128)(2,1)} custom-call(bf16[16,2048,256]{2,1,0:T(8,128)(2,1)} %left.1.left_ref, bf16[64,256]{1,0:T(8,128)(2,1)} %constant.89.clone.lag_ref, bf16[4,256,128]{2,1,0:T(8,128)(2,1)} %get-tuple-element.67.rest_0_, bf16[4,256,128]{2,1,0:T(8,128)(2,1)} %copy-done.1, bf16[4,256,128]{2,1,0:T(8,128)(2,1)} %copy-done.2, ...), custom_call_target="tpu_custom_call" | custom-call | tf_op jit(solution)/shard_map/correlate/pallas_call | solution.py:283
  (81 shorter events, 0.8 us)
Async XLA Ops:
  12.0 7.8 %copy-start.27 = (bf16[512,128]{1,0:T(8,128)(2,1)S(1)}, bf16[512,128]{1,0:T(8,128)(2,1)}, u32[]{:S(2)}) copy-start(bf16[512,128]{1,0:T(8,128)(2,1)} %get-tuple-element.46) | copy-start | bytes 393220
  12.0 10.3 %copy-start.25 = (bf16[512,128]{1,0:T(8,128)(2,1)S(1)}, bf16[512,128]{1,0:T(8,128)(2,1)}, u32[]{:S(2)}) copy-start(bf16[512,128]{1,0:T(8,128)(2,1)} %get-tuple-element.47) | copy-start | bytes 393220
  12.0 11.9 %copy-start.22 = (bf16[512,128]{1,0:T(8,128)(2,1)S(1)}, bf16[512,128]{1,0:T(8,128)(2,1)}, u32[]{:S(2)}) copy-start(bf16[512,128]{1,0:T(8,128)(2,1)} %get-tuple-element.48) | copy-start | bytes 393220
  12.0 13.9 %copy-start.20 = (bf16[512,128]{1,0:T(8,128)(2,1)S(1)}, bf16[512,128]{1,0:T(8,128)(2,1)}, u32[]{:S(2)}) copy-start(bf16[512,128]{1,0:T(8,128)(2,1)} %get-tuple-element.49) | copy-start | bytes 393220
  12.1 13.9 %copy-start.18 = (bf16[512,128]{1,0:T(8,128)(2,1)S(1)}, bf16[512,128]{1,0:T(8,128)(2,1)}, u32[]{:S(2)}) copy-start(bf16[512,128]{1,0:T(8,128)(2,1)} %get-tuple-element.50) | copy-start | bytes 393220
  12.1 16.3 %copy-start.17 = (bf16[512,128]{1,0:T(8,128)(2,1)S(1)}, bf16[512,128]{1,0:T(8,128)(2,1)}, u32[]{:S(2)}) copy-start(bf16[512,128]{1,0:T(8,128)(2,1)} %get-tuple-element.51) | copy-start | bytes 393220
  12.1 17.2 %copy-start.16 = (bf16[512,128]{1,0:T(8,128)(2,1)S(1)}, bf16[512,128]{1,0:T(8,128)(2,1)}, u32[]{:S(2)}) copy-start(bf16[512,128]{1,0:T(8,128)(2,1)} %get-tuple-element.52) | copy-start | bytes 393220
  12.1 40.8 %all-to-all-start = ((bf16[16,512,128]{2,1,0:T(8,128)(2,1)}), bf16[16,512,128]{2,1,0:T(8,128)(2,1)S(1)}, u32[]{:S(2)}, u32[]{:S(2)}) async-start(bf16[16,512,128]{2,1,0:T(8,128)(2,1)} %bitcast.14), calls=%async_computation | async-start | bytes 4194304 | tf_op jit(solution)/shard_map/all_to_all | solution.py:229
  19.8 8.5 %collective-permute-start = (bf16[512,128]{1,0:T(8,128)(2,1)S(1)}, bf16[512,128]{1,0:T(8,128)(2,1)S(1)}, u32[]{:S(2)}, u32[]{:S(2)}) collective-permute-start(bf16[512,128]{1,0:T(8,128)(2,1)S(1)} %copy-done.27), channel_id=1, source_target_pairs={{0,1},{1,2},{2,3},{3,4},{4,5},{5,6},{6,7},{7,0},{8,9},{9,10},{10,1... | collective-permute-start | bytes 393224 | tf_op jit(solution)/shard_map/ppermute | solution.py:213
  22.3 6.9 %collective-permute-start.1 = (bf16[512,128]{1,0:T(8,128)(2,1)S(1)}, bf16[512,128]{1,0:T(8,128)(2,1)S(1)}, u32[]{:S(2)}, u32[]{:S(2)}) collective-permute-start(bf16[512,128]{1,0:T(8,128)(2,1)S(1)} %copy-done.25), channel_id=1, source_target_pairs={{0,2},{1,3},{2,4},{3,5},{4,6},{5,7},{6,0},{7,1},{8,10},{9,11},{10,... | collective-permute-start | bytes 393224 | tf_op jit(solution)/shard_map/ppermute | solution.py:213
  24.0 6.5 %collective-permute-start.2 = (bf16[512,128]{1,0:T(8,128)(2,1)S(1)}, bf16[512,128]{1,0:T(8,128)(2,1)S(1)}, u32[]{:S(2)}, u32[]{:S(2)}) collective-permute-start(bf16[512,128]{1,0:T(8,128)(2,1)S(1)} %copy-done.22), channel_id=1, source_target_pairs={{0,3},{1,4},{2,5},{3,6},{4,7},{5,0},{6,1},{7,2},{8,11},{9,12},{10,... | collective-permute-start | bytes 393224 | tf_op jit(solution)/shard_map/ppermute | solution.py:213
  26.0 11.5 %collective-permute-start.3 = (bf16[512,128]{1,0:T(8,128)(2,1)S(1)}, bf16[512,128]{1,0:T(8,128)(2,1)S(1)}, u32[]{:S(2)}, u32[]{:S(2)}) collective-permute-start(bf16[512,128]{1,0:T(8,128)(2,1)S(1)} %copy-done.20), channel_id=1, source_target_pairs={{0,4},{1,5},{2,6},{3,7},{4,0},{5,1},{6,2},{7,3},{8,12},{9,13},{10,... | collective-permute-start | bytes 393224 | tf_op jit(solution)/shard_map/ppermute | solution.py:213
  26.0 12.1 %collective-permute-start.4 = (bf16[512,128]{1,0:T(8,128)(2,1)S(1)}, bf16[512,128]{1,0:T(8,128)(2,1)S(1)}, u32[]{:S(2)}, u32[]{:S(2)}) collective-permute-start(bf16[512,128]{1,0:T(8,128)(2,1)S(1)} %copy-done.18), channel_id=1, source_target_pairs={{0,5},{1,6},{2,7},{3,0},{4,1},{5,2},{6,3},{7,4},{8,13},{9,14},{10,... | collective-permute-start | bytes 393224 | tf_op jit(solution)/shard_map/ppermute | solution.py:213
  28.3 10.1 %copy-start.19 = (bf16[512,128]{1,0:T(8,128)(2,1)}, bf16[512,128]{1,0:T(8,128)(2,1)S(1)}, u32[]{:S(2)}) copy-start(bf16[512,128]{1,0:T(8,128)(2,1)S(1)} %collective-permute-done.rest_1_) | copy-start | bytes 393220
  28.3 9.8 %collective-permute-start.5 = (bf16[512,128]{1,0:T(8,128)(2,1)S(1)}, bf16[512,128]{1,0:T(8,128)(2,1)S(1)}, u32[]{:S(2)}, u32[]{:S(2)}) collective-permute-start(bf16[512,128]{1,0:T(8,128)(2,1)S(1)} %copy-done.17), channel_id=1, source_target_pairs={{0,6},{1,7},{2,0},{3,1},{4,2},{5,3},{6,4},{7,5},{8,14},{9,15},{10,... | collective-permute-start | bytes 393224 | tf_op jit(solution)/shard_map/ppermute | solution.py:213
  29.2 9.2 %copy-start.21 = (bf16[512,128]{1,0:T(8,128)(2,1)}, bf16[512,128]{1,0:T(8,128)(2,1)S(1)}, u32[]{:S(2)}) copy-start(bf16[512,128]{1,0:T(8,128)(2,1)S(1)} %collective-permute-done.1.rest_2_) | copy-start | bytes 393220
  29.2 9.2 %collective-permute-start.6 = (bf16[512,128]{1,0:T(8,128)(2,1)S(1)}, bf16[512,128]{1,0:T(8,128)(2,1)S(1)}, u32[]{:S(2)}, u32[]{:S(2)}) collective-permute-start(bf16[512,128]{1,0:T(8,128)(2,1)S(1)} %copy-done.16), channel_id=1, source_target_pairs={{0,7},{1,0},{2,1},{3,2},{4,3},{5,4},{6,5},{7,6},{8,15},{9,8},{10,9... | collective-permute-start | bytes 393224 | tf_op jit(solution)/shard_map/ppermute | solution.py:213
  30.5 7.9 %copy-start.23 = (bf16[512,128]{1,0:T(8,128)(2,1)}, bf16[512,128]{1,0:T(8,128)(2,1)S(1)}, u32[]{:S(2)}) copy-start(bf16[512,128]{1,0:T(8,128)(2,1)S(1)} %collective-permute-done.2.rest_3_) | copy-start | bytes 393220
  37.5 0.9 copy-start.24
  52.9 1.3 copy-start
  52.9 8.3 %copy-start.8 = (s32[128,4]{0,1:T(4,128)S(1)}, s32[128,4]{0,1:T(4,128)}, u32[]{:S(2)}) copy-start(s32[128,4]{0,1:T(4,128)} %param.8) | copy-start | bytes 6148
  54.2 41.5 %all-to-all-start.1 = ((bf16[16,512,128]{2,1,0:T(8,128)(2,1)}), bf16[16,512,128]{2,1,0:T(8,128)(2,1)}, u32[]{:S(2)}, u32[]{:S(2)}) async-start(bf16[16,512,128]{2,1,0:T(8,128)(2,1)} %bitcast.13), calls=%async_computation.1 | async-start | bytes 4194304 | tf_op jit(solution)/shard_map/all_to_all | solution.py:229
  66.0 6.2 %collective-permute-start.7 = (bf16[4,256,128]{2,1,0:T(8,128)(2,1)}, bf16[4,256,128]{2,1,0:T(8,128)(2,1)S(1)}, u32[]{:S(2)}, u32[]{:S(2)}) collective-permute-start(bf16[4,256,128]{2,1,0:T(8,128)(2,1)} %get-tuple-element.59), channel_id=1, source_target_pairs={{0,1},{1,2},{2,3},{3,4},{4,5},{5,6},{6,7},{7,0},{8,9},{9,10},{10,1... | collective-permute-start | bytes 786440 | tf_op jit(solution)/shard_map/ppermute | solution.py:246
  66.0 15.2 %collective-permute-start.8 = (bf16[4,256,128]{2,1,0:T(8,128)(2,1)}, bf16[4,256,128]{2,1,0:T(8,128)(2,1)S(1)}, u32[]{:S(2)}, u32[]{:S(2)}) collective-permute-start(bf16[4,256,128]{2,1,0:T(8,128)(2,1)} %get-tuple-element.60), channel_id=1, source_target_pairs={{0,2},{1,3},{2,4},{3,5},{4,6},{5,7},{6,0},{7,1},{8,10},{9,11},{10,... | collective-permute-start | bytes 786440 | tf_op jit(solution)/shard_map/ppermute | solution.py:246
  67.4 24.6 %collective-permute-start.9 = (bf16[4,256,128]{2,1,0:T(8,128)(2,1)}, bf16[4,256,128]{2,1,0:T(8,128)(2,1)S(1)}, u32[]{:S(2)}, u32[]{:S(2)}) collective-permute-start(bf16[4,256,128]{2,1,0:T(8,128)(2,1)} %get-tuple-element.61), channel_id=1, source_target_pairs={{0,3},{1,4},{2,5},{3,6},{4,7},{5,0},{6,1},{7,2},{8,11},{9,12},{10,... | collective-permute-start | bytes 786440 | tf_op jit(solution)/shard_map/ppermute | solution.py:246
  70.2 21.8 %collective-permute-start.10 = (bf16[4,256,128]{2,1,0:T(8,128)(2,1)}, bf16[4,256,128]{2,1,0:T(8,128)(2,1)S(1)}, u32[]{:S(2)}, u32[]{:S(2)}) collective-permute-start(bf16[4,256,128]{2,1,0:T(8,128)(2,1)} %get-tuple-element.62), channel_id=1, source_target_pairs={{0,4},{1,5},{2,6},{3,7},{4,0},{5,1},{6,2},{7,3},{8,12},{9,13},{10,... | collective-permute-start | bytes 786440 | tf_op jit(solution)/shard_map/ppermute | solution.py:246
  71.0 21.0 %collective-permute-start.11 = (bf16[4,256,128]{2,1,0:T(8,128)(2,1)}, bf16[4,256,128]{2,1,0:T(8,128)(2,1)S(1)}, u32[]{:S(2)}, u32[]{:S(2)}) collective-permute-start(bf16[4,256,128]{2,1,0:T(8,128)(2,1)} %get-tuple-element.63), channel_id=1, source_target_pairs={{0,5},{1,6},{2,7},{3,0},{4,1},{5,2},{6,3},{7,4},{8,13},{9,14},{10,... | collective-permute-start | bytes 786440 | tf_op jit(solution)/shard_map/ppermute | solution.py:246
  72.2 53.4 %copy-start.9 = (bf16[4,256,128]{2,1,0:T(8,128)(2,1)}, bf16[4,256,128]{2,1,0:T(8,128)(2,1)S(1)}, u32[]{:S(2)}) copy-start(bf16[4,256,128]{2,1,0:T(8,128)(2,1)S(1)} %collective-permute-done.7.rest_1_) | copy-start | bytes 786436
  72.2 20.6 %collective-permute-start.12 = (bf16[4,256,128]{2,1,0:T(8,128)(2,1)}, bf16[4,256,128]{2,1,0:T(8,128)(2,1)S(1)}, u32[]{:S(2)}, u32[]{:S(2)}) collective-permute-start(bf16[4,256,128]{2,1,0:T(8,128)(2,1)} %get-tuple-element.64), channel_id=1, source_target_pairs={{0,6},{1,7},{2,0},{3,1},{4,2},{5,3},{6,4},{7,5},{8,14},{9,15},{10,... | collective-permute-start | bytes 786440 | tf_op jit(solution)/shard_map/ppermute | solution.py:246
  81.1 44.5 %copy-start.10 = (bf16[4,256,128]{2,1,0:T(8,128)(2,1)}, bf16[4,256,128]{2,1,0:T(8,128)(2,1)S(1)}, u32[]{:S(2)}) copy-start(bf16[4,256,128]{2,1,0:T(8,128)(2,1)S(1)} %collective-permute-done.8.rest_2_) | copy-start | bytes 786436
  81.2 12.8 %collective-permute-start.13 = (bf16[4,256,128]{2,1,0:T(8,128)(2,1)}, bf16[4,256,128]{2,1,0:T(8,128)(2,1)S(1)}, u32[]{:S(2)}, u32[]{:S(2)}) collective-permute-start(bf16[4,256,128]{2,1,0:T(8,128)(2,1)} %get-tuple-element.65), channel_id=1, source_target_pairs={{0,7},{1,0},{2,1},{3,2},{4,3},{5,4},{6,5},{7,6},{8,15},{9,8},{10,9... | collective-permute-start | bytes 786440 | tf_op jit(solution)/shard_map/ppermute | solution.py:246
  92.0 33.6 %copy-start.11 = (bf16[4,256,128]{2,1,0:T(8,128)(2,1)}, bf16[4,256,128]{2,1,0:T(8,128)(2,1)S(1)}, u32[]{:S(2)}) copy-start(bf16[4,256,128]{2,1,0:T(8,128)(2,1)S(1)} %collective-permute-done.9.rest_3_) | copy-start | bytes 786436
  92.0 33.6 %copy-start.12 = (bf16[4,256,128]{2,1,0:T(8,128)(2,1)}, bf16[4,256,128]{2,1,0:T(8,128)(2,1)S(1)}, u32[]{:S(2)}) copy-start(bf16[4,256,128]{2,1,0:T(8,128)(2,1)S(1)} %collective-permute-done.10.rest_4_) | copy-start | bytes 786436
  92.0 33.6 %copy-start.13 = (bf16[4,256,128]{2,1,0:T(8,128)(2,1)}, bf16[4,256,128]{2,1,0:T(8,128)(2,1)S(1)}, u32[]{:S(2)}) copy-start(bf16[4,256,128]{2,1,0:T(8,128)(2,1)S(1)} %collective-permute-done.11.rest_5_) | copy-start | bytes 786436
  92.8 32.8 %copy-start.14 = (bf16[4,256,128]{2,1,0:T(8,128)(2,1)}, bf16[4,256,128]{2,1,0:T(8,128)(2,1)S(1)}, u32[]{:S(2)}) copy-start(bf16[4,256,128]{2,1,0:T(8,128)(2,1)S(1)} %collective-permute-done.12.rest_6_) | copy-start | bytes 786436
  94.0 31.7 %copy-start.15 = (bf16[4,256,128]{2,1,0:T(8,128)(2,1)}, bf16[4,256,128]{2,1,0:T(8,128)(2,1)S(1)}, u32[]{:S(2)}) copy-start(bf16[4,256,128]{2,1,0:T(8,128)(2,1)S(1)} %collective-permute-done.13.rest_7_) | copy-start | bytes 786436
  99.4 6.9 %collective-permute-start.14 = (bf16[4,256,128]{2,1,0:T(8,128)(2,1)}, bf16[4,256,128]{2,1,0:T(8,128)(2,1)S(1)}, u32[]{:S(2)}, u32[]{:S(2)}) collective-permute-start(bf16[4,256,128]{2,1,0:T(8,128)(2,1)} %get-tuple-element.68), channel_id=1, source_target_pairs={{0,1},{1,2},{2,3},{3,4},{4,5},{5,6},{6,7},{7,0},{8,9},{9,10},{10,1... | collective-permute-start | bytes 786440 | tf_op jit(solution)/shard_map/ppermute | solution.py:246
  99.4 26.2 %collective-permute-start.15 = (bf16[4,256,128]{2,1,0:T(8,128)(2,1)}, bf16[4,256,128]{2,1,0:T(8,128)(2,1)S(1)}, u32[]{:S(2)}, u32[]{:S(2)}) collective-permute-start(bf16[4,256,128]{2,1,0:T(8,128)(2,1)} %get-tuple-element.69), channel_id=1, source_target_pairs={{0,2},{1,3},{2,4},{3,5},{4,6},{5,7},{6,0},{7,1},{8,10},{9,11},{10,... | collective-permute-start | bytes 786440 | tf_op jit(solution)/shard_map/ppermute | solution.py:246
  101.6 37.4 %collective-permute-start.16 = (bf16[4,256,128]{2,1,0:T(8,128)(2,1)}, bf16[4,256,128]{2,1,0:T(8,128)(2,1)S(1)}, u32[]{:S(2)}, u32[]{:S(2)}) collective-permute-start(bf16[4,256,128]{2,1,0:T(8,128)(2,1)} %get-tuple-element.70), channel_id=1, source_target_pairs={{0,3},{1,4},{2,5},{3,6},{4,7},{5,0},{6,1},{7,2},{8,11},{9,12},{10,... | collective-permute-start | bytes 786440 | tf_op jit(solution)/shard_map/ppermute | solution.py:246
  102.2 36.8 %collective-permute-start.17 = (bf16[4,256,128]{2,1,0:T(8,128)(2,1)}, bf16[4,256,128]{2,1,0:T(8,128)(2,1)S(1)}, u32[]{:S(2)}, u32[]{:S(2)}) collective-permute-start(bf16[4,256,128]{2,1,0:T(8,128)(2,1)} %get-tuple-element.71), channel_id=1, source_target_pairs={{0,4},{1,5},{2,6},{3,7},{4,0},{5,1},{6,2},{7,3},{8,12},{9,13},{10,... | collective-permute-start | bytes 786440 | tf_op jit(solution)/shard_map/ppermute | solution.py:246
  103.7 35.3 %collective-permute-start.18 = (bf16[4,256,128]{2,1,0:T(8,128)(2,1)}, bf16[4,256,128]{2,1,0:T(8,128)(2,1)S(1)}, u32[]{:S(2)}, u32[]{:S(2)}) collective-permute-start(bf16[4,256,128]{2,1,0:T(8,128)(2,1)} %get-tuple-element.72), channel_id=1, source_target_pairs={{0,5},{1,6},{2,7},{3,0},{4,1},{5,2},{6,3},{7,4},{8,13},{9,14},{10,... | collective-permute-start | bytes 786440 | tf_op jit(solution)/shard_map/ppermute | solution.py:246
  106.3 32.6 %copy-start.1 = (bf16[4,256,128]{2,1,0:T(8,128)(2,1)}, bf16[4,256,128]{2,1,0:T(8,128)(2,1)S(1)}, u32[]{:S(2)}) copy-start(bf16[4,256,128]{2,1,0:T(8,128)(2,1)S(1)} %collective-permute-done.14.rest_1_) | copy-start | bytes 786436
  106.3 32.7 %collective-permute-start.19 = (bf16[4,256,128]{2,1,0:T(8,128)(2,1)}, bf16[4,256,128]{2,1,0:T(8,128)(2,1)S(1)}, u32[]{:S(2)}, u32[]{:S(2)}) collective-permute-start(bf16[4,256,128]{2,1,0:T(8,128)(2,1)} %get-tuple-element.73), channel_id=1, source_target_pairs={{0,6},{1,7},{2,0},{3,1},{4,2},{5,3},{6,4},{7,5},{8,14},{9,15},{10,... | collective-permute-start | bytes 786440 | tf_op jit(solution)/shard_map/ppermute | solution.py:246
  125.6 13.4 %copy-start.2 = (bf16[4,256,128]{2,1,0:T(8,128)(2,1)}, bf16[4,256,128]{2,1,0:T(8,128)(2,1)S(1)}, u32[]{:S(2)}) copy-start(bf16[4,256,128]{2,1,0:T(8,128)(2,1)S(1)} %collective-permute-done.15.rest_2_) | copy-start | bytes 786436
  125.6 13.5 %collective-permute-start.20 = (bf16[4,256,128]{2,1,0:T(8,128)(2,1)}, bf16[4,256,128]{2,1,0:T(8,128)(2,1)S(1)}, u32[]{:S(2)}, u32[]{:S(2)}) collective-permute-start(bf16[4,256,128]{2,1,0:T(8,128)(2,1)} %get-tuple-element.74), channel_id=1, source_target_pairs={{0,7},{1,0},{2,1},{3,2},{4,3},{5,4},{6,5},{7,6},{8,15},{9,8},{10,9... | collective-permute-start | bytes 786440 | tf_op jit(solution)/shard_map/ppermute | solution.py:246
  139.0 0.9 copy-start.5
  139.1 0.9 copy-start.6
  139.1 1.0 copy-start.7
  (5 other events, 3.5 us)

commit v3 on v1

v3 whole, which is shorter than its diff:
```python
import functools
import math

import jax
import jax.numpy as jnp
import ml_dtypes
import numpy as np
from jax import lax
from jax.experimental import pallas as pl
from jax.experimental.pallas import tpu as pltpu
from jax.sharding import PartitionSpec as P

WS = 512
BINS = 128
LAGS = 64
BCH = 128
OCT = BINS // 8
ROWS = OCT * 32
SPLIT = (5, 5, 4, 2)
BEGIN = tuple(sum(SPLIT[:c]) for c in range(len(SPLIT)))
LAST = len(SPLIT) - 1
HOPS = ((0, 0), (1, 0), (3, 0), (1, 1), (3, 1), (2, 0), (2, 1), (0, 1))
VMEM_LIMIT = 56 * 1024 * 1024
PARAMS = pltpu.CompilerParams(vmem_limit_bytes=VMEM_LIMIT)


def forward_table():
    t = np.arange(WS)
    f = np.arange(1, BINS + 1)
    angle = (f[:, None] * t[None, :] % WS) * (2.0 * math.pi / WS)
    return np.concatenate([np.cos(angle), -np.sin(angle)], 0).astype(ml_dtypes.bfloat16)


def lag_table():
    f = np.arange(1, BINS + 1)
    s = np.arange(LAGS) - LAGS // 2
    angle = (s[:, None] * f[None, :] % WS) * (2.0 * math.pi / WS)
    both = np.stack([np.cos(angle), -np.sin(angle)], 1).reshape(LAGS, 2, OCT, 8)
    return both.transpose(0, 2, 1, 3).reshape(LAGS, 2 * BINS).astype(ml_dtypes.bfloat16)


def target(me, hop, members):
    z = lax.rem(me // 2 + hop[0], members // 2)
    return 2 * z + lax.rem(me + hop[1], 2)


def spectra_kernel(members, groups, meta, x_ref, table_ref, white_ref, send_ref, *own_refs):
    step = pl.program_id(0)
    polarity = 1.0 - 2.0 * meta[2 * groups + step].astype(jnp.float32)
    for w in range(2):
        spectra = lax.dot_general(
            table_ref[...],
            x_ref[:, w * WS : (w + 1) * WS],
            (((1,), (1,)), ((), ())),
            preferred_element_type=jnp.float32,
        )
        power = jnp.sum(spectra * spectra, axis=0, keepdims=True) / BINS
        white = spectra * (polarity / jnp.sqrt(power + 1e-06))
        for o in range(OCT):
            tile = jnp.concatenate(
                [white[o * 8 : o * 8 + 8], white[BINS + o * 8 : BINS + o * 8 + 8]], 0
            )
            white_ref[step, o * 32 + w * 16 : o * 32 + w * 16 + 16, :] = tile.astype(jnp.bfloat16)

    @pl.when(step == members - 1)
    def _():
        me = meta[2 * groups + members]
        for j in range(2 * groups):
            send_ref[j] = white_ref[meta[j], : 32 * SPLIT[0], :]
        for hop, own_ref in zip(HOPS, own_refs, strict=True):
            own_ref[...] = white_ref[target(me, hop, members)]


def send_kernel(meta, white_ref, *send_refs):
    for c, send_ref in enumerate(send_refs, 1):
        for j in range(send_ref.shape[0]):
            send_ref[j] = white_ref[meta[j], pl.ds(32 * BEGIN[c], 32 * SPLIT[c]), :]


def pack_kernel(members, pairs, meta, in_ref, *out_refs):
    me = meta[members * pairs]
    for hop, out_ref in zip(HOPS, out_refs, strict=True):
        to = target(me, hop, members)
        for q in range(pairs):
            out_ref[q] = in_ref[meta[to * pairs + q]]


def cross_octet(octet, local, own_refs, part_refs, rows_ref, store):
    pairs = part_refs[0].shape[0]
    depth = 32 * len(own_refs)
    at = pl.ds(pl.multiple_of(octet * 32, 32), 32)
    own = jnp.concatenate([r[at, :] for r in own_refs], 0).astype(jnp.float32)
    halves = own.reshape(depth // 16, 2, 8, BCH)
    turned = jnp.stack([halves[:, 1], -halves[:, 0]], axis=1).reshape(depth, BCH)
    rows_ref[0] = own.T
    rows_ref[1] = turned.T
    at = pl.ds(pl.multiple_of(local * 32, 32), 32)
    right = jnp.concatenate(
        [jnp.concatenate([r[q, at, :] for r in part_refs], 0) for q in range(pairs)], 1
    )
    same = (
        lax.broadcasted_iota(jnp.int32, (8, depth), 0)
        == lax.broadcasted_iota(jnp.int32, (8, depth), 1) % 8
    )
    for i0 in range(0, BCH, 16):
        tiles = []
        for i in range(i0, i0 + 16):
            for v in range(2):
                row = rows_ref[v, pl.ds(i, 8, stride=0), :]
                tiles.append(jnp.where(same, row, 0.0))
        left = jnp.concatenate(tiles, 0).astype(jnp.bfloat16)
        cross = jnp.dot(left, right, preferred_element_type=jnp.float32)
        store(i0, cross.astype(jnp.bfloat16).reshape(16, 16, pairs * BCH))


def cross_kernel(members, begin, *refs):
    own_refs, part_refs = refs[:members], refs[members : 2 * members]
    cross_ref, rows_ref = refs[2 * members :]
    step = pl.program_id(0)

    def store(i0, value):
        cross_ref[0, i0 : i0 + 16] = value

    cross_octet(begin + step, step, own_refs, part_refs, rows_ref, store)


def pair_kernel(members, lag_ref, *refs):
    own_refs, part_refs = refs[:members], refs[members : 2 * members]
    early_refs = refs[2 * members : 2 * members + LAST]
    out_ref, cross_ref, rows_ref, sem = refs[2 * members + LAST :]
    pairs = out_ref.shape[0]
    octets = SPLIT[LAST]
    step = pl.program_id(0)

    def fetch(c, block):
        at = pl.ds(block * 8, 8)
        return pltpu.make_async_copy(
            early_refs[c].at[:, at],
            cross_ref.at[pl.ds(BEGIN[c], SPLIT[c]), at],
            sem.at[c, block],
        )

    @pl.when(step == 0)
    def _():
        for block in range(BCH // 8):
            for c in range(LAST):
                fetch(c, block).start()

    @pl.when(step < octets)
    def _():
        def store(i0, value):
            cross_ref[BEGIN[LAST] + step, i0 : i0 + 16] = value

        cross_octet(BEGIN[LAST] + step, step, own_refs, part_refs, rows_ref, store)

    @pl.when(step >= octets)
    def _():
        block = step - octets
        for c in range(LAST):
            fetch(c, block).wait()
        scale = 1.0 / math.sqrt(members * 2 * BINS)
        for ii in range(8):
            right = cross_ref[:, block * 8 + ii].reshape(2 * BINS, pairs * BCH)
            lagged = jnp.dot(lag_ref[...], right, preferred_element_type=jnp.float32)
            lagged = (lagged * scale).astype(jnp.bfloat16)
            for q in range(pairs):
                out_ref[q, :, ii * BCH : (ii + 1) * BCH] = lagged[:, q * BCH : (q + 1) * BCH]


def whole(shape):
    return pl.BlockSpec(shape, lambda *_: (0,) * len(shape))


def bf16(*shape):
    return jax.ShapeDtypeStruct(shape, jnp.bfloat16)


def prefetched(grid, in_shapes, out_shapes):
    return pltpu.PrefetchScalarGridSpec(
        num_scalar_prefetch=1,
        grid=grid,
        in_specs=[whole(s) for s in in_shapes],
        out_specs=[whole(s) for s in out_shapes],
    )


def correlate(own, parts, early, pairs):
    members = len(own)
    octets = SPLIT[LAST]

    def after(s):
        return jnp.maximum(s - octets, 0)

    return pl.pallas_call(
        functools.partial(pair_kernel, members),
        grid=(octets + BCH // 8,),
        in_specs=[whole((LAGS, 2 * BINS))]
        + [whole(x.shape) for x in (*own, *parts)]
        + [pl.BlockSpec(memory_space=pl.ANY)] * LAST,
        out_specs=pl.BlockSpec((pairs, LAGS, 8 * BCH), lambda s: (0, 0, after(s))),
        out_shape=bf16(pairs, LAGS, BCH * BCH),
        scratch_shapes=[
            pltpu.VMEM((OCT, BCH, 16, pairs * BCH), jnp.bfloat16),
            pltpu.VMEM((2, BCH, 32 * members), jnp.float32),
            pltpu.SemaphoreType.DMA((LAST, BCH // 8)),
        ],
        compiler_params=PARAMS,
        name="correlate",
    )(jnp.asarray(lag_table()), *own, *parts, *early)


def crossed(c, own, parts, pairs):
    members = len(own)
    return pl.pallas_call(
        functools.partial(cross_kernel, members, BEGIN[c]),
        grid=(SPLIT[c],),
        in_specs=[whole(x.shape) for x in (*own, *parts)],
        out_specs=pl.BlockSpec((1, BCH, 16, pairs * BCH), lambda s: (s, 0, 0, 0)),
        out_shape=bf16(SPLIT[c], BCH, 16, pairs * BCH),
        scratch_shapes=[pltpu.VMEM((2, BCH, 32 * members), jnp.float32)],
        compiler_params=PARAMS,
        cost_estimate=pl.CostEstimate(
            flops=2_000_000_000 * SPLIT[c], bytes_accessed=2**21 * SPLIT[c], transcendentals=0
        ),
        name="cross",
    )(*own, *parts)


def shards(record, deck_ids, partners):
    groups = lax.axis_size("blk")
    members = lax.axis_size("win")
    group = lax.axis_index("blk")
    member = lax.axis_index("win")
    pairs = partners.shape[1]

    def move(pieces):
        moved = [pieces[0]]
        for (dz, dc), piece in zip(HOPS[1:], pieces[1:], strict=True):
            ring = members // 2
            way = [(m, (m // 2 + dz) % ring * 2 + (m + dc) % 2) for m in range(members)]
            moved.append(lax.ppermute(piece, "win", way))
        return moved

    listed = partners.reshape(groups, members * pairs)
    here = listed // members == group
    first = jnp.min(jnp.where(here, listed % members, members), axis=1)
    second = jnp.max(jnp.where(here, listed % members, -1), axis=1)
    slots = jnp.stack([first, second], axis=1).reshape(-1)
    decks = lax.dynamic_slice_in_dim(deck_ids, group * members, members, 0)
    meta = jnp.concatenate([slots, decks, member.reshape(1)]).astype(jnp.int32)
    wanted = lax.dynamic_slice_in_dim(listed, group, 1, 0).reshape(-1)
    lower = (wanted[None, :] // members == wanted[:, None] // members) & (
        wanted[None, :] < wanted[:, None]
    )
    place = 2 * (wanted // members) + jnp.any(lower, axis=1).astype(jnp.int32)
    place = jnp.concatenate([place, member.reshape(1)]).astype(jnp.int32)

    white_shape = (members, ROWS, BCH)
    send_shapes = [(2 * groups, 32 * n, BCH) for n in SPLIT]
    shapes = [white_shape, send_shapes[0]] + [(ROWS, BCH)] * members
    white, send, *own = pl.pallas_call(
        functools.partial(spectra_kernel, members, groups),
        grid_spec=pltpu.PrefetchScalarGridSpec(
            num_scalar_prefetch=1,
            grid=(members,),
            in_specs=[
                pl.BlockSpec((BCH, 2 * WS), lambda b, meta: (b, 0)),
                whole((2 * BINS, WS)),
            ],
            out_specs=[whole(s) for s in shapes],
        ),
        out_shape=[bf16(*s) for s in shapes],
        compiler_params=PARAMS,
        name="spectra",
    )(meta, record, jnp.asarray(forward_table()))
    sends = pl.pallas_call(
        send_kernel,
        grid_spec=prefetched((1,), [white_shape], send_shapes[1:]),
        out_shape=[bf16(*s) for s in send_shapes[1:]],
        compiler_params=PARAMS,
        cost_estimate=pl.CostEstimate(flops=0, bytes_accessed=2**23, transcendentals=0),
        name="send",
    )(meta, white)
    sends = [send, *sends]
    own = move(own)

    early = []
    parts = None
    for c, octets in enumerate(SPLIT):
        got = lax.all_to_all(
            sends[c].reshape(groups, 64 * octets, BCH),
            "blk",
            split_axis=0,
            concat_axis=0,
            tiled=True,
        )
        if c == 0:
            got, own, place = lax.optimization_barrier((got, own, place))
        else:
            got, parts = lax.optimization_barrier((got, parts))
            early.append(crossed(c - 1, own, parts, pairs))
        if c >= 2:
            got, early[c - 2] = lax.optimization_barrier((got, early[c - 2]))
        if c < LAST:
            got, sends[c + 1] = lax.optimization_barrier((got, sends[c + 1]))
        parts = pl.pallas_call(
            functools.partial(pack_kernel, members, pairs),
            grid_spec=prefetched(
                (1,), [send_shapes[c]], [(pairs, 32 * octets, BCH)] * members
            ),
            out_shape=[bf16(pairs, 32 * octets, BCH)] * members,
            compiler_params=PARAMS,
            name="pack",
        )(place, got.reshape(send_shapes[c]))
        parts = move(parts)
    return correlate(own, parts, early, pairs)


def solution(mesh):
    return jax.shard_map(
        shards,
        mesh=mesh,
        in_specs=(P("blk", "win"), P(), P()),
        out_specs=P(("blk", "win"), None, None),
        check_vma=False,
    )
```

time: 370 us -> 163 us (0.44)
  Pallas kernels: 210 us -> 62.1 us
  waiting for transfers between devices: 126 us -> 11.4 us
  starting transfers between devices: 27.7 us -> 80 us
  local copies, waits for them, and re-layouts: 2.03 us -> 5.76 us
    pallas_call x1 -> x4, Pallas kernels: 129 us -> 11.8 us  [shards(): pl.pallas_call(functools.partial(pack_kernel, members, pairs), grid_spec=...]
    all_to_all x1 -> x4, waiting for transfers between devices: 61.2 us -> 1.65 us  [shards(): lax.all_to_all(sends[c].reshape(groups, 64 * octets, BCH), 'blk', split_a...]
    ppermute x14 -> x35, waiting for transfers between devices: 65.2 us -> 9.79 us  [move(): moved.append(lax.ppermute(piece, 'win', way))]
    ppermute x14 -> x35, starting transfers between devices: 20 us -> 54 us  [move(): moved.append(lax.ppermute(piece, 'win', way))]
    pallas_call x1 -> x5, Pallas kernels: 72.3 us -> 41.8 us  [the longest x3 23.3 us: crossed(): pl.pallas_call(functools.partial(cross_kernel, members, BEGIN[c]), grid=(...]
    all_to_all x1 -> x4, starting transfers between devices: 7.65 us -> 26 us  [shards(): lax.all_to_all(sends[c].reshape(groups, 64 * octets, BCH), 'blk', split_a...]
    unnamed x45 -> x97, local copies, waits for them, and re-layouts: 0.88 us -> 4.6 us
  transfers between devices with their start and end apart: 15 -> 39, of which waited for: 11 -> 5; matrix products, arithmetic and copies ran while one was open for 0% -> 1% of each run, Pallas kernels for 0% -> 16%
where the time goes in v3:
time: 163 us; the launch traced here: 162 us
  starting transfers between devices  80 us (49%)
  Pallas kernels  62.1 us (38%)
  waiting for transfers between devices  11.4 us (7%)
  local copies, waits for them, and re-layouts  5.76 us (4%)
  other arithmetic  2.37 us (1%)
    ppermute x35, starting transfers between devices, move(): moved.append(lax.ppermute(piece, 'win', way))  54 us
    all_to_all x4, starting transfers between devices, shards(): lax.all_to_all(sends[c].reshape(groups, 64 * octets, BCH), 'blk', split_a...  26 us
    pallas_call x3, Pallas kernels, crossed(): pl.pallas_call(functools.partial(cross_kernel, members, BEGIN[c]), grid=(...  23.3 us
    pallas_call x1, Pallas kernels, correlate(): pl.pallas_call(functools.partial(pair_kernel, members), grid=(octets + BC...  14.9 us
    pallas_call x4, Pallas kernels, shards(): pl.pallas_call(functools.partial(pack_kernel, members, pairs), grid_spec=...  11.8 us
    ppermute x35, waiting for transfers between devices, move(): moved.append(lax.ppermute(piece, 'win', way))  9.79 us
    pallas_call x1, Pallas kernels, shards(): pl.pallas_call(functools.partial(spectra_kernel, members, groups), grid_s...  8.47 us
    unnamed x97, local copies, waits for them, and re-layouts  4.6 us
  transfers between devices with their start and end apart: 39, of which 5 were waited for; matrix products, arithmetic and copies ran while one was open for 1% of the time, Pallas kernels for 16%

profile of v3, /device:TPU:1, one launch (start us, length us, event | category | flops | bytes accessed | tf_op | source)
XLA Modules:
  0.0 162.5 jit_solution(17274065019172788039)
XLA Ops:
  0.0 0.7 select_reduce_fusion.1
  1.3 0.7 dynamic_slice.6
  2.6 8.5 %spectra.1 = (bf16[8,512,128]{2,1,0:T(8,128)(2,1)}, bf16[32,160,128]{2,1,0:T(8,128)(2,1)}, bf16[512,128]{1,0:T(8,128)(2,1)}, bf16[512,128]{1,0:T(8,128)(2,1)}, b...) custom-call(s32[41]{0:T(128)} %pad_add_fusion.1.meta, ...), custom_call_target="tpu_custom_call" | custom-call | tf_op jit(solution)/shard_map/spectra/pallas_call | solution.py:261
  11.2 7.7 %all-to-all-start = ((bf16[16,320,128]{2,1,0:T(8,128)(2,1)}), bf16[16,320,128]{2,1,0:T(8,128)(2,1)S(1)}, u32[]{:S(2)}, u32[]{:S(2)}) async-start(bf16[16,320,128]{2,1,0:T(8,128)(2,1)} %bitcast.21), calls=%async_computation | async-start | bytes 2621440 | tf_op jit(solution)/shard_map/all_to_all | solution.py:290
  18.9 1.7 %collective-permute-start = (bf16[512,128]{1,0:T(8,128)(2,1)S(1)}, bf16[512,128]{1,0:T(8,128)(2,1)S(1)}, u32[]{:S(2)}, u32[]{:S(2)}) collective-permute-start(bf16[512,128]{1,0:T(8,128)(2,1)S(1)} %copy-done.47), channel_id=1, source_target_pairs={{0,2},{1,3},{2,4},{3,5},{4,6},{5,7},{6,0},{7,1},{8,10},{9,11},{10,... | collective-permute-start | bytes 393224 | tf_op jit(solution)/shard_map/ppermute | solution.py:241
  20.6 2.2 %collective-permute-start.1 = (bf16[512,128]{1,0:T(8,128)(2,1)S(1)}, bf16[512,128]{1,0:T(8,128)(2,1)S(1)}, u32[]{:S(2)}, u32[]{:S(2)}) collective-permute-start(bf16[512,128]{1,0:T(8,128)(2,1)S(1)} %copy-done.46), channel_id=1, source_target_pairs={{0,6},{1,7},{2,0},{3,1},{4,2},{5,3},{6,4},{7,5},{8,14},{9,15},{10,... | collective-permute-start | bytes 393224 | tf_op jit(solution)/shard_map/ppermute | solution.py:241
  22.8 0.7 collective-permute-start.2
  23.5 2.3 %collective-permute-start.3 = (bf16[512,128]{1,0:T(8,128)(2,1)S(1)}, bf16[512,128]{1,0:T(8,128)(2,1)S(1)}, u32[]{:S(2)}, u32[]{:S(2)}) collective-permute-start(bf16[512,128]{1,0:T(8,128)(2,1)S(1)} %copy-done.44), channel_id=1, source_target_pairs={{0,7},{1,6},{2,1},{3,0},{4,3},{5,2},{6,5},{7,4},{8,15},{9,14},{10,... | collective-permute-start | bytes 393224 | tf_op jit(solution)/shard_map/ppermute | solution.py:241
  25.8 1.1 collective-permute-start.4
  27.3 3.4 %collective-permute-start.5 = (bf16[512,128]{1,0:T(8,128)(2,1)S(1)}, bf16[512,128]{1,0:T(8,128)(2,1)S(1)}, u32[]{:S(2)}, u32[]{:S(2)}) collective-permute-start(bf16[512,128]{1,0:T(8,128)(2,1)S(1)} %copy-done.41), channel_id=1, source_target_pairs={{0,5},{1,4},{2,7},{3,6},{4,1},{5,0},{6,3},{7,2},{8,13},{9,12},{10,... | collective-permute-start | bytes 393224 | tf_op jit(solution)/shard_map/ppermute | solution.py:241
  30.8 3.6 %send.1 = (bf16[32,160,128]{2,1,0:T(8,128)(2,1)}, bf16[32,128,128]{2,1,0:T(8,128)(2,1)}, bf16[32,64,128]{2,1,0:T(8,128)(2,1)}) custom-call(s32[41]{0:T(128)} %pad_add_fusion.1.meta, bf16[8,512,128]{2,1,0:T(8,128)(2,1)} %get-tuple-element.116.white_ref), custom_call_target="tpu_custom_call" | custom-call | bytes 8388608 | tf_op jit(solution)/shard_map/send/pallas_call | solution.py:276
  34.4 0.6 pad_add_fusion.2.meta
  35.1 1.0 collective-permute-done.5.refs_6_
  36.1 1.6 %all-to-all-done = bf16[16,320,128]{2,1,0:T(8,128)(2,1)S(1)} async-done(((bf16[16,320,128]{2,1,0:T(8,128)(2,1)}), bf16[16,320,128]{2,1,0:T(8,128)(2,1)S(1)}, u32[]{:S(2)}, u32[]{:S(2)}) %all-to-all-start) | async-done | bytes 1310752 | tf_op jit(solution)/shard_map/all_to_all | solution.py:290
  37.8 5.4 %all-to-all-start.1 = ((bf16[16,320,128]{2,1,0:T(8,128)(2,1)}), bf16[16,320,128]{2,1,0:T(8,128)(2,1)S(1)}, u32[]{:S(2)}, u32[]{:S(2)}) async-start(bf16[16,320,128]{2,1,0:T(8,128)(2,1)} %bitcast.20), calls=%async_computation.1 | async-start | bytes 2621440 | tf_op jit(solution)/shard_map/all_to_all | solution.py:290
  43.2 3.1 %pack.4 = (bf16[4,160,128]{2,1,0:T(8,128)(2,1)}, bf16[4,160,128]{2,1,0:T(8,128)(2,1)}, bf16[4,160,128]{2,1,0:T(8,128)(2,1)}, bf16[4,160,128]{2,1,0:T(8,128)(2,1)...) custom-call(s32[33]{0:T(128)} %pad_add_fusion.2.meta, ...), custom_call_target="tpu_custom_call" | custom-call | tf_op jit(solution)/shard_map/pack/pallas_call | solution.py:306
  46.3 1.7 %collective-permute-start.7 = (bf16[4,160,128]{2,1,0:T(8,128)(2,1)}, bf16[4,160,128]{2,1,0:T(8,128)(2,1)S(1)}, u32[]{:S(2)}, u32[]{:S(2)}) collective-permute-start(bf16[4,160,128]{2,1,0:T(8,128)(2,1)} %get-tuple-element.121), channel_id=1, source_target_pairs={{0,2},{1,3},{2,4},{3,5},{4,6},{5,7},{6,0},{7,1},{8,10},{9,11},{10,... | collective-permute-start | bytes 491528 | tf_op jit(solution)/shard_map/ppermute | solution.py:241
  48.0 2.2 %collective-permute-start.8 = (bf16[4,160,128]{2,1,0:T(8,128)(2,1)}, bf16[4,160,128]{2,1,0:T(8,128)(2,1)S(1)}, u32[]{:S(2)}, u32[]{:S(2)}) collective-permute-start(bf16[4,160,128]{2,1,0:T(8,128)(2,1)} %get-tuple-element.122), channel_id=1, source_target_pairs={{0,6},{1,7},{2,0},{3,1},{4,2},{5,3},{6,4},{7,5},{8,14},{9,15},{10,... | collective-permute-start | bytes 491528 | tf_op jit(solution)/shard_map/ppermute | solution.py:241
  50.2 1.0 collective-permute-start.9
  51.1 2.1 %collective-permute-start.10 = (bf16[4,160,128]{2,1,0:T(8,128)(2,1)}, bf16[4,160,128]{2,1,0:T(8,128)(2,1)S(1)}, u32[]{:S(2)}, u32[]{:S(2)}) collective-permute-start(bf16[4,160,128]{2,1,0:T(8,128)(2,1)} %get-tuple-element.124), channel_id=1, source_target_pairs={{0,7},{1,6},{2,1},{3,0},{4,3},{5,2},{6,5},{7,4},{8,15},{9,14},{10,... | collective-permute-start | bytes 491528 | tf_op jit(solution)/shard_map/ppermute | solution.py:241
  53.3 1.2 collective-permute-start.11
  54.5 3.4 %collective-permute-start.12 = (bf16[4,160,128]{2,1,0:T(8,128)(2,1)}, bf16[4,160,128]{2,1,0:T(8,128)(2,1)S(1)}, u32[]{:S(2)}, u32[]{:S(2)}) collective-permute-start(bf16[4,160,128]{2,1,0:T(8,128)(2,1)} %get-tuple-element.126), channel_id=1, source_target_pairs={{0,5},{1,4},{2,7},{3,6},{4,1},{5,0},{6,3},{7,2},{8,13},{9,12},{10,... | collective-permute-start | bytes 491528 | tf_op jit(solution)/shard_map/ppermute | solution.py:241
  58.2 4.8 %collective-permute-done.11.refs_13_ = bf16[4,160,128]{2,1,0:T(8,128)(2,1)S(1)} collective-permute-done((bf16[4,160,128]{2,1,0:T(8,128)(2,1)}, bf16[4,160,128]{2,1,0:T(8,128)(2,1)S(1)}, u32[]{:S(2)}, u32[]{:S(2)}) %collective-permute-start.11) | collective-permute-done | bytes 163872 | tf_op jit(solution)/shard_map/ppermute | solution.py:241
  63.0 3.5 %collective-permute-done.12.refs_14_ = bf16[4,160,128]{2,1,0:T(8,128)(2,1)S(1)} collective-permute-done((bf16[4,160,128]{2,1,0:T(8,128)(2,1)}, bf16[4,160,128]{2,1,0:T(8,128)(2,1)S(1)}, u32[]{:S(2)}, u32[]{:S(2)}) %collective-permute-start.12) | collective-permute-done | bytes 163872 | tf_op jit(solution)/shard_map/ppermute | solution.py:241
  66.5 0.7 copy-done.31
  67.2 1.1 copy-done.1
  68.3 3.1 %pack.5 = (bf16[4,160,128]{2,1,0:T(8,128)(2,1)}, bf16[4,160,128]{2,1,0:T(8,128)(2,1)}, bf16[4,160,128]{2,1,0:T(8,128)(2,1)}, bf16[4,160,128]{2,1,0:T(8,128)(2,1)...) custom-call(s32[33]{0:T(128)} %pad_add_fusion.2.meta, ...), custom_call_target="tpu_custom_call" | custom-call | tf_op jit(solution)/shard_map/pack/pallas_call | solution.py:306
  71.5 1.2 collective-permute-start.14
  72.6 1.6 collective-permute-start.15
  74.2 6.9 %all-to-all-start.2 = ((bf16[16,256,128]{2,1,0:T(8,128)(2,1)}), bf16[16,256,128]{2,1,0:T(8,128)(2,1)S(1)}, u32[]{:S(2)}, u32[]{:S(2)}) async-start(bf16[16,256,128]{2,1,0:T(8,128)(2,1)} %bitcast.22), calls=%async_computation.2 | async-start | bytes 2097152 | tf_op jit(solution)/shard_map/all_to_all | solution.py:290
  81.4 2.7 %collective-permute-start.17 = (bf16[4,160,128]{2,1,0:T(8,128)(2,1)}, bf16[4,160,128]{2,1,0:T(8,128)(2,1)S(1)}, u32[]{:S(2)}, u32[]{:S(2)}) collective-permute-start(bf16[4,160,128]{2,1,0:T(8,128)(2,1)} %get-tuple-element.136), channel_id=1, source_target_pairs={{0,7},{1,6},{2,1},{3,0},{4,3},{5,2},{6,5},{7,4},{8,15},{9,14},{10,... | collective-permute-start | bytes 491528 | tf_op jit(solution)/shard_map/ppermute | solution.py:241
  84.1 4.4 %collective-permute-start.19 = (bf16[4,160,128]{2,1,0:T(8,128)(2,1)S(1)}, bf16[4,160,128]{2,1,0:T(8,128)(2,1)S(1)}, u32[]{:S(2)}, u32[]{:S(2)}) collective-permute-start(bf16[4,160,128]{2,1,0:T(8,128)(2,1)S(1)} %copy-done.33), channel_id=1, source_target_pairs={{0,5},{1,4},{2,7},{3,6},{4,1},{5,0},{6,3},{7,2},{8,13},{9,12},{10,... | collective-permute-start | bytes 491528 | tf_op jit(solution)/shard_map/ppermute | solution.py:241
  88.7 8.1 %cross.3.refs_16_ = bf16[5,128,16,512]{3,2,1,0:T(8,128)(2,1)} custom-call(bf16[512,128]{1,0:T(8,128)(2,1)} %get-tuple-element.106.refs_0_, bf16[512,128]{1,0:T(8,128)(2,1)} %copy-done.4, bf16[512,128]{1,0:T(8,128)(2,1)} %copy-done.5, bf16[512,128]{1,0:T(8,128)(2,1)} %copy-done.6, bf16[512,128]{1,0:T(8,128)(2,1)} %copy-done.7, bf16[512,128]{1,0:T(8,128)(2,1)} %copy-done.8, ...), custom_call_target="tpu_custom_call" | custom-call | flops 10000000000 | bytes 10485760 | tf_op jit(solution)/shard_map/cross/pallas_call | solution.py:214
  96.9 1.1 copy-done.2
  98.0 2.9 %pack.6 = (bf16[4,128,128]{2,1,0:T(8,128)(2,1)}, bf16[4,128,128]{2,1,0:T(8,128)(2,1)}, bf16[4,128,128]{2,1,0:T(8,128)(2,1)}, bf16[4,128,128]{2,1,0:T(8,128)(2,1)...) custom-call(s32[33]{0:T(128)} %pad_add_fusion.2.meta, ...), custom_call_target="tpu_custom_call" | custom-call | tf_op jit(solution)/shard_map/pack/pallas_call | solution.py:306
  100.9 0.7 collective-permute-start.21
  101.6 2.9 %collective-permute-start.22 = (bf16[4,128,128]{2,1,0:T(8,128)(2,1)}, bf16[4,128,128]{2,1,0:T(8,128)(2,1)S(1)}, u32[]{:S(2)}, u32[]{:S(2)}) collective-permute-start(bf16[4,128,128]{2,1,0:T(8,128)(2,1)} %get-tuple-element.155), channel_id=1, source_target_pairs={{0,6},{1,7},{2,0},{3,1},{4,2},{5,3},{6,4},{7,5},{8,14},{9,15},{10,... | collective-permute-start | bytes 393224 | tf_op jit(solution)/shard_map/ppermute | solution.py:241
  104.5 5.9 %all-to-all-start.3 = ((bf16[16,128,128]{2,1,0:T(8,128)(2,1)}), bf16[16,128,128]{2,1,0:T(8,128)(2,1)S(1)}, u32[]{:S(2)}, u32[]{:S(2)}) async-start(bf16[16,128,128]{2,1,0:T(8,128)(2,1)} %bitcast.10), calls=%async_computation.3 | async-start | bytes 1048576 | tf_op jit(solution)/shard_map/all_to_all | solution.py:290
  110.5 2.9 %collective-permute-start.24 = (bf16[4,128,128]{2,1,0:T(8,128)(2,1)}, bf16[4,128,128]{2,1,0:T(8,128)(2,1)S(1)}, u32[]{:S(2)}, u32[]{:S(2)}) collective-permute-start(bf16[4,128,128]{2,1,0:T(8,128)(2,1)} %get-tuple-element.157), channel_id=1, source_target_pairs={{0,7},{1,6},{2,1},{3,0},{4,3},{5,2},{6,5},{7,4},{8,15},{9,14},{10,... | collective-permute-start | bytes 393224 | tf_op jit(solution)/shard_map/ppermute | solution.py:241
  113.5 4.4 %collective-permute-start.26 = (bf16[4,128,128]{2,1,0:T(8,128)(2,1)}, bf16[4,128,128]{2,1,0:T(8,128)(2,1)S(1)}, u32[]{:S(2)}, u32[]{:S(2)}) collective-permute-start(bf16[4,128,128]{2,1,0:T(8,128)(2,1)} %get-tuple-element.159), channel_id=1, source_target_pairs={{0,5},{1,4},{2,7},{3,6},{4,1},{5,0},{6,3},{7,2},{8,13},{9,12},{10,... | collective-permute-start | bytes 393224 | tf_op jit(solution)/shard_map/ppermute | solution.py:241
  118.0 8.2 %cross.4.refs_17_ = bf16[5,128,16,512]{3,2,1,0:T(8,128)(2,1)} custom-call(bf16[512,128]{1,0:T(8,128)(2,1)} %get-tuple-element.106.refs_0_, bf16[512,128]{1,0:T(8,128)(2,1)} %copy-done.4, bf16[512,128]{1,0:T(8,128)(2,1)} %copy-done.5, bf16[512,128]{1,0:T(8,128)(2,1)} %copy-done.6, bf16[512,128]{1,0:T(8,128)(2,1)} %copy-done.7, bf16[512,128]{1,0:T(8,128)(2,1)} %copy-done.8, ...), custom_call_target="tpu_custom_call" | custom-call | flops 10000000000 | bytes 10485760 | tf_op jit(solution)/shard_map/cross/pallas_call | solution.py:214
  126.4 0.9 copy-done.3
  127.3 2.6 %pack.7 = (bf16[4,64,128]{2,1,0:T(8,128)(2,1)}, bf16[4,64,128]{2,1,0:T(8,128)(2,1)}, bf16[4,64,128]{2,1,0:T(8,128)(2,1)}, bf16[4,64,128]{2,1,0:T(8,128)(2,1)}, b...) custom-call(s32[33]{0:T(128)} %pad_add_fusion.2.meta, ...), custom_call_target="tpu_custom_call" | custom-call | tf_op jit(solution)/shard_map/pack/pallas_call | solution.py:306
  129.8 2.7 %collective-permute-start.29 = (bf16[4,64,128]{2,1,0:T(8,128)(2,1)}, bf16[4,64,128]{2,1,0:T(8,128)(2,1)S(1)}, u32[]{:S(2)}, u32[]{:S(2)}) collective-permute-start(bf16[4,64,128]{2,1,0:T(8,128)(2,1)} %get-tuple-element.173), channel_id=1, source_target_pairs={{0,6},{1,7},{2,0},{3,1},{4,2},{5,3},{6,4},{7,5},{8,14},{9,15},{10,... | collective-permute-start | bytes 196616 | tf_op jit(solution)/shard_map/ppermute | solution.py:241
  132.5 3.0 %collective-permute-start.31 = (bf16[4,64,128]{2,1,0:T(8,128)(2,1)}, bf16[4,64,128]{2,1,0:T(8,128)(2,1)S(1)}, u32[]{:S(2)}, u32[]{:S(2)}) collective-permute-start(bf16[4,64,128]{2,1,0:T(8,128)(2,1)} %get-tuple-element.175), channel_id=1, source_target_pairs={{0,7},{1,6},{2,1},{3,0},{4,3},{5,2},{6,5},{7,4},{8,15},{9,14},{10,... | collective-permute-start | bytes 196616 | tf_op jit(solution)/shard_map/ppermute | solution.py:241
  135.5 4.2 %collective-permute-start.33 = (bf16[4,64,128]{2,1,0:T(8,128)(2,1)}, bf16[4,64,128]{2,1,0:T(8,128)(2,1)S(1)}, u32[]{:S(2)}, u32[]{:S(2)}) collective-permute-start(bf16[4,64,128]{2,1,0:T(8,128)(2,1)} %get-tuple-element.177), channel_id=1, source_target_pairs={{0,5},{1,4},{2,7},{3,6},{4,1},{5,0},{6,3},{7,2},{8,13},{9,12},{10,... | collective-permute-start | bytes 196616 | tf_op jit(solution)/shard_map/ppermute | solution.py:241
  139.7 7.0 %cross.5.refs_18_ = bf16[4,128,16,512]{3,2,1,0:T(8,128)(2,1)} custom-call(bf16[512,128]{1,0:T(8,128)(2,1)} %get-tuple-element.106.refs_0_, bf16[512,128]{1,0:T(8,128)(2,1)} %copy-done.4, bf16[512,128]{1,0:T(8,128)(2,1)} %copy-done.5, bf16[512,128]{1,0:T(8,128)(2,1)} %copy-done.6, bf16[512,128]{1,0:T(8,128)(2,1)} %copy-done.7, bf16[512,128]{1,0:T(8,128)(2,1)} %copy-done.8, ...), custom_call_target="tpu_custom_call" | custom-call | flops 8000000000 | bytes 8388608 | tf_op jit(solution)/shard_map/cross/pallas_call | solution.py:214
  147.4 14.9 %correlate.1 = bf16[4,64,16384]{2,1,0:T(8,128)(2,1)} custom-call(bf16[64,256]{1,0:T(8,128)(2,1)} %constant.86.clone.lag_ref, bf16[512,128]{1,0:T(8,128)(2,1)} %get-tuple-element.106.refs_0_, bf16[512,128]{1,0:T(8,128)(2,1)} %copy-done.4, bf16[512,128]{1,0:T(8,128)(2,1)} %copy-done.5, bf16[512,128]{1,0:T(8,128)(2,1)} %copy-done.6, ...), custom_call_target="tpu_custom_call" | custom-call | tf_op jit(solution)/shard_map/correlate/pallas_call | solution.py:194
  (153 shorter events, 3.4 us)
Async XLA Ops:
  2.6 24.3 %copy-start.18 = (s32[128,4]{0,1:T(4,128)S(1)}, s32[128,4]{0,1:T(4,128)}, u32[]{:S(2)}) copy-start(s32[128,4]{0,1:T(4,128)} %param.7) | copy-start | bytes 6148
  11.2 26.6 %all-to-all-start = ((bf16[16,320,128]{2,1,0:T(8,128)(2,1)}), bf16[16,320,128]{2,1,0:T(8,128)(2,1)S(1)}, u32[]{:S(2)}, u32[]{:S(2)}) async-start(bf16[16,320,128]{2,1,0:T(8,128)(2,1)} %bitcast.21), calls=%async_computation | async-start | bytes 2621440 | tf_op jit(solution)/shard_map/all_to_all | solution.py:290
  18.9 8.4 %collective-permute-start = (bf16[512,128]{1,0:T(8,128)(2,1)S(1)}, bf16[512,128]{1,0:T(8,128)(2,1)S(1)}, u32[]{:S(2)}, u32[]{:S(2)}) collective-permute-start(bf16[512,128]{1,0:T(8,128)(2,1)S(1)} %copy-done.47), channel_id=1, source_target_pairs={{0,2},{1,3},{2,4},{3,5},{4,6},{5,7},{6,0},{7,1},{8,10},{9,11},{10,... | collective-permute-start | bytes 393224 | tf_op jit(solution)/shard_map/ppermute | solution.py:241
  20.6 10.1 %collective-permute-start.1 = (bf16[512,128]{1,0:T(8,128)(2,1)S(1)}, bf16[512,128]{1,0:T(8,128)(2,1)S(1)}, u32[]{:S(2)}, u32[]{:S(2)}) collective-permute-start(bf16[512,128]{1,0:T(8,128)(2,1)S(1)} %copy-done.46), channel_id=1, source_target_pairs={{0,6},{1,7},{2,0},{3,1},{4,2},{5,3},{6,4},{7,5},{8,14},{9,15},{10,... | collective-permute-start | bytes 393224 | tf_op jit(solution)/shard_map/ppermute | solution.py:241
  22.8 12.2 %collective-permute-start.2 = (bf16[512,128]{1,0:T(8,128)(2,1)S(1)}, bf16[512,128]{1,0:T(8,128)(2,1)S(1)}, u32[]{:S(2)}, u32[]{:S(2)}) collective-permute-start(bf16[512,128]{1,0:T(8,128)(2,1)S(1)} %copy-done.45), channel_id=1, source_target_pairs={{0,3},{1,2},{2,5},{3,4},{4,7},{5,6},{6,1},{7,0},{8,11},{9,10},{10,... | collective-permute-start | bytes 393224 | tf_op jit(solution)/shard_map/ppermute | solution.py:241
  23.5 11.5 %collective-permute-start.3 = (bf16[512,128]{1,0:T(8,128)(2,1)S(1)}, bf16[512,128]{1,0:T(8,128)(2,1)S(1)}, u32[]{:S(2)}, u32[]{:S(2)}) collective-permute-start(bf16[512,128]{1,0:T(8,128)(2,1)S(1)} %copy-done.44), channel_id=1, source_target_pairs={{0,7},{1,6},{2,1},{3,0},{4,3},{5,2},{6,5},{7,4},{8,15},{9,14},{10,... | collective-permute-start | bytes 393224 | tf_op jit(solution)/shard_map/ppermute | solution.py:241
  25.8 9.3 %collective-permute-start.4 = (bf16[512,128]{1,0:T(8,128)(2,1)S(1)}, bf16[512,128]{1,0:T(8,128)(2,1)S(1)}, u32[]{:S(2)}, u32[]{:S(2)}) collective-permute-start(bf16[512,128]{1,0:T(8,128)(2,1)S(1)} %copy-done.43), channel_id=1, source_target_pairs={{0,4},{1,5},{2,6},{3,7},{4,0},{5,1},{6,2},{7,3},{8,12},{9,13},{10,... | collective-permute-start | bytes 393224 | tf_op jit(solution)/shard_map/ppermute | solution.py:241
  27.3 8.8 %collective-permute-start.5 = (bf16[512,128]{1,0:T(8,128)(2,1)S(1)}, bf16[512,128]{1,0:T(8,128)(2,1)S(1)}, u32[]{:S(2)}, u32[]{:S(2)}) collective-permute-start(bf16[512,128]{1,0:T(8,128)(2,1)S(1)} %copy-done.41), channel_id=1, source_target_pairs={{0,5},{1,4},{2,7},{3,6},{4,1},{5,0},{6,3},{7,2},{8,13},{9,12},{10,... | collective-permute-start | bytes 393224 | tf_op jit(solution)/shard_map/ppermute | solution.py:241
  30.7 5.4 %collective-permute-start.6 = (bf16[512,128]{1,0:T(8,128)(2,1)S(1)}, bf16[512,128]{1,0:T(8,128)(2,1)S(1)}, u32[]{:S(2)}, u32[]{:S(2)}) collective-permute-start(bf16[512,128]{1,0:T(8,128)(2,1)S(1)} %copy-done.40), channel_id=1, source_target_pairs={{0,1},{1,0},{2,3},{3,2},{4,5},{5,4},{6,7},{7,6},{8,9},{9,8},{10,11... | collective-permute-start | bytes 393224 | tf_op jit(solution)/shard_map/ppermute | solution.py:241
  35.0 36.4 %copy-start.6 = (bf16[512,128]{1,0:T(8,128)(2,1)}, bf16[512,128]{1,0:T(8,128)(2,1)S(1)}, u32[]{:S(2)}) copy-start(bf16[512,128]{1,0:T(8,128)(2,1)S(1)} %collective-permute-done.2.refs_3_) | copy-start | bytes 393220
  35.1 36.4 %copy-start.7 = (bf16[512,128]{1,0:T(8,128)(2,1)}, bf16[512,128]{1,0:T(8,128)(2,1)S(1)}, u32[]{:S(2)}) copy-start(bf16[512,128]{1,0:T(8,128)(2,1)S(1)} %collective-permute-done.3.refs_4_) | copy-start | bytes 393220
  35.1 36.3 %copy-start.8 = (bf16[512,128]{1,0:T(8,128)(2,1)}, bf16[512,128]{1,0:T(8,128)(2,1)S(1)}, u32[]{:S(2)}) copy-start(bf16[512,128]{1,0:T(8,128)(2,1)S(1)} %collective-permute-done.4.refs_5_) | copy-start | bytes 393220
  36.1 35.3 %copy-start.9 = (bf16[512,128]{1,0:T(8,128)(2,1)}, bf16[512,128]{1,0:T(8,128)(2,1)S(1)}, u32[]{:S(2)}) copy-start(bf16[512,128]{1,0:T(8,128)(2,1)S(1)} %collective-permute-done.5.refs_6_) | copy-start | bytes 393220
  36.1 35.3 %copy-start.10 = (bf16[512,128]{1,0:T(8,128)(2,1)}, bf16[512,128]{1,0:T(8,128)(2,1)S(1)}, u32[]{:S(2)}) copy-start(bf16[512,128]{1,0:T(8,128)(2,1)S(1)} %collective-permute-done.6.refs_7_) | copy-start | bytes 393220
  37.8 29.4 %all-to-all-start.1 = ((bf16[16,320,128]{2,1,0:T(8,128)(2,1)}), bf16[16,320,128]{2,1,0:T(8,128)(2,1)S(1)}, u32[]{:S(2)}, u32[]{:S(2)}) async-start(bf16[16,320,128]{2,1,0:T(8,128)(2,1)} %bitcast.20), calls=%async_computation.1 | async-start | bytes 2621440 | tf_op jit(solution)/shard_map/all_to_all | solution.py:290
  46.3 8.1 %collective-permute-start.7 = (bf16[4,160,128]{2,1,0:T(8,128)(2,1)}, bf16[4,160,128]{2,1,0:T(8,128)(2,1)S(1)}, u32[]{:S(2)}, u32[]{:S(2)}) collective-permute-start(bf16[4,160,128]{2,1,0:T(8,128)(2,1)} %get-tuple-element.121), channel_id=1, source_target_pairs={{0,2},{1,3},{2,4},{3,5},{4,6},{5,7},{6,0},{7,1},{8,10},{9,11},{10,... | collective-permute-start | bytes 491528 | tf_op jit(solution)/shard_map/ppermute | solution.py:241
  48.0 9.8 %collective-permute-start.8 = (bf16[4,160,128]{2,1,0:T(8,128)(2,1)}, bf16[4,160,128]{2,1,0:T(8,128)(2,1)S(1)}, u32[]{:S(2)}, u32[]{:S(2)}) collective-permute-start(bf16[4,160,128]{2,1,0:T(8,128)(2,1)} %get-tuple-element.122), channel_id=1, source_target_pairs={{0,6},{1,7},{2,0},{3,1},{4,2},{5,3},{6,4},{7,5},{8,14},{9,15},{10,... | collective-permute-start | bytes 491528 | tf_op jit(solution)/shard_map/ppermute | solution.py:241
  50.2 7.7 %collective-permute-start.9 = (bf16[4,160,128]{2,1,0:T(8,128)(2,1)}, bf16[4,160,128]{2,1,0:T(8,128)(2,1)S(1)}, u32[]{:S(2)}, u32[]{:S(2)}) collective-permute-start(bf16[4,160,128]{2,1,0:T(8,128)(2,1)} %get-tuple-element.123), channel_id=1, source_target_pairs={{0,3},{1,2},{2,5},{3,4},{4,7},{5,6},{6,1},{7,0},{8,11},{9,10},{10,... | collective-permute-start | bytes 491528 | tf_op jit(solution)/shard_map/ppermute | solution.py:241
  51.1 7.1 %collective-permute-start.10 = (bf16[4,160,128]{2,1,0:T(8,128)(2,1)}, bf16[4,160,128]{2,1,0:T(8,128)(2,1)S(1)}, u32[]{:S(2)}, u32[]{:S(2)}) collective-permute-start(bf16[4,160,128]{2,1,0:T(8,128)(2,1)} %get-tuple-element.124), channel_id=1, source_target_pairs={{0,7},{1,6},{2,1},{3,0},{4,3},{5,2},{6,5},{7,4},{8,15},{9,14},{10,... | collective-permute-start | bytes 491528 | tf_op jit(solution)/shard_map/ppermute | solution.py:241
  53.3 9.7 %collective-permute-start.11 = (bf16[4,160,128]{2,1,0:T(8,128)(2,1)}, bf16[4,160,128]{2,1,0:T(8,128)(2,1)S(1)}, u32[]{:S(2)}, u32[]{:S(2)}) collective-permute-start(bf16[4,160,128]{2,1,0:T(8,128)(2,1)} %get-tuple-element.125), channel_id=1, source_target_pairs={{0,4},{1,5},{2,6},{3,7},{4,0},{5,1},{6,2},{7,3},{8,12},{9,13},{10,... | collective-permute-start | bytes 491528 | tf_op jit(solution)/shard_map/ppermute | solution.py:241
  54.5 34.2 %copy-start.23 = (bf16[4,160,128]{2,1,0:T(8,128)(2,1)}, bf16[4,160,128]{2,1,0:T(8,128)(2,1)S(1)}, u32[]{:S(2)}) copy-start(bf16[4,160,128]{2,1,0:T(8,128)(2,1)S(1)} %collective-permute-done.7.refs_9_) | copy-start | bytes 491524
  54.5 12.0 %collective-permute-start.12 = (bf16[4,160,128]{2,1,0:T(8,128)(2,1)}, bf16[4,160,128]{2,1,0:T(8,128)(2,1)S(1)}, u32[]{:S(2)}, u32[]{:S(2)}) collective-permute-start(bf16[4,160,128]{2,1,0:T(8,128)(2,1)} %get-tuple-element.126), channel_id=1, source_target_pairs={{0,5},{1,4},{2,7},{3,6},{4,1},{5,0},{6,3},{7,2},{8,13},{9,12},{10,... | collective-permute-start | bytes 491528 | tf_op jit(solution)/shard_map/ppermute | solution.py:241
  57.8 9.4 %collective-permute-start.13 = (bf16[4,160,128]{2,1,0:T(8,128)(2,1)}, bf16[4,160,128]{2,1,0:T(8,128)(2,1)}, u32[]{:S(2)}, u32[]{:S(2)}) collective-permute-start(bf16[4,160,128]{2,1,0:T(8,128)(2,1)} %get-tuple-element.127), channel_id=1, source_target_pairs={{0,1},{1,0},{2,3},{3,2},{4,5},{5,4},{6,7},{7,6},{8,9},{9,8},{10,11... | collective-permute-start | bytes 491528 | tf_op jit(solution)/shard_map/ppermute | solution.py:241
  71.5 12.7 %collective-permute-start.14 = (bf16[4,160,128]{2,1,0:T(8,128)(2,1)}, bf16[4,160,128]{2,1,0:T(8,128)(2,1)S(1)}, u32[]{:S(2)}, u32[]{:S(2)}) collective-permute-start(bf16[4,160,128]{2,1,0:T(8,128)(2,1)} %get-tuple-element.133), channel_id=1, source_target_pairs={{0,2},{1,3},{2,4},{3,5},{4,6},{5,7},{6,0},{7,1},{8,10},{9,11},{10,... | collective-permute-start | bytes 491528 | tf_op jit(solution)/shard_map/ppermute | solution.py:241
  72.6 15.9 %collective-permute-start.15 = (bf16[4,160,128]{2,1,0:T(8,128)(2,1)}, bf16[4,160,128]{2,1,0:T(8,128)(2,1)S(1)}, u32[]{:S(2)}, u32[]{:S(2)}) collective-permute-start(bf16[4,160,128]{2,1,0:T(8,128)(2,1)} %get-tuple-element.134), channel_id=1, source_target_pairs={{0,6},{1,7},{2,0},{3,1},{4,2},{5,3},{6,4},{7,5},{8,14},{9,15},{10,... | collective-permute-start | bytes 491528 | tf_op jit(solution)/shard_map/ppermute | solution.py:241
  74.2 22.7 %all-to-all-start.2 = ((bf16[16,256,128]{2,1,0:T(8,128)(2,1)}), bf16[16,256,128]{2,1,0:T(8,128)(2,1)S(1)}, u32[]{:S(2)}, u32[]{:S(2)}) async-start(bf16[16,256,128]{2,1,0:T(8,128)(2,1)} %bitcast.22), calls=%async_computation.2 | async-start | bytes 2097152 | tf_op jit(solution)/shard_map/all_to_all | solution.py:290
  81.1 15.7 %collective-permute-start.16 = (bf16[4,160,128]{2,1,0:T(8,128)(2,1)}, bf16[4,160,128]{2,1,0:T(8,128)(2,1)S(1)}, u32[]{:S(2)}, u32[]{:S(2)}) collective-permute-start(bf16[4,160,128]{2,1,0:T(8,128)(2,1)} %get-tuple-element.135), channel_id=1, source_target_pairs={{0,3},{1,2},{2,5},{3,4},{4,7},{5,6},{6,1},{7,0},{8,11},{9,10},{10,... | collective-permute-start | bytes 491528 | tf_op jit(solution)/shard_map/ppermute | solution.py:241
  81.4 15.4 %collective-permute-start.17 = (bf16[4,160,128]{2,1,0:T(8,128)(2,1)}, bf16[4,160,128]{2,1,0:T(8,128)(2,1)S(1)}, u32[]{:S(2)}, u32[]{:S(2)}) collective-permute-start(bf16[4,160,128]{2,1,0:T(8,128)(2,1)} %get-tuple-element.136), channel_id=1, source_target_pairs={{0,7},{1,6},{2,1},{3,0},{4,3},{5,2},{6,5},{7,4},{8,15},{9,14},{10,... | collective-permute-start | bytes 491528 | tf_op jit(solution)/shard_map/ppermute | solution.py:241
  84.1 12.7 %collective-permute-start.18 = (bf16[4,160,128]{2,1,0:T(8,128)(2,1)}, bf16[4,160,128]{2,1,0:T(8,128)(2,1)S(1)}, u32[]{:S(2)}, u32[]{:S(2)}) collective-permute-start(bf16[4,160,128]{2,1,0:T(8,128)(2,1)} %get-tuple-element.137), channel_id=1, source_target_pairs={{0,4},{1,5},{2,6},{3,7},{4,0},{5,1},{6,2},{7,3},{8,12},{9,13},{10,... | collective-permute-start | bytes 491528 | tf_op jit(solution)/shard_map/ppermute | solution.py:241
  84.1 12.7 %collective-permute-start.19 = (bf16[4,160,128]{2,1,0:T(8,128)(2,1)S(1)}, bf16[4,160,128]{2,1,0:T(8,128)(2,1)S(1)}, u32[]{:S(2)}, u32[]{:S(2)}) collective-permute-start(bf16[4,160,128]{2,1,0:T(8,128)(2,1)S(1)} %copy-done.33), channel_id=1, source_target_pairs={{0,5},{1,4},{2,7},{3,6},{4,1},{5,0},{6,3},{7,2},{8,13},{9,12},{10,... | collective-permute-start | bytes 491528 | tf_op jit(solution)/shard_map/ppermute | solution.py:241
  88.6 8.3 %collective-permute-start.20 = (bf16[4,160,128]{2,1,0:T(8,128)(2,1)S(1)}, bf16[4,160,128]{2,1,0:T(8,128)(2,1)S(1)}, u32[]{:S(2)}, u32[]{:S(2)}) collective-permute-start(bf16[4,160,128]{2,1,0:T(8,128)(2,1)S(1)} %copy-done.32), channel_id=1, source_target_pairs={{0,1},{1,0},{2,3},{3,2},{4,5},{5,4},{6,7},{7,6},{8,9},{9,8},{10,11... | collective-permute-start | bytes 491528 | tf_op jit(solution)/shard_map/ppermute | solution.py:241
  96.8 21.2 %copy-start.21 = (bf16[4,160,128]{2,1,0:T(8,128)(2,1)}, bf16[4,160,128]{2,1,0:T(8,128)(2,1)S(1)}, u32[]{:S(2)}) copy-start(bf16[4,160,128]{2,1,0:T(8,128)(2,1)S(1)} %collective-permute-done.16.refs_11_) | copy-start | bytes 491524
  96.8 21.2 %copy-start.22 = (bf16[4,160,128]{2,1,0:T(8,128)(2,1)}, bf16[4,160,128]{2,1,0:T(8,128)(2,1)S(1)}, u32[]{:S(2)}) copy-start(bf16[4,160,128]{2,1,0:T(8,128)(2,1)S(1)} %collective-permute-done.17.refs_12_) | copy-start | bytes 491524
  100.9 12.6 %collective-permute-start.21 = (bf16[4,128,128]{2,1,0:T(8,128)(2,1)}, bf16[4,128,128]{2,1,0:T(8,128)(2,1)S(1)}, u32[]{:S(2)}, u32[]{:S(2)}) collective-permute-start(bf16[4,128,128]{2,1,0:T(8,128)(2,1)} %get-tuple-element.154), channel_id=1, source_target_pairs={{0,2},{1,3},{2,4},{3,5},{4,6},{5,7},{6,0},{7,1},{8,10},{9,11},{10,... | collective-permute-start | bytes 393224 | tf_op jit(solution)/shard_map/ppermute | solution.py:241
  101.6 16.4 %collective-permute-start.22 = (bf16[4,128,128]{2,1,0:T(8,128)(2,1)}, bf16[4,128,128]{2,1,0:T(8,128)(2,1)S(1)}, u32[]{:S(2)}, u32[]{:S(2)}) collective-permute-start(bf16[4,128,128]{2,1,0:T(8,128)(2,1)} %get-tuple-element.155), channel_id=1, source_target_pairs={{0,6},{1,7},{2,0},{3,1},{4,2},{5,3},{6,4},{7,5},{8,14},{9,15},{10,... | collective-permute-start | bytes 393224 | tf_op jit(solution)/shard_map/ppermute | solution.py:241
  104.5 21.9 %all-to-all-start.3 = ((bf16[16,128,128]{2,1,0:T(8,128)(2,1)}), bf16[16,128,128]{2,1,0:T(8,128)(2,1)S(1)}, u32[]{:S(2)}, u32[]{:S(2)}) async-start(bf16[16,128,128]{2,1,0:T(8,128)(2,1)} %bitcast.10), calls=%async_computation.3 | async-start | bytes 1048576 | tf_op jit(solution)/shard_map/all_to_all | solution.py:290
  110.4 15.8 %collective-permute-start.23 = (bf16[4,128,128]{2,1,0:T(8,128)(2,1)}, bf16[4,128,128]{2,1,0:T(8,128)(2,1)S(1)}, u32[]{:S(2)}, u32[]{:S(2)}) collective-permute-start(bf16[4,128,128]{2,1,0:T(8,128)(2,1)} %get-tuple-element.156), channel_id=1, source_target_pairs={{0,3},{1,2},{2,5},{3,4},{4,7},{5,6},{6,1},{7,0},{8,11},{9,10},{10,... | collective-permute-start | bytes 393224 | tf_op jit(solution)/shard_map/ppermute | solution.py:241
  110.5 15.7 %collective-permute-start.24 = (bf16[4,128,128]{2,1,0:T(8,128)(2,1)}, bf16[4,128,128]{2,1,0:T(8,128)(2,1)S(1)}, u32[]{:S(2)}, u32[]{:S(2)}) collective-permute-start(bf16[4,128,128]{2,1,0:T(8,128)(2,1)} %get-tuple-element.157), channel_id=1, source_target_pairs={{0,7},{1,6},{2,1},{3,0},{4,3},{5,2},{6,5},{7,4},{8,15},{9,14},{10,... | collective-permute-start | bytes 393224 | tf_op jit(solution)/shard_map/ppermute | solution.py:241
  113.5 12.8 %collective-permute-start.25 = (bf16[4,128,128]{2,1,0:T(8,128)(2,1)}, bf16[4,128,128]{2,1,0:T(8,128)(2,1)S(1)}, u32[]{:S(2)}, u32[]{:S(2)}) collective-permute-start(bf16[4,128,128]{2,1,0:T(8,128)(2,1)} %get-tuple-element.158), channel_id=1, source_target_pairs={{0,4},{1,5},{2,6},{3,7},{4,0},{5,1},{6,2},{7,3},{8,12},{9,13},{10,... | collective-permute-start | bytes 393224 | tf_op jit(solution)/shard_map/ppermute | solution.py:241
  113.5 12.8 %collective-permute-start.26 = (bf16[4,128,128]{2,1,0:T(8,128)(2,1)}, bf16[4,128,128]{2,1,0:T(8,128)(2,1)S(1)}, u32[]{:S(2)}, u32[]{:S(2)}) collective-permute-start(bf16[4,128,128]{2,1,0:T(8,128)(2,1)} %get-tuple-element.159), channel_id=1, source_target_pairs={{0,5},{1,4},{2,7},{3,6},{4,1},{5,0},{6,3},{7,2},{8,13},{9,12},{10,... | collective-permute-start | bytes 393224 | tf_op jit(solution)/shard_map/ppermute | solution.py:241
  117.9 8.4 %collective-permute-start.27 = (bf16[4,128,128]{2,1,0:T(8,128)(2,1)}, bf16[4,128,128]{2,1,0:T(8,128)(2,1)S(1)}, u32[]{:S(2)}, u32[]{:S(2)}) collective-permute-start(bf16[4,128,128]{2,1,0:T(8,128)(2,1)} %get-tuple-element.160), channel_id=1, source_target_pairs={{0,1},{1,0},{2,3},{3,2},{4,5},{5,4},{6,7},{7,6},{8,9},{9,8},{10,11... | collective-permute-start | bytes 393224 | tf_op jit(solution)/shard_map/ppermute | solution.py:241
  129.8 5.6 %collective-permute-start.28 = (bf16[4,64,128]{2,1,0:T(8,128)(2,1)}, bf16[4,64,128]{2,1,0:T(8,128)(2,1)S(1)}, u32[]{:S(2)}, u32[]{:S(2)}) collective-permute-start(bf16[4,64,128]{2,1,0:T(8,128)(2,1)} %get-tuple-element.172), channel_id=1, source_target_pairs={{0,2},{1,3},{2,4},{3,5},{4,6},{5,7},{6,0},{7,1},{8,10},{9,11},{10,... | collective-permute-start | bytes 196616 | tf_op jit(solution)/shard_map/ppermute | solution.py:241
  129.8 9.8 %collective-permute-start.29 = (bf16[4,64,128]{2,1,0:T(8,128)(2,1)}, bf16[4,64,128]{2,1,0:T(8,128)(2,1)S(1)}, u32[]{:S(2)}, u32[]{:S(2)}) collective-permute-start(bf16[4,64,128]{2,1,0:T(8,128)(2,1)} %get-tuple-element.173), channel_id=1, source_target_pairs={{0,6},{1,7},{2,0},{3,1},{4,2},{5,3},{6,4},{7,5},{8,14},{9,15},{10,... | collective-permute-start | bytes 196616 | tf_op jit(solution)/shard_map/ppermute | solution.py:241
  132.5 14.2 %collective-permute-start.30 = (bf16[4,64,128]{2,1,0:T(8,128)(2,1)}, bf16[4,64,128]{2,1,0:T(8,128)(2,1)S(1)}, u32[]{:S(2)}, u32[]{:S(2)}) collective-permute-start(bf16[4,64,128]{2,1,0:T(8,128)(2,1)} %get-tuple-element.174), channel_id=1, source_target_pairs={{0,3},{1,2},{2,5},{3,4},{4,7},{5,6},{6,1},{7,0},{8,11},{9,10},{10,... | collective-permute-start | bytes 196616 | tf_op jit(solution)/shard_map/ppermute | solution.py:241
  132.5 14.2 %collective-permute-start.31 = (bf16[4,64,128]{2,1,0:T(8,128)(2,1)}, bf16[4,64,128]{2,1,0:T(8,128)(2,1)S(1)}, u32[]{:S(2)}, u32[]{:S(2)}) collective-permute-start(bf16[4,64,128]{2,1,0:T(8,128)(2,1)} %get-tuple-element.175), channel_id=1, source_target_pairs={{0,7},{1,6},{2,1},{3,0},{4,3},{5,2},{6,5},{7,4},{8,15},{9,14},{10,... | collective-permute-start | bytes 196616 | tf_op jit(solution)/shard_map/ppermute | solution.py:241
  135.5 11.2 %collective-permute-start.32 = (bf16[4,64,128]{2,1,0:T(8,128)(2,1)}, bf16[4,64,128]{2,1,0:T(8,128)(2,1)S(1)}, u32[]{:S(2)}, u32[]{:S(2)}) collective-permute-start(bf16[4,64,128]{2,1,0:T(8,128)(2,1)} %get-tuple-element.176), channel_id=1, source_target_pairs={{0,4},{1,5},{2,6},{3,7},{4,0},{5,1},{6,2},{7,3},{8,12},{9,13},{10,... | collective-permute-start | bytes 196616 | tf_op jit(solution)/shard_map/ppermute | solution.py:241
  135.5 11.3 %collective-permute-start.33 = (bf16[4,64,128]{2,1,0:T(8,128)(2,1)}, bf16[4,64,128]{2,1,0:T(8,128)(2,1)S(1)}, u32[]{:S(2)}, u32[]{:S(2)}) collective-permute-start(bf16[4,64,128]{2,1,0:T(8,128)(2,1)} %get-tuple-element.177), channel_id=1, source_target_pairs={{0,5},{1,4},{2,7},{3,6},{4,1},{5,0},{6,3},{7,2},{8,13},{9,12},{10,... | collective-permute-start | bytes 196616 | tf_op jit(solution)/shard_map/ppermute | solution.py:241
  139.6 7.1 %collective-permute-start.34 = (bf16[4,64,128]{2,1,0:T(8,128)(2,1)}, bf16[4,64,128]{2,1,0:T(8,128)(2,1)S(1)}, u32[]{:S(2)}, u32[]{:S(2)}) collective-permute-start(bf16[4,64,128]{2,1,0:T(8,128)(2,1)} %get-tuple-element.178), channel_id=1, source_target_pairs={{0,1},{1,0},{2,3},{3,2},{4,5},{5,4},{6,7},{7,6},{8,9},{9,8},{10,11... | collective-permute-start | bytes 196616 | tf_op jit(solution)/shard_map/ppermute | solution.py:241
  (39 other events, 388.2 us)

commit v4 on v3

--- a/solution.py
+++ b/solution.py
@@ -16,12 +16,12 @@
 BCH = 128
 OCT = BINS // 8
 ROWS = OCT * 32
-SPLIT = (5, 5, 4, 2)
+SPLIT = (7, 9)
 BEGIN = tuple(sum(SPLIT[:c]) for c in range(len(SPLIT)))
 LAST = len(SPLIT) - 1
+AT_ONCE = 4
 HOPS = ((0, 0), (1, 0), (3, 0), (1, 1), (3, 1), (2, 0), (2, 1), (0, 1))
-VMEM_LIMIT = 56 * 1024 * 1024
-PARAMS = pltpu.CompilerParams(vmem_limit_bytes=VMEM_LIMIT)
+IN_VMEM = pl.BlockSpec(memory_space=pltpu.VMEM)
 
 
 def forward_table():
@@ -46,7 +46,6 @@
 
 def spectra_kernel(members, groups, meta, x_ref, table_ref, white_ref, send_ref, *own_refs):
     step = pl.program_id(0)
-    polarity = 1.0 - 2.0 * meta[2 * groups + step].astype(jnp.float32)
     for w in range(2):
         spectra = lax.dot_general(
             table_ref[...],
@@ -55,14 +54,20 @@
             preferred_element_type=jnp.float32,
         )
         power = jnp.sum(spectra * spectra, axis=0, keepdims=True) / BINS
-        white = spectra * (polarity / jnp.sqrt(power + 1e-06))
-        for o in range(OCT):
-            tile = jnp.concatenate(
-                [white[o * 8 : o * 8 + 8], white[BINS + o * 8 : BINS + o * 8 + 8]], 0
-            )
-            white_ref[step, o * 32 + w * 16 : o * 32 + w * 16 + 16, :] = tile.astype(jnp.bfloat16)
-
-    @pl.when(step == members - 1)
+        root = jnp.sqrt(power + 1e-06)
+        for b in range(AT_ONCE):
+            block = step * AT_ONCE + b
+            at = slice(b * BCH, (b + 1) * BCH)
+            polarity = 1.0 - 2.0 * meta[2 * groups + block].astype(jnp.float32)
+            white = spectra[:, at] * (polarity / root[:, at])
+            for o in range(OCT):
+                tile = jnp.concatenate(
+                    [white[o * 8 : o * 8 + 8], white[BINS + o * 8 : BINS + o * 8 + 8]], 0
+                )
+                row = o * 32 + w * 16
+                white_ref[block, row : row + 16, :] = tile.astype(jnp.bfloat16)
+
+    @pl.when(step == members // AT_ONCE - 1)
     def _():
         me = meta[2 * groups + members]
         for j in range(2 * groups):
@@ -167,20 +172,17 @@
                 out_ref[q, :, ii * BCH : (ii + 1) * BCH] = lagged[:, q * BCH : (q + 1) * BCH]
 
 
-def whole(shape):
-    return pl.BlockSpec(shape, lambda *_: (0,) * len(shape))
+def params(mib):
+    return pltpu.CompilerParams(vmem_limit_bytes=mib * 1024 * 1024)
 
 
 def bf16(*shape):
     return jax.ShapeDtypeStruct(shape, jnp.bfloat16)
 
 
-def prefetched(grid, in_shapes, out_shapes):
+def prefetched(n_in, n_out):
     return pltpu.PrefetchScalarGridSpec(
-        num_scalar_prefetch=1,
-        grid=grid,
-        in_specs=[whole(s) for s in in_shapes],
-        out_specs=[whole(s) for s in out_shapes],
+        num_scalar_prefetch=1, grid=(), in_specs=[IN_VMEM] * n_in, out_specs=[IN_VMEM] * n_out
     )
 
 
@@ -194,8 +196,7 @@
     return pl.pallas_call(
         functools.partial(pair_kernel, members),
         grid=(octets + BCH // 8,),
-        in_specs=[whole((LAGS, 2 * BINS))]
-        + [whole(x.shape) for x in (*own, *parts)]
+        in_specs=[IN_VMEM] * (1 + 2 * members)
         + [pl.BlockSpec(memory_space=pl.ANY)] * LAST,
         out_specs=pl.BlockSpec((pairs, LAGS, 8 * BCH), lambda s: (0, 0, after(s))),
         out_shape=bf16(pairs, LAGS, BCH * BCH),
@@ -204,7 +205,7 @@
             pltpu.VMEM((2, BCH, 32 * members), jnp.float32),
             pltpu.SemaphoreType.DMA((LAST, BCH // 8)),
         ],
-        compiler_params=PARAMS,
+        compiler_params=params(44),
         name="correlate",
     )(jnp.asarray(lag_table()), *own, *parts, *early)
 
@@ -214,11 +215,11 @@
     return pl.pallas_call(
         functools.partial(cross_kernel, members, BEGIN[c]),
         grid=(SPLIT[c],),
-        in_specs=[whole(x.shape) for x in (*own, *parts)],
+        in_specs=[IN_VMEM] * (2 * members),
         out_specs=pl.BlockSpec((1, BCH, 16, pairs * BCH), lambda s: (s, 0, 0, 0)),
         out_shape=bf16(SPLIT[c], BCH, 16, pairs * BCH),
         scratch_shapes=[pltpu.VMEM((2, BCH, 32 * members), jnp.float32)],
-        compiler_params=PARAMS,
+        compiler_params=params(20),
         cost_estimate=pl.CostEstimate(
             flops=2_000_000_000 * SPLIT[c], bytes_accessed=2**21 * SPLIT[c], transcendentals=0
         ),
@@ -262,22 +263,22 @@
         functools.partial(spectra_kernel, members, groups),
         grid_spec=pltpu.PrefetchScalarGridSpec(
             num_scalar_prefetch=1,
-            grid=(members,),
+            grid=(members // AT_ONCE,),
             in_specs=[
-                pl.BlockSpec((BCH, 2 * WS), lambda b, meta: (b, 0)),
-                whole((2 * BINS, WS)),
+                pl.BlockSpec((AT_ONCE * BCH, 2 * WS), lambda b, meta: (b, 0)),
+                IN_VMEM,
             ],
-            out_specs=[whole(s) for s in shapes],
+            out_specs=[IN_VMEM] * len(shapes),
         ),
         out_shape=[bf16(*s) for s in shapes],
-        compiler_params=PARAMS,
+        compiler_params=params(16),
         name="spectra",
     )(meta, record, jnp.asarray(forward_table()))
     sends = pl.pallas_call(
         send_kernel,
-        grid_spec=prefetched((1,), [white_shape], send_shapes[1:]),
+        grid_spec=prefetched(1, LAST),
         out_shape=[bf16(*s) for s in send_shapes[1:]],
-        compiler_params=PARAMS,
+        compiler_params=params(16),
         cost_estimate=pl.CostEstimate(flops=0, bytes_accessed=2**23, transcendentals=0),
         name="send",
     )(meta, white)
@@ -305,11 +306,9 @@
             got, sends[c + 1] = lax.optimization_barrier((got, sends[c + 1]))
         parts = pl.pallas_call(
             functools.partial(pack_kernel, members, pairs),
-            grid_spec=prefetched(
-                (1,), [send_shapes[c]], [(pairs, 32 * octets, BCH)] * members
-            ),
+            grid_spec=prefetched(1, members),
             out_shape=[bf16(pairs, 32 * octets, BCH)] * members,
-            compiler_params=PARAMS,
+            compiler_params=params(16),
             name="pack",
         )(place, got.reshape(send_shapes[c]))
         parts = move(parts)

time: 163 us -> 135 us (0.83)
  Pallas kernels: 62.1 us -> 31.6 us
  starting transfers between devices: 80 us -> 51.4 us
  local copies, waits for them, and re-layouts: 5.76 us -> 22.7 us
  waiting for transfers between devices: 11.4 us -> 27.6 us
    pallas_call x3 -> x1, Pallas kernels: 23.3 us -> 6.62 us  [crossed(): pl.pallas_call(functools.partial(cross_kernel, members, BEGIN[c]), grid=(...]
    unnamed x97 -> x67, local copies, waits for them, and re-layouts: 4.6 us -> 20.7 us
    ppermute x35 -> x21, starting transfers between devices: 54 us -> 39.2 us  [move(): moved.append(lax.ppermute(piece, 'win', way))]
    all_to_all x4 -> x2, starting transfers between devices: 26 us -> 12.2 us  [shards(): lax.all_to_all(sends[c].reshape(groups, 64 * octets, BCH), 'blk', split_a...]
    pallas_call x4 -> x2, Pallas kernels: 11.8 us -> 1.39 us  [shards(): pl.pallas_call(functools.partial(pack_kernel, members, pairs), grid_spec=...]
    all_to_all x4 -> x2, waiting for transfers between devices: 1.65 us -> 11.7 us  [shards(): lax.all_to_all(sends[c].reshape(groups, 64 * octets, BCH), 'blk', split_a...]
    pallas_call x1, Pallas kernels: 8.47 us -> 1.83 us  [shards(): pl.pallas_call(functools.partial(spectra_kernel, members, groups), grid_s...]
    ppermute x35 -> x21, waiting for transfers between devices: 9.79 us -> 15.9 us  [move(): moved.append(lax.ppermute(piece, 'win', way))]
  transfers between devices with their start and end apart: 39 -> 23, of which waited for: 5 -> 7; matrix products, arithmetic and copies ran while one was open for 1% -> 1% of each run, Pallas kernels for 16% -> 5%
where the time goes in v4:
time: 135 us
  starting transfers between devices  51.4 us (38%)
  Pallas kernels  31.6 us (23%)
  waiting for transfers between devices  27.6 us (20%)
  local copies, waits for them, and re-layouts  22.7 us (17%)
    ppermute x21, starting transfers between devices, move(): moved.append(lax.ppermute(piece, 'win', way))  39.2 us
    unnamed x67, local copies, waits for them, and re-layouts  20.7 us
    pallas_call x1, Pallas kernels, correlate(): pl.pallas_call(functools.partial(pair_kernel, members), grid=(octets + BC...  19.7 us
    ppermute x21, waiting for transfers between devices, move(): moved.append(lax.ppermute(piece, 'win', way))  15.9 us
    all_to_all x2, starting transfers between devices, shards(): lax.all_to_all(sends[c].reshape(groups, 64 * octets, BCH), 'blk', split_a...  12.2 us
    all_to_all x2, waiting for transfers between devices, shards(): lax.all_to_all(sends[c].reshape(groups, 64 * octets, BCH), 'blk', split_a...  11.7 us
    pallas_call x1, Pallas kernels, crossed(): pl.pallas_call(functools.partial(cross_kernel, members, BEGIN[c]), grid=(...  6.62 us
  transfers between devices with their start and end apart: 23, of which 7 were waited for; matrix products, arithmetic and copies ran while one was open for 1% of the time, Pallas kernels for 5%

profile of v4, /device:TPU:1, one launch (start us, length us, event | category | flops | bytes accessed | tf_op | source)
XLA Modules:
  0.0 134.8 jit_solution(11422292926505074827)
XLA Ops:
  0.0 0.7 select_reduce_fusion.1
  1.3 0.7 dynamic_slice.6
  2.1 1.6 %copy-done.3 = bf16[1024,1024]{1,0:T(8,128)(2,1)S(1)} copy-done((bf16[1024,1024]{1,0:T(8,128)(2,1)S(1)}, bf16[1024,1024]{1,0:T(8,128)(2,1)}, u32[]{:S(2)}) %copy-start.3) | copy-done | bytes 2097176
  3.7 0.9 copy-done.5
  4.7 1.8 %spectra.1 = (bf16[8,512,128]{2,1,0:T(8,128)(2,1)S(1)}, bf16[32,224,128]{2,1,0:T(8,128)(2,1)S(1)}, bf16[512,128]{1,0:T(8,128)(2,1)S(1)}, bf16[512,128]{1,0:T(8,1...) custom-call(s32[41]{0:T(128)S(1)} %pad_add_fusion.1.meta, ...), custom_call_target="tpu_custom_call" | custom-call | tf_op jit(solution)/shard_map/spectra/pallas_call | solution.py:262
  6.5 1.3 copy-done.4
  9.8 7.7 %all-to-all-start = ((bf16[16,448,128]{2,1,0:T(8,128)(2,1)}), bf16[16,448,128]{2,1,0:T(8,128)(2,1)S(1)}, u32[]{:S(2)}, u32[]{:S(2)}) async-start(bf16[16,448,128]{2,1,0:T(8,128)(2,1)} %bitcast.14), calls=%async_computation | async-start | bytes 3670016 | tf_op jit(solution)/shard_map/all_to_all | solution.py:291
  17.5 1.7 %collective-permute-start = (bf16[512,128]{1,0:T(8,128)(2,1)}, bf16[512,128]{1,0:T(8,128)(2,1)S(1)}, u32[]{:S(2)}, u32[]{:S(2)}) collective-permute-start(bf16[512,128]{1,0:T(8,128)(2,1)} %copy-done.31), channel_id=1, source_target_pairs={{0,2},{1,3},{2,4},{3,5},{4,6},{5,7},{6,0},{7,1},{8,10},{9,11},{10,... | collective-permute-start | bytes 393224 | tf_op jit(solution)/shard_map/ppermute | solution.py:242
  19.2 2.2 %collective-permute-start.1 = (bf16[512,128]{1,0:T(8,128)(2,1)}, bf16[512,128]{1,0:T(8,128)(2,1)S(1)}, u32[]{:S(2)}, u32[]{:S(2)}) collective-permute-start(bf16[512,128]{1,0:T(8,128)(2,1)} %copy-done.30), channel_id=1, source_target_pairs={{0,6},{1,7},{2,0},{3,1},{4,2},{5,3},{6,4},{7,5},{8,14},{9,15},{10,... | collective-permute-start | bytes 393224 | tf_op jit(solution)/shard_map/ppermute | solution.py:242
  22.1 2.3 %collective-permute-start.3 = (bf16[512,128]{1,0:T(8,128)(2,1)}, bf16[512,128]{1,0:T(8,128)(2,1)S(1)}, u32[]{:S(2)}, u32[]{:S(2)}) collective-permute-start(bf16[512,128]{1,0:T(8,128)(2,1)} %copy-done.28), channel_id=1, source_target_pairs={{0,7},{1,6},{2,1},{3,0},{4,3},{5,2},{6,5},{7,4},{8,15},{9,14},{10,... | collective-permute-start | bytes 393224 | tf_op jit(solution)/shard_map/ppermute | solution.py:242
  24.4 1.0 collective-permute-start.4
  25.4 0.7 copy.10
  26.2 0.9 reshape.90
  27.3 3.4 %collective-permute-start.5 = (bf16[512,128]{1,0:T(8,128)(2,1)}, bf16[512,128]{1,0:T(8,128)(2,1)S(1)}, u32[]{:S(2)}, u32[]{:S(2)}) collective-permute-start(bf16[512,128]{1,0:T(8,128)(2,1)} %copy-done.26), channel_id=1, source_target_pairs={{0,5},{1,4},{2,7},{3,6},{4,1},{5,0},{6,3},{7,2},{8,13},{9,12},{10,... | collective-permute-start | bytes 393224 | tf_op jit(solution)/shard_map/ppermute | solution.py:242
  30.8 2.1 %send.1 = bf16[32,288,128]{2,1,0:T(8,128)(2,1)} custom-call(s32[41]{0:T(128)S(1)} %pad_add_fusion.1.meta, bf16[8,512,128]{2,1,0:T(8,128)(2,1)S(1)} %get-tuple-element.71.white_ref), custom_call_target="tpu_custom_call" | custom-call | bytes 8388608 | tf_op jit(solution)/shard_map/send/pallas_call | solution.py:277
  33.0 2.3 %collective-permute-done.5.refs_6_ = bf16[512,128]{1,0:T(8,128)(2,1)S(1)} collective-permute-done((bf16[512,128]{1,0:T(8,128)(2,1)}, bf16[512,128]{1,0:T(8,128)(2,1)S(1)}, u32[]{:S(2)}, u32[]{:S(2)}) %collective-permute-start.5) | collective-permute-done | bytes 131104 | tf_op jit(solution)/shard_map/ppermute | solution.py:242
  36.6 7.6 %all-to-all-done = bf16[16,448,128]{2,1,0:T(8,128)(2,1)S(1)} async-done(((bf16[16,448,128]{2,1,0:T(8,128)(2,1)}), bf16[16,448,128]{2,1,0:T(8,128)(2,1)S(1)}, u32[]{:S(2)}, u32[]{:S(2)}) %all-to-all-start) | async-done | bytes 1835040 | tf_op jit(solution)/shard_map/all_to_all | solution.py:291
  44.3 1.3 copy-done.1
  45.5 4.4 %all-to-all-start.1 = ((bf16[16,576,128]{2,1,0:T(8,128)(2,1)}), bf16[16,576,128]{2,1,0:T(8,128)(2,1)S(1)}, u32[]{:S(2)}, u32[]{:S(2)}) async-start(bf16[16,576,128]{2,1,0:T(8,128)(2,1)} %bitcast.6), calls=%async_computation.1 | async-start | bytes 4718592 | tf_op jit(solution)/shard_map/all_to_all | solution.py:291
  50.0 1.5 %copy-done.2 = bf16[16,448,128]{2,1,0:T(8,128)(2,1)S(1)} copy-done((bf16[16,448,128]{2,1,0:T(8,128)(2,1)S(1)}, bf16[16,448,128]{2,1,0:T(8,128)(2,1)}, u32[]{:S(2)}) %copy-start.2) | copy-done | bytes 1835032
  52.2 1.7 %collective-permute-start.7 = (bf16[4,224,128]{2,1,0:T(8,128)(2,1)S(1)}, bf16[4,224,128]{2,1,0:T(8,128)(2,1)S(1)}, u32[]{:S(2)}, u32[]{:S(2)}) collective-permute-start(bf16[4,224,128]{2,1,0:T(8,128)(2,1)S(1)} %get-tuple-element.75), channel_id=1, source_target_pairs={{0,2},{1,3},{2,4},{3,5},{4,6},{5,7},{6,0},{7,1},{8,10},{9,11},{10,... | collective-permute-start | bytes 688136 | tf_op jit(solution)/shard_map/ppermute | solution.py:242
  53.9 2.2 %collective-permute-start.8 = (bf16[4,224,128]{2,1,0:T(8,128)(2,1)S(1)}, bf16[4,224,128]{2,1,0:T(8,128)(2,1)S(1)}, u32[]{:S(2)}, u32[]{:S(2)}) collective-permute-start(bf16[4,224,128]{2,1,0:T(8,128)(2,1)S(1)} %get-tuple-element.76), channel_id=1, source_target_pairs={{0,6},{1,7},{2,0},{3,1},{4,2},{5,3},{6,4},{7,5},{8,14},{9,15},{10,... | collective-permute-start | bytes 688136 | tf_op jit(solution)/shard_map/ppermute | solution.py:242
  56.1 1.1 collective-permute-start.9
  57.2 2.1 %collective-permute-start.10 = (bf16[4,224,128]{2,1,0:T(8,128)(2,1)S(1)}, bf16[4,224,128]{2,1,0:T(8,128)(2,1)S(1)}, u32[]{:S(2)}, u32[]{:S(2)}) collective-permute-start(bf16[4,224,128]{2,1,0:T(8,128)(2,1)S(1)} %get-tuple-element.78), channel_id=1, source_target_pairs={{0,7},{1,6},{2,1},{3,0},{4,3},{5,2},{6,5},{7,4},{8,15},{9,14},{10,... | collective-permute-start | bytes 688136 | tf_op jit(solution)/shard_map/ppermute | solution.py:242
  59.3 1.2 collective-permute-start.11
  60.5 0.7 copy-done.11
  61.2 4.8 %collective-permute-start.12 = (bf16[4,224,128]{2,1,0:T(8,128)(2,1)S(1)}, bf16[4,224,128]{2,1,0:T(8,128)(2,1)S(1)}, u32[]{:S(2)}, u32[]{:S(2)}) collective-permute-start(bf16[4,224,128]{2,1,0:T(8,128)(2,1)S(1)} %get-tuple-element.80), channel_id=1, source_target_pairs={{0,5},{1,4},{2,7},{3,6},{4,1},{5,0},{6,3},{7,2},{8,13},{9,12},{10,... | collective-permute-start | bytes 688136 | tf_op jit(solution)/shard_map/ppermute | solution.py:242
  66.0 0.7 copy-done.13
  66.7 0.7 collective-permute-done.9.refs_11_
  67.4 0.7 copy-done.15
  68.1 0.7 copy-done.17
  68.8 2.8 %collective-permute-done.11.refs_13_ = bf16[4,224,128]{2,1,0:T(8,128)(2,1)S(1)} collective-permute-done((bf16[4,224,128]{2,1,0:T(8,128)(2,1)S(1)}, bf16[4,224,128]{2,1,0:T(8,128)(2,1)S(1)}, u32[]{:S(2)}, u32[]{:S(2)}) %collective-permute-start.11) | collective-permute-done | bytes 229408 | tf_op jit(solution)/shard_map/ppermute | solution.py:242
  71.6 0.7 copy-done.19
  72.3 5.5 %collective-permute-done.12.refs_14_ = bf16[4,224,128]{2,1,0:T(8,128)(2,1)S(1)} collective-permute-done((bf16[4,224,128]{2,1,0:T(8,128)(2,1)S(1)}, bf16[4,224,128]{2,1,0:T(8,128)(2,1)S(1)}, u32[]{:S(2)}, u32[]{:S(2)}) %collective-permute-start.12) | collective-permute-done | bytes 229408 | tf_op jit(solution)/shard_map/ppermute | solution.py:242
  77.8 0.7 copy-done.21
  78.5 0.7 copy-done.23
  79.2 4.0 %all-to-all-done.1 = bf16[16,576,128]{2,1,0:T(8,128)(2,1)S(1)} async-done(((bf16[16,576,128]{2,1,0:T(8,128)(2,1)}), bf16[16,576,128]{2,1,0:T(8,128)(2,1)S(1)}, u32[]{:S(2)}, u32[]{:S(2)}) %all-to-all-start.1) | async-done | bytes 2359328 | tf_op jit(solution)/shard_map/all_to_all | solution.py:291
  83.2 0.7 pack.3
  83.9 1.7 %collective-permute-start.14 = (bf16[4,288,128]{2,1,0:T(8,128)(2,1)S(1)}, bf16[4,288,128]{2,1,0:T(8,128)(2,1)S(1)}, u32[]{:S(2)}, u32[]{:S(2)}) collective-permute-start(bf16[4,288,128]{2,1,0:T(8,128)(2,1)S(1)} %get-tuple-element.84), channel_id=1, source_target_pairs={{0,2},{1,3},{2,4},{3,5},{4,6},{5,7},{6,0},{7,1},{8,10},{9,11},{10,... | collective-permute-start | bytes 884744 | tf_op jit(solution)/shard_map/ppermute | solution.py:242
  85.6 2.2 %collective-permute-start.15 = (bf16[4,288,128]{2,1,0:T(8,128)(2,1)S(1)}, bf16[4,288,128]{2,1,0:T(8,128)(2,1)S(1)}, u32[]{:S(2)}, u32[]{:S(2)}) collective-permute-start(bf16[4,288,128]{2,1,0:T(8,128)(2,1)S(1)} %get-tuple-element.85), channel_id=1, source_target_pairs={{0,6},{1,7},{2,0},{3,1},{4,2},{5,3},{6,4},{7,5},{8,14},{9,15},{10,... | collective-permute-start | bytes 884744 | tf_op jit(solution)/shard_map/ppermute | solution.py:242
  87.8 2.3 %collective-permute-start.16 = (bf16[4,288,128]{2,1,0:T(8,128)(2,1)S(1)}, bf16[4,288,128]{2,1,0:T(8,128)(2,1)S(1)}, u32[]{:S(2)}, u32[]{:S(2)}) collective-permute-start(bf16[4,288,128]{2,1,0:T(8,128)(2,1)S(1)} %get-tuple-element.86), channel_id=1, source_target_pairs={{0,3},{1,2},{2,5},{3,4},{4,7},{5,6},{6,1},{7,0},{8,11},{9,10},{10,... | collective-permute-start | bytes 884744 | tf_op jit(solution)/shard_map/ppermute | solution.py:242
  90.1 2.1 %collective-permute-start.17 = (bf16[4,288,128]{2,1,0:T(8,128)(2,1)S(1)}, bf16[4,288,128]{2,1,0:T(8,128)(2,1)S(1)}, u32[]{:S(2)}, u32[]{:S(2)}) collective-permute-start(bf16[4,288,128]{2,1,0:T(8,128)(2,1)S(1)} %get-tuple-element.87), channel_id=1, source_target_pairs={{0,7},{1,6},{2,1},{3,0},{4,3},{5,2},{6,5},{7,4},{8,15},{9,14},{10,... | collective-permute-start | bytes 884744 | tf_op jit(solution)/shard_map/ppermute | solution.py:242
  92.2 1.2 collective-permute-start.18
  93.4 5.3 %collective-permute-start.19 = (bf16[4,288,128]{2,1,0:T(8,128)(2,1)S(1)}, bf16[4,288,128]{2,1,0:T(8,128)(2,1)S(1)}, u32[]{:S(2)}, u32[]{:S(2)}) collective-permute-start(bf16[4,288,128]{2,1,0:T(8,128)(2,1)S(1)} %get-tuple-element.89), channel_id=1, source_target_pairs={{0,5},{1,4},{2,7},{3,6},{4,1},{5,0},{6,3},{7,2},{8,13},{9,12},{10,... | collective-permute-start | bytes 884744 | tf_op jit(solution)/shard_map/ppermute | solution.py:242
  98.8 6.6 %cross.1.refs_16_ = bf16[7,128,16,512]{3,2,1,0:T(8,128)(2,1)S(1)} custom-call(bf16[512,128]{1,0:T(8,128)(2,1)S(1)} %get-tuple-element.61.refs_0_, bf16[512,128]{1,0:T(8,128)(2,1)S(1)} %collective-permute-done.refs_1_, bf16[512,128]{1,0:T(8,128)(2,1)S(1)} %collective-permute-done.1.refs_2_, bf16[512,128]{1,0:T(8,128)(2,1)S(1)} %collective-permute-done.2.refs_3_, ...), custom_call_target="tpu_custom_call" | custom-call | flops 14000000000 | bytes 14680064 | tf_op jit(solution)/shard_map/cross/pallas_call | solution.py:215
  105.4 5.2 %copy-done = bf16[7,128,16,512]{3,2,1,0:T(8,128)(2,1)} copy-done((bf16[7,128,16,512]{3,2,1,0:T(8,128)(2,1)}, bf16[7,128,16,512]{3,2,1,0:T(8,128)(2,1)S(1)}, u32[]{:S(2)}) %copy-start) | copy-done | bytes 14680088
  110.6 4.5 %collective-permute-done.19.refs_14_ = bf16[4,288,128]{2,1,0:T(8,128)(2,1)S(1)} collective-permute-done((bf16[4,288,128]{2,1,0:T(8,128)(2,1)S(1)}, bf16[4,288,128]{2,1,0:T(8,128)(2,1)S(1)}, u32[]{:S(2)}, u32[]{:S(2)}) %collective-permute-start.19) | collective-permute-done | bytes 294944 | tf_op jit(solution)/shard_map/ppermute | solution.py:242
  115.2 19.7 %correlate.1 = bf16[4,64,16384]{2,1,0:T(8,128)(2,1)} custom-call(bf16[64,256]{1,0:T(8,128)(2,1)S(1)} %copy-done.10, bf16[512,128]{1,0:T(8,128)(2,1)S(1)} %get-tuple-element.61.refs_0_, bf16[512,128]{1,0:T(8,128)(2,1)S(1)} %collective-permute-done.refs_1_, bf16[512,128]{1,0:T(8,128)(2,1)S(1)} %collective-permute-done.1.refs_2_, ...), custom_call_target="tpu_custom_call" | custom-call | tf_op jit(solution)/shard_map/correlate/pallas_call | solution.py:196
  (87 shorter events, 5.7 us)
Async XLA Ops:
  2.1 1.6 %copy-start.3 = (bf16[1024,1024]{1,0:T(8,128)(2,1)S(1)}, bf16[1024,1024]{1,0:T(8,128)(2,1)}, u32[]{:S(2)}) copy-start(bf16[1024,1024]{1,0:T(8,128)(2,1)} %x_ref.1) | copy-start | bytes 6291460
  3.7 0.9 copy-start.5
  6.5 1.3 copy-start.4
  9.7 7.8 %copy-start.25 = (bf16[512,128]{1,0:T(8,128)(2,1)}, bf16[512,128]{1,0:T(8,128)(2,1)S(1)}, u32[]{:S(2)}) copy-start(bf16[512,128]{1,0:T(8,128)(2,1)S(1)} %get-tuple-element.60) | copy-start | bytes 393220
  9.7 9.5 %copy-start.26 = (bf16[512,128]{1,0:T(8,128)(2,1)}, bf16[512,128]{1,0:T(8,128)(2,1)S(1)}, u32[]{:S(2)}) copy-start(bf16[512,128]{1,0:T(8,128)(2,1)S(1)} %get-tuple-element.59) | copy-start | bytes 393220
  9.8 11.7 %copy-start.27 = (bf16[512,128]{1,0:T(8,128)(2,1)}, bf16[512,128]{1,0:T(8,128)(2,1)S(1)}, u32[]{:S(2)}) copy-start(bf16[512,128]{1,0:T(8,128)(2,1)S(1)} %get-tuple-element.58) | copy-start | bytes 393220
  9.8 12.3 %copy-start.28 = (bf16[512,128]{1,0:T(8,128)(2,1)}, bf16[512,128]{1,0:T(8,128)(2,1)S(1)}, u32[]{:S(2)}) copy-start(bf16[512,128]{1,0:T(8,128)(2,1)S(1)} %get-tuple-element.57) | copy-start | bytes 393220
  9.8 15.7 %copy-start.32 = (s32[128,4]{0,1:T(4,128)S(1)}, s32[128,4]{0,1:T(4,128)}, u32[]{:S(2)}) copy-start(s32[128,4]{0,1:T(4,128)} %param.7) | copy-start | bytes 6148
  9.8 34.5 %all-to-all-start = ((bf16[16,448,128]{2,1,0:T(8,128)(2,1)}), bf16[16,448,128]{2,1,0:T(8,128)(2,1)S(1)}, u32[]{:S(2)}, u32[]{:S(2)}) async-start(bf16[16,448,128]{2,1,0:T(8,128)(2,1)} %bitcast.14), calls=%async_computation | async-start | bytes 3670016 | tf_op jit(solution)/shard_map/all_to_all | solution.py:291
  17.5 9.8 %collective-permute-start = (bf16[512,128]{1,0:T(8,128)(2,1)}, bf16[512,128]{1,0:T(8,128)(2,1)S(1)}, u32[]{:S(2)}, u32[]{:S(2)}) collective-permute-start(bf16[512,128]{1,0:T(8,128)(2,1)} %copy-done.31), channel_id=1, source_target_pairs={{0,2},{1,3},{2,4},{3,5},{4,6},{5,7},{6,0},{7,1},{8,10},{9,11},{10,... | collective-permute-start | bytes 393224 | tf_op jit(solution)/shard_map/ppermute | solution.py:242
  19.2 11.5 %collective-permute-start.1 = (bf16[512,128]{1,0:T(8,128)(2,1)}, bf16[512,128]{1,0:T(8,128)(2,1)S(1)}, u32[]{:S(2)}, u32[]{:S(2)}) collective-permute-start(bf16[512,128]{1,0:T(8,128)(2,1)} %copy-done.30), channel_id=1, source_target_pairs={{0,6},{1,7},{2,0},{3,1},{4,2},{5,3},{6,4},{7,5},{8,14},{9,15},{10,... | collective-permute-start | bytes 393224 | tf_op jit(solution)/shard_map/ppermute | solution.py:242
  21.4 11.5 %collective-permute-start.2 = (bf16[512,128]{1,0:T(8,128)(2,1)}, bf16[512,128]{1,0:T(8,128)(2,1)S(1)}, u32[]{:S(2)}, u32[]{:S(2)}) collective-permute-start(bf16[512,128]{1,0:T(8,128)(2,1)} %copy-done.29), channel_id=1, source_target_pairs={{0,3},{1,2},{2,5},{3,4},{4,7},{5,6},{6,1},{7,0},{8,11},{9,10},{10,... | collective-permute-start | bytes 393224 | tf_op jit(solution)/shard_map/ppermute | solution.py:242
  22.1 10.9 %collective-permute-start.3 = (bf16[512,128]{1,0:T(8,128)(2,1)}, bf16[512,128]{1,0:T(8,128)(2,1)S(1)}, u32[]{:S(2)}, u32[]{:S(2)}) collective-permute-start(bf16[512,128]{1,0:T(8,128)(2,1)} %copy-done.28), channel_id=1, source_target_pairs={{0,7},{1,6},{2,1},{3,0},{4,3},{5,2},{6,5},{7,4},{8,15},{9,14},{10,... | collective-permute-start | bytes 393224 | tf_op jit(solution)/shard_map/ppermute | solution.py:242
  24.4 8.6 %collective-permute-start.4 = (bf16[512,128]{1,0:T(8,128)(2,1)}, bf16[512,128]{1,0:T(8,128)(2,1)}, u32[]{:S(2)}, u32[]{:S(2)}) collective-permute-start(bf16[512,128]{1,0:T(8,128)(2,1)} %copy-done.27), channel_id=1, source_target_pairs={{0,4},{1,5},{2,6},{3,7},{4,0},{5,1},{6,2},{7,3},{8,12},{9,13},{10,... | collective-permute-start | bytes 393224 | tf_op jit(solution)/shard_map/ppermute | solution.py:242
  27.3 8.0 %collective-permute-start.5 = (bf16[512,128]{1,0:T(8,128)(2,1)}, bf16[512,128]{1,0:T(8,128)(2,1)S(1)}, u32[]{:S(2)}, u32[]{:S(2)}) collective-permute-start(bf16[512,128]{1,0:T(8,128)(2,1)} %copy-done.26), channel_id=1, source_target_pairs={{0,5},{1,4},{2,7},{3,6},{4,1},{5,0},{6,3},{7,2},{8,13},{9,12},{10,... | collective-permute-start | bytes 393224 | tf_op jit(solution)/shard_map/ppermute | solution.py:242
  30.8 5.2 %collective-permute-start.6 = (bf16[512,128]{1,0:T(8,128)(2,1)}, bf16[512,128]{1,0:T(8,128)(2,1)S(1)}, u32[]{:S(2)}, u32[]{:S(2)}) collective-permute-start(bf16[512,128]{1,0:T(8,128)(2,1)} %copy-done.25), channel_id=1, source_target_pairs={{0,1},{1,0},{2,3},{3,2},{4,5},{5,4},{6,7},{7,6},{8,9},{9,8},{10,11... | collective-permute-start | bytes 393224 | tf_op jit(solution)/shard_map/ppermute | solution.py:242
  44.2 1.3 copy-start.1
  45.5 37.6 %all-to-all-start.1 = ((bf16[16,576,128]{2,1,0:T(8,128)(2,1)}), bf16[16,576,128]{2,1,0:T(8,128)(2,1)S(1)}, u32[]{:S(2)}, u32[]{:S(2)}) async-start(bf16[16,576,128]{2,1,0:T(8,128)(2,1)} %bitcast.6), calls=%async_computation.1 | async-start | bytes 4718592 | tf_op jit(solution)/shard_map/all_to_all | solution.py:291
  50.0 1.5 %copy-start.2 = (bf16[16,448,128]{2,1,0:T(8,128)(2,1)S(1)}, bf16[16,448,128]{2,1,0:T(8,128)(2,1)}, u32[]{:S(2)}) copy-start(bf16[16,448,128]{2,1,0:T(8,128)(2,1)} %copy-done.1) | copy-start | bytes 5505028
  51.5 47.2 %copy-start.7 = (bf16[512,128]{1,0:T(8,128)(2,1)S(1)}, bf16[512,128]{1,0:T(8,128)(2,1)}, u32[]{:S(2)}) copy-start(bf16[512,128]{1,0:T(8,128)(2,1)} %copy-done.6) | copy-start | bytes 393220
  51.5 47.2 %copy-start.9 = (bf16[512,128]{1,0:T(8,128)(2,1)S(1)}, bf16[512,128]{1,0:T(8,128)(2,1)}, u32[]{:S(2)}) copy-start(bf16[512,128]{1,0:T(8,128)(2,1)} %copy-done.8) | copy-start | bytes 393220
  52.2 8.3 %collective-permute-start.7 = (bf16[4,224,128]{2,1,0:T(8,128)(2,1)S(1)}, bf16[4,224,128]{2,1,0:T(8,128)(2,1)S(1)}, u32[]{:S(2)}, u32[]{:S(2)}) collective-permute-start(bf16[4,224,128]{2,1,0:T(8,128)(2,1)S(1)} %get-tuple-element.75), channel_id=1, source_target_pairs={{0,2},{1,3},{2,4},{3,5},{4,6},{5,7},{6,0},{7,1},{8,10},{9,11},{10,... | collective-permute-start | bytes 688136 | tf_op jit(solution)/shard_map/ppermute | solution.py:242
  53.9 12.1 %collective-permute-start.8 = (bf16[4,224,128]{2,1,0:T(8,128)(2,1)S(1)}, bf16[4,224,128]{2,1,0:T(8,128)(2,1)S(1)}, u32[]{:S(2)}, u32[]{:S(2)}) collective-permute-start(bf16[4,224,128]{2,1,0:T(8,128)(2,1)S(1)} %get-tuple-element.76), channel_id=1, source_target_pairs={{0,6},{1,7},{2,0},{3,1},{4,2},{5,3},{6,4},{7,5},{8,14},{9,15},{10,... | collective-permute-start | bytes 688136 | tf_op jit(solution)/shard_map/ppermute | solution.py:242
  56.1 11.3 %collective-permute-start.9 = (bf16[4,224,128]{2,1,0:T(8,128)(2,1)S(1)}, bf16[4,224,128]{2,1,0:T(8,128)(2,1)S(1)}, u32[]{:S(2)}, u32[]{:S(2)}) collective-permute-start(bf16[4,224,128]{2,1,0:T(8,128)(2,1)S(1)} %get-tuple-element.77), channel_id=1, source_target_pairs={{0,3},{1,2},{2,5},{3,4},{4,7},{5,6},{6,1},{7,0},{8,11},{9,10},{10,... | collective-permute-start | bytes 688136 | tf_op jit(solution)/shard_map/ppermute | solution.py:242
  57.2 10.9 %collective-permute-start.10 = (bf16[4,224,128]{2,1,0:T(8,128)(2,1)S(1)}, bf16[4,224,128]{2,1,0:T(8,128)(2,1)S(1)}, u32[]{:S(2)}, u32[]{:S(2)}) collective-permute-start(bf16[4,224,128]{2,1,0:T(8,128)(2,1)S(1)} %get-tuple-element.78), channel_id=1, source_target_pairs={{0,7},{1,6},{2,1},{3,0},{4,3},{5,2},{6,5},{7,4},{8,15},{9,14},{10,... | collective-permute-start | bytes 688136 | tf_op jit(solution)/shard_map/ppermute | solution.py:242
  59.3 12.3 %collective-permute-start.11 = (bf16[4,224,128]{2,1,0:T(8,128)(2,1)S(1)}, bf16[4,224,128]{2,1,0:T(8,128)(2,1)S(1)}, u32[]{:S(2)}, u32[]{:S(2)}) collective-permute-start(bf16[4,224,128]{2,1,0:T(8,128)(2,1)S(1)} %get-tuple-element.79), channel_id=1, source_target_pairs={{0,4},{1,5},{2,6},{3,7},{4,0},{5,1},{6,2},{7,3},{8,12},{9,13},{10,... | collective-permute-start | bytes 688136 | tf_op jit(solution)/shard_map/ppermute | solution.py:242
  60.5 0.7 copy-start.11
  61.2 16.6 %collective-permute-start.12 = (bf16[4,224,128]{2,1,0:T(8,128)(2,1)S(1)}, bf16[4,224,128]{2,1,0:T(8,128)(2,1)S(1)}, u32[]{:S(2)}, u32[]{:S(2)}) collective-permute-start(bf16[4,224,128]{2,1,0:T(8,128)(2,1)S(1)} %get-tuple-element.80), channel_id=1, source_target_pairs={{0,5},{1,4},{2,7},{3,6},{4,1},{5,0},{6,3},{7,2},{8,13},{9,12},{10,... | collective-permute-start | bytes 688136 | tf_op jit(solution)/shard_map/ppermute | solution.py:242
  66.0 0.7 copy-start.13
  66.7 11.8 %collective-permute-start.13 = (bf16[4,224,128]{2,1,0:T(8,128)(2,1)S(1)}, bf16[4,224,128]{2,1,0:T(8,128)(2,1)S(1)}, u32[]{:S(2)}, u32[]{:S(2)}) collective-permute-start(bf16[4,224,128]{2,1,0:T(8,128)(2,1)S(1)} %get-tuple-element.81), channel_id=1, source_target_pairs={{0,1},{1,0},{2,3},{3,2},{4,5},{5,4},{6,7},{7,6},{8,9},{9,8},{10,11... | collective-permute-start | bytes 688136 | tf_op jit(solution)/shard_map/ppermute | solution.py:242
  67.4 0.7 copy-start.15
  78.5 0.7 copy-start.23
  83.2 15.6 %copy-start.12 = (bf16[4,224,128]{2,1,0:T(8,128)(2,1)S(1)}, bf16[4,224,128]{2,1,0:T(8,128)(2,1)}, u32[]{:S(2)}) copy-start(bf16[4,224,128]{2,1,0:T(8,128)(2,1)} %copy-done.11) | copy-start | bytes 688132
  83.2 15.6 %copy-start.14 = (bf16[4,224,128]{2,1,0:T(8,128)(2,1)S(1)}, bf16[4,224,128]{2,1,0:T(8,128)(2,1)}, u32[]{:S(2)}) copy-start(bf16[4,224,128]{2,1,0:T(8,128)(2,1)} %copy-done.13) | copy-start | bytes 688132
  83.2 15.6 %copy-start.16 = (bf16[4,224,128]{2,1,0:T(8,128)(2,1)S(1)}, bf16[4,224,128]{2,1,0:T(8,128)(2,1)}, u32[]{:S(2)}) copy-start(bf16[4,224,128]{2,1,0:T(8,128)(2,1)} %copy-done.15) | copy-start | bytes 688132
  83.2 15.6 %copy-start.18 = (bf16[4,224,128]{2,1,0:T(8,128)(2,1)S(1)}, bf16[4,224,128]{2,1,0:T(8,128)(2,1)}, u32[]{:S(2)}) copy-start(bf16[4,224,128]{2,1,0:T(8,128)(2,1)} %copy-done.17) | copy-start | bytes 688132
  83.2 15.6 %copy-start.20 = (bf16[4,224,128]{2,1,0:T(8,128)(2,1)S(1)}, bf16[4,224,128]{2,1,0:T(8,128)(2,1)}, u32[]{:S(2)}) copy-start(bf16[4,224,128]{2,1,0:T(8,128)(2,1)} %copy-done.19) | copy-start | bytes 688132
  83.2 15.6 %copy-start.22 = (bf16[4,224,128]{2,1,0:T(8,128)(2,1)S(1)}, bf16[4,224,128]{2,1,0:T(8,128)(2,1)}, u32[]{:S(2)}) copy-start(bf16[4,224,128]{2,1,0:T(8,128)(2,1)} %copy-done.21) | copy-start | bytes 688132
  83.2 15.6 %copy-start.24 = (bf16[4,224,128]{2,1,0:T(8,128)(2,1)S(1)}, bf16[4,224,128]{2,1,0:T(8,128)(2,1)}, u32[]{:S(2)}) copy-start(bf16[4,224,128]{2,1,0:T(8,128)(2,1)} %copy-done.23) | copy-start | bytes 688132
  83.9 9.5 %collective-permute-start.14 = (bf16[4,288,128]{2,1,0:T(8,128)(2,1)S(1)}, bf16[4,288,128]{2,1,0:T(8,128)(2,1)S(1)}, u32[]{:S(2)}, u32[]{:S(2)}) collective-permute-start(bf16[4,288,128]{2,1,0:T(8,128)(2,1)S(1)} %get-tuple-element.84), channel_id=1, source_target_pairs={{0,2},{1,3},{2,4},{3,5},{4,6},{5,7},{6,0},{7,1},{8,10},{9,11},{10,... | collective-permute-start | bytes 884744 | tf_op jit(solution)/shard_map/ppermute | solution.py:242
  85.6 13.1 %collective-permute-start.15 = (bf16[4,288,128]{2,1,0:T(8,128)(2,1)S(1)}, bf16[4,288,128]{2,1,0:T(8,128)(2,1)S(1)}, u32[]{:S(2)}, u32[]{:S(2)}) collective-permute-start(bf16[4,288,128]{2,1,0:T(8,128)(2,1)S(1)} %get-tuple-element.85), channel_id=1, source_target_pairs={{0,6},{1,7},{2,0},{3,1},{4,2},{5,3},{6,4},{7,5},{8,14},{9,15},{10,... | collective-permute-start | bytes 884744 | tf_op jit(solution)/shard_map/ppermute | solution.py:242
  87.8 22.8 %collective-permute-start.16 = (bf16[4,288,128]{2,1,0:T(8,128)(2,1)S(1)}, bf16[4,288,128]{2,1,0:T(8,128)(2,1)S(1)}, u32[]{:S(2)}, u32[]{:S(2)}) collective-permute-start(bf16[4,288,128]{2,1,0:T(8,128)(2,1)S(1)} %get-tuple-element.86), channel_id=1, source_target_pairs={{0,3},{1,2},{2,5},{3,4},{4,7},{5,6},{6,1},{7,0},{8,11},{9,10},{10,... | collective-permute-start | bytes 884744 | tf_op jit(solution)/shard_map/ppermute | solution.py:242
  90.1 20.6 %collective-permute-start.17 = (bf16[4,288,128]{2,1,0:T(8,128)(2,1)S(1)}, bf16[4,288,128]{2,1,0:T(8,128)(2,1)S(1)}, u32[]{:S(2)}, u32[]{:S(2)}) collective-permute-start(bf16[4,288,128]{2,1,0:T(8,128)(2,1)S(1)} %get-tuple-element.87), channel_id=1, source_target_pairs={{0,7},{1,6},{2,1},{3,0},{4,3},{5,2},{6,5},{7,4},{8,15},{9,14},{10,... | collective-permute-start | bytes 884744 | tf_op jit(solution)/shard_map/ppermute | solution.py:242
  92.2 18.4 %collective-permute-start.18 = (bf16[4,288,128]{2,1,0:T(8,128)(2,1)S(1)}, bf16[4,288,128]{2,1,0:T(8,128)(2,1)S(1)}, u32[]{:S(2)}, u32[]{:S(2)}) collective-permute-start(bf16[4,288,128]{2,1,0:T(8,128)(2,1)S(1)} %get-tuple-element.88), channel_id=1, source_target_pairs={{0,4},{1,5},{2,6},{3,7},{4,0},{5,1},{6,2},{7,3},{8,12},{9,13},{10,... | collective-permute-start | bytes 884744 | tf_op jit(solution)/shard_map/ppermute | solution.py:242
  93.4 21.8 %collective-permute-start.19 = (bf16[4,288,128]{2,1,0:T(8,128)(2,1)S(1)}, bf16[4,288,128]{2,1,0:T(8,128)(2,1)S(1)}, u32[]{:S(2)}, u32[]{:S(2)}) collective-permute-start(bf16[4,288,128]{2,1,0:T(8,128)(2,1)S(1)} %get-tuple-element.89), channel_id=1, source_target_pairs={{0,5},{1,4},{2,7},{3,6},{4,1},{5,0},{6,3},{7,2},{8,13},{9,12},{10,... | collective-permute-start | bytes 884744 | tf_op jit(solution)/shard_map/ppermute | solution.py:242
  98.7 16.5 %copy-start.10 = (bf16[64,256]{1,0:T(8,128)(2,1)S(1)}, bf16[64,256]{1,0:T(8,128)(2,1)}, u32[]{:S(2)}) copy-start(bf16[64,256]{1,0:T(8,128)(2,1)} %constant.86.clone.lag_ref) | copy-start | bytes 98308
  98.7 16.5 %collective-permute-start.20 = (bf16[4,288,128]{2,1,0:T(8,128)(2,1)S(1)}, bf16[4,288,128]{2,1,0:T(8,128)(2,1)S(1)}, u32[]{:S(2)}, u32[]{:S(2)}) collective-permute-start(bf16[4,288,128]{2,1,0:T(8,128)(2,1)S(1)} %get-tuple-element.90), channel_id=1, source_target_pairs={{0,1},{1,0},{2,3},{3,2},{4,5},{5,4},{6,7},{7,6},{8,9},{9,8},{10,11... | collective-permute-start | bytes 884744 | tf_op jit(solution)/shard_map/ppermute | solution.py:242
  105.4 5.2 %copy-start = (bf16[7,128,16,512]{3,2,1,0:T(8,128)(2,1)}, bf16[7,128,16,512]{3,2,1,0:T(8,128)(2,1)S(1)}, u32[]{:S(2)}) copy-start(bf16[7,128,16,512]{3,2,1,0:T(8,128)(2,1)S(1)} %cross.1.refs_16_) | copy-start | bytes 44040196
  (8 other events, 5.3 us)

commit v5 on v4

v5 whole, which is shorter than its diff:
```python
import functools
import math

import jax
import jax.numpy as jnp
import ml_dtypes
import numpy as np
from jax import lax
from jax.experimental import pallas as pl
from jax.experimental.pallas import tpu as pltpu
from jax.sharding import PartitionSpec as P

WS = 512
BINS = 128
LAGS = 64
BCH = 128
OCT = BINS // 8
ROWS = OCT * 32
SPLIT = (8, 8)
BEGIN = tuple(sum(SPLIT[:c]) for c in range(len(SPLIT)))
LAST = len(SPLIT) - 1
AT_ONCE = 4
LAG_BLOCK = 16
HOPS = ((0, 0), (1, 0), (3, 0), (1, 1), (3, 1), (2, 0), (2, 1), (0, 1))
IN_HBM = pl.BlockSpec(memory_space=pltpu.HBM)
IN_VMEM = pl.BlockSpec(memory_space=pltpu.VMEM)


def forward_table():
    t = np.arange(WS)
    f = np.arange(1, BINS + 1)
    angle = (f[:, None] * t[None, :] % WS) * (2.0 * math.pi / WS)
    return np.concatenate([np.cos(angle), -np.sin(angle)], 0).astype(ml_dtypes.bfloat16)


def lag_table():
    f = np.arange(1, BINS + 1)
    s = np.arange(LAGS) - LAGS // 2
    angle = (s[:, None] * f[None, :] % WS) * (2.0 * math.pi / WS)
    both = np.stack([np.cos(angle), -np.sin(angle)], 1).reshape(LAGS, 2, OCT, 8)
    return both.transpose(0, 2, 1, 3).reshape(LAGS, 2 * BINS).astype(ml_dtypes.bfloat16)


def target(me, hop, members):
    z = lax.rem(me // 2 + hop[0], members // 2)
    return 2 * z + lax.rem(me + hop[1], 2)


def spectra_kernel(members, groups, partners, decks, record_ref, factor_ref, *refs):
    send_refs, own_refs = refs[: LAST + 1], refs[LAST + 1 : LAST + 1 + members]
    x_ref, table_ref, white_ref, slots, in_sem, send_sem, own_sem = refs[LAST + 1 + members :]
    group, me = lax.axis_index("blk"), lax.axis_index("win")
    table_copy = pltpu.make_async_copy(factor_ref, table_ref, in_sem.at[members // AT_ONCE])
    table_copy.start()
    copies = []
    for step in range(members // AT_ONCE):
        at = pl.ds(step * AT_ONCE * BCH, AT_ONCE * BCH)
        copies.append(pltpu.make_async_copy(record_ref.at[at], x_ref.at[at], in_sem.at[step]))
        copies[step].start()

    def wanted(g, _):
        low, high = jnp.int32(members), jnp.int32(-1)
        for m in range(members):
            for q in range(partners.shape[0]):
                block = partners[q, g * members + m] - group * members
                here = (block >= 0) & (block < members)
                low = jnp.minimum(low, jnp.where(here, block, members))
                high = jnp.maximum(high, jnp.where(here, block, -1))
        slots[2 * g] = low
        slots[2 * g + 1] = high
        return 0

    lax.fori_loop(0, groups, wanted, 0)
    table_copy.wait()
    for step, copy in enumerate(copies):
        copy.wait()
        first = step * AT_ONCE
        for w in range(2):
            spectra = lax.dot_general(
                table_ref[...],
                x_ref[first * BCH : (first + AT_ONCE) * BCH, w * WS : (w + 1) * WS],
                (((1,), (1,)), ((), ())),
                preferred_element_type=jnp.float32,
            )
            power = jnp.sum(spectra * spectra, axis=0, keepdims=True) / BINS
            root = jnp.sqrt(power + 1e-06)
            for b in range(AT_ONCE):
                at = slice(b * BCH, (b + 1) * BCH)
                deck = decks[group * members + first + b]
                white = spectra[:, at] * ((1.0 - 2.0 * deck.astype(jnp.float32)) / root[:, at])
                for o in range(OCT):
                    tile = jnp.concatenate(
                        [white[o * 8 : o * 8 + 8], white[BINS + o * 8 : BINS + o * 8 + 8]], 0
                    )
                    row = o * 32 + w * 16
                    white_ref[first + b, row : row + 16, :] = tile.astype(jnp.bfloat16)
    copies = []
    for c, send_ref in enumerate(send_refs):
        for j in range(2 * groups):
            piece = white_ref.at[slots[j], pl.ds(32 * BEGIN[c], 32 * SPLIT[c])]
            copies.append(pltpu.make_async_copy(piece, send_ref.at[j], send_sem.at[c, j]))
    for k, hop in enumerate(HOPS):
        piece = white_ref.at[target(me, hop, members)]
        copies.append(pltpu.make_async_copy(piece, own_refs[k], own_sem.at[k]))
    for copy in copies:
        copy.start()
    for copy in copies:
        copy.wait()


def pack_kernel(members, pairs, meta, in_ref, *out_refs):
    me = meta[members * pairs]
    for hop, out_ref in zip(HOPS, out_refs, strict=True):
        to = target(me, hop, members)
        for q in range(pairs):
            out_ref[q] = in_ref[meta[to * pairs + q]]


def cross_octet(octet, local, own_refs, part_refs, rows_ref, store):
    pairs = part_refs[0].shape[0]
    depth = 32 * len(own_refs)
    at = pl.ds(pl.multiple_of(octet * 32, 32), 32)
    own = jnp.concatenate([r[at, :] for r in own_refs], 0).astype(jnp.float32)
    halves = own.reshape(depth // 16, 2, 8, BCH)
    turned = jnp.stack([halves[:, 1], -halves[:, 0]], axis=1).reshape(depth, BCH)
    rows_ref[0] = own.T
    rows_ref[1] = turned.T
    at = pl.ds(pl.multiple_of(local * 32, 32), 32)
    right = jnp.concatenate(
        [jnp.concatenate([r[q, at, :] for r in part_refs], 0) for q in range(pairs)], 1
    )
    same = (
        lax.broadcasted_iota(jnp.int32, (8, depth), 0)
        == lax.broadcasted_iota(jnp.int32, (8, depth), 1) % 8
    )
    for i0 in range(0, BCH, 16):
        tiles = []
        for i in range(i0, i0 + 16):
            for v in range(2):
                row = rows_ref[v, pl.ds(i, 8, stride=0), :]
                tiles.append(jnp.where(same, row, 0.0))
        left = jnp.concatenate(tiles, 0).astype(jnp.bfloat16)
        cross = jnp.dot(left, right, preferred_element_type=jnp.float32)
        store(i0, cross.astype(jnp.bfloat16).reshape(16, 16, pairs * BCH))


def chunk_kernel(c, members, lag_ref, *refs):
    own_refs, part_refs = refs[:members], refs[members : 2 * members]
    before_ref = refs[2 * members] if c else None
    out_ref, cross_ref, rows_ref = refs[-3:]
    pairs = part_refs[0].shape[0]
    octets = SPLIT[c]
    step = pl.program_id(0)

    @pl.when(step < octets)
    def _():
        def store(i0, value):
            cross_ref[step, i0 : i0 + 16] = value

        cross_octet(BEGIN[c] + step, step, own_refs, part_refs, rows_ref, store)

    @pl.when(step >= octets)
    def _():
        scale = 1.0 / math.sqrt(members * 2 * BINS)
        for ii in range(LAG_BLOCK):
            i = (step - octets) * LAG_BLOCK + ii
            right = cross_ref[:, i].reshape(16 * octets, pairs * BCH)
            lagged = jnp.dot(lag_ref[...], right, preferred_element_type=jnp.float32)
            if c:
                lagged = lagged + before_ref[i]
            if c < LAST:
                out_ref[i] = lagged
                continue
            lagged = (lagged * scale).astype(jnp.bfloat16)
            for q in range(pairs):
                out_ref[q, :, ii * BCH : (ii + 1) * BCH] = lagged[:, q * BCH : (q + 1) * BCH]


def params(mib):
    return pltpu.CompilerParams(vmem_limit_bytes=mib * 1024 * 1024)


def bf16(*shape):
    return jax.ShapeDtypeStruct(shape, jnp.bfloat16)


def prefetched(n_in, n_out):
    return pltpu.PrefetchScalarGridSpec(
        num_scalar_prefetch=1, grid=(), in_specs=[IN_VMEM] * n_in, out_specs=[IN_VMEM] * n_out
    )


def chunk(c, own, parts, before, pairs):
    members = len(own)
    octets = SPLIT[c]
    lags = jnp.asarray(lag_table()[:, 16 * BEGIN[c] : 16 * (BEGIN[c] + octets)])
    blocks = BCH // LAG_BLOCK
    if c == LAST:
        out = bf16(pairs, LAGS, BCH * BCH)
        out_spec = pl.BlockSpec(
            (pairs, LAGS, LAG_BLOCK * BCH), lambda s: (0, 0, jnp.maximum(s - octets, 0))
        )
    else:
        out = jax.ShapeDtypeStruct((BCH, LAGS, pairs * BCH), jnp.float32)
        out_spec = IN_VMEM
    return pl.pallas_call(
        functools.partial(chunk_kernel, c, members),
        grid=(octets + blocks,),
        in_specs=[IN_VMEM] * (1 + 2 * members + len(before)),
        out_specs=out_spec,
        out_shape=out,
        scratch_shapes=[
            pltpu.VMEM((octets, BCH, 16, pairs * BCH), jnp.bfloat16),
            pltpu.VMEM((2, BCH, 32 * members), jnp.float32),
        ],
        compiler_params=params(40),
        cost_estimate=pl.CostEstimate(
            flops=2_500_000_000 * octets, bytes_accessed=2**21 * octets, transcendentals=0
        ),
        name="chunk",
    )(lags, *own, *parts, *before)


def shards(record, deck_ids, partners):
    groups = lax.axis_size("blk")
    members = lax.axis_size("win")
    group = lax.axis_index("blk")
    member = lax.axis_index("win")
    pairs = partners.shape[1]

    def move(pieces):
        moved = [pieces[0]]
        for (dz, dc), piece in zip(HOPS[1:], pieces[1:], strict=True):
            ring = members // 2
            way = [(m, (m // 2 + dz) % ring * 2 + (m + dc) % 2) for m in range(members)]
            moved.append(lax.ppermute(piece, "win", way))
        return moved

    listed = partners.reshape(groups, members * pairs)
    wanted = lax.dynamic_slice_in_dim(listed, group, 1, 0).reshape(-1)
    lower = (wanted[None, :] // members == wanted[:, None] // members) & (
        wanted[None, :] < wanted[:, None]
    )
    place = 2 * (wanted // members) + jnp.any(lower, axis=1).astype(jnp.int32)
    place = jnp.concatenate([place, member.reshape(1)]).astype(jnp.int32)

    send_shapes = [(2 * groups, 32 * n, BCH) for n in SPLIT]
    shapes = send_shapes + [(ROWS, BCH)] * members
    outs = pl.pallas_call(
        functools.partial(spectra_kernel, members, groups),
        grid_spec=pltpu.PrefetchScalarGridSpec(
            num_scalar_prefetch=2,
            grid=(),
            in_specs=[IN_HBM] * 2,
            out_specs=[IN_HBM] * len(shapes),
            scratch_shapes=[
                pltpu.VMEM((members * BCH, 2 * WS), jnp.bfloat16),
                pltpu.VMEM((2 * BINS, WS), jnp.bfloat16),
                pltpu.VMEM((members, ROWS, BCH), jnp.bfloat16),
                pltpu.SMEM((2 * groups,), jnp.int32),
                pltpu.SemaphoreType.DMA((members // AT_ONCE + 1,)),
                pltpu.SemaphoreType.DMA((LAST + 1, 2 * groups)),
                pltpu.SemaphoreType.DMA((members,)),
            ],
        ),
        out_shape=[bf16(*s) for s in shapes],
        compiler_params=params(58),
        name="spectra",
    )(partners.T, deck_ids, record, jnp.asarray(forward_table()))
    sends, own = list(outs[: LAST + 1]), list(outs[LAST + 1 :])
    own = move(own)

    before = []
    parts = None
    for c, octets in enumerate(SPLIT):
        got = lax.all_to_all(
            sends[c].reshape(groups, 64 * octets, BCH),
            "blk",
            split_axis=0,
            concat_axis=0,
            tiled=True,
        )
        if c == 0:
            got, own, place = lax.optimization_barrier((got, own, place))
        else:
            got, parts = lax.optimization_barrier((got, parts))
            before = [chunk(c - 1, own, parts, before, pairs)]
        if c < LAST:
            got, sends[c + 1] = lax.optimization_barrier((got, sends[c + 1]))
        parts = pl.pallas_call(
            functools.partial(pack_kernel, members, pairs),
            grid_spec=prefetched(1, members),
            out_shape=[bf16(pairs, 32 * octets, BCH)] * members,
            compiler_params=params(16),
            name="pack",
        )(place, got.reshape(send_shapes[c]))
        parts = move(parts)
    return chunk(LAST, own, parts, before, pairs)


def solution(mesh):
    return jax.shard_map(
        shards,
        mesh=mesh,
        in_specs=(P("blk", "win"), P(), P()),
        out_specs=P(("blk", "win"), None, None),
        check_vma=False,
    )
```

time: 135 us -> 130 us (0.963)
  local copies, waits for them, and re-layouts: 22.7 us -> 0.24 us
  Pallas kernels: 31.6 us -> 44.4 us
  waiting for transfers between devices: 27.6 us -> 33.3 us
    unnamed x67 -> x19, local copies, waits for them, and re-layouts: 20.7 us -> 0.15 us
    pallas_call x3 -> x2, Pallas kernels: 28.4 us -> 34.7 us  [chunk(): pl.pallas_call(functools.partial(chunk_kernel, c, members), grid=(octets...]
    pallas_call x1, Pallas kernels: 1.83 us -> 6.76 us  [shards(): pl.pallas_call(functools.partial(spectra_kernel, members, groups), grid_s...]
    ppermute x21, waiting for transfers between devices: 15.9 us -> 20.3 us  [move(): moved.append(lax.ppermute(piece, 'win', way))]
    pallas_call x2, Pallas kernels: 1.39 us -> 2.96 us  [shards(): pl.pallas_call(functools.partial(pack_kernel, members, pairs), grid_spec=...]
  transfers between devices with their start and end apart: 23 -> 23, of which waited for: 7 -> 7; matrix products, arithmetic and copies ran while one was open for 1% -> 0% of each run, Pallas kernels for 5% -> 13%
where the time goes in v5:
time: 130 us; the launch traced here: 129 us
  starting transfers between devices  50.8 us (39%)
  Pallas kernels  44.4 us (34%)
  waiting for transfers between devices  33.3 us (26%)
    ppermute x21, starting transfers between devices, move(): moved.append(lax.ppermute(piece, 'win', way))  38.6 us
    pallas_call x2, Pallas kernels, chunk(): pl.pallas_call(functools.partial(chunk_kernel, c, members), grid=(octets...  34.7 us
    ppermute x21, waiting for transfers between devices, move(): moved.append(lax.ppermute(piece, 'win', way))  20.3 us
    all_to_all x2, waiting for transfers between devices, shards(): lax.all_to_all(sends[c].reshape(groups, 64 * octets, BCH), 'blk', split_a...  13 us
    all_to_all x2, starting transfers between devices, shards(): lax.all_to_all(sends[c].reshape(groups, 64 * octets, BCH), 'blk', split_a...  12.2 us
    pallas_call x1, Pallas kernels, shards(): pl.pallas_call(functools.partial(spectra_kernel, members, groups), grid_s...  6.76 us
    pallas_call x2, Pallas kernels, shards(): pl.pallas_call(functools.partial(pack_kernel, members, pairs), grid_spec=...  2.96 us
  transfers between devices with their start and end apart: 23, of which 7 were waited for; matrix products, arithmetic and copies ran while one was open for 0% of the time, Pallas kernels for 13%

profile of v5, /device:TPU:1, one launch (start us, length us, event | category | flops | bytes accessed | tf_op | source)
XLA Modules:
  0.0 129.3 jit_solution(10512125597914920095)
XLA Ops:
  0.0 6.8 %spectra.1 = (bf16[32,256,128]{2,1,0:T(8,128)(2,1)}, bf16[32,256,128]{2,1,0:T(8,128)(2,1)}, bf16[512,128]{1,0:T(8,128)(2,1)}, bf16[512,128]{1,0:T(8,128)(2,1)}, ...) custom-call(s32[4,128]{1,0:T(4,128)} %bitcast.14, ...), custom_call_target="tpu_custom_call" | custom-call | tf_op jit(solution)/shard_map/spectra/pallas_call | solution.py:249
  6.8 0.0 copy-start.3
  6.8 7.7 %all-to-all-start = ((bf16[16,512,128]{2,1,0:T(8,128)(2,1)}), bf16[16,512,128]{2,1,0:T(8,128)(2,1)S(1)}, u32[]{:S(2)}, u32[]{:S(2)}) async-start(bf16[16,512,128]{2,1,0:T(8,128)(2,1)} %bitcast.13), calls=%async_computation | async-start | bytes 4194304 | tf_op jit(solution)/shard_map/all_to_all | solution.py:276
  14.6 1.7 %collective-permute-start = (bf16[512,128]{1,0:T(8,128)(2,1)S(1)}, bf16[512,128]{1,0:T(8,128)(2,1)S(1)}, u32[]{:S(2)}, u32[]{:S(2)}) collective-permute-start(bf16[512,128]{1,0:T(8,128)(2,1)S(1)} %copy-done.8), channel_id=1, source_target_pairs={{0,2},{1,3},{2,4},{3,5},{4,6},{5,7},{6,0},{7,1},{8,10},{9,11},{10,... | collective-permute-start | bytes 393224 | tf_op jit(solution)/shard_map/ppermute | solution.py:236
  16.3 2.2 %collective-permute-start.1 = (bf16[512,128]{1,0:T(8,128)(2,1)S(1)}, bf16[512,128]{1,0:T(8,128)(2,1)S(1)}, u32[]{:S(2)}, u32[]{:S(2)}) collective-permute-start(bf16[512,128]{1,0:T(8,128)(2,1)S(1)} %copy-done.7), channel_id=1, source_target_pairs={{0,6},{1,7},{2,0},{3,1},{4,2},{5,3},{6,4},{7,5},{8,14},{9,15},{10,... | collective-permute-start | bytes 393224 | tf_op jit(solution)/shard_map/ppermute | solution.py:236
  18.5 0.7 collective-permute-start.2
  19.2 2.3 %collective-permute-start.3 = (bf16[512,128]{1,0:T(8,128)(2,1)}, bf16[512,128]{1,0:T(8,128)(2,1)S(1)}, u32[]{:S(2)}, u32[]{:S(2)}) collective-permute-start(bf16[512,128]{1,0:T(8,128)(2,1)} %get-tuple-element.57), channel_id=1, source_target_pairs={{0,7},{1,6},{2,1},{3,0},{4,3},{5,2},{6,5},{7,4},{8,15},{9,14},{10,... | collective-permute-start | bytes 393224 | tf_op jit(solution)/shard_map/ppermute | solution.py:236
  21.5 1.0 collective-permute-start.4
  22.5 0.1 copy.8
  22.6 0.1 reshape.82
  22.7 0.2 and_reduce_fusion
  22.9 0.0 collective-permute-done.refs_1_
  22.9 3.4 %collective-permute-start.5 = (bf16[512,128]{1,0:T(8,128)(2,1)S(1)}, bf16[512,128]{1,0:T(8,128)(2,1)S(1)}, u32[]{:S(2)}, u32[]{:S(2)}) collective-permute-start(bf16[512,128]{1,0:T(8,128)(2,1)S(1)} %copy-done.5), channel_id=1, source_target_pairs={{0,5},{1,4},{2,7},{3,6},{4,1},{5,0},{6,3},{7,2},{8,13},{9,12},{10,... | collective-permute-start | bytes 393224 | tf_op jit(solution)/shard_map/ppermute | solution.py:236
  26.3 0.0 collective-permute-done.1.refs_2_
  26.4 0.1 pad_add_fusion.meta
  26.5 1.8 %collective-permute-done.4.refs_5_ = bf16[512,128]{1,0:T(8,128)(2,1)S(1)} collective-permute-done((bf16[512,128]{1,0:T(8,128)(2,1)S(1)}, bf16[512,128]{1,0:T(8,128)(2,1)S(1)}, u32[]{:S(2)}, u32[]{:S(2)}) %collective-permute-start.4) | collective-permute-done | bytes 131104 | tf_op jit(solution)/shard_map/ppermute | solution.py:236
  28.3 3.8 %collective-permute-done.5.refs_6_ = bf16[512,128]{1,0:T(8,128)(2,1)S(1)} collective-permute-done((bf16[512,128]{1,0:T(8,128)(2,1)S(1)}, bf16[512,128]{1,0:T(8,128)(2,1)S(1)}, u32[]{:S(2)}, u32[]{:S(2)}) %collective-permute-start.5) | collective-permute-done | bytes 131104 | tf_op jit(solution)/shard_map/ppermute | solution.py:236
  32.1 13.0 %all-to-all-done = bf16[16,512,128]{2,1,0:T(8,128)(2,1)S(1)} async-done(((bf16[16,512,128]{2,1,0:T(8,128)(2,1)}), bf16[16,512,128]{2,1,0:T(8,128)(2,1)S(1)}, u32[]{:S(2)}, u32[]{:S(2)}) %all-to-all-start) | async-done | bytes 2097184 | tf_op jit(solution)/shard_map/all_to_all | solution.py:276
  45.1 4.4 %all-to-all-start.1 = ((bf16[16,512,128]{2,1,0:T(8,128)(2,1)}), bf16[16,512,128]{2,1,0:T(8,128)(2,1)}, u32[]{:S(2)}, u32[]{:S(2)}) async-start(bf16[16,512,128]{2,1,0:T(8,128)(2,1)} %bitcast.12), calls=%async_computation.1 | async-start | bytes 4194304 | tf_op jit(solution)/shard_map/all_to_all | solution.py:276
  49.5 0.0 copy-start.2
  49.5 0.7 pack.2
  50.2 1.7 %collective-permute-start.7 = (bf16[4,256,128]{2,1,0:T(8,128)(2,1)S(1)}, bf16[4,256,128]{2,1,0:T(8,128)(2,1)S(1)}, u32[]{:S(2)}, u32[]{:S(2)}) collective-permute-start(bf16[4,256,128]{2,1,0:T(8,128)(2,1)S(1)} %get-tuple-element.75), channel_id=1, source_target_pairs={{0,2},{1,3},{2,4},{3,5},{4,6},{5,7},{6,0},{7,1},{8,10},{9,11},{10,... | collective-permute-start | bytes 786440 | tf_op jit(solution)/shard_map/ppermute | solution.py:236
  51.9 2.2 %collective-permute-start.8 = (bf16[4,256,128]{2,1,0:T(8,128)(2,1)S(1)}, bf16[4,256,128]{2,1,0:T(8,128)(2,1)S(1)}, u32[]{:S(2)}, u32[]{:S(2)}) collective-permute-start(bf16[4,256,128]{2,1,0:T(8,128)(2,1)S(1)} %get-tuple-element.76), channel_id=1, source_target_pairs={{0,6},{1,7},{2,0},{3,1},{4,2},{5,3},{6,4},{7,5},{8,14},{9,15},{10,... | collective-permute-start | bytes 786440 | tf_op jit(solution)/shard_map/ppermute | solution.py:236
  54.1 1.8 %collective-permute-start.9 = (bf16[4,256,128]{2,1,0:T(8,128)(2,1)S(1)}, bf16[4,256,128]{2,1,0:T(8,128)(2,1)S(1)}, u32[]{:S(2)}, u32[]{:S(2)}) collective-permute-start(bf16[4,256,128]{2,1,0:T(8,128)(2,1)S(1)} %get-tuple-element.77), channel_id=1, source_target_pairs={{0,3},{1,2},{2,5},{3,4},{4,7},{5,6},{6,1},{7,0},{8,11},{9,10},{10,... | collective-permute-start | bytes 786440 | tf_op jit(solution)/shard_map/ppermute | solution.py:236
  56.0 2.1 %collective-permute-start.10 = (bf16[4,256,128]{2,1,0:T(8,128)(2,1)S(1)}, bf16[4,256,128]{2,1,0:T(8,128)(2,1)S(1)}, u32[]{:S(2)}, u32[]{:S(2)}) collective-permute-start(bf16[4,256,128]{2,1,0:T(8,128)(2,1)S(1)} %get-tuple-element.78), channel_id=1, source_target_pairs={{0,7},{1,6},{2,1},{3,0},{4,3},{5,2},{6,5},{7,4},{8,15},{9,14},{10,... | collective-permute-start | bytes 786440 | tf_op jit(solution)/shard_map/ppermute | solution.py:236
  58.1 1.2 collective-permute-start.11
  59.3 0.0 collective-permute-done.7.refs_9_
  59.3 4.7 %collective-permute-start.12 = (bf16[4,256,128]{2,1,0:T(8,128)(2,1)S(1)}, bf16[4,256,128]{2,1,0:T(8,128)(2,1)S(1)}, u32[]{:S(2)}, u32[]{:S(2)}) collective-permute-start(bf16[4,256,128]{2,1,0:T(8,128)(2,1)S(1)} %get-tuple-element.80), channel_id=1, source_target_pairs={{0,5},{1,4},{2,7},{3,6},{4,1},{5,0},{6,3},{7,2},{8,13},{9,12},{10,... | collective-permute-start | bytes 786440 | tf_op jit(solution)/shard_map/ppermute | solution.py:236
  64.0 0.0 collective-permute-done.8.refs_10_
  64.0 0.0 collective-permute-start.13
  64.0 3.0 %collective-permute-done.9.refs_11_ = bf16[4,256,128]{2,1,0:T(8,128)(2,1)S(1)} collective-permute-done((bf16[4,256,128]{2,1,0:T(8,128)(2,1)S(1)}, bf16[4,256,128]{2,1,0:T(8,128)(2,1)S(1)}, u32[]{:S(2)}, u32[]{:S(2)}) %collective-permute-start.9) | collective-permute-done | bytes 262176 | tf_op jit(solution)/shard_map/ppermute | solution.py:236
  67.0 0.4 collective-permute-done.10.refs_12_
  67.4 4.5 %collective-permute-done.11.refs_13_ = bf16[4,256,128]{2,1,0:T(8,128)(2,1)S(1)} collective-permute-done((bf16[4,256,128]{2,1,0:T(8,128)(2,1)S(1)}, bf16[4,256,128]{2,1,0:T(8,128)(2,1)S(1)}, u32[]{:S(2)}, u32[]{:S(2)}) %collective-permute-start.11) | collective-permute-done | bytes 262176 | tf_op jit(solution)/shard_map/ppermute | solution.py:236
  71.9 6.7 %collective-permute-done.12.refs_14_ = bf16[4,256,128]{2,1,0:T(8,128)(2,1)S(1)} collective-permute-done((bf16[4,256,128]{2,1,0:T(8,128)(2,1)S(1)}, bf16[4,256,128]{2,1,0:T(8,128)(2,1)S(1)}, u32[]{:S(2)}, u32[]{:S(2)}) %collective-permute-start.12) | collective-permute-done | bytes 262176 | tf_op jit(solution)/shard_map/ppermute | solution.py:236
  78.7 2.3 %pack.3 = (bf16[4,256,128]{2,1,0:T(8,128)(2,1)S(1)}, bf16[4,256,128]{2,1,0:T(8,128)(2,1)S(1)}, bf16[4,256,128]{2,1,0:T(8,128)(2,1)S(1)}, bf16[4,256,128]{2,1,0:T...) custom-call(s32[33]{0:T(128)S(1)} %pad_add_fusion.meta, ...), custom_call_target="tpu_custom_call" | custom-call | tf_op jit(solution)/shard_map/pack/pallas_call | solution.py:290
  80.9 1.0 collective-permute-start.14
  81.9 1.8 %collective-permute-start.15 = (bf16[4,256,128]{2,1,0:T(8,128)(2,1)S(1)}, bf16[4,256,128]{2,1,0:T(8,128)(2,1)S(1)}, u32[]{:S(2)}, u32[]{:S(2)}) collective-permute-start(bf16[4,256,128]{2,1,0:T(8,128)(2,1)S(1)} %get-tuple-element.85), channel_id=1, source_target_pairs={{0,6},{1,7},{2,0},{3,1},{4,2},{5,3},{6,4},{7,5},{8,14},{9,15},{10,... | collective-permute-start | bytes 786440 | tf_op jit(solution)/shard_map/ppermute | solution.py:236
  83.7 3.2 %collective-permute-start.16 = (bf16[4,256,128]{2,1,0:T(8,128)(2,1)S(1)}, bf16[4,256,128]{2,1,0:T(8,128)(2,1)S(1)}, u32[]{:S(2)}, u32[]{:S(2)}) collective-permute-start(bf16[4,256,128]{2,1,0:T(8,128)(2,1)S(1)} %get-tuple-element.86), channel_id=1, source_target_pairs={{0,3},{1,2},{2,5},{3,4},{4,7},{5,6},{6,1},{7,0},{8,11},{9,10},{10,... | collective-permute-start | bytes 786440 | tf_op jit(solution)/shard_map/ppermute | solution.py:236
  86.9 2.1 %collective-permute-start.17 = (bf16[4,256,128]{2,1,0:T(8,128)(2,1)S(1)}, bf16[4,256,128]{2,1,0:T(8,128)(2,1)S(1)}, u32[]{:S(2)}, u32[]{:S(2)}) collective-permute-start(bf16[4,256,128]{2,1,0:T(8,128)(2,1)S(1)} %get-tuple-element.87), channel_id=1, source_target_pairs={{0,7},{1,6},{2,1},{3,0},{4,3},{5,2},{6,5},{7,4},{8,15},{9,14},{10,... | collective-permute-start | bytes 786440 | tf_op jit(solution)/shard_map/ppermute | solution.py:236
  89.0 1.2 collective-permute-start.18
  90.2 4.3 %collective-permute-start.19 = (bf16[4,256,128]{2,1,0:T(8,128)(2,1)S(1)}, bf16[4,256,128]{2,1,0:T(8,128)(2,1)S(1)}, u32[]{:S(2)}, u32[]{:S(2)}) collective-permute-start(bf16[4,256,128]{2,1,0:T(8,128)(2,1)S(1)} %get-tuple-element.89), channel_id=1, source_target_pairs={{0,5},{1,4},{2,7},{3,6},{4,1},{5,0},{6,3},{7,2},{8,13},{9,12},{10,... | collective-permute-start | bytes 786440 | tf_op jit(solution)/shard_map/ppermute | solution.py:236
  94.5 0.0 collective-permute-done.15.refs_10_
  94.5 0.0 collective-permute-start.20
  94.5 15.8 %chunk.2.refs_16_ = f32[128,64,512]{2,1,0:T(8,128)} custom-call(bf16[64,128]{1,0:T(8,128)(2,1)S(1)} %copy-done.2, bf16[512,128]{1,0:T(8,128)(2,1)S(1)} %copy-done, bf16[512,128]{1,0:T(8,128)(2,1)S(1)} %collective-permute-done.refs_1_, bf16[512,128]{1,0:T(8,128)(2,1)S(1)} %collective-permute-done.1.refs_2_, ...), custom_call_target="tpu_custom_call" | custom-call | flops 20000000000 | bytes 16777216 | tf_op jit(solution)/shard_map/chunk/pallas_call | solution.py:206
  110.3 0.0 collective-permute-done.16.refs_11_
  110.3 0.0 collective-permute-done.17.refs_12_
  110.3 0.0 collective-permute-done.18.refs_13_
  110.3 19.0 %chunk.3 = bf16[4,64,16384]{2,1,0:T(8,128)(2,1)} custom-call(bf16[64,128]{1,0:T(8,128)(2,1)S(1)} %copy-done.1, bf16[512,128]{1,0:T(8,128)(2,1)S(1)} %copy-done, bf16[512,128]{1,0:T(8,128)(2,1)S(1)} %collective-permute-done.refs_1_, bf16[512,128]{1,0:T(8,128)(2,1)S(1)} %collective-permute-done.1.refs_2_, bf16[512,128]{1,0:T(8,128)(2,1)S(1)} %collective-permute-done.2.refs_3_, ...), custom_call_target="tpu_custom_call" | custom-call | flops 20000000000 | bytes 16777216 | tf_op jit(solution)/shard_map/chunk/pallas_call | solution.py:206
  (28 shorter events, 0.1 us)
Async XLA Ops:
  6.8 7.8 %copy-start.8 = (bf16[512,128]{1,0:T(8,128)(2,1)S(1)}, bf16[512,128]{1,0:T(8,128)(2,1)}, u32[]{:S(2)}) copy-start(bf16[512,128]{1,0:T(8,128)(2,1)} %get-tuple-element.54) | copy-start | bytes 393220
  6.8 9.5 %copy-start.7 = (bf16[512,128]{1,0:T(8,128)(2,1)S(1)}, bf16[512,128]{1,0:T(8,128)(2,1)}, u32[]{:S(2)}) copy-start(bf16[512,128]{1,0:T(8,128)(2,1)} %get-tuple-element.55) | copy-start | bytes 393220
  6.8 14.7 %copy-start.6 = (bf16[512,128]{1,0:T(8,128)(2,1)S(1)}, bf16[512,128]{1,0:T(8,128)(2,1)}, u32[]{:S(2)}) copy-start(bf16[512,128]{1,0:T(8,128)(2,1)} %get-tuple-element.58) | copy-start | bytes 393220
  6.8 15.7 %copy-start.3 = (s32[128,4]{0,1:T(4,128)S(1)}, s32[128,4]{0,1:T(4,128)}, u32[]{:S(2)}) copy-start(s32[128,4]{0,1:T(4,128)} %param.8) | copy-start | bytes 6148
  6.8 16.1 %copy-start.5 = (bf16[512,128]{1,0:T(8,128)(2,1)S(1)}, bf16[512,128]{1,0:T(8,128)(2,1)}, u32[]{:S(2)}) copy-start(bf16[512,128]{1,0:T(8,128)(2,1)} %get-tuple-element.59) | copy-start | bytes 393220
  6.8 19.5 %copy-start.4 = (bf16[512,128]{1,0:T(8,128)(2,1)S(1)}, bf16[512,128]{1,0:T(8,128)(2,1)}, u32[]{:S(2)}) copy-start(bf16[512,128]{1,0:T(8,128)(2,1)} %get-tuple-element.60) | copy-start | bytes 393220
  6.8 38.2 %all-to-all-start = ((bf16[16,512,128]{2,1,0:T(8,128)(2,1)}), bf16[16,512,128]{2,1,0:T(8,128)(2,1)S(1)}, u32[]{:S(2)}, u32[]{:S(2)}) async-start(bf16[16,512,128]{2,1,0:T(8,128)(2,1)} %bitcast.13), calls=%async_computation | async-start | bytes 4194304 | tf_op jit(solution)/shard_map/all_to_all | solution.py:276
  14.6 8.3 %collective-permute-start = (bf16[512,128]{1,0:T(8,128)(2,1)S(1)}, bf16[512,128]{1,0:T(8,128)(2,1)S(1)}, u32[]{:S(2)}, u32[]{:S(2)}) collective-permute-start(bf16[512,128]{1,0:T(8,128)(2,1)S(1)} %copy-done.8), channel_id=1, source_target_pairs={{0,2},{1,3},{2,4},{3,5},{4,6},{5,7},{6,0},{7,1},{8,10},{9,11},{10,... | collective-permute-start | bytes 393224 | tf_op jit(solution)/shard_map/ppermute | solution.py:236
  16.3 10.1 %collective-permute-start.1 = (bf16[512,128]{1,0:T(8,128)(2,1)S(1)}, bf16[512,128]{1,0:T(8,128)(2,1)S(1)}, u32[]{:S(2)}, u32[]{:S(2)}) collective-permute-start(bf16[512,128]{1,0:T(8,128)(2,1)S(1)} %copy-done.7), channel_id=1, source_target_pairs={{0,6},{1,7},{2,0},{3,1},{4,2},{5,3},{6,4},{7,5},{8,14},{9,15},{10,... | collective-permute-start | bytes 393224 | tf_op jit(solution)/shard_map/ppermute | solution.py:236
  18.5 8.0 %collective-permute-start.2 = (bf16[512,128]{1,0:T(8,128)(2,1)}, bf16[512,128]{1,0:T(8,128)(2,1)S(1)}, u32[]{:S(2)}, u32[]{:S(2)}) collective-permute-start(bf16[512,128]{1,0:T(8,128)(2,1)} %get-tuple-element.56), channel_id=1, source_target_pairs={{0,3},{1,2},{2,5},{3,4},{4,7},{5,6},{6,1},{7,0},{8,11},{9,10},{10,... | collective-permute-start | bytes 393224 | tf_op jit(solution)/shard_map/ppermute | solution.py:236
  19.2 7.3 %collective-permute-start.3 = (bf16[512,128]{1,0:T(8,128)(2,1)}, bf16[512,128]{1,0:T(8,128)(2,1)S(1)}, u32[]{:S(2)}, u32[]{:S(2)}) collective-permute-start(bf16[512,128]{1,0:T(8,128)(2,1)} %get-tuple-element.57), channel_id=1, source_target_pairs={{0,7},{1,6},{2,1},{3,0},{4,3},{5,2},{6,5},{7,4},{8,15},{9,14},{10,... | collective-permute-start | bytes 393224 | tf_op jit(solution)/shard_map/ppermute | solution.py:236
  21.5 6.8 %collective-permute-start.4 = (bf16[512,128]{1,0:T(8,128)(2,1)S(1)}, bf16[512,128]{1,0:T(8,128)(2,1)S(1)}, u32[]{:S(2)}, u32[]{:S(2)}) collective-permute-start(bf16[512,128]{1,0:T(8,128)(2,1)S(1)} %copy-done.6), channel_id=1, source_target_pairs={{0,4},{1,5},{2,6},{3,7},{4,0},{5,1},{6,2},{7,3},{8,12},{9,13},{10,... | collective-permute-start | bytes 393224 | tf_op jit(solution)/shard_map/ppermute | solution.py:236
  22.9 9.2 %collective-permute-start.5 = (bf16[512,128]{1,0:T(8,128)(2,1)S(1)}, bf16[512,128]{1,0:T(8,128)(2,1)S(1)}, u32[]{:S(2)}, u32[]{:S(2)}) collective-permute-start(bf16[512,128]{1,0:T(8,128)(2,1)S(1)} %copy-done.5), channel_id=1, source_target_pairs={{0,5},{1,4},{2,7},{3,6},{4,1},{5,0},{6,3},{7,2},{8,13},{9,12},{10,... | collective-permute-start | bytes 393224 | tf_op jit(solution)/shard_map/ppermute | solution.py:236
  26.4 5.7 %collective-permute-start.6 = (bf16[512,128]{1,0:T(8,128)(2,1)S(1)}, bf16[512,128]{1,0:T(8,128)(2,1)S(1)}, u32[]{:S(2)}, u32[]{:S(2)}) collective-permute-start(bf16[512,128]{1,0:T(8,128)(2,1)S(1)} %copy-done.4), channel_id=1, source_target_pairs={{0,1},{1,0},{2,3},{3,2},{4,5},{5,4},{6,7},{7,6},{8,9},{9,8},{10,11... | collective-permute-start | bytes 393224 | tf_op jit(solution)/shard_map/ppermute | solution.py:236
  45.1 33.6 %all-to-all-start.1 = ((bf16[16,512,128]{2,1,0:T(8,128)(2,1)}), bf16[16,512,128]{2,1,0:T(8,128)(2,1)}, u32[]{:S(2)}, u32[]{:S(2)}) async-start(bf16[16,512,128]{2,1,0:T(8,128)(2,1)} %bitcast.12), calls=%async_computation.1 | async-start | bytes 4194304 | tf_op jit(solution)/shard_map/all_to_all | solution.py:276
  49.5 45.0 %copy-start = (bf16[512,128]{1,0:T(8,128)(2,1)S(1)}, bf16[512,128]{1,0:T(8,128)(2,1)}, u32[]{:S(2)}) copy-start(bf16[512,128]{1,0:T(8,128)(2,1)} %get-tuple-element.61.refs_0_) | copy-start | bytes 393220
  49.5 45.0 %copy-start.2 = (bf16[64,128]{1,0:T(8,128)(2,1)S(1)}, bf16[64,128]{1,0:T(8,128)(2,1)}, u32[]{:S(2)}) copy-start(bf16[64,128]{1,0:T(8,128)(2,1)} %constant.57.clone.lag_ref) | copy-start | bytes 49156
  50.2 9.0 %collective-permute-start.7 = (bf16[4,256,128]{2,1,0:T(8,128)(2,1)S(1)}, bf16[4,256,128]{2,1,0:T(8,128)(2,1)S(1)}, u32[]{:S(2)}, u32[]{:S(2)}) collective-permute-start(bf16[4,256,128]{2,1,0:T(8,128)(2,1)S(1)} %get-tuple-element.75), channel_id=1, source_target_pairs={{0,2},{1,3},{2,4},{3,5},{4,6},{5,7},{6,0},{7,1},{8,10},{9,11},{10,... | collective-permute-start | bytes 786440 | tf_op jit(solution)/shard_map/ppermute | solution.py:236
  51.9 12.1 %collective-permute-start.8 = (bf16[4,256,128]{2,1,0:T(8,128)(2,1)S(1)}, bf16[4,256,128]{2,1,0:T(8,128)(2,1)S(1)}, u32[]{:S(2)}, u32[]{:S(2)}) collective-permute-start(bf16[4,256,128]{2,1,0:T(8,128)(2,1)S(1)} %get-tuple-element.76), channel_id=1, source_target_pairs={{0,6},{1,7},{2,0},{3,1},{4,2},{5,3},{6,4},{7,5},{8,14},{9,15},{10,... | collective-permute-start | bytes 786440 | tf_op jit(solution)/shard_map/ppermute | solution.py:236
  54.1 12.9 %collective-permute-start.9 = (bf16[4,256,128]{2,1,0:T(8,128)(2,1)S(1)}, bf16[4,256,128]{2,1,0:T(8,128)(2,1)S(1)}, u32[]{:S(2)}, u32[]{:S(2)}) collective-permute-start(bf16[4,256,128]{2,1,0:T(8,128)(2,1)S(1)} %get-tuple-element.77), channel_id=1, source_target_pairs={{0,3},{1,2},{2,5},{3,4},{4,7},{5,6},{6,1},{7,0},{8,11},{9,10},{10,... | collective-permute-start | bytes 786440 | tf_op jit(solution)/shard_map/ppermute | solution.py:236
  56.0 11.4 %collective-permute-start.10 = (bf16[4,256,128]{2,1,0:T(8,128)(2,1)S(1)}, bf16[4,256,128]{2,1,0:T(8,128)(2,1)S(1)}, u32[]{:S(2)}, u32[]{:S(2)}) collective-permute-start(bf16[4,256,128]{2,1,0:T(8,128)(2,1)S(1)} %get-tuple-element.78), channel_id=1, source_target_pairs={{0,7},{1,6},{2,1},{3,0},{4,3},{5,2},{6,5},{7,4},{8,15},{9,14},{10,... | collective-permute-start | bytes 786440 | tf_op jit(solution)/shard_map/ppermute | solution.py:236
  58.1 13.8 %collective-permute-start.11 = (bf16[4,256,128]{2,1,0:T(8,128)(2,1)S(1)}, bf16[4,256,128]{2,1,0:T(8,128)(2,1)S(1)}, u32[]{:S(2)}, u32[]{:S(2)}) collective-permute-start(bf16[4,256,128]{2,1,0:T(8,128)(2,1)S(1)} %get-tuple-element.79), channel_id=1, source_target_pairs={{0,4},{1,5},{2,6},{3,7},{4,0},{5,1},{6,2},{7,3},{8,12},{9,13},{10,... | collective-permute-start | bytes 786440 | tf_op jit(solution)/shard_map/ppermute | solution.py:236
  59.3 19.4 %collective-permute-start.12 = (bf16[4,256,128]{2,1,0:T(8,128)(2,1)S(1)}, bf16[4,256,128]{2,1,0:T(8,128)(2,1)S(1)}, u32[]{:S(2)}, u32[]{:S(2)}) collective-permute-start(bf16[4,256,128]{2,1,0:T(8,128)(2,1)S(1)} %get-tuple-element.80), channel_id=1, source_target_pairs={{0,5},{1,4},{2,7},{3,6},{4,1},{5,0},{6,3},{7,2},{8,13},{9,12},{10,... | collective-permute-start | bytes 786440 | tf_op jit(solution)/shard_map/ppermute | solution.py:236
  64.0 14.7 %collective-permute-start.13 = (bf16[4,256,128]{2,1,0:T(8,128)(2,1)S(1)}, bf16[4,256,128]{2,1,0:T(8,128)(2,1)S(1)}, u32[]{:S(2)}, u32[]{:S(2)}) collective-permute-start(bf16[4,256,128]{2,1,0:T(8,128)(2,1)S(1)} %get-tuple-element.81), channel_id=1, source_target_pairs={{0,1},{1,0},{2,3},{3,2},{4,5},{5,4},{6,7},{7,6},{8,9},{9,8},{10,11... | collective-permute-start | bytes 786440 | tf_op jit(solution)/shard_map/ppermute | solution.py:236
  80.9 9.3 %collective-permute-start.14 = (bf16[4,256,128]{2,1,0:T(8,128)(2,1)S(1)}, bf16[4,256,128]{2,1,0:T(8,128)(2,1)S(1)}, u32[]{:S(2)}, u32[]{:S(2)}) collective-permute-start(bf16[4,256,128]{2,1,0:T(8,128)(2,1)S(1)} %get-tuple-element.84), channel_id=1, source_target_pairs={{0,2},{1,3},{2,4},{3,5},{4,6},{5,7},{6,0},{7,1},{8,10},{9,11},{10,... | collective-permute-start | bytes 786440 | tf_op jit(solution)/shard_map/ppermute | solution.py:236
  81.9 12.6 %collective-permute-start.15 = (bf16[4,256,128]{2,1,0:T(8,128)(2,1)S(1)}, bf16[4,256,128]{2,1,0:T(8,128)(2,1)S(1)}, u32[]{:S(2)}, u32[]{:S(2)}) collective-permute-start(bf16[4,256,128]{2,1,0:T(8,128)(2,1)S(1)} %get-tuple-element.85), channel_id=1, source_target_pairs={{0,6},{1,7},{2,0},{3,1},{4,2},{5,3},{6,4},{7,5},{8,14},{9,15},{10,... | collective-permute-start | bytes 786440 | tf_op jit(solution)/shard_map/ppermute | solution.py:236
  83.7 26.6 %collective-permute-start.16 = (bf16[4,256,128]{2,1,0:T(8,128)(2,1)S(1)}, bf16[4,256,128]{2,1,0:T(8,128)(2,1)S(1)}, u32[]{:S(2)}, u32[]{:S(2)}) collective-permute-start(bf16[4,256,128]{2,1,0:T(8,128)(2,1)S(1)} %get-tuple-element.86), channel_id=1, source_target_pairs={{0,3},{1,2},{2,5},{3,4},{4,7},{5,6},{6,1},{7,0},{8,11},{9,10},{10,... | collective-permute-start | bytes 786440 | tf_op jit(solution)/shard_map/ppermute | solution.py:236
  86.9 23.4 %collective-permute-start.17 = (bf16[4,256,128]{2,1,0:T(8,128)(2,1)S(1)}, bf16[4,256,128]{2,1,0:T(8,128)(2,1)S(1)}, u32[]{:S(2)}, u32[]{:S(2)}) collective-permute-start(bf16[4,256,128]{2,1,0:T(8,128)(2,1)S(1)} %get-tuple-element.87), channel_id=1, source_target_pairs={{0,7},{1,6},{2,1},{3,0},{4,3},{5,2},{6,5},{7,4},{8,15},{9,14},{10,... | collective-permute-start | bytes 786440 | tf_op jit(solution)/shard_map/ppermute | solution.py:236
  89.0 21.3 %collective-permute-start.18 = (bf16[4,256,128]{2,1,0:T(8,128)(2,1)S(1)}, bf16[4,256,128]{2,1,0:T(8,128)(2,1)S(1)}, u32[]{:S(2)}, u32[]{:S(2)}) collective-permute-start(bf16[4,256,128]{2,1,0:T(8,128)(2,1)S(1)} %get-tuple-element.88), channel_id=1, source_target_pairs={{0,4},{1,5},{2,6},{3,7},{4,0},{5,1},{6,2},{7,3},{8,12},{9,13},{10,... | collective-permute-start | bytes 786440 | tf_op jit(solution)/shard_map/ppermute | solution.py:236
  90.2 20.1 %collective-permute-start.19 = (bf16[4,256,128]{2,1,0:T(8,128)(2,1)S(1)}, bf16[4,256,128]{2,1,0:T(8,128)(2,1)S(1)}, u32[]{:S(2)}, u32[]{:S(2)}) collective-permute-start(bf16[4,256,128]{2,1,0:T(8,128)(2,1)S(1)} %get-tuple-element.89), channel_id=1, source_target_pairs={{0,5},{1,4},{2,7},{3,6},{4,1},{5,0},{6,3},{7,2},{8,13},{9,12},{10,... | collective-permute-start | bytes 786440 | tf_op jit(solution)/shard_map/ppermute | solution.py:236
  94.5 15.8 %copy-start.1 = (bf16[64,128]{1,0:T(8,128)(2,1)S(1)}, bf16[64,128]{1,0:T(8,128)(2,1)}, u32[]{:S(2)}) copy-start(bf16[64,128]{1,0:T(8,128)(2,1)} %constant.58.clone.lag_ref) | copy-start | bytes 49156
  94.5 15.8 %collective-permute-start.20 = (bf16[4,256,128]{2,1,0:T(8,128)(2,1)S(1)}, bf16[4,256,128]{2,1,0:T(8,128)(2,1)S(1)}, u32[]{:S(2)}, u32[]{:S(2)}) collective-permute-start(bf16[4,256,128]{2,1,0:T(8,128)(2,1)S(1)} %get-tuple-element.90), channel_id=1, source_target_pairs={{0,1},{1,0},{2,3},{3,2},{4,5},{5,4},{6,7},{7,6},{8,9},{9,8},{10,11... | collective-permute-start | bytes 786440 | tf_op jit(solution)/shard_map/ppermute | solution.py:236

commit v6 on v5

--- a/solution.py
+++ b/solution.py
@@ -146,11 +146,25 @@
 
 def chunk_kernel(c, members, lag_ref, *refs):
     own_refs, part_refs = refs[:members], refs[members : 2 * members]
-    before_ref = refs[2 * members] if c else None
-    out_ref, cross_ref, rows_ref = refs[-3:]
+    refs = refs[2 * members :]
+    if c:
+        before_ref, out_ref, cross_ref, rows_ref, held_ref, sem = refs
+    else:
+        out_ref, cross_ref, rows_ref = refs
     pairs = part_refs[0].shape[0]
     octets = SPLIT[c]
     step = pl.program_id(0)
+
+    def fetch(block):
+        at = pl.ds(block * LAG_BLOCK, LAG_BLOCK)
+        return pltpu.make_async_copy(before_ref.at[at], held_ref.at[at], sem.at[block])
+
+    if c:
+
+        @pl.when(step == 0)
+        def _():
+            for block in range(BCH // LAG_BLOCK):
+                fetch(block).start()
 
     @pl.when(step < octets)
     def _():
@@ -162,14 +176,16 @@
     @pl.when(step >= octets)
     def _():
         scale = 1.0 / math.sqrt(members * 2 * BINS)
+        if c:
+            fetch(step - octets).wait()
         for ii in range(LAG_BLOCK):
             i = (step - octets) * LAG_BLOCK + ii
             right = cross_ref[:, i].reshape(16 * octets, pairs * BCH)
             lagged = jnp.dot(lag_ref[...], right, preferred_element_type=jnp.float32)
             if c:
-                lagged = lagged + before_ref[i]
+                lagged = lagged + held_ref[i]
             if c < LAST:
-                out_ref[i] = lagged
+                out_ref[ii] = lagged
                 continue
             lagged = (lagged * scale).astype(jnp.bfloat16)
             for q in range(pairs):
@@ -195,25 +211,30 @@
     octets = SPLIT[c]
     lags = jnp.asarray(lag_table()[:, 16 * BEGIN[c] : 16 * (BEGIN[c] + octets)])
     blocks = BCH // LAG_BLOCK
+    sums = (BCH, LAGS, pairs * BCH)
+
+    def after(s):
+        return jnp.maximum(s - octets, 0)
+
     if c == LAST:
         out = bf16(pairs, LAGS, BCH * BCH)
-        out_spec = pl.BlockSpec(
-            (pairs, LAGS, LAG_BLOCK * BCH), lambda s: (0, 0, jnp.maximum(s - octets, 0))
-        )
+        out_spec = pl.BlockSpec((pairs, LAGS, LAG_BLOCK * BCH), lambda s: (0, 0, after(s)))
     else:
-        out = jax.ShapeDtypeStruct((BCH, LAGS, pairs * BCH), jnp.float32)
-        out_spec = IN_VMEM
+        out = jax.ShapeDtypeStruct(sums, jnp.float32)
+        out_spec = pl.BlockSpec((LAG_BLOCK, *sums[1:]), lambda s: (after(s), 0, 0))
+    held = [pltpu.VMEM(sums, jnp.float32), pltpu.SemaphoreType.DMA((blocks,))] if c else []
     return pl.pallas_call(
         functools.partial(chunk_kernel, c, members),
         grid=(octets + blocks,),
-        in_specs=[IN_VMEM] * (1 + 2 * members + len(before)),
+        in_specs=[IN_VMEM] * (1 + 2 * members) + [IN_HBM] * len(before),
         out_specs=out_spec,
         out_shape=out,
         scratch_shapes=[
             pltpu.VMEM((octets, BCH, 16, pairs * BCH), jnp.bfloat16),
             pltpu.VMEM((2, BCH, 32 * members), jnp.float32),
+            *held,
         ],
-        compiler_params=params(40),
+        compiler_params=params(48),
         cost_estimate=pl.CostEstimate(
             flops=2_500_000_000 * octets, bytes_accessed=2**21 * octets, transcendentals=0
         ),

time: 130 us -> 123 us (0.946)
  Pallas kernels: 44.4 us -> 37.4 us
    pallas_call x2, Pallas kernels: 34.7 us -> 27.7 us  [chunk(): pl.pallas_call(functools.partial(chunk_kernel, c, members), grid=(octets...]
  transfers between devices with their start and end apart: 23 -> 23, of which waited for: 7 -> 8; matrix products, arithmetic and copies ran while one was open for 0% -> 0% of each run, Pallas kernels for 13% -> 12%
where the time goes in v6:
time: 123 us
  starting transfers between devices  50.8 us (41%)
  Pallas kernels  37.4 us (30%)
  waiting for transfers between devices  33.7 us (27%)
    ppermute x21, starting transfers between devices, move(): moved.append(lax.ppermute(piece, 'win', way))  38.6 us
    pallas_call x2, Pallas kernels, chunk(): pl.pallas_call(functools.partial(chunk_kernel, c, members), grid=(octets...  27.7 us
    ppermute x21, waiting for transfers between devices, move(): moved.append(lax.ppermute(piece, 'win', way))  20.7 us
    all_to_all x2, waiting for transfers between devices, shards(): lax.all_to_all(sends[c].reshape(groups, 64 * octets, BCH), 'blk', split_a...  13 us
    all_to_all x2, starting transfers between devices, shards(): lax.all_to_all(sends[c].reshape(groups, 64 * octets, BCH), 'blk', split_a...  12.2 us
    pallas_call x1, Pallas kernels, shards(): pl.pallas_call(functools.partial(spectra_kernel, members, groups), grid_s...  6.76 us
    pallas_call x2, Pallas kernels, shards(): pl.pallas_call(functools.partial(pack_kernel, members, pairs), grid_spec=...  2.96 us
  transfers between devices with their start and end apart: 23, of which 8 were waited for; matrix products, arithmetic and copies ran while one was open for 0% of the time, Pallas kernels for 12%

profile of v6, /device:TPU:1, one launch (start us, length us, event | category | flops | bytes accessed | tf_op | source)
XLA Modules:
  0.0 122.7 jit_solution(974271201815035646)
XLA Ops:
  0.0 6.8 %spectra.1 = (bf16[32,256,128]{2,1,0:T(8,128)(2,1)}, bf16[32,256,128]{2,1,0:T(8,128)(2,1)}, bf16[512,128]{1,0:T(8,128)(2,1)}, bf16[512,128]{1,0:T(8,128)(2,1)}, ...) custom-call(s32[4,128]{1,0:T(4,128)} %bitcast.14, ...), custom_call_target="tpu_custom_call" | custom-call | tf_op jit(solution)/shard_map/spectra/pallas_call | solution.py:270
  6.8 0.0 copy-start.3
  6.8 7.7 %all-to-all-start = ((bf16[16,512,128]{2,1,0:T(8,128)(2,1)}), bf16[16,512,128]{2,1,0:T(8,128)(2,1)S(1)}, u32[]{:S(2)}, u32[]{:S(2)}) async-start(bf16[16,512,128]{2,1,0:T(8,128)(2,1)} %bitcast.13), calls=%async_computation | async-start | bytes 4194304 | tf_op jit(solution)/shard_map/all_to_all | solution.py:297
  14.6 1.7 %collective-permute-start = (bf16[512,128]{1,0:T(8,128)(2,1)S(1)}, bf16[512,128]{1,0:T(8,128)(2,1)S(1)}, u32[]{:S(2)}, u32[]{:S(2)}) collective-permute-start(bf16[512,128]{1,0:T(8,128)(2,1)S(1)} %copy-done.8), channel_id=1, source_target_pairs={{0,2},{1,3},{2,4},{3,5},{4,6},{5,7},{6,0},{7,1},{8,10},{9,11},{10,... | collective-permute-start | bytes 393224 | tf_op jit(solution)/shard_map/ppermute | solution.py:257
  16.3 2.2 %collective-permute-start.1 = (bf16[512,128]{1,0:T(8,128)(2,1)S(1)}, bf16[512,128]{1,0:T(8,128)(2,1)S(1)}, u32[]{:S(2)}, u32[]{:S(2)}) collective-permute-start(bf16[512,128]{1,0:T(8,128)(2,1)S(1)} %copy-done.7), channel_id=1, source_target_pairs={{0,6},{1,7},{2,0},{3,1},{4,2},{5,3},{6,4},{7,5},{8,14},{9,15},{10,... | collective-permute-start | bytes 393224 | tf_op jit(solution)/shard_map/ppermute | solution.py:257
  18.5 0.7 collective-permute-start.2
  19.2 2.3 %collective-permute-start.3 = (bf16[512,128]{1,0:T(8,128)(2,1)}, bf16[512,128]{1,0:T(8,128)(2,1)S(1)}, u32[]{:S(2)}, u32[]{:S(2)}) collective-permute-start(bf16[512,128]{1,0:T(8,128)(2,1)} %get-tuple-element.57), channel_id=1, source_target_pairs={{0,7},{1,6},{2,1},{3,0},{4,3},{5,2},{6,5},{7,4},{8,15},{9,14},{10,... | collective-permute-start | bytes 393224 | tf_op jit(solution)/shard_map/ppermute | solution.py:257
  21.5 1.0 collective-permute-start.4
  22.5 0.1 copy.8
  22.6 0.1 reshape.82
  22.7 0.2 and_reduce_fusion
  22.9 0.0 collective-permute-done.refs_1_
  22.9 3.4 %collective-permute-start.5 = (bf16[512,128]{1,0:T(8,128)(2,1)S(1)}, bf16[512,128]{1,0:T(8,128)(2,1)S(1)}, u32[]{:S(2)}, u32[]{:S(2)}) collective-permute-start(bf16[512,128]{1,0:T(8,128)(2,1)S(1)} %copy-done.5), channel_id=1, source_target_pairs={{0,5},{1,4},{2,7},{3,6},{4,1},{5,0},{6,3},{7,2},{8,13},{9,12},{10,... | collective-permute-start | bytes 393224 | tf_op jit(solution)/shard_map/ppermute | solution.py:257
  26.3 0.0 collective-permute-done.1.refs_2_
  26.4 0.1 pad_add_fusion.meta
  26.5 0.0 collective-permute-done.2.refs_3_
  26.5 1.8 %collective-permute-done.4.refs_5_ = bf16[512,128]{1,0:T(8,128)(2,1)S(1)} collective-permute-done((bf16[512,128]{1,0:T(8,128)(2,1)S(1)}, bf16[512,128]{1,0:T(8,128)(2,1)S(1)}, u32[]{:S(2)}, u32[]{:S(2)}) %collective-permute-start.4) | collective-permute-done | bytes 131104 | tf_op jit(solution)/shard_map/ppermute | solution.py:257
  28.3 3.8 %collective-permute-done.5.refs_6_ = bf16[512,128]{1,0:T(8,128)(2,1)S(1)} collective-permute-done((bf16[512,128]{1,0:T(8,128)(2,1)S(1)}, bf16[512,128]{1,0:T(8,128)(2,1)S(1)}, u32[]{:S(2)}, u32[]{:S(2)}) %collective-permute-start.5) | collective-permute-done | bytes 131104 | tf_op jit(solution)/shard_map/ppermute | solution.py:257
  32.1 0.0 collective-permute-done.6.refs_7_
  32.1 13.0 %all-to-all-done = bf16[16,512,128]{2,1,0:T(8,128)(2,1)S(1)} async-done(((bf16[16,512,128]{2,1,0:T(8,128)(2,1)}), bf16[16,512,128]{2,1,0:T(8,128)(2,1)S(1)}, u32[]{:S(2)}, u32[]{:S(2)}) %all-to-all-start) | async-done | bytes 2097184 | tf_op jit(solution)/shard_map/all_to_all | solution.py:297
  45.1 4.4 %all-to-all-start.1 = ((bf16[16,512,128]{2,1,0:T(8,128)(2,1)}), bf16[16,512,128]{2,1,0:T(8,128)(2,1)}, u32[]{:S(2)}, u32[]{:S(2)}) async-start(bf16[16,512,128]{2,1,0:T(8,128)(2,1)} %bitcast.12), calls=%async_computation.1 | async-start | bytes 4194304 | tf_op jit(solution)/shard_map/all_to_all | solution.py:297
  49.5 0.0 copy-start.2
  49.5 0.7 pack.2
  50.2 1.7 %collective-permute-start.7 = (bf16[4,256,128]{2,1,0:T(8,128)(2,1)S(1)}, bf16[4,256,128]{2,1,0:T(8,128)(2,1)S(1)}, u32[]{:S(2)}, u32[]{:S(2)}) collective-permute-start(bf16[4,256,128]{2,1,0:T(8,128)(2,1)S(1)} %get-tuple-element.75), channel_id=1, source_target_pairs={{0,2},{1,3},{2,4},{3,5},{4,6},{5,7},{6,0},{7,1},{8,10},{9,11},{10,... | collective-permute-start | bytes 786440 | tf_op jit(solution)/shard_map/ppermute | solution.py:257
  51.9 2.2 %collective-permute-start.8 = (bf16[4,256,128]{2,1,0:T(8,128)(2,1)S(1)}, bf16[4,256,128]{2,1,0:T(8,128)(2,1)S(1)}, u32[]{:S(2)}, u32[]{:S(2)}) collective-permute-start(bf16[4,256,128]{2,1,0:T(8,128)(2,1)S(1)} %get-tuple-element.76), channel_id=1, source_target_pairs={{0,6},{1,7},{2,0},{3,1},{4,2},{5,3},{6,4},{7,5},{8,14},{9,15},{10,... | collective-permute-start | bytes 786440 | tf_op jit(solution)/shard_map/ppermute | solution.py:257
  54.1 1.8 %collective-permute-start.9 = (bf16[4,256,128]{2,1,0:T(8,128)(2,1)S(1)}, bf16[4,256,128]{2,1,0:T(8,128)(2,1)S(1)}, u32[]{:S(2)}, u32[]{:S(2)}) collective-permute-start(bf16[4,256,128]{2,1,0:T(8,128)(2,1)S(1)} %get-tuple-element.77), channel_id=1, source_target_pairs={{0,3},{1,2},{2,5},{3,4},{4,7},{5,6},{6,1},{7,0},{8,11},{9,10},{10,... | collective-permute-start | bytes 786440 | tf_op jit(solution)/shard_map/ppermute | solution.py:257
  56.0 2.1 %collective-permute-start.10 = (bf16[4,256,128]{2,1,0:T(8,128)(2,1)S(1)}, bf16[4,256,128]{2,1,0:T(8,128)(2,1)S(1)}, u32[]{:S(2)}, u32[]{:S(2)}) collective-permute-start(bf16[4,256,128]{2,1,0:T(8,128)(2,1)S(1)} %get-tuple-element.78), channel_id=1, source_target_pairs={{0,7},{1,6},{2,1},{3,0},{4,3},{5,2},{6,5},{7,4},{8,15},{9,14},{10,... | collective-permute-start | bytes 786440 | tf_op jit(solution)/shard_map/ppermute | solution.py:257
  58.1 1.2 collective-permute-start.11
  59.3 0.0 collective-permute-done.7.refs_9_
  59.3 4.7 %collective-permute-start.12 = (bf16[4,256,128]{2,1,0:T(8,128)(2,1)S(1)}, bf16[4,256,128]{2,1,0:T(8,128)(2,1)S(1)}, u32[]{:S(2)}, u32[]{:S(2)}) collective-permute-start(bf16[4,256,128]{2,1,0:T(8,128)(2,1)S(1)} %get-tuple-element.80), channel_id=1, source_target_pairs={{0,5},{1,4},{2,7},{3,6},{4,1},{5,0},{6,3},{7,2},{8,13},{9,12},{10,... | collective-permute-start | bytes 786440 | tf_op jit(solution)/shard_map/ppermute | solution.py:257
  64.0 3.0 %collective-permute-done.9.refs_11_ = bf16[4,256,128]{2,1,0:T(8,128)(2,1)S(1)} collective-permute-done((bf16[4,256,128]{2,1,0:T(8,128)(2,1)S(1)}, bf16[4,256,128]{2,1,0:T(8,128)(2,1)S(1)}, u32[]{:S(2)}, u32[]{:S(2)}) %collective-permute-start.9) | collective-permute-done | bytes 262176 | tf_op jit(solution)/shard_map/ppermute | solution.py:257
  67.0 0.4 collective-permute-done.10.refs_12_
  67.4 4.5 %collective-permute-done.11.refs_13_ = bf16[4,256,128]{2,1,0:T(8,128)(2,1)S(1)} collective-permute-done((bf16[4,256,128]{2,1,0:T(8,128)(2,1)S(1)}, bf16[4,256,128]{2,1,0:T(8,128)(2,1)S(1)}, u32[]{:S(2)}, u32[]{:S(2)}) %collective-permute-start.11) | collective-permute-done | bytes 262176 | tf_op jit(solution)/shard_map/ppermute | solution.py:257
  71.9 6.7 %collective-permute-done.12.refs_14_ = bf16[4,256,128]{2,1,0:T(8,128)(2,1)S(1)} collective-permute-done((bf16[4,256,128]{2,1,0:T(8,128)(2,1)S(1)}, bf16[4,256,128]{2,1,0:T(8,128)(2,1)S(1)}, u32[]{:S(2)}, u32[]{:S(2)}) %collective-permute-start.12) | collective-permute-done | bytes 262176 | tf_op jit(solution)/shard_map/ppermute | solution.py:257
  78.7 2.3 %pack.3 = (bf16[4,256,128]{2,1,0:T(8,128)(2,1)S(1)}, bf16[4,256,128]{2,1,0:T(8,128)(2,1)S(1)}, bf16[4,256,128]{2,1,0:T(8,128)(2,1)S(1)}, bf16[4,256,128]{2,1,0:T...) custom-call(s32[33]{0:T(128)S(1)} %pad_add_fusion.meta, ...), custom_call_target="tpu_custom_call" | custom-call | tf_op jit(solution)/shard_map/pack/pallas_call | solution.py:311
  80.9 1.0 collective-permute-start.14
  81.9 1.8 %collective-permute-start.15 = (bf16[4,256,128]{2,1,0:T(8,128)(2,1)S(1)}, bf16[4,256,128]{2,1,0:T(8,128)(2,1)S(1)}, u32[]{:S(2)}, u32[]{:S(2)}) collective-permute-start(bf16[4,256,128]{2,1,0:T(8,128)(2,1)S(1)} %get-tuple-element.85), channel_id=1, source_target_pairs={{0,6},{1,7},{2,0},{3,1},{4,2},{5,3},{6,4},{7,5},{8,14},{9,15},{10,... | collective-permute-start | bytes 786440 | tf_op jit(solution)/shard_map/ppermute | solution.py:257
  83.7 3.2 %collective-permute-start.16 = (bf16[4,256,128]{2,1,0:T(8,128)(2,1)S(1)}, bf16[4,256,128]{2,1,0:T(8,128)(2,1)S(1)}, u32[]{:S(2)}, u32[]{:S(2)}) collective-permute-start(bf16[4,256,128]{2,1,0:T(8,128)(2,1)S(1)} %get-tuple-element.86), channel_id=1, source_target_pairs={{0,3},{1,2},{2,5},{3,4},{4,7},{5,6},{6,1},{7,0},{8,11},{9,10},{10,... | collective-permute-start | bytes 786440 | tf_op jit(solution)/shard_map/ppermute | solution.py:257
  86.9 2.1 %collective-permute-start.17 = (bf16[4,256,128]{2,1,0:T(8,128)(2,1)S(1)}, bf16[4,256,128]{2,1,0:T(8,128)(2,1)S(1)}, u32[]{:S(2)}, u32[]{:S(2)}) collective-permute-start(bf16[4,256,128]{2,1,0:T(8,128)(2,1)S(1)} %get-tuple-element.87), channel_id=1, source_target_pairs={{0,7},{1,6},{2,1},{3,0},{4,3},{5,2},{6,5},{7,4},{8,15},{9,14},{10,... | collective-permute-start | bytes 786440 | tf_op jit(solution)/shard_map/ppermute | solution.py:257
  89.0 1.2 collective-permute-start.18
  90.2 4.3 %collective-permute-start.19 = (bf16[4,256,128]{2,1,0:T(8,128)(2,1)S(1)}, bf16[4,256,128]{2,1,0:T(8,128)(2,1)S(1)}, u32[]{:S(2)}, u32[]{:S(2)}) collective-permute-start(bf16[4,256,128]{2,1,0:T(8,128)(2,1)S(1)} %get-tuple-element.89), channel_id=1, source_target_pairs={{0,5},{1,4},{2,7},{3,6},{4,1},{5,0},{6,3},{7,2},{8,13},{9,12},{10,... | collective-permute-start | bytes 786440 | tf_op jit(solution)/shard_map/ppermute | solution.py:257
  94.5 0.0 collective-permute-done.15.refs_10_
  94.5 14.4 %chunk.2.refs_16_ = f32[128,64,512]{2,1,0:T(8,128)} custom-call(bf16[64,128]{1,0:T(8,128)(2,1)S(1)} %copy-done.2, bf16[512,128]{1,0:T(8,128)(2,1)S(1)} %copy-done, bf16[512,128]{1,0:T(8,128)(2,1)S(1)} %collective-permute-done.refs_1_, bf16[512,128]{1,0:T(8,128)(2,1)S(1)} %collective-permute-done.1.refs_2_, ...), custom_call_target="tpu_custom_call" | custom-call | flops 20000000000 | bytes 16777216 | tf_op jit(solution)/shard_map/chunk/pallas_call | solution.py:226
  108.9 0.0 collective-permute-done.16.refs_11_
  108.9 0.0 collective-permute-done.17.refs_12_
  108.9 0.0 collective-permute-done.18.refs_13_
  108.9 0.4 collective-permute-done.19.refs_14_
  109.4 13.3 %chunk.3 = bf16[4,64,16384]{2,1,0:T(8,128)(2,1)} custom-call(bf16[64,128]{1,0:T(8,128)(2,1)S(1)} %copy-done.1, bf16[512,128]{1,0:T(8,128)(2,1)S(1)} %copy-done, bf16[512,128]{1,0:T(8,128)(2,1)S(1)} %collective-permute-done.refs_1_, bf16[512,128]{1,0:T(8,128)(2,1)S(1)} %collective-permute-done.1.refs_2_, bf16[512,128]{1,0:T(8,128)(2,1)S(1)} %collective-permute-done.2.refs_3_, ...), custom_call_target="tpu_custom_call" | custom-call | flops 20000000000 | bytes 16777216 | tf_op jit(solution)/shard_map/chunk/pallas_call | solution.py:226
  (28 shorter events, 0.1 us)
Async XLA Ops:
  6.8 7.8 %copy-start.8 = (bf16[512,128]{1,0:T(8,128)(2,1)S(1)}, bf16[512,128]{1,0:T(8,128)(2,1)}, u32[]{:S(2)}) copy-start(bf16[512,128]{1,0:T(8,128)(2,1)} %get-tuple-element.54) | copy-start | bytes 393220
  6.8 9.5 %copy-start.7 = (bf16[512,128]{1,0:T(8,128)(2,1)S(1)}, bf16[512,128]{1,0:T(8,128)(2,1)}, u32[]{:S(2)}) copy-start(bf16[512,128]{1,0:T(8,128)(2,1)} %get-tuple-element.55) | copy-start | bytes 393220
  6.8 14.7 %copy-start.6 = (bf16[512,128]{1,0:T(8,128)(2,1)S(1)}, bf16[512,128]{1,0:T(8,128)(2,1)}, u32[]{:S(2)}) copy-start(bf16[512,128]{1,0:T(8,128)(2,1)} %get-tuple-element.58) | copy-start | bytes 393220
  6.8 15.7 %copy-start.3 = (s32[128,4]{0,1:T(4,128)S(1)}, s32[128,4]{0,1:T(4,128)}, u32[]{:S(2)}) copy-start(s32[128,4]{0,1:T(4,128)} %param.8) | copy-start | bytes 6148
  6.8 16.1 %copy-start.5 = (bf16[512,128]{1,0:T(8,128)(2,1)S(1)}, bf16[512,128]{1,0:T(8,128)(2,1)}, u32[]{:S(2)}) copy-start(bf16[512,128]{1,0:T(8,128)(2,1)} %get-tuple-element.59) | copy-start | bytes 393220
  6.8 19.5 %copy-start.4 = (bf16[512,128]{1,0:T(8,128)(2,1)S(1)}, bf16[512,128]{1,0:T(8,128)(2,1)}, u32[]{:S(2)}) copy-start(bf16[512,128]{1,0:T(8,128)(2,1)} %get-tuple-element.60) | copy-start | bytes 393220
  6.8 38.2 %all-to-all-start = ((bf16[16,512,128]{2,1,0:T(8,128)(2,1)}), bf16[16,512,128]{2,1,0:T(8,128)(2,1)S(1)}, u32[]{:S(2)}, u32[]{:S(2)}) async-start(bf16[16,512,128]{2,1,0:T(8,128)(2,1)} %bitcast.13), calls=%async_computation | async-start | bytes 4194304 | tf_op jit(solution)/shard_map/all_to_all | solution.py:297
  14.6 8.3 %collective-permute-start = (bf16[512,128]{1,0:T(8,128)(2,1)S(1)}, bf16[512,128]{1,0:T(8,128)(2,1)S(1)}, u32[]{:S(2)}, u32[]{:S(2)}) collective-permute-start(bf16[512,128]{1,0:T(8,128)(2,1)S(1)} %copy-done.8), channel_id=1, source_target_pairs={{0,2},{1,3},{2,4},{3,5},{4,6},{5,7},{6,0},{7,1},{8,10},{9,11},{10,... | collective-permute-start | bytes 393224 | tf_op jit(solution)/shard_map/ppermute | solution.py:257
  16.3 10.1 %collective-permute-start.1 = (bf16[512,128]{1,0:T(8,128)(2,1)S(1)}, bf16[512,128]{1,0:T(8,128)(2,1)S(1)}, u32[]{:S(2)}, u32[]{:S(2)}) collective-permute-start(bf16[512,128]{1,0:T(8,128)(2,1)S(1)} %copy-done.7), channel_id=1, source_target_pairs={{0,6},{1,7},{2,0},{3,1},{4,2},{5,3},{6,4},{7,5},{8,14},{9,15},{10,... | collective-permute-start | bytes 393224 | tf_op jit(solution)/shard_map/ppermute | solution.py:257
  18.5 8.0 %collective-permute-start.2 = (bf16[512,128]{1,0:T(8,128)(2,1)}, bf16[512,128]{1,0:T(8,128)(2,1)S(1)}, u32[]{:S(2)}, u32[]{:S(2)}) collective-permute-start(bf16[512,128]{1,0:T(8,128)(2,1)} %get-tuple-element.56), channel_id=1, source_target_pairs={{0,3},{1,2},{2,5},{3,4},{4,7},{5,6},{6,1},{7,0},{8,11},{9,10},{10,... | collective-permute-start | bytes 393224 | tf_op jit(solution)/shard_map/ppermute | solution.py:257
  19.2 7.3 %collective-permute-start.3 = (bf16[512,128]{1,0:T(8,128)(2,1)}, bf16[512,128]{1,0:T(8,128)(2,1)S(1)}, u32[]{:S(2)}, u32[]{:S(2)}) collective-permute-start(bf16[512,128]{1,0:T(8,128)(2,1)} %get-tuple-element.57), channel_id=1, source_target_pairs={{0,7},{1,6},{2,1},{3,0},{4,3},{5,2},{6,5},{7,4},{8,15},{9,14},{10,... | collective-permute-start | bytes 393224 | tf_op jit(solution)/shard_map/ppermute | solution.py:257
  21.5 6.8 %collective-permute-start.4 = (bf16[512,128]{1,0:T(8,128)(2,1)S(1)}, bf16[512,128]{1,0:T(8,128)(2,1)S(1)}, u32[]{:S(2)}, u32[]{:S(2)}) collective-permute-start(bf16[512,128]{1,0:T(8,128)(2,1)S(1)} %copy-done.6), channel_id=1, source_target_pairs={{0,4},{1,5},{2,6},{3,7},{4,0},{5,1},{6,2},{7,3},{8,12},{9,13},{10,... | collective-permute-start | bytes 393224 | tf_op jit(solution)/shard_map/ppermute | solution.py:257
  22.9 9.2 %collective-permute-start.5 = (bf16[512,128]{1,0:T(8,128)(2,1)S(1)}, bf16[512,128]{1,0:T(8,128)(2,1)S(1)}, u32[]{:S(2)}, u32[]{:S(2)}) collective-permute-start(bf16[512,128]{1,0:T(8,128)(2,1)S(1)} %copy-done.5), channel_id=1, source_target_pairs={{0,5},{1,4},{2,7},{3,6},{4,1},{5,0},{6,3},{7,2},{8,13},{9,12},{10,... | collective-permute-start | bytes 393224 | tf_op jit(solution)/shard_map/ppermute | solution.py:257
  26.4 5.7 %collective-permute-start.6 = (bf16[512,128]{1,0:T(8,128)(2,1)S(1)}, bf16[512,128]{1,0:T(8,128)(2,1)S(1)}, u32[]{:S(2)}, u32[]{:S(2)}) collective-permute-start(bf16[512,128]{1,0:T(8,128)(2,1)S(1)} %copy-done.4), channel_id=1, source_target_pairs={{0,1},{1,0},{2,3},{3,2},{4,5},{5,4},{6,7},{7,6},{8,9},{9,8},{10,11... | collective-permute-start | bytes 393224 | tf_op jit(solution)/shard_map/ppermute | solution.py:257
  45.1 33.6 %all-to-all-start.1 = ((bf16[16,512,128]{2,1,0:T(8,128)(2,1)}), bf16[16,512,128]{2,1,0:T(8,128)(2,1)}, u32[]{:S(2)}, u32[]{:S(2)}) async-start(bf16[16,512,128]{2,1,0:T(8,128)(2,1)} %bitcast.12), calls=%async_computation.1 | async-start | bytes 4194304 | tf_op jit(solution)/shard_map/all_to_all | solution.py:297
  49.5 45.0 %copy-start = (bf16[512,128]{1,0:T(8,128)(2,1)S(1)}, bf16[512,128]{1,0:T(8,128)(2,1)}, u32[]{:S(2)}) copy-start(bf16[512,128]{1,0:T(8,128)(2,1)} %get-tuple-element.61.refs_0_) | copy-start | bytes 393220
  49.5 45.0 %copy-start.2 = (bf16[64,128]{1,0:T(8,128)(2,1)S(1)}, bf16[64,128]{1,0:T(8,128)(2,1)}, u32[]{:S(2)}) copy-start(bf16[64,128]{1,0:T(8,128)(2,1)} %constant.57.clone.lag_ref) | copy-start | bytes 49156
  50.2 9.0 %collective-permute-start.7 = (bf16[4,256,128]{2,1,0:T(8,128)(2,1)S(1)}, bf16[4,256,128]{2,1,0:T(8,128)(2,1)S(1)}, u32[]{:S(2)}, u32[]{:S(2)}) collective-permute-start(bf16[4,256,128]{2,1,0:T(8,128)(2,1)S(1)} %get-tuple-element.75), channel_id=1, source_target_pairs={{0,2},{1,3},{2,4},{3,5},{4,6},{5,7},{6,0},{7,1},{8,10},{9,11},{10,... | collective-permute-start | bytes 786440 | tf_op jit(solution)/shard_map/ppermute | solution.py:257
  51.9 12.1 %collective-permute-start.8 = (bf16[4,256,128]{2,1,0:T(8,128)(2,1)S(1)}, bf16[4,256,128]{2,1,0:T(8,128)(2,1)S(1)}, u32[]{:S(2)}, u32[]{:S(2)}) collective-permute-start(bf16[4,256,128]{2,1,0:T(8,128)(2,1)S(1)} %get-tuple-element.76), channel_id=1, source_target_pairs={{0,6},{1,7},{2,0},{3,1},{4,2},{5,3},{6,4},{7,5},{8,14},{9,15},{10,... | collective-permute-start | bytes 786440 | tf_op jit(solution)/shard_map/ppermute | solution.py:257
  54.1 12.9 %collective-permute-start.9 = (bf16[4,256,128]{2,1,0:T(8,128)(2,1)S(1)}, bf16[4,256,128]{2,1,0:T(8,128)(2,1)S(1)}, u32[]{:S(2)}, u32[]{:S(2)}) collective-permute-start(bf16[4,256,128]{2,1,0:T(8,128)(2,1)S(1)} %get-tuple-element.77), channel_id=1, source_target_pairs={{0,3},{1,2},{2,5},{3,4},{4,7},{5,6},{6,1},{7,0},{8,11},{9,10},{10,... | collective-permute-start | bytes 786440 | tf_op jit(solution)/shard_map/ppermute | solution.py:257
  56.0 11.4 %collective-permute-start.10 = (bf16[4,256,128]{2,1,0:T(8,128)(2,1)S(1)}, bf16[4,256,128]{2,1,0:T(8,128)(2,1)S(1)}, u32[]{:S(2)}, u32[]{:S(2)}) collective-permute-start(bf16[4,256,128]{2,1,0:T(8,128)(2,1)S(1)} %get-tuple-element.78), channel_id=1, source_target_pairs={{0,7},{1,6},{2,1},{3,0},{4,3},{5,2},{6,5},{7,4},{8,15},{9,14},{10,... | collective-permute-start | bytes 786440 | tf_op jit(solution)/shard_map/ppermute | solution.py:257
  58.1 13.8 %collective-permute-start.11 = (bf16[4,256,128]{2,1,0:T(8,128)(2,1)S(1)}, bf16[4,256,128]{2,1,0:T(8,128)(2,1)S(1)}, u32[]{:S(2)}, u32[]{:S(2)}) collective-permute-start(bf16[4,256,128]{2,1,0:T(8,128)(2,1)S(1)} %get-tuple-element.79), channel_id=1, source_target_pairs={{0,4},{1,5},{2,6},{3,7},{4,0},{5,1},{6,2},{7,3},{8,12},{9,13},{10,... | collective-permute-start | bytes 786440 | tf_op jit(solution)/shard_map/ppermute | solution.py:257
  59.3 19.4 %collective-permute-start.12 = (bf16[4,256,128]{2,1,0:T(8,128)(2,1)S(1)}, bf16[4,256,128]{2,1,0:T(8,128)(2,1)S(1)}, u32[]{:S(2)}, u32[]{:S(2)}) collective-permute-start(bf16[4,256,128]{2,1,0:T(8,128)(2,1)S(1)} %get-tuple-element.80), channel_id=1, source_target_pairs={{0,5},{1,4},{2,7},{3,6},{4,1},{5,0},{6,3},{7,2},{8,13},{9,12},{10,... | collective-permute-start | bytes 786440 | tf_op jit(solution)/shard_map/ppermute | solution.py:257
  64.0 14.7 %collective-permute-start.13 = (bf16[4,256,128]{2,1,0:T(8,128)(2,1)S(1)}, bf16[4,256,128]{2,1,0:T(8,128)(2,1)S(1)}, u32[]{:S(2)}, u32[]{:S(2)}) collective-permute-start(bf16[4,256,128]{2,1,0:T(8,128)(2,1)S(1)} %get-tuple-element.81), channel_id=1, source_target_pairs={{0,1},{1,0},{2,3},{3,2},{4,5},{5,4},{6,7},{7,6},{8,9},{9,8},{10,11... | collective-permute-start | bytes 786440 | tf_op jit(solution)/shard_map/ppermute | solution.py:257
  80.9 9.3 %collective-permute-start.14 = (bf16[4,256,128]{2,1,0:T(8,128)(2,1)S(1)}, bf16[4,256,128]{2,1,0:T(8,128)(2,1)S(1)}, u32[]{:S(2)}, u32[]{:S(2)}) collective-permute-start(bf16[4,256,128]{2,1,0:T(8,128)(2,1)S(1)} %get-tuple-element.84), channel_id=1, source_target_pairs={{0,2},{1,3},{2,4},{3,5},{4,6},{5,7},{6,0},{7,1},{8,10},{9,11},{10,... | collective-permute-start | bytes 786440 | tf_op jit(solution)/shard_map/ppermute | solution.py:257
  81.9 12.6 %collective-permute-start.15 = (bf16[4,256,128]{2,1,0:T(8,128)(2,1)S(1)}, bf16[4,256,128]{2,1,0:T(8,128)(2,1)S(1)}, u32[]{:S(2)}, u32[]{:S(2)}) collective-permute-start(bf16[4,256,128]{2,1,0:T(8,128)(2,1)S(1)} %get-tuple-element.85), channel_id=1, source_target_pairs={{0,6},{1,7},{2,0},{3,1},{4,2},{5,3},{6,4},{7,5},{8,14},{9,15},{10,... | collective-permute-start | bytes 786440 | tf_op jit(solution)/shard_map/ppermute | solution.py:257
  83.7 25.2 %collective-permute-start.16 = (bf16[4,256,128]{2,1,0:T(8,128)(2,1)S(1)}, bf16[4,256,128]{2,1,0:T(8,128)(2,1)S(1)}, u32[]{:S(2)}, u32[]{:S(2)}) collective-permute-start(bf16[4,256,128]{2,1,0:T(8,128)(2,1)S(1)} %get-tuple-element.86), channel_id=1, source_target_pairs={{0,3},{1,2},{2,5},{3,4},{4,7},{5,6},{6,1},{7,0},{8,11},{9,10},{10,... | collective-permute-start | bytes 786440 | tf_op jit(solution)/shard_map/ppermute | solution.py:257
  86.9 22.0 %collective-permute-start.17 = (bf16[4,256,128]{2,1,0:T(8,128)(2,1)S(1)}, bf16[4,256,128]{2,1,0:T(8,128)(2,1)S(1)}, u32[]{:S(2)}, u32[]{:S(2)}) collective-permute-start(bf16[4,256,128]{2,1,0:T(8,128)(2,1)S(1)} %get-tuple-element.87), channel_id=1, source_target_pairs={{0,7},{1,6},{2,1},{3,0},{4,3},{5,2},{6,5},{7,4},{8,15},{9,14},{10,... | collective-permute-start | bytes 786440 | tf_op jit(solution)/shard_map/ppermute | solution.py:257
  89.0 19.9 %collective-permute-start.18 = (bf16[4,256,128]{2,1,0:T(8,128)(2,1)S(1)}, bf16[4,256,128]{2,1,0:T(8,128)(2,1)S(1)}, u32[]{:S(2)}, u32[]{:S(2)}) collective-permute-start(bf16[4,256,128]{2,1,0:T(8,128)(2,1)S(1)} %get-tuple-element.88), channel_id=1, source_target_pairs={{0,4},{1,5},{2,6},{3,7},{4,0},{5,1},{6,2},{7,3},{8,12},{9,13},{10,... | collective-permute-start | bytes 786440 | tf_op jit(solution)/shard_map/ppermute | solution.py:257
  90.2 19.2 %collective-permute-start.19 = (bf16[4,256,128]{2,1,0:T(8,128)(2,1)S(1)}, bf16[4,256,128]{2,1,0:T(8,128)(2,1)S(1)}, u32[]{:S(2)}, u32[]{:S(2)}) collective-permute-start(bf16[4,256,128]{2,1,0:T(8,128)(2,1)S(1)} %get-tuple-element.89), channel_id=1, source_target_pairs={{0,5},{1,4},{2,7},{3,6},{4,1},{5,0},{6,3},{7,2},{8,13},{9,12},{10,... | collective-permute-start | bytes 786440 | tf_op jit(solution)/shard_map/ppermute | solution.py:257
  94.5 14.9 %copy-start.1 = (bf16[64,128]{1,0:T(8,128)(2,1)S(1)}, bf16[64,128]{1,0:T(8,128)(2,1)}, u32[]{:S(2)}) copy-start(bf16[64,128]{1,0:T(8,128)(2,1)} %constant.58.clone.lag_ref) | copy-start | bytes 49156
  94.5 14.9 %collective-permute-start.20 = (bf16[4,256,128]{2,1,0:T(8,128)(2,1)S(1)}, bf16[4,256,128]{2,1,0:T(8,128)(2,1)S(1)}, u32[]{:S(2)}, u32[]{:S(2)}) collective-permute-start(bf16[4,256,128]{2,1,0:T(8,128)(2,1)S(1)} %get-tuple-element.90), channel_id=1, source_target_pairs={{0,1},{1,0},{2,3},{3,2},{4,5},{5,4},{6,7},{7,6},{8,9},{9,8},{10,11... | collective-permute-start | bytes 786440 | tf_op jit(solution)/shard_map/ppermute | solution.py:257

commit v7 on v5

--- a/solution.py
+++ b/solution.py
@@ -20,8 +20,8 @@
 BEGIN = tuple(sum(SPLIT[:c]) for c in range(len(SPLIT)))
 LAST = len(SPLIT) - 1
 AT_ONCE = 4
-LAG_BLOCK = 16
-HOPS = ((0, 0), (1, 0), (3, 0), (1, 1), (3, 1), (2, 0), (2, 1), (0, 1))
+LAG_BLOCK = 32
+HOPS = ((0, 0), (1, 0), (3, 0), (2, 0), (1, 1), (3, 1), (2, 1), (0, 1))
 IN_HBM = pl.BlockSpec(memory_space=pltpu.HBM)
 IN_VMEM = pl.BlockSpec(memory_space=pltpu.VMEM)
 
@@ -146,8 +146,11 @@
 
 def chunk_kernel(c, members, lag_ref, *refs):
     own_refs, part_refs = refs[:members], refs[members : 2 * members]
-    before_ref = refs[2 * members] if c else None
-    out_ref, cross_ref, rows_ref = refs[-3:]
+    refs = refs[2 * members :]
+    if c:
+        before_ref, out_ref, cross_ref, rows_ref = refs
+    else:
+        out_ref, cross_ref, rows_ref = refs
     pairs = part_refs[0].shape[0]
     octets = SPLIT[c]
     step = pl.program_id(0)
@@ -184,24 +187,21 @@
     return jax.ShapeDtypeStruct(shape, jnp.bfloat16)
 
 
-def prefetched(n_in, n_out):
-    return pltpu.PrefetchScalarGridSpec(
-        num_scalar_prefetch=1, grid=(), in_specs=[IN_VMEM] * n_in, out_specs=[IN_VMEM] * n_out
-    )
-
-
 def chunk(c, own, parts, before, pairs):
     members = len(own)
     octets = SPLIT[c]
     lags = jnp.asarray(lag_table()[:, 16 * BEGIN[c] : 16 * (BEGIN[c] + octets)])
     blocks = BCH // LAG_BLOCK
+    sums = (BCH, LAGS, pairs * BCH)
+
+    def after(s):
+        return jnp.maximum(s - octets, 0)
+
     if c == LAST:
         out = bf16(pairs, LAGS, BCH * BCH)
-        out_spec = pl.BlockSpec(
-            (pairs, LAGS, LAG_BLOCK * BCH), lambda s: (0, 0, jnp.maximum(s - octets, 0))
-        )
+        out_spec = pl.BlockSpec((pairs, LAGS, LAG_BLOCK * BCH), lambda s: (0, 0, after(s)))
     else:
-        out = jax.ShapeDtypeStruct((BCH, LAGS, pairs * BCH), jnp.float32)
+        out = jax.ShapeDtypeStruct(sums, jnp.float32)
         out_spec = IN_VMEM
     return pl.pallas_call(
         functools.partial(chunk_kernel, c, members),
@@ -213,7 +213,7 @@
             pltpu.VMEM((octets, BCH, 16, pairs * BCH), jnp.bfloat16),
             pltpu.VMEM((2, BCH, 32 * members), jnp.float32),
         ],
-        compiler_params=params(40),
+        compiler_params=params(22),
         cost_estimate=pl.CostEstimate(
             flops=2_500_000_000 * octets, bytes_accessed=2**21 * octets, transcendentals=0
         ),
@@ -289,7 +289,12 @@
             got, sends[c + 1] = lax.optimization_barrier((got, sends[c + 1]))
         parts = pl.pallas_call(
             functools.partial(pack_kernel, members, pairs),
-            grid_spec=prefetched(1, members),
+            grid_spec=pltpu.PrefetchScalarGridSpec(
+                num_scalar_prefetch=1,
+                grid=(),
+                in_specs=[IN_VMEM],
+                out_specs=[IN_VMEM] * members,
+            ),
             out_shape=[bf16(pairs, 32 * octets, BCH)] * members,
             compiler_params=params(16),
             name="pack",

time: 130 us -> 120 us (0.923)
  Pallas kernels: 44.4 us -> 31.1 us
  starting transfers between devices: 50.8 us -> 57 us
  waiting for transfers between devices: 33.3 us -> 30.5 us
    pallas_call x2, Pallas kernels: 34.7 us -> 21.4 us  [chunk(): pl.pallas_call(functools.partial(chunk_kernel, c, members), grid=(octets...]
    ppermute x21, starting transfers between devices: 38.6 us -> 44.8 us  [move(): moved.append(lax.ppermute(piece, 'win', way))]
    ppermute x21, waiting for transfers between devices: 20.3 us -> 17.5 us  [move(): moved.append(lax.ppermute(piece, 'win', way))]
  transfers between devices with their start and end apart: 23 -> 23, of which waited for: 7 -> 9; matrix products, arithmetic and copies ran while one was open for 0% -> 0% of each run, Pallas kernels for 13% -> 8%
where the time goes in v7:
time: 120 us; the launch traced here: 119 us
  starting transfers between devices  57 us (48%)
  Pallas kernels  31.1 us (26%)
  waiting for transfers between devices  30.5 us (25%)
    ppermute x21, starting transfers between devices, move(): moved.append(lax.ppermute(piece, 'win', way))  44.8 us
    pallas_call x2, Pallas kernels, chunk(): pl.pallas_call(functools.partial(chunk_kernel, c, members), grid=(octets...  21.4 us
    ppermute x21, waiting for transfers between devices, move(): moved.append(lax.ppermute(piece, 'win', way))  17.5 us
    all_to_all x2, waiting for transfers between devices, shards(): lax.all_to_all(sends[c].reshape(groups, 64 * octets, BCH), 'blk', split_a...  13 us
    all_to_all x2, starting transfers between devices, shards(): lax.all_to_all(sends[c].reshape(groups, 64 * octets, BCH), 'blk', split_a...  12.2 us
    pallas_call x1, Pallas kernels, shards(): pl.pallas_call(functools.partial(spectra_kernel, members, groups), grid_s...  6.76 us
    pallas_call x2, Pallas kernels, shards(): pl.pallas_call(functools.partial(pack_kernel, members, pairs), grid_spec=...  2.96 us
  transfers between devices with their start and end apart: 23, of which 9 were waited for; matrix products, arithmetic and copies ran while one was open for 0% of the time, Pallas kernels for 8%

profile of v7, /device:TPU:1, one launch (start us, length us, event | category | flops | bytes accessed | tf_op | source)
XLA Modules:
  0.0 119.4 jit_solution(8616093425640401831)
XLA Ops:
  0.0 6.8 %spectra.1 = (bf16[32,256,128]{2,1,0:T(8,128)(2,1)}, bf16[32,256,128]{2,1,0:T(8,128)(2,1)}, bf16[512,128]{1,0:T(8,128)(2,1)}, bf16[512,128]{1,0:T(8,128)(2,1)}, ...) custom-call(s32[4,128]{1,0:T(4,128)} %bitcast.14, ...), custom_call_target="tpu_custom_call" | custom-call | tf_op jit(solution)/shard_map/spectra/pallas_call | solution.py:249
  6.8 0.0 copy-start.3
  6.8 7.7 %all-to-all-start = ((bf16[16,512,128]{2,1,0:T(8,128)(2,1)}), bf16[16,512,128]{2,1,0:T(8,128)(2,1)S(1)}, u32[]{:S(2)}, u32[]{:S(2)}) async-start(bf16[16,512,128]{2,1,0:T(8,128)(2,1)} %bitcast.13), calls=%async_computation | async-start | bytes 4194304 | tf_op jit(solution)/shard_map/all_to_all | solution.py:276
  14.6 1.7 %collective-permute-start = (bf16[512,128]{1,0:T(8,128)(2,1)S(1)}, bf16[512,128]{1,0:T(8,128)(2,1)S(1)}, u32[]{:S(2)}, u32[]{:S(2)}) collective-permute-start(bf16[512,128]{1,0:T(8,128)(2,1)S(1)} %copy-done.8), channel_id=1, source_target_pairs={{0,2},{1,3},{2,4},{3,5},{4,6},{5,7},{6,0},{7,1},{8,10},{9,11},{10,... | collective-permute-start | bytes 393224 | tf_op jit(solution)/shard_map/ppermute | solution.py:236
  16.3 2.2 %collective-permute-start.1 = (bf16[512,128]{1,0:T(8,128)(2,1)S(1)}, bf16[512,128]{1,0:T(8,128)(2,1)S(1)}, u32[]{:S(2)}, u32[]{:S(2)}) collective-permute-start(bf16[512,128]{1,0:T(8,128)(2,1)S(1)} %copy-done.7), channel_id=1, source_target_pairs={{0,6},{1,7},{2,0},{3,1},{4,2},{5,3},{6,4},{7,5},{8,14},{9,15},{10,... | collective-permute-start | bytes 393224 | tf_op jit(solution)/shard_map/ppermute | solution.py:236
  18.5 1.2 %collective-permute-start.2 = (bf16[512,128]{1,0:T(8,128)(2,1)}, bf16[512,128]{1,0:T(8,128)(2,1)S(1)}, u32[]{:S(2)}, u32[]{:S(2)}) collective-permute-start(bf16[512,128]{1,0:T(8,128)(2,1)} %get-tuple-element.56), channel_id=1, source_target_pairs={{0,4},{1,5},{2,6},{3,7},{4,0},{5,1},{6,2},{7,3},{8,12},{9,13},{10,... | collective-permute-start | bytes 393224 | tf_op jit(solution)/shard_map/ppermute | solution.py:236
  19.7 2.4 %collective-permute-start.3 = (bf16[512,128]{1,0:T(8,128)(2,1)}, bf16[512,128]{1,0:T(8,128)(2,1)S(1)}, u32[]{:S(2)}, u32[]{:S(2)}) collective-permute-start(bf16[512,128]{1,0:T(8,128)(2,1)} %get-tuple-element.57), channel_id=1, source_target_pairs={{0,3},{1,2},{2,5},{3,4},{4,7},{5,6},{6,1},{7,0},{8,11},{9,10},{10,... | collective-permute-start | bytes 393224 | tf_op jit(solution)/shard_map/ppermute | solution.py:236
  22.1 0.5 collective-permute-start.4
  22.7 0.1 copy.8
  22.8 0.1 reshape.82
  22.9 0.2 and_reduce_fusion
  23.1 0.0 collective-permute-done.refs_1_
  23.1 2.0 %collective-permute-start.5 = (bf16[512,128]{1,0:T(8,128)(2,1)S(1)}, bf16[512,128]{1,0:T(8,128)(2,1)S(1)}, u32[]{:S(2)}, u32[]{:S(2)}) collective-permute-start(bf16[512,128]{1,0:T(8,128)(2,1)S(1)} %copy-done.5), channel_id=1, source_target_pairs={{0,5},{1,4},{2,7},{3,6},{4,1},{5,0},{6,3},{7,2},{8,13},{9,12},{10,... | collective-permute-start | bytes 393224 | tf_op jit(solution)/shard_map/ppermute | solution.py:236
  25.1 0.0 collective-permute-done.1.refs_2_
  25.1 0.0 collective-permute-start.6
  25.2 0.1 pad_add_fusion.meta
  25.2 0.2 collective-permute-done.2.refs_3_
  25.4 3.8 %collective-permute-done.3.refs_4_ = bf16[512,128]{1,0:T(8,128)(2,1)S(1)} collective-permute-done((bf16[512,128]{1,0:T(8,128)(2,1)}, bf16[512,128]{1,0:T(8,128)(2,1)S(1)}, u32[]{:S(2)}, u32[]{:S(2)}) %collective-permute-start.3) | collective-permute-done | bytes 131104 | tf_op jit(solution)/shard_map/ppermute | solution.py:236
  29.2 0.1 collective-permute-done.4.refs_5_
  29.3 2.8 %collective-permute-done.5.refs_6_ = bf16[512,128]{1,0:T(8,128)(2,1)S(1)} collective-permute-done((bf16[512,128]{1,0:T(8,128)(2,1)S(1)}, bf16[512,128]{1,0:T(8,128)(2,1)S(1)}, u32[]{:S(2)}, u32[]{:S(2)}) %collective-permute-start.5) | collective-permute-done | bytes 131104 | tf_op jit(solution)/shard_map/ppermute | solution.py:236
  32.1 0.0 collective-permute-done.6.refs_7_
  32.1 13.0 %all-to-all-done = bf16[16,512,128]{2,1,0:T(8,128)(2,1)S(1)} async-done(((bf16[16,512,128]{2,1,0:T(8,128)(2,1)}), bf16[16,512,128]{2,1,0:T(8,128)(2,1)S(1)}, u32[]{:S(2)}, u32[]{:S(2)}) %all-to-all-start) | async-done | bytes 2097184 | tf_op jit(solution)/shard_map/all_to_all | solution.py:276
  45.1 4.4 %all-to-all-start.1 = ((bf16[16,512,128]{2,1,0:T(8,128)(2,1)}), bf16[16,512,128]{2,1,0:T(8,128)(2,1)}, u32[]{:S(2)}, u32[]{:S(2)}) async-start(bf16[16,512,128]{2,1,0:T(8,128)(2,1)} %bitcast.12), calls=%async_computation.1 | async-start | bytes 4194304 | tf_op jit(solution)/shard_map/all_to_all | solution.py:276
  49.5 0.0 copy-start.2
  49.5 0.7 pack.2
  50.2 1.7 %collective-permute-start.7 = (bf16[4,256,128]{2,1,0:T(8,128)(2,1)S(1)}, bf16[4,256,128]{2,1,0:T(8,128)(2,1)S(1)}, u32[]{:S(2)}, u32[]{:S(2)}) collective-permute-start(bf16[4,256,128]{2,1,0:T(8,128)(2,1)S(1)} %get-tuple-element.75), channel_id=1, source_target_pairs={{0,2},{1,3},{2,4},{3,5},{4,6},{5,7},{6,0},{7,1},{8,10},{9,11},{10,... | collective-permute-start | bytes 786440 | tf_op jit(solution)/shard_map/ppermute | solution.py:236
  51.9 2.2 %collective-permute-start.8 = (bf16[4,256,128]{2,1,0:T(8,128)(2,1)S(1)}, bf16[4,256,128]{2,1,0:T(8,128)(2,1)S(1)}, u32[]{:S(2)}, u32[]{:S(2)}) collective-permute-start(bf16[4,256,128]{2,1,0:T(8,128)(2,1)S(1)} %get-tuple-element.76), channel_id=1, source_target_pairs={{0,6},{1,7},{2,0},{3,1},{4,2},{5,3},{6,4},{7,5},{8,14},{9,15},{10,... | collective-permute-start | bytes 786440 | tf_op jit(solution)/shard_map/ppermute | solution.py:236
  54.1 1.2 %collective-permute-start.9 = (bf16[4,256,128]{2,1,0:T(8,128)(2,1)S(1)}, bf16[4,256,128]{2,1,0:T(8,128)(2,1)S(1)}, u32[]{:S(2)}, u32[]{:S(2)}) collective-permute-start(bf16[4,256,128]{2,1,0:T(8,128)(2,1)S(1)} %get-tuple-element.77), channel_id=1, source_target_pairs={{0,4},{1,5},{2,6},{3,7},{4,0},{5,1},{6,2},{7,3},{8,12},{9,13},{10,... | collective-permute-start | bytes 786440 | tf_op jit(solution)/shard_map/ppermute | solution.py:236
  55.4 3.6 %collective-permute-start.10 = (bf16[4,256,128]{2,1,0:T(8,128)(2,1)S(1)}, bf16[4,256,128]{2,1,0:T(8,128)(2,1)S(1)}, u32[]{:S(2)}, u32[]{:S(2)}) collective-permute-start(bf16[4,256,128]{2,1,0:T(8,128)(2,1)S(1)} %get-tuple-element.78), channel_id=1, source_target_pairs={{0,3},{1,2},{2,5},{3,4},{4,7},{5,6},{6,1},{7,0},{8,11},{9,10},{10,... | collective-permute-start | bytes 786440 | tf_op jit(solution)/shard_map/ppermute | solution.py:236
  58.9 0.0 collective-permute-start.11
  58.9 0.0 collective-permute-done.7.refs_9_
  59.0 9.8 %collective-permute-start.12 = (bf16[4,256,128]{2,1,0:T(8,128)(2,1)S(1)}, bf16[4,256,128]{2,1,0:T(8,128)(2,1)S(1)}, u32[]{:S(2)}, u32[]{:S(2)}) collective-permute-start(bf16[4,256,128]{2,1,0:T(8,128)(2,1)S(1)} %get-tuple-element.80), channel_id=1, source_target_pairs={{0,5},{1,4},{2,7},{3,6},{4,1},{5,0},{6,3},{7,2},{8,13},{9,12},{10,... | collective-permute-start | bytes 786440 | tf_op jit(solution)/shard_map/ppermute | solution.py:236
  68.8 0.0 collective-permute-done.8.refs_10_
  68.8 4.9 %collective-permute-done.10.refs_12_ = bf16[4,256,128]{2,1,0:T(8,128)(2,1)S(1)} collective-permute-done((bf16[4,256,128]{2,1,0:T(8,128)(2,1)S(1)}, bf16[4,256,128]{2,1,0:T(8,128)(2,1)S(1)}, u32[]{:S(2)}, u32[]{:S(2)}) %collective-permute-start.10) | collective-permute-done | bytes 262176 | tf_op jit(solution)/shard_map/ppermute | solution.py:236
  73.7 0.8 collective-permute-done.11.refs_13_
  74.5 4.1 %collective-permute-done.12.refs_14_ = bf16[4,256,128]{2,1,0:T(8,128)(2,1)S(1)} collective-permute-done((bf16[4,256,128]{2,1,0:T(8,128)(2,1)S(1)}, bf16[4,256,128]{2,1,0:T(8,128)(2,1)S(1)}, u32[]{:S(2)}, u32[]{:S(2)}) %collective-permute-start.12) | collective-permute-done | bytes 262176 | tf_op jit(solution)/shard_map/ppermute | solution.py:236
  78.7 0.0 all-to-all-done.1
  78.7 2.3 %pack.3 = (bf16[4,256,128]{2,1,0:T(8,128)(2,1)S(1)}, bf16[4,256,128]{2,1,0:T(8,128)(2,1)S(1)}, bf16[4,256,128]{2,1,0:T(8,128)(2,1)S(1)}, bf16[4,256,128]{2,1,0:T...) custom-call(s32[33]{0:T(128)S(1)} %pad_add_fusion.meta, ...), custom_call_target="tpu_custom_call" | custom-call | tf_op jit(solution)/shard_map/pack/pallas_call | solution.py:290
  80.9 0.9 collective-permute-start.14
  81.9 1.8 %collective-permute-start.15 = (bf16[4,256,128]{2,1,0:T(8,128)(2,1)S(1)}, bf16[4,256,128]{2,1,0:T(8,128)(2,1)S(1)}, u32[]{:S(2)}, u32[]{:S(2)}) collective-permute-start(bf16[4,256,128]{2,1,0:T(8,128)(2,1)S(1)} %get-tuple-element.85), channel_id=1, source_target_pairs={{0,6},{1,7},{2,0},{3,1},{4,2},{5,3},{6,4},{7,5},{8,14},{9,15},{10,... | collective-permute-start | bytes 786440 | tf_op jit(solution)/shard_map/ppermute | solution.py:236
  83.7 0.1 collective-permute-start.16
  83.8 6.1 %collective-permute-start.17 = (bf16[4,256,128]{2,1,0:T(8,128)(2,1)S(1)}, bf16[4,256,128]{2,1,0:T(8,128)(2,1)S(1)}, u32[]{:S(2)}, u32[]{:S(2)}) collective-permute-start(bf16[4,256,128]{2,1,0:T(8,128)(2,1)S(1)} %get-tuple-element.87), channel_id=1, source_target_pairs={{0,3},{1,2},{2,5},{3,4},{4,7},{5,6},{6,1},{7,0},{8,11},{9,10},{10,... | collective-permute-start | bytes 786440 | tf_op jit(solution)/shard_map/ppermute | solution.py:236
  89.9 0.0 collective-permute-start.18
  89.9 7.2 %collective-permute-start.19 = (bf16[4,256,128]{2,1,0:T(8,128)(2,1)S(1)}, bf16[4,256,128]{2,1,0:T(8,128)(2,1)S(1)}, u32[]{:S(2)}, u32[]{:S(2)}) collective-permute-start(bf16[4,256,128]{2,1,0:T(8,128)(2,1)S(1)} %get-tuple-element.89), channel_id=1, source_target_pairs={{0,5},{1,4},{2,7},{3,6},{4,1},{5,0},{6,3},{7,2},{8,13},{9,12},{10,... | collective-permute-start | bytes 786440 | tf_op jit(solution)/shard_map/ppermute | solution.py:236
  97.1 0.0 collective-permute-start.20
  97.2 9.3 %chunk.2.refs_16_ = f32[128,64,512]{2,1,0:T(8,128)S(1)} custom-call(bf16[64,128]{1,0:T(8,128)(2,1)S(1)} %copy-done.2, bf16[512,128]{1,0:T(8,128)(2,1)S(1)} %copy-done, bf16[512,128]{1,0:T(8,128)(2,1)S(1)} %collective-permute-done.refs_1_, bf16[512,128]{1,0:T(8,128)(2,1)S(1)} %collective-permute-done.1.refs_2_, ...), custom_call_target="tpu_custom_call" | custom-call | flops 20000000000 | bytes 16777216 | tf_op jit(solution)/shard_map/chunk/pallas_call | solution.py:206
  106.5 0.8 collective-permute-done.19.refs_14_
  107.3 12.1 %chunk.3 = bf16[4,64,16384]{2,1,0:T(8,128)(2,1)} custom-call(bf16[64,128]{1,0:T(8,128)(2,1)S(1)} %copy-done.1, bf16[512,128]{1,0:T(8,128)(2,1)S(1)} %copy-done, bf16[512,128]{1,0:T(8,128)(2,1)S(1)} %collective-permute-done.refs_1_, bf16[512,128]{1,0:T(8,128)(2,1)S(1)} %collective-permute-done.1.refs_2_, bf16[512,128]{1,0:T(8,128)(2,1)S(1)} %collective-permute-done.2.refs_3_, ...), custom_call_target="tpu_custom_call" | custom-call | flops 20000000000 | bytes 16777216 | tf_op jit(solution)/shard_map/chunk/pallas_call | solution.py:206
  (28 shorter events, 0.1 us)
Async XLA Ops:
  6.8 7.8 %copy-start.8 = (bf16[512,128]{1,0:T(8,128)(2,1)S(1)}, bf16[512,128]{1,0:T(8,128)(2,1)}, u32[]{:S(2)}) copy-start(bf16[512,128]{1,0:T(8,128)(2,1)} %get-tuple-element.54) | copy-start | bytes 393220
  6.8 9.5 %copy-start.7 = (bf16[512,128]{1,0:T(8,128)(2,1)S(1)}, bf16[512,128]{1,0:T(8,128)(2,1)}, u32[]{:S(2)}) copy-start(bf16[512,128]{1,0:T(8,128)(2,1)} %get-tuple-element.55) | copy-start | bytes 393220
  6.8 15.3 %copy-start.6 = (bf16[512,128]{1,0:T(8,128)(2,1)S(1)}, bf16[512,128]{1,0:T(8,128)(2,1)}, u32[]{:S(2)}) copy-start(bf16[512,128]{1,0:T(8,128)(2,1)} %get-tuple-element.58) | copy-start | bytes 393220
  6.8 15.9 %copy-start.3 = (s32[128,4]{0,1:T(4,128)S(1)}, s32[128,4]{0,1:T(4,128)}, u32[]{:S(2)}) copy-start(s32[128,4]{0,1:T(4,128)} %param.8) | copy-start | bytes 6148
  6.8 16.3 %copy-start.5 = (bf16[512,128]{1,0:T(8,128)(2,1)S(1)}, bf16[512,128]{1,0:T(8,128)(2,1)}, u32[]{:S(2)}) copy-start(bf16[512,128]{1,0:T(8,128)(2,1)} %get-tuple-element.59) | copy-start | bytes 393220
  6.8 18.3 %copy-start.4 = (bf16[512,128]{1,0:T(8,128)(2,1)S(1)}, bf16[512,128]{1,0:T(8,128)(2,1)}, u32[]{:S(2)}) copy-start(bf16[512,128]{1,0:T(8,128)(2,1)} %get-tuple-element.60) | copy-start | bytes 393220
  6.8 38.2 %all-to-all-start = ((bf16[16,512,128]{2,1,0:T(8,128)(2,1)}), bf16[16,512,128]{2,1,0:T(8,128)(2,1)S(1)}, u32[]{:S(2)}, u32[]{:S(2)}) async-start(bf16[16,512,128]{2,1,0:T(8,128)(2,1)} %bitcast.13), calls=%async_computation | async-start | bytes 4194304 | tf_op jit(solution)/shard_map/all_to_all | solution.py:276
  14.6 8.5 %collective-permute-start = (bf16[512,128]{1,0:T(8,128)(2,1)S(1)}, bf16[512,128]{1,0:T(8,128)(2,1)S(1)}, u32[]{:S(2)}, u32[]{:S(2)}) collective-permute-start(bf16[512,128]{1,0:T(8,128)(2,1)S(1)} %copy-done.8), channel_id=1, source_target_pairs={{0,2},{1,3},{2,4},{3,5},{4,6},{5,7},{6,0},{7,1},{8,10},{9,11},{10,... | collective-permute-start | bytes 393224 | tf_op jit(solution)/shard_map/ppermute | solution.py:236
  16.3 8.9 %collective-permute-start.1 = (bf16[512,128]{1,0:T(8,128)(2,1)S(1)}, bf16[512,128]{1,0:T(8,128)(2,1)S(1)}, u32[]{:S(2)}, u32[]{:S(2)}) collective-permute-start(bf16[512,128]{1,0:T(8,128)(2,1)S(1)} %copy-done.7), channel_id=1, source_target_pairs={{0,6},{1,7},{2,0},{3,1},{4,2},{5,3},{6,4},{7,5},{8,14},{9,15},{10,... | collective-permute-start | bytes 393224 | tf_op jit(solution)/shard_map/ppermute | solution.py:236
  18.5 6.9 %collective-permute-start.2 = (bf16[512,128]{1,0:T(8,128)(2,1)}, bf16[512,128]{1,0:T(8,128)(2,1)S(1)}, u32[]{:S(2)}, u32[]{:S(2)}) collective-permute-start(bf16[512,128]{1,0:T(8,128)(2,1)} %get-tuple-element.56), channel_id=1, source_target_pairs={{0,4},{1,5},{2,6},{3,7},{4,0},{5,1},{6,2},{7,3},{8,12},{9,13},{10,... | collective-permute-start | bytes 393224 | tf_op jit(solution)/shard_map/ppermute | solution.py:236
  19.7 9.5 %collective-permute-start.3 = (bf16[512,128]{1,0:T(8,128)(2,1)}, bf16[512,128]{1,0:T(8,128)(2,1)S(1)}, u32[]{:S(2)}, u32[]{:S(2)}) collective-permute-start(bf16[512,128]{1,0:T(8,128)(2,1)} %get-tuple-element.57), channel_id=1, source_target_pairs={{0,3},{1,2},{2,5},{3,4},{4,7},{5,6},{6,1},{7,0},{8,11},{9,10},{10,... | collective-permute-start | bytes 393224 | tf_op jit(solution)/shard_map/ppermute | solution.py:236
  22.1 7.1 %collective-permute-start.4 = (bf16[512,128]{1,0:T(8,128)(2,1)S(1)}, bf16[512,128]{1,0:T(8,128)(2,1)S(1)}, u32[]{:S(2)}, u32[]{:S(2)}) collective-permute-start(bf16[512,128]{1,0:T(8,128)(2,1)S(1)} %copy-done.6), channel_id=1, source_target_pairs={{0,7},{1,6},{2,1},{3,0},{4,3},{5,2},{6,5},{7,4},{8,15},{9,14},{10,... | collective-permute-start | bytes 393224 | tf_op jit(solution)/shard_map/ppermute | solution.py:236
  23.1 9.0 %collective-permute-start.5 = (bf16[512,128]{1,0:T(8,128)(2,1)S(1)}, bf16[512,128]{1,0:T(8,128)(2,1)S(1)}, u32[]{:S(2)}, u32[]{:S(2)}) collective-permute-start(bf16[512,128]{1,0:T(8,128)(2,1)S(1)} %copy-done.5), channel_id=1, source_target_pairs={{0,5},{1,4},{2,7},{3,6},{4,1},{5,0},{6,3},{7,2},{8,13},{9,12},{10,... | collective-permute-start | bytes 393224 | tf_op jit(solution)/shard_map/ppermute | solution.py:236
  25.1 6.9 %collective-permute-start.6 = (bf16[512,128]{1,0:T(8,128)(2,1)S(1)}, bf16[512,128]{1,0:T(8,128)(2,1)S(1)}, u32[]{:S(2)}, u32[]{:S(2)}) collective-permute-start(bf16[512,128]{1,0:T(8,128)(2,1)S(1)} %copy-done.4), channel_id=1, source_target_pairs={{0,1},{1,0},{2,3},{3,2},{4,5},{5,4},{6,7},{7,6},{8,9},{9,8},{10,11... | collective-permute-start | bytes 393224 | tf_op jit(solution)/shard_map/ppermute | solution.py:236
  45.1 33.6 %all-to-all-start.1 = ((bf16[16,512,128]{2,1,0:T(8,128)(2,1)}), bf16[16,512,128]{2,1,0:T(8,128)(2,1)}, u32[]{:S(2)}, u32[]{:S(2)}) async-start(bf16[16,512,128]{2,1,0:T(8,128)(2,1)} %bitcast.12), calls=%async_computation.1 | async-start | bytes 4194304 | tf_op jit(solution)/shard_map/all_to_all | solution.py:276
  49.5 47.6 %copy-start = (bf16[512,128]{1,0:T(8,128)(2,1)S(1)}, bf16[512,128]{1,0:T(8,128)(2,1)}, u32[]{:S(2)}) copy-start(bf16[512,128]{1,0:T(8,128)(2,1)} %get-tuple-element.61.refs_0_) | copy-start | bytes 393220
  49.5 47.6 %copy-start.2 = (bf16[64,128]{1,0:T(8,128)(2,1)S(1)}, bf16[64,128]{1,0:T(8,128)(2,1)}, u32[]{:S(2)}) copy-start(bf16[64,128]{1,0:T(8,128)(2,1)} %constant.57.clone.lag_ref) | copy-start | bytes 49156
  50.2 8.7 %collective-permute-start.7 = (bf16[4,256,128]{2,1,0:T(8,128)(2,1)S(1)}, bf16[4,256,128]{2,1,0:T(8,128)(2,1)S(1)}, u32[]{:S(2)}, u32[]{:S(2)}) collective-permute-start(bf16[4,256,128]{2,1,0:T(8,128)(2,1)S(1)} %get-tuple-element.75), channel_id=1, source_target_pairs={{0,2},{1,3},{2,4},{3,5},{4,6},{5,7},{6,0},{7,1},{8,10},{9,11},{10,... | collective-permute-start | bytes 786440 | tf_op jit(solution)/shard_map/ppermute | solution.py:236
  51.9 16.9 %collective-permute-start.8 = (bf16[4,256,128]{2,1,0:T(8,128)(2,1)S(1)}, bf16[4,256,128]{2,1,0:T(8,128)(2,1)S(1)}, u32[]{:S(2)}, u32[]{:S(2)}) collective-permute-start(bf16[4,256,128]{2,1,0:T(8,128)(2,1)S(1)} %get-tuple-element.76), channel_id=1, source_target_pairs={{0,6},{1,7},{2,0},{3,1},{4,2},{5,3},{6,4},{7,5},{8,14},{9,15},{10,... | collective-permute-start | bytes 786440 | tf_op jit(solution)/shard_map/ppermute | solution.py:236
  54.1 14.6 %collective-permute-start.9 = (bf16[4,256,128]{2,1,0:T(8,128)(2,1)S(1)}, bf16[4,256,128]{2,1,0:T(8,128)(2,1)S(1)}, u32[]{:S(2)}, u32[]{:S(2)}) collective-permute-start(bf16[4,256,128]{2,1,0:T(8,128)(2,1)S(1)} %get-tuple-element.77), channel_id=1, source_target_pairs={{0,4},{1,5},{2,6},{3,7},{4,0},{5,1},{6,2},{7,3},{8,12},{9,13},{10,... | collective-permute-start | bytes 786440 | tf_op jit(solution)/shard_map/ppermute | solution.py:236
  55.4 18.4 %collective-permute-start.10 = (bf16[4,256,128]{2,1,0:T(8,128)(2,1)S(1)}, bf16[4,256,128]{2,1,0:T(8,128)(2,1)S(1)}, u32[]{:S(2)}, u32[]{:S(2)}) collective-permute-start(bf16[4,256,128]{2,1,0:T(8,128)(2,1)S(1)} %get-tuple-element.78), channel_id=1, source_target_pairs={{0,3},{1,2},{2,5},{3,4},{4,7},{5,6},{6,1},{7,0},{8,11},{9,10},{10,... | collective-permute-start | bytes 786440 | tf_op jit(solution)/shard_map/ppermute | solution.py:236
  58.9 15.6 %collective-permute-start.11 = (bf16[4,256,128]{2,1,0:T(8,128)(2,1)S(1)}, bf16[4,256,128]{2,1,0:T(8,128)(2,1)S(1)}, u32[]{:S(2)}, u32[]{:S(2)}) collective-permute-start(bf16[4,256,128]{2,1,0:T(8,128)(2,1)S(1)} %get-tuple-element.79), channel_id=1, source_target_pairs={{0,7},{1,6},{2,1},{3,0},{4,3},{5,2},{6,5},{7,4},{8,15},{9,14},{10,... | collective-permute-start | bytes 786440 | tf_op jit(solution)/shard_map/ppermute | solution.py:236
  59.0 19.7 %collective-permute-start.12 = (bf16[4,256,128]{2,1,0:T(8,128)(2,1)S(1)}, bf16[4,256,128]{2,1,0:T(8,128)(2,1)S(1)}, u32[]{:S(2)}, u32[]{:S(2)}) collective-permute-start(bf16[4,256,128]{2,1,0:T(8,128)(2,1)S(1)} %get-tuple-element.80), channel_id=1, source_target_pairs={{0,5},{1,4},{2,7},{3,6},{4,1},{5,0},{6,3},{7,2},{8,13},{9,12},{10,... | collective-permute-start | bytes 786440 | tf_op jit(solution)/shard_map/ppermute | solution.py:236
  68.8 9.9 %collective-permute-start.13 = (bf16[4,256,128]{2,1,0:T(8,128)(2,1)S(1)}, bf16[4,256,128]{2,1,0:T(8,128)(2,1)S(1)}, u32[]{:S(2)}, u32[]{:S(2)}) collective-permute-start(bf16[4,256,128]{2,1,0:T(8,128)(2,1)S(1)} %get-tuple-element.81), channel_id=1, source_target_pairs={{0,1},{1,0},{2,3},{3,2},{4,5},{5,4},{6,7},{7,6},{8,9},{9,8},{10,11... | collective-permute-start | bytes 786440 | tf_op jit(solution)/shard_map/ppermute | solution.py:236
  80.9 8.9 %collective-permute-start.14 = (bf16[4,256,128]{2,1,0:T(8,128)(2,1)S(1)}, bf16[4,256,128]{2,1,0:T(8,128)(2,1)S(1)}, u32[]{:S(2)}, u32[]{:S(2)}) collective-permute-start(bf16[4,256,128]{2,1,0:T(8,128)(2,1)S(1)} %get-tuple-element.84), channel_id=1, source_target_pairs={{0,2},{1,3},{2,4},{3,5},{4,6},{5,7},{6,0},{7,1},{8,10},{9,11},{10,... | collective-permute-start | bytes 786440 | tf_op jit(solution)/shard_map/ppermute | solution.py:236
  81.9 15.3 %collective-permute-start.15 = (bf16[4,256,128]{2,1,0:T(8,128)(2,1)S(1)}, bf16[4,256,128]{2,1,0:T(8,128)(2,1)S(1)}, u32[]{:S(2)}, u32[]{:S(2)}) collective-permute-start(bf16[4,256,128]{2,1,0:T(8,128)(2,1)S(1)} %get-tuple-element.85), channel_id=1, source_target_pairs={{0,6},{1,7},{2,0},{3,1},{4,2},{5,3},{6,4},{7,5},{8,14},{9,15},{10,... | collective-permute-start | bytes 786440 | tf_op jit(solution)/shard_map/ppermute | solution.py:236
  83.7 22.8 %collective-permute-start.16 = (bf16[4,256,128]{2,1,0:T(8,128)(2,1)S(1)}, bf16[4,256,128]{2,1,0:T(8,128)(2,1)S(1)}, u32[]{:S(2)}, u32[]{:S(2)}) collective-permute-start(bf16[4,256,128]{2,1,0:T(8,128)(2,1)S(1)} %get-tuple-element.86), channel_id=1, source_target_pairs={{0,4},{1,5},{2,6},{3,7},{4,0},{5,1},{6,2},{7,3},{8,12},{9,13},{10,... | collective-permute-start | bytes 786440 | tf_op jit(solution)/shard_map/ppermute | solution.py:236
  83.8 22.7 %collective-permute-start.17 = (bf16[4,256,128]{2,1,0:T(8,128)(2,1)S(1)}, bf16[4,256,128]{2,1,0:T(8,128)(2,1)S(1)}, u32[]{:S(2)}, u32[]{:S(2)}) collective-permute-start(bf16[4,256,128]{2,1,0:T(8,128)(2,1)S(1)} %get-tuple-element.87), channel_id=1, source_target_pairs={{0,3},{1,2},{2,5},{3,4},{4,7},{5,6},{6,1},{7,0},{8,11},{9,10},{10,... | collective-permute-start | bytes 786440 | tf_op jit(solution)/shard_map/ppermute | solution.py:236
  89.9 16.6 %collective-permute-start.18 = (bf16[4,256,128]{2,1,0:T(8,128)(2,1)S(1)}, bf16[4,256,128]{2,1,0:T(8,128)(2,1)S(1)}, u32[]{:S(2)}, u32[]{:S(2)}) collective-permute-start(bf16[4,256,128]{2,1,0:T(8,128)(2,1)S(1)} %get-tuple-element.88), channel_id=1, source_target_pairs={{0,7},{1,6},{2,1},{3,0},{4,3},{5,2},{6,5},{7,4},{8,15},{9,14},{10,... | collective-permute-start | bytes 786440 | tf_op jit(solution)/shard_map/ppermute | solution.py:236
  89.9 17.4 %collective-permute-start.19 = (bf16[4,256,128]{2,1,0:T(8,128)(2,1)S(1)}, bf16[4,256,128]{2,1,0:T(8,128)(2,1)S(1)}, u32[]{:S(2)}, u32[]{:S(2)}) collective-permute-start(bf16[4,256,128]{2,1,0:T(8,128)(2,1)S(1)} %get-tuple-element.89), channel_id=1, source_target_pairs={{0,5},{1,4},{2,7},{3,6},{4,1},{5,0},{6,3},{7,2},{8,13},{9,12},{10,... | collective-permute-start | bytes 786440 | tf_op jit(solution)/shard_map/ppermute | solution.py:236
  97.1 10.2 %copy-start.1 = (bf16[64,128]{1,0:T(8,128)(2,1)S(1)}, bf16[64,128]{1,0:T(8,128)(2,1)}, u32[]{:S(2)}) copy-start(bf16[64,128]{1,0:T(8,128)(2,1)} %constant.58.clone.lag_ref) | copy-start | bytes 49156
  97.1 10.2 %collective-permute-start.20 = (bf16[4,256,128]{2,1,0:T(8,128)(2,1)S(1)}, bf16[4,256,128]{2,1,0:T(8,128)(2,1)S(1)}, u32[]{:S(2)}, u32[]{:S(2)}) collective-permute-start(bf16[4,256,128]{2,1,0:T(8,128)(2,1)S(1)} %get-tuple-element.90), channel_id=1, source_target_pairs={{0,1},{1,0},{2,3},{3,2},{4,5},{5,4},{6,7},{7,6},{8,9},{9,8},{10,11... | collective-permute-start | bytes 786440 | tf_op jit(solution)/shard_map/ppermute | solution.py:236

commit v8 on v7

--- a/solution.py
+++ b/solution.py
@@ -19,7 +19,8 @@
 SPLIT = (8, 8)
 BEGIN = tuple(sum(SPLIT[:c]) for c in range(len(SPLIT)))
 LAST = len(SPLIT) - 1
-AT_ONCE = 4
+AT_ONCE = 8
+AT_STEP = 4
 LAG_BLOCK = 32
 HOPS = ((0, 0), (1, 0), (3, 0), (2, 0), (1, 1), (3, 1), (2, 1), (0, 1))
 IN_HBM = pl.BlockSpec(memory_space=pltpu.HBM)
@@ -148,25 +149,36 @@
     own_refs, part_refs = refs[:members], refs[members : 2 * members]
     refs = refs[2 * members :]
     if c:
-        before_ref, out_ref, cross_ref, rows_ref = refs
+        before_ref, out_ref, cross_ref, rows_ref, *refs = refs
     else:
-        out_ref, cross_ref, rows_ref = refs
+        out_ref, cross_ref, rows_ref, *refs = refs
     pairs = part_refs[0].shape[0]
     octets = SPLIT[c]
     step = pl.program_id(0)
-
-    @pl.when(step < octets)
+    turns = octets // AT_STEP
+
+    if c == LAST:
+        made_ref, sem = refs
+
+    def give(part):
+        at = pl.ds(pl.multiple_of(part * 8 * BCH, 8 * BCH), 8 * BCH)
+        return pltpu.make_async_copy(made_ref.at[:, :, at], out_ref.at[:, :, at], sem.at[part])
+
+    @pl.when(step < turns)
     def _():
-        def store(i0, value):
-            cross_ref[step, i0 : i0 + 16] = value
-
-        cross_octet(BEGIN[c] + step, step, own_refs, part_refs, rows_ref, store)
-
-    @pl.when(step >= octets)
+        for n in range(AT_STEP):
+            local = step * AT_STEP + n
+
+            def store(i0, value, local=local):
+                cross_ref[local, i0 : i0 + 16] = value
+
+            cross_octet(BEGIN[c] + local, local, own_refs, part_refs, rows_ref.at[n], store)
+
+    @pl.when(step >= turns)
     def _():
         scale = 1.0 / math.sqrt(members * 2 * BINS)
         for ii in range(LAG_BLOCK):
-            i = (step - octets) * LAG_BLOCK + ii
+            i = (step - turns) * LAG_BLOCK + ii
             right = cross_ref[:, i].reshape(16 * octets, pairs * BCH)
             lagged = jnp.dot(lag_ref[...], right, preferred_element_type=jnp.float32)
             if c:
@@ -175,8 +187,18 @@
                 out_ref[i] = lagged
                 continue
             lagged = (lagged * scale).astype(jnp.bfloat16)
+            at = pl.ds(pl.multiple_of(i * BCH, BCH), BCH)
             for q in range(pairs):
-                out_ref[q, :, ii * BCH : (ii + 1) * BCH] = lagged[:, q * BCH : (q + 1) * BCH]
+                made_ref[q, :, at] = lagged[:, q * BCH : (q + 1) * BCH]
+            if ii % 8 == 7:
+                give(i // 8).start()
+
+    if c == LAST:
+
+        @pl.when(step == turns + BCH // LAG_BLOCK - 1)
+        def _():
+            for part in range(BCH // 8):
+                give(part).wait()
 
 
 def params(mib):
@@ -194,26 +216,24 @@
     blocks = BCH // LAG_BLOCK
     sums = (BCH, LAGS, pairs * BCH)
 
-    def after(s):
-        return jnp.maximum(s - octets, 0)
-
     if c == LAST:
         out = bf16(pairs, LAGS, BCH * BCH)
-        out_spec = pl.BlockSpec((pairs, LAGS, LAG_BLOCK * BCH), lambda s: (0, 0, after(s)))
+        made = [pltpu.VMEM(out.shape, jnp.bfloat16), pltpu.SemaphoreType.DMA((BCH // 8,))]
     else:
         out = jax.ShapeDtypeStruct(sums, jnp.float32)
-        out_spec = IN_VMEM
+        made = []
     return pl.pallas_call(
         functools.partial(chunk_kernel, c, members),
-        grid=(octets + blocks,),
+        grid=(octets // AT_STEP + blocks,),
         in_specs=[IN_VMEM] * (1 + 2 * members + len(before)),
-        out_specs=out_spec,
+        out_specs=IN_HBM if c == LAST else IN_VMEM,
         out_shape=out,
         scratch_shapes=[
             pltpu.VMEM((octets, BCH, 16, pairs * BCH), jnp.bfloat16),
-            pltpu.VMEM((2, BCH, 32 * members), jnp.float32),
+            pltpu.VMEM((AT_STEP, 2, BCH, 32 * members), jnp.float32),
+            *made,
         ],
-        compiler_params=params(22),
+        compiler_params=params(28),
         cost_estimate=pl.CostEstimate(
             flops=2_500_000_000 * octets, bytes_accessed=2**21 * octets, transcendentals=0
         ),

time: 120 us -> 117 us (0.975)
  Pallas kernels: 31.1 us -> 27 us
  waiting for transfers between devices: 30.5 us -> 32 us
    pallas_call x2, Pallas kernels: 21.4 us -> 17.6 us  [chunk(): pl.pallas_call(functools.partial(chunk_kernel, c, members), grid=(octets...]
    ppermute x21, waiting for transfers between devices: 17.5 us -> 19 us  [move(): moved.append(lax.ppermute(piece, 'win', way))]
  transfers between devices with their start and end apart: 23 -> 23, of which waited for: 9 -> 9; matrix products, arithmetic and copies ran while one was open for 0% -> 0% of each run, Pallas kernels for 8% -> 7%
where the time goes in v8:
time: 117 us
  starting transfers between devices  57 us (49%)
  waiting for transfers between devices  32 us (27%)
  Pallas kernels  27 us (23%)
    ppermute x21, starting transfers between devices, move(): moved.append(lax.ppermute(piece, 'win', way))  44.8 us
    ppermute x21, waiting for transfers between devices, move(): moved.append(lax.ppermute(piece, 'win', way))  19 us
    pallas_call x2, Pallas kernels, chunk(): pl.pallas_call(functools.partial(chunk_kernel, c, members), grid=(octets...  17.6 us
    all_to_all x2, waiting for transfers between devices, shards(): lax.all_to_all(sends[c].reshape(groups, 64 * octets, BCH), 'blk', split_a...  13 us
    all_to_all x2, starting transfers between devices, shards(): lax.all_to_all(sends[c].reshape(groups, 64 * octets, BCH), 'blk', split_a...  12.2 us
    pallas_call x1, Pallas kernels, shards(): pl.pallas_call(functools.partial(spectra_kernel, members, groups), grid_s...  6.51 us
    pallas_call x2, Pallas kernels, shards(): pl.pallas_call(functools.partial(pack_kernel, members, pairs), grid_spec=...  2.96 us
  transfers between devices with their start and end apart: 23, of which 9 were waited for; matrix products, arithmetic and copies ran while one was open for 0% of the time, Pallas kernels for 7%

profile of v8, /device:TPU:1, one launch (start us, length us, event | category | flops | bytes accessed | tf_op | source)
XLA Modules:
  0.0 117.0 jit_solution(14696600586111748778)
XLA Ops:
  0.0 6.5 %spectra.1 = (bf16[32,256,128]{2,1,0:T(8,128)(2,1)}, bf16[32,256,128]{2,1,0:T(8,128)(2,1)}, bf16[512,128]{1,0:T(8,128)(2,1)}, bf16[512,128]{1,0:T(8,128)(2,1)}, ...) custom-call(s32[4,128]{1,0:T(4,128)} %bitcast.14, ...), custom_call_target="tpu_custom_call" | custom-call | tf_op jit(solution)/shard_map/spectra/pallas_call | solution.py:269
  6.5 0.0 copy-start.3
  6.6 7.7 %all-to-all-start = ((bf16[16,512,128]{2,1,0:T(8,128)(2,1)}), bf16[16,512,128]{2,1,0:T(8,128)(2,1)S(1)}, u32[]{:S(2)}, u32[]{:S(2)}) async-start(bf16[16,512,128]{2,1,0:T(8,128)(2,1)} %bitcast.13), calls=%async_computation | async-start | bytes 4194304 | tf_op jit(solution)/shard_map/all_to_all | solution.py:296
  14.3 1.7 %collective-permute-start = (bf16[512,128]{1,0:T(8,128)(2,1)S(1)}, bf16[512,128]{1,0:T(8,128)(2,1)S(1)}, u32[]{:S(2)}, u32[]{:S(2)}) collective-permute-start(bf16[512,128]{1,0:T(8,128)(2,1)S(1)} %copy-done.8), channel_id=1, source_target_pairs={{0,2},{1,3},{2,4},{3,5},{4,6},{5,7},{6,0},{7,1},{8,10},{9,11},{10,... | collective-permute-start | bytes 393224 | tf_op jit(solution)/shard_map/ppermute | solution.py:256
  16.0 2.2 %collective-permute-start.1 = (bf16[512,128]{1,0:T(8,128)(2,1)S(1)}, bf16[512,128]{1,0:T(8,128)(2,1)S(1)}, u32[]{:S(2)}, u32[]{:S(2)}) collective-permute-start(bf16[512,128]{1,0:T(8,128)(2,1)S(1)} %copy-done.7), channel_id=1, source_target_pairs={{0,6},{1,7},{2,0},{3,1},{4,2},{5,3},{6,4},{7,5},{8,14},{9,15},{10,... | collective-permute-start | bytes 393224 | tf_op jit(solution)/shard_map/ppermute | solution.py:256
  18.2 1.2 %collective-permute-start.2 = (bf16[512,128]{1,0:T(8,128)(2,1)}, bf16[512,128]{1,0:T(8,128)(2,1)S(1)}, u32[]{:S(2)}, u32[]{:S(2)}) collective-permute-start(bf16[512,128]{1,0:T(8,128)(2,1)} %get-tuple-element.56), channel_id=1, source_target_pairs={{0,4},{1,5},{2,6},{3,7},{4,0},{5,1},{6,2},{7,3},{8,12},{9,13},{10,... | collective-permute-start | bytes 393224 | tf_op jit(solution)/shard_map/ppermute | solution.py:256
  19.5 2.4 %collective-permute-start.3 = (bf16[512,128]{1,0:T(8,128)(2,1)}, bf16[512,128]{1,0:T(8,128)(2,1)S(1)}, u32[]{:S(2)}, u32[]{:S(2)}) collective-permute-start(bf16[512,128]{1,0:T(8,128)(2,1)} %get-tuple-element.57), channel_id=1, source_target_pairs={{0,3},{1,2},{2,5},{3,4},{4,7},{5,6},{6,1},{7,0},{8,11},{9,10},{10,... | collective-permute-start | bytes 393224 | tf_op jit(solution)/shard_map/ppermute | solution.py:256
  21.9 0.5 collective-permute-start.4
  22.4 0.1 copy.8
  22.5 0.1 reshape.82
  22.7 0.2 and_reduce_fusion
  22.9 2.0 %collective-permute-start.5 = (bf16[512,128]{1,0:T(8,128)(2,1)S(1)}, bf16[512,128]{1,0:T(8,128)(2,1)S(1)}, u32[]{:S(2)}, u32[]{:S(2)}) collective-permute-start(bf16[512,128]{1,0:T(8,128)(2,1)S(1)} %copy-done.5), channel_id=1, source_target_pairs={{0,5},{1,4},{2,7},{3,6},{4,1},{5,0},{6,3},{7,2},{8,13},{9,12},{10,... | collective-permute-start | bytes 393224 | tf_op jit(solution)/shard_map/ppermute | solution.py:256
  24.9 0.0 collective-permute-done.1.refs_2_
  24.9 0.0 collective-permute-start.6
  24.9 0.1 pad_add_fusion.meta
  25.0 0.2 collective-permute-done.2.refs_3_
  25.2 3.8 %collective-permute-done.3.refs_4_ = bf16[512,128]{1,0:T(8,128)(2,1)S(1)} collective-permute-done((bf16[512,128]{1,0:T(8,128)(2,1)}, bf16[512,128]{1,0:T(8,128)(2,1)S(1)}, u32[]{:S(2)}, u32[]{:S(2)}) %collective-permute-start.3) | collective-permute-done | bytes 131104 | tf_op jit(solution)/shard_map/ppermute | solution.py:256
  28.9 0.1 collective-permute-done.4.refs_5_
  29.0 2.8 %collective-permute-done.5.refs_6_ = bf16[512,128]{1,0:T(8,128)(2,1)S(1)} collective-permute-done((bf16[512,128]{1,0:T(8,128)(2,1)S(1)}, bf16[512,128]{1,0:T(8,128)(2,1)S(1)}, u32[]{:S(2)}, u32[]{:S(2)}) %collective-permute-start.5) | collective-permute-done | bytes 131104 | tf_op jit(solution)/shard_map/ppermute | solution.py:256
  31.8 0.0 collective-permute-done.6.refs_7_
  31.8 13.0 %all-to-all-done = bf16[16,512,128]{2,1,0:T(8,128)(2,1)S(1)} async-done(((bf16[16,512,128]{2,1,0:T(8,128)(2,1)}), bf16[16,512,128]{2,1,0:T(8,128)(2,1)S(1)}, u32[]{:S(2)}, u32[]{:S(2)}) %all-to-all-start) | async-done | bytes 2097184 | tf_op jit(solution)/shard_map/all_to_all | solution.py:296
  44.8 4.4 %all-to-all-start.1 = ((bf16[16,512,128]{2,1,0:T(8,128)(2,1)}), bf16[16,512,128]{2,1,0:T(8,128)(2,1)}, u32[]{:S(2)}, u32[]{:S(2)}) async-start(bf16[16,512,128]{2,1,0:T(8,128)(2,1)} %bitcast.12), calls=%async_computation.1 | async-start | bytes 4194304 | tf_op jit(solution)/shard_map/all_to_all | solution.py:296
  49.3 0.0 copy-start.2
  49.3 0.7 pack.2
  50.0 1.7 %collective-permute-start.7 = (bf16[4,256,128]{2,1,0:T(8,128)(2,1)S(1)}, bf16[4,256,128]{2,1,0:T(8,128)(2,1)S(1)}, u32[]{:S(2)}, u32[]{:S(2)}) collective-permute-start(bf16[4,256,128]{2,1,0:T(8,128)(2,1)S(1)} %get-tuple-element.75), channel_id=1, source_target_pairs={{0,2},{1,3},{2,4},{3,5},{4,6},{5,7},{6,0},{7,1},{8,10},{9,11},{10,... | collective-permute-start | bytes 786440 | tf_op jit(solution)/shard_map/ppermute | solution.py:256
  51.7 2.2 %collective-permute-start.8 = (bf16[4,256,128]{2,1,0:T(8,128)(2,1)S(1)}, bf16[4,256,128]{2,1,0:T(8,128)(2,1)S(1)}, u32[]{:S(2)}, u32[]{:S(2)}) collective-permute-start(bf16[4,256,128]{2,1,0:T(8,128)(2,1)S(1)} %get-tuple-element.76), channel_id=1, source_target_pairs={{0,6},{1,7},{2,0},{3,1},{4,2},{5,3},{6,4},{7,5},{8,14},{9,15},{10,... | collective-permute-start | bytes 786440 | tf_op jit(solution)/shard_map/ppermute | solution.py:256
  53.9 1.2 %collective-permute-start.9 = (bf16[4,256,128]{2,1,0:T(8,128)(2,1)S(1)}, bf16[4,256,128]{2,1,0:T(8,128)(2,1)S(1)}, u32[]{:S(2)}, u32[]{:S(2)}) collective-permute-start(bf16[4,256,128]{2,1,0:T(8,128)(2,1)S(1)} %get-tuple-element.77), channel_id=1, source_target_pairs={{0,4},{1,5},{2,6},{3,7},{4,0},{5,1},{6,2},{7,3},{8,12},{9,13},{10,... | collective-permute-start | bytes 786440 | tf_op jit(solution)/shard_map/ppermute | solution.py:256
  55.1 3.6 %collective-permute-start.10 = (bf16[4,256,128]{2,1,0:T(8,128)(2,1)S(1)}, bf16[4,256,128]{2,1,0:T(8,128)(2,1)S(1)}, u32[]{:S(2)}, u32[]{:S(2)}) collective-permute-start(bf16[4,256,128]{2,1,0:T(8,128)(2,1)S(1)} %get-tuple-element.78), channel_id=1, source_target_pairs={{0,3},{1,2},{2,5},{3,4},{4,7},{5,6},{6,1},{7,0},{8,11},{9,10},{10,... | collective-permute-start | bytes 786440 | tf_op jit(solution)/shard_map/ppermute | solution.py:256
  58.7 9.8 %collective-permute-start.12 = (bf16[4,256,128]{2,1,0:T(8,128)(2,1)S(1)}, bf16[4,256,128]{2,1,0:T(8,128)(2,1)S(1)}, u32[]{:S(2)}, u32[]{:S(2)}) collective-permute-start(bf16[4,256,128]{2,1,0:T(8,128)(2,1)S(1)} %get-tuple-element.80), channel_id=1, source_target_pairs={{0,5},{1,4},{2,7},{3,6},{4,1},{5,0},{6,3},{7,2},{8,13},{9,12},{10,... | collective-permute-start | bytes 786440 | tf_op jit(solution)/shard_map/ppermute | solution.py:256
  68.5 0.0 collective-permute-done.8.refs_10_
  68.5 0.0 collective-permute-start.13
  68.5 0.0 collective-permute-done.9.refs_11_
  68.5 4.9 %collective-permute-done.10.refs_12_ = bf16[4,256,128]{2,1,0:T(8,128)(2,1)S(1)} collective-permute-done((bf16[4,256,128]{2,1,0:T(8,128)(2,1)S(1)}, bf16[4,256,128]{2,1,0:T(8,128)(2,1)S(1)}, u32[]{:S(2)}, u32[]{:S(2)}) %collective-permute-start.10) | collective-permute-done | bytes 262176 | tf_op jit(solution)/shard_map/ppermute | solution.py:256
  73.5 0.8 collective-permute-done.11.refs_13_
  74.3 4.1 %collective-permute-done.12.refs_14_ = bf16[4,256,128]{2,1,0:T(8,128)(2,1)S(1)} collective-permute-done((bf16[4,256,128]{2,1,0:T(8,128)(2,1)S(1)}, bf16[4,256,128]{2,1,0:T(8,128)(2,1)S(1)}, u32[]{:S(2)}, u32[]{:S(2)}) %collective-permute-start.12) | collective-permute-done | bytes 262176 | tf_op jit(solution)/shard_map/ppermute | solution.py:256
  78.4 0.0 collective-permute-done.13.refs_15_
  78.4 0.0 all-to-all-done.1
  78.4 2.3 %pack.3 = (bf16[4,256,128]{2,1,0:T(8,128)(2,1)S(1)}, bf16[4,256,128]{2,1,0:T(8,128)(2,1)S(1)}, bf16[4,256,128]{2,1,0:T(8,128)(2,1)S(1)}, bf16[4,256,128]{2,1,0:T...) custom-call(s32[33]{0:T(128)S(1)} %pad_add_fusion.meta, ...), custom_call_target="tpu_custom_call" | custom-call | tf_op jit(solution)/shard_map/pack/pallas_call | solution.py:310
  80.7 0.9 collective-permute-start.14
  81.6 1.8 %collective-permute-start.15 = (bf16[4,256,128]{2,1,0:T(8,128)(2,1)S(1)}, bf16[4,256,128]{2,1,0:T(8,128)(2,1)S(1)}, u32[]{:S(2)}, u32[]{:S(2)}) collective-permute-start(bf16[4,256,128]{2,1,0:T(8,128)(2,1)S(1)} %get-tuple-element.85), channel_id=1, source_target_pairs={{0,6},{1,7},{2,0},{3,1},{4,2},{5,3},{6,4},{7,5},{8,14},{9,15},{10,... | collective-permute-start | bytes 786440 | tf_op jit(solution)/shard_map/ppermute | solution.py:256
  83.4 0.1 collective-permute-start.16
  83.5 6.1 %collective-permute-start.17 = (bf16[4,256,128]{2,1,0:T(8,128)(2,1)S(1)}, bf16[4,256,128]{2,1,0:T(8,128)(2,1)S(1)}, u32[]{:S(2)}, u32[]{:S(2)}) collective-permute-start(bf16[4,256,128]{2,1,0:T(8,128)(2,1)S(1)} %get-tuple-element.87), channel_id=1, source_target_pairs={{0,3},{1,2},{2,5},{3,4},{4,7},{5,6},{6,1},{7,0},{8,11},{9,10},{10,... | collective-permute-start | bytes 786440 | tf_op jit(solution)/shard_map/ppermute | solution.py:256
  89.6 0.0 collective-permute-start.18
  89.6 7.2 %collective-permute-start.19 = (bf16[4,256,128]{2,1,0:T(8,128)(2,1)S(1)}, bf16[4,256,128]{2,1,0:T(8,128)(2,1)S(1)}, u32[]{:S(2)}, u32[]{:S(2)}) collective-permute-start(bf16[4,256,128]{2,1,0:T(8,128)(2,1)S(1)} %get-tuple-element.89), channel_id=1, source_target_pairs={{0,5},{1,4},{2,7},{3,6},{4,1},{5,0},{6,3},{7,2},{8,13},{9,12},{10,... | collective-permute-start | bytes 786440 | tf_op jit(solution)/shard_map/ppermute | solution.py:256
  96.9 0.0 collective-permute-start.20
  96.9 7.8 %chunk.2.refs_16_ = f32[128,64,512]{2,1,0:T(8,128)S(1)} custom-call(bf16[64,128]{1,0:T(8,128)(2,1)S(1)} %copy-done.2, bf16[512,128]{1,0:T(8,128)(2,1)S(1)} %copy-done, bf16[512,128]{1,0:T(8,128)(2,1)S(1)} %collective-permute-done.refs_1_, bf16[512,128]{1,0:T(8,128)(2,1)S(1)} %collective-permute-done.1.refs_2_, ...), custom_call_target="tpu_custom_call" | custom-call | flops 20000000000 | bytes 16777216 | tf_op jit(solution)/shard_map/chunk/pallas_call | solution.py:225
  104.8 2.3 %collective-permute-done.19.refs_14_ = bf16[4,256,128]{2,1,0:T(8,128)(2,1)S(1)} collective-permute-done((bf16[4,256,128]{2,1,0:T(8,128)(2,1)S(1)}, bf16[4,256,128]{2,1,0:T(8,128)(2,1)S(1)}, u32[]{:S(2)}, u32[]{:S(2)}) %collective-permute-start.19) | collective-permute-done | bytes 262176 | tf_op jit(solution)/shard_map/ppermute | solution.py:256
  107.1 9.7 %chunk.3 = bf16[4,64,16384]{2,1,0:T(8,128)(2,1)} custom-call(bf16[64,128]{1,0:T(8,128)(2,1)S(1)} %copy-done.1, bf16[512,128]{1,0:T(8,128)(2,1)S(1)} %copy-done, bf16[512,128]{1,0:T(8,128)(2,1)S(1)} %collective-permute-done.refs_1_, bf16[512,128]{1,0:T(8,128)(2,1)S(1)} %collective-permute-done.1.refs_2_, bf16[512,128]{1,0:T(8,128)(2,1)S(1)} %collective-permute-done.2.refs_3_, ...), custom_call_target="tpu_custom_call" | custom-call | flops 20000000000 | bytes 16777216 | tf_op jit(solution)/shard_map/chunk/pallas_call | solution.py:225
  (28 shorter events, 0.1 us)
Async XLA Ops:
  6.5 7.8 %copy-start.8 = (bf16[512,128]{1,0:T(8,128)(2,1)S(1)}, bf16[512,128]{1,0:T(8,128)(2,1)}, u32[]{:S(2)}) copy-start(bf16[512,128]{1,0:T(8,128)(2,1)} %get-tuple-element.54) | copy-start | bytes 393220
  6.5 9.5 %copy-start.7 = (bf16[512,128]{1,0:T(8,128)(2,1)S(1)}, bf16[512,128]{1,0:T(8,128)(2,1)}, u32[]{:S(2)}) copy-start(bf16[512,128]{1,0:T(8,128)(2,1)} %get-tuple-element.55) | copy-start | bytes 393220
  6.5 15.3 %copy-start.6 = (bf16[512,128]{1,0:T(8,128)(2,1)S(1)}, bf16[512,128]{1,0:T(8,128)(2,1)}, u32[]{:S(2)}) copy-start(bf16[512,128]{1,0:T(8,128)(2,1)} %get-tuple-element.58) | copy-start | bytes 393220
  6.5 15.9 %copy-start.3 = (s32[128,4]{0,1:T(4,128)S(1)}, s32[128,4]{0,1:T(4,128)}, u32[]{:S(2)}) copy-start(s32[128,4]{0,1:T(4,128)} %param.8) | copy-start | bytes 6148
  6.6 16.3 %copy-start.5 = (bf16[512,128]{1,0:T(8,128)(2,1)S(1)}, bf16[512,128]{1,0:T(8,128)(2,1)}, u32[]{:S(2)}) copy-start(bf16[512,128]{1,0:T(8,128)(2,1)} %get-tuple-element.59) | copy-start | bytes 393220
  6.6 18.3 %copy-start.4 = (bf16[512,128]{1,0:T(8,128)(2,1)S(1)}, bf16[512,128]{1,0:T(8,128)(2,1)}, u32[]{:S(2)}) copy-start(bf16[512,128]{1,0:T(8,128)(2,1)} %get-tuple-element.60) | copy-start | bytes 393220
  6.6 38.2 %all-to-all-start = ((bf16[16,512,128]{2,1,0:T(8,128)(2,1)}), bf16[16,512,128]{2,1,0:T(8,128)(2,1)S(1)}, u32[]{:S(2)}, u32[]{:S(2)}) async-start(bf16[16,512,128]{2,1,0:T(8,128)(2,1)} %bitcast.13), calls=%async_computation | async-start | bytes 4194304 | tf_op jit(solution)/shard_map/all_to_all | solution.py:296
  14.3 8.5 %collective-permute-start = (bf16[512,128]{1,0:T(8,128)(2,1)S(1)}, bf16[512,128]{1,0:T(8,128)(2,1)S(1)}, u32[]{:S(2)}, u32[]{:S(2)}) collective-permute-start(bf16[512,128]{1,0:T(8,128)(2,1)S(1)} %copy-done.8), channel_id=1, source_target_pairs={{0,2},{1,3},{2,4},{3,5},{4,6},{5,7},{6,0},{7,1},{8,10},{9,11},{10,... | collective-permute-start | bytes 393224 | tf_op jit(solution)/shard_map/ppermute | solution.py:256
  16.0 8.9 %collective-permute-start.1 = (bf16[512,128]{1,0:T(8,128)(2,1)S(1)}, bf16[512,128]{1,0:T(8,128)(2,1)S(1)}, u32[]{:S(2)}, u32[]{:S(2)}) collective-permute-start(bf16[512,128]{1,0:T(8,128)(2,1)S(1)} %copy-done.7), channel_id=1, source_target_pairs={{0,6},{1,7},{2,0},{3,1},{4,2},{5,3},{6,4},{7,5},{8,14},{9,15},{10,... | collective-permute-start | bytes 393224 | tf_op jit(solution)/shard_map/ppermute | solution.py:256
  18.2 6.9 %collective-permute-start.2 = (bf16[512,128]{1,0:T(8,128)(2,1)}, bf16[512,128]{1,0:T(8,128)(2,1)S(1)}, u32[]{:S(2)}, u32[]{:S(2)}) collective-permute-start(bf16[512,128]{1,0:T(8,128)(2,1)} %get-tuple-element.56), channel_id=1, source_target_pairs={{0,4},{1,5},{2,6},{3,7},{4,0},{5,1},{6,2},{7,3},{8,12},{9,13},{10,... | collective-permute-start | bytes 393224 | tf_op jit(solution)/shard_map/ppermute | solution.py:256
  19.5 9.5 %collective-permute-start.3 = (bf16[512,128]{1,0:T(8,128)(2,1)}, bf16[512,128]{1,0:T(8,128)(2,1)S(1)}, u32[]{:S(2)}, u32[]{:S(2)}) collective-permute-start(bf16[512,128]{1,0:T(8,128)(2,1)} %get-tuple-element.57), channel_id=1, source_target_pairs={{0,3},{1,2},{2,5},{3,4},{4,7},{5,6},{6,1},{7,0},{8,11},{9,10},{10,... | collective-permute-start | bytes 393224 | tf_op jit(solution)/shard_map/ppermute | solution.py:256
  21.9 7.1 %collective-permute-start.4 = (bf16[512,128]{1,0:T(8,128)(2,1)S(1)}, bf16[512,128]{1,0:T(8,128)(2,1)S(1)}, u32[]{:S(2)}, u32[]{:S(2)}) collective-permute-start(bf16[512,128]{1,0:T(8,128)(2,1)S(1)} %copy-done.6), channel_id=1, source_target_pairs={{0,7},{1,6},{2,1},{3,0},{4,3},{5,2},{6,5},{7,4},{8,15},{9,14},{10,... | collective-permute-start | bytes 393224 | tf_op jit(solution)/shard_map/ppermute | solution.py:256
  22.9 9.0 %collective-permute-start.5 = (bf16[512,128]{1,0:T(8,128)(2,1)S(1)}, bf16[512,128]{1,0:T(8,128)(2,1)S(1)}, u32[]{:S(2)}, u32[]{:S(2)}) collective-permute-start(bf16[512,128]{1,0:T(8,128)(2,1)S(1)} %copy-done.5), channel_id=1, source_target_pairs={{0,5},{1,4},{2,7},{3,6},{4,1},{5,0},{6,3},{7,2},{8,13},{9,12},{10,... | collective-permute-start | bytes 393224 | tf_op jit(solution)/shard_map/ppermute | solution.py:256
  24.9 6.9 %collective-permute-start.6 = (bf16[512,128]{1,0:T(8,128)(2,1)S(1)}, bf16[512,128]{1,0:T(8,128)(2,1)S(1)}, u32[]{:S(2)}, u32[]{:S(2)}) collective-permute-start(bf16[512,128]{1,0:T(8,128)(2,1)S(1)} %copy-done.4), channel_id=1, source_target_pairs={{0,1},{1,0},{2,3},{3,2},{4,5},{5,4},{6,7},{7,6},{8,9},{9,8},{10,11... | collective-permute-start | bytes 393224 | tf_op jit(solution)/shard_map/ppermute | solution.py:256
  44.8 33.6 %all-to-all-start.1 = ((bf16[16,512,128]{2,1,0:T(8,128)(2,1)}), bf16[16,512,128]{2,1,0:T(8,128)(2,1)}, u32[]{:S(2)}, u32[]{:S(2)}) async-start(bf16[16,512,128]{2,1,0:T(8,128)(2,1)} %bitcast.12), calls=%async_computation.1 | async-start | bytes 4194304 | tf_op jit(solution)/shard_map/all_to_all | solution.py:296
  49.3 47.6 %copy-start = (bf16[512,128]{1,0:T(8,128)(2,1)S(1)}, bf16[512,128]{1,0:T(8,128)(2,1)}, u32[]{:S(2)}) copy-start(bf16[512,128]{1,0:T(8,128)(2,1)} %get-tuple-element.61.refs_0_) | copy-start | bytes 393220
  49.3 47.6 %copy-start.2 = (bf16[64,128]{1,0:T(8,128)(2,1)S(1)}, bf16[64,128]{1,0:T(8,128)(2,1)}, u32[]{:S(2)}) copy-start(bf16[64,128]{1,0:T(8,128)(2,1)} %constant.57.clone.lag_ref) | copy-start | bytes 49156
  50.0 8.7 %collective-permute-start.7 = (bf16[4,256,128]{2,1,0:T(8,128)(2,1)S(1)}, bf16[4,256,128]{2,1,0:T(8,128)(2,1)S(1)}, u32[]{:S(2)}, u32[]{:S(2)}) collective-permute-start(bf16[4,256,128]{2,1,0:T(8,128)(2,1)S(1)} %get-tuple-element.75), channel_id=1, source_target_pairs={{0,2},{1,3},{2,4},{3,5},{4,6},{5,7},{6,0},{7,1},{8,10},{9,11},{10,... | collective-permute-start | bytes 786440 | tf_op jit(solution)/shard_map/ppermute | solution.py:256
  51.7 16.9 %collective-permute-start.8 = (bf16[4,256,128]{2,1,0:T(8,128)(2,1)S(1)}, bf16[4,256,128]{2,1,0:T(8,128)(2,1)S(1)}, u32[]{:S(2)}, u32[]{:S(2)}) collective-permute-start(bf16[4,256,128]{2,1,0:T(8,128)(2,1)S(1)} %get-tuple-element.76), channel_id=1, source_target_pairs={{0,6},{1,7},{2,0},{3,1},{4,2},{5,3},{6,4},{7,5},{8,14},{9,15},{10,... | collective-permute-start | bytes 786440 | tf_op jit(solution)/shard_map/ppermute | solution.py:256
  53.9 14.6 %collective-permute-start.9 = (bf16[4,256,128]{2,1,0:T(8,128)(2,1)S(1)}, bf16[4,256,128]{2,1,0:T(8,128)(2,1)S(1)}, u32[]{:S(2)}, u32[]{:S(2)}) collective-permute-start(bf16[4,256,128]{2,1,0:T(8,128)(2,1)S(1)} %get-tuple-element.77), channel_id=1, source_target_pairs={{0,4},{1,5},{2,6},{3,7},{4,0},{5,1},{6,2},{7,3},{8,12},{9,13},{10,... | collective-permute-start | bytes 786440 | tf_op jit(solution)/shard_map/ppermute | solution.py:256
  55.1 18.4 %collective-permute-start.10 = (bf16[4,256,128]{2,1,0:T(8,128)(2,1)S(1)}, bf16[4,256,128]{2,1,0:T(8,128)(2,1)S(1)}, u32[]{:S(2)}, u32[]{:S(2)}) collective-permute-start(bf16[4,256,128]{2,1,0:T(8,128)(2,1)S(1)} %get-tuple-element.78), channel_id=1, source_target_pairs={{0,3},{1,2},{2,5},{3,4},{4,7},{5,6},{6,1},{7,0},{8,11},{9,10},{10,... | collective-permute-start | bytes 786440 | tf_op jit(solution)/shard_map/ppermute | solution.py:256
  58.7 15.6 %collective-permute-start.11 = (bf16[4,256,128]{2,1,0:T(8,128)(2,1)S(1)}, bf16[4,256,128]{2,1,0:T(8,128)(2,1)S(1)}, u32[]{:S(2)}, u32[]{:S(2)}) collective-permute-start(bf16[4,256,128]{2,1,0:T(8,128)(2,1)S(1)} %get-tuple-element.79), channel_id=1, source_target_pairs={{0,7},{1,6},{2,1},{3,0},{4,3},{5,2},{6,5},{7,4},{8,15},{9,14},{10,... | collective-permute-start | bytes 786440 | tf_op jit(solution)/shard_map/ppermute | solution.py:256
  58.7 19.7 %collective-permute-start.12 = (bf16[4,256,128]{2,1,0:T(8,128)(2,1)S(1)}, bf16[4,256,128]{2,1,0:T(8,128)(2,1)S(1)}, u32[]{:S(2)}, u32[]{:S(2)}) collective-permute-start(bf16[4,256,128]{2,1,0:T(8,128)(2,1)S(1)} %get-tuple-element.80), channel_id=1, source_target_pairs={{0,5},{1,4},{2,7},{3,6},{4,1},{5,0},{6,3},{7,2},{8,13},{9,12},{10,... | collective-permute-start | bytes 786440 | tf_op jit(solution)/shard_map/ppermute | solution.py:256
  68.5 9.9 %collective-permute-start.13 = (bf16[4,256,128]{2,1,0:T(8,128)(2,1)S(1)}, bf16[4,256,128]{2,1,0:T(8,128)(2,1)S(1)}, u32[]{:S(2)}, u32[]{:S(2)}) collective-permute-start(bf16[4,256,128]{2,1,0:T(8,128)(2,1)S(1)} %get-tuple-element.81), channel_id=1, source_target_pairs={{0,1},{1,0},{2,3},{3,2},{4,5},{5,4},{6,7},{7,6},{8,9},{9,8},{10,11... | collective-permute-start | bytes 786440 | tf_op jit(solution)/shard_map/ppermute | solution.py:256
  80.7 8.9 %collective-permute-start.14 = (bf16[4,256,128]{2,1,0:T(8,128)(2,1)S(1)}, bf16[4,256,128]{2,1,0:T(8,128)(2,1)S(1)}, u32[]{:S(2)}, u32[]{:S(2)}) collective-permute-start(bf16[4,256,128]{2,1,0:T(8,128)(2,1)S(1)} %get-tuple-element.84), channel_id=1, source_target_pairs={{0,2},{1,3},{2,4},{3,5},{4,6},{5,7},{6,0},{7,1},{8,10},{9,11},{10,... | collective-permute-start | bytes 786440 | tf_op jit(solution)/shard_map/ppermute | solution.py:256
  81.6 15.3 %collective-permute-start.15 = (bf16[4,256,128]{2,1,0:T(8,128)(2,1)S(1)}, bf16[4,256,128]{2,1,0:T(8,128)(2,1)S(1)}, u32[]{:S(2)}, u32[]{:S(2)}) collective-permute-start(bf16[4,256,128]{2,1,0:T(8,128)(2,1)S(1)} %get-tuple-element.85), channel_id=1, source_target_pairs={{0,6},{1,7},{2,0},{3,1},{4,2},{5,3},{6,4},{7,5},{8,14},{9,15},{10,... | collective-permute-start | bytes 786440 | tf_op jit(solution)/shard_map/ppermute | solution.py:256
  83.4 21.3 %collective-permute-start.16 = (bf16[4,256,128]{2,1,0:T(8,128)(2,1)S(1)}, bf16[4,256,128]{2,1,0:T(8,128)(2,1)S(1)}, u32[]{:S(2)}, u32[]{:S(2)}) collective-permute-start(bf16[4,256,128]{2,1,0:T(8,128)(2,1)S(1)} %get-tuple-element.86), channel_id=1, source_target_pairs={{0,4},{1,5},{2,6},{3,7},{4,0},{5,1},{6,2},{7,3},{8,12},{9,13},{10,... | collective-permute-start | bytes 786440 | tf_op jit(solution)/shard_map/ppermute | solution.py:256
  83.5 21.2 %collective-permute-start.17 = (bf16[4,256,128]{2,1,0:T(8,128)(2,1)S(1)}, bf16[4,256,128]{2,1,0:T(8,128)(2,1)S(1)}, u32[]{:S(2)}, u32[]{:S(2)}) collective-permute-start(bf16[4,256,128]{2,1,0:T(8,128)(2,1)S(1)} %get-tuple-element.87), channel_id=1, source_target_pairs={{0,3},{1,2},{2,5},{3,4},{4,7},{5,6},{6,1},{7,0},{8,11},{9,10},{10,... | collective-permute-start | bytes 786440 | tf_op jit(solution)/shard_map/ppermute | solution.py:256
  89.6 15.1 %collective-permute-start.18 = (bf16[4,256,128]{2,1,0:T(8,128)(2,1)S(1)}, bf16[4,256,128]{2,1,0:T(8,128)(2,1)S(1)}, u32[]{:S(2)}, u32[]{:S(2)}) collective-permute-start(bf16[4,256,128]{2,1,0:T(8,128)(2,1)S(1)} %get-tuple-element.88), channel_id=1, source_target_pairs={{0,7},{1,6},{2,1},{3,0},{4,3},{5,2},{6,5},{7,4},{8,15},{9,14},{10,... | collective-permute-start | bytes 786440 | tf_op jit(solution)/shard_map/ppermute | solution.py:256
  89.6 17.4 %collective-permute-start.19 = (bf16[4,256,128]{2,1,0:T(8,128)(2,1)S(1)}, bf16[4,256,128]{2,1,0:T(8,128)(2,1)S(1)}, u32[]{:S(2)}, u32[]{:S(2)}) collective-permute-start(bf16[4,256,128]{2,1,0:T(8,128)(2,1)S(1)} %get-tuple-element.89), channel_id=1, source_target_pairs={{0,5},{1,4},{2,7},{3,6},{4,1},{5,0},{6,3},{7,2},{8,13},{9,12},{10,... | collective-permute-start | bytes 786440 | tf_op jit(solution)/shard_map/ppermute | solution.py:256
  96.9 10.2 %copy-start.1 = (bf16[64,128]{1,0:T(8,128)(2,1)S(1)}, bf16[64,128]{1,0:T(8,128)(2,1)}, u32[]{:S(2)}) copy-start(bf16[64,128]{1,0:T(8,128)(2,1)} %constant.58.clone.lag_ref) | copy-start | bytes 49156
  96.9 10.2 %collective-permute-start.20 = (bf16[4,256,128]{2,1,0:T(8,128)(2,1)S(1)}, bf16[4,256,128]{2,1,0:T(8,128)(2,1)S(1)}, u32[]{:S(2)}, u32[]{:S(2)}) collective-permute-start(bf16[4,256,128]{2,1,0:T(8,128)(2,1)S(1)} %get-tuple-element.90), channel_id=1, source_target_pairs={{0,1},{1,0},{2,3},{3,2},{4,5},{5,4},{6,7},{7,6},{8,9},{9,8},{10,11... | collective-permute-start | bytes 786440 | tf_op jit(solution)/shard_map/ppermute | solution.py:256

commit v9 on v8

--- a/solution.py
+++ b/solution.py
@@ -124,8 +124,8 @@
     own = jnp.concatenate([r[at, :] for r in own_refs], 0).astype(jnp.float32)
     halves = own.reshape(depth // 16, 2, 8, BCH)
     turned = jnp.stack([halves[:, 1], -halves[:, 0]], axis=1).reshape(depth, BCH)
-    rows_ref[0] = own.T
-    rows_ref[1] = turned.T
+    rows_ref[0, :BCH] = own.T
+    rows_ref[1, :BCH] = turned.T
     at = pl.ds(pl.multiple_of(local * 32, 32), 32)
     right = jnp.concatenate(
         [jnp.concatenate([r[q, at, :] for r in part_refs], 0) for q in range(pairs)], 1
@@ -230,7 +230,7 @@
         out_shape=out,
         scratch_shapes=[
             pltpu.VMEM((octets, BCH, 16, pairs * BCH), jnp.bfloat16),
-            pltpu.VMEM((AT_STEP, 2, BCH, 32 * members), jnp.float32),
+            pltpu.VMEM((AT_STEP, 2, BCH + 8, 32 * members), jnp.float32),
             *made,
         ],
         compiler_params=params(28),

time: 117 us -> 117 us (level)
  no operation moved by 1% of the time
where the time goes in v9:
time: 117 us
  starting transfers between devices  57 us (49%)
  waiting for transfers between devices  32 us (27%)
  Pallas kernels  27.1 us (23%)
    ppermute x21, starting transfers between devices, move(): moved.append(lax.ppermute(piece, 'win', way))  44.8 us
    ppermute x21, waiting for transfers between devices, move(): moved.append(lax.ppermute(piece, 'win', way))  19 us
    pallas_call x2, Pallas kernels, chunk(): pl.pallas_call(functools.partial(chunk_kernel, c, members), grid=(octets...  17.6 us
    all_to_all x2, waiting for transfers between devices, shards(): lax.all_to_all(sends[c].reshape(groups, 64 * octets, BCH), 'blk', split_a...  13 us
    all_to_all x2, starting transfers between devices, shards(): lax.all_to_all(sends[c].reshape(groups, 64 * octets, BCH), 'blk', split_a...  12.2 us
    pallas_call x1, Pallas kernels, shards(): pl.pallas_call(functools.partial(spectra_kernel, members, groups), grid_s...  6.51 us
    pallas_call x2, Pallas kernels, shards(): pl.pallas_call(functools.partial(pack_kernel, members, pairs), grid_spec=...  2.96 us
  transfers between devices with their start and end apart: 23, of which 9 were waited for; matrix products, arithmetic and copies ran while one was open for 0% of the time, Pallas kernels for 7%

profile of v9, /device:TPU:1, one launch (start us, length us, event | category | flops | bytes accessed | tf_op | source)
XLA Modules:
  0.0 117.0 jit_solution(4501261372679934012)
XLA Ops:
  0.0 6.5 %spectra.1 = (bf16[32,256,128]{2,1,0:T(8,128)(2,1)}, bf16[32,256,128]{2,1,0:T(8,128)(2,1)}, bf16[512,128]{1,0:T(8,128)(2,1)}, bf16[512,128]{1,0:T(8,128)(2,1)}, ...) custom-call(s32[4,128]{1,0:T(4,128)} %bitcast.14, ...), custom_call_target="tpu_custom_call" | custom-call | tf_op jit(solution)/shard_map/spectra/pallas_call | solution.py:269
  6.5 0.0 copy-start.3
  6.6 7.7 %all-to-all-start = ((bf16[16,512,128]{2,1,0:T(8,128)(2,1)}), bf16[16,512,128]{2,1,0:T(8,128)(2,1)S(1)}, u32[]{:S(2)}, u32[]{:S(2)}) async-start(bf16[16,512,128]{2,1,0:T(8,128)(2,1)} %bitcast.13), calls=%async_computation | async-start | bytes 4194304 | tf_op jit(solution)/shard_map/all_to_all | solution.py:296
  14.3 1.7 %collective-permute-start = (bf16[512,128]{1,0:T(8,128)(2,1)S(1)}, bf16[512,128]{1,0:T(8,128)(2,1)S(1)}, u32[]{:S(2)}, u32[]{:S(2)}) collective-permute-start(bf16[512,128]{1,0:T(8,128)(2,1)S(1)} %copy-done.8), channel_id=1, source_target_pairs={{0,2},{1,3},{2,4},{3,5},{4,6},{5,7},{6,0},{7,1},{8,10},{9,11},{10,... | collective-permute-start | bytes 393224 | tf_op jit(solution)/shard_map/ppermute | solution.py:256
  16.0 2.2 %collective-permute-start.1 = (bf16[512,128]{1,0:T(8,128)(2,1)S(1)}, bf16[512,128]{1,0:T(8,128)(2,1)S(1)}, u32[]{:S(2)}, u32[]{:S(2)}) collective-permute-start(bf16[512,128]{1,0:T(8,128)(2,1)S(1)} %copy-done.7), channel_id=1, source_target_pairs={{0,6},{1,7},{2,0},{3,1},{4,2},{5,3},{6,4},{7,5},{8,14},{9,15},{10,... | collective-permute-start | bytes 393224 | tf_op jit(solution)/shard_map/ppermute | solution.py:256
  18.2 1.2 %collective-permute-start.2 = (bf16[512,128]{1,0:T(8,128)(2,1)}, bf16[512,128]{1,0:T(8,128)(2,1)S(1)}, u32[]{:S(2)}, u32[]{:S(2)}) collective-permute-start(bf16[512,128]{1,0:T(8,128)(2,1)} %get-tuple-element.56), channel_id=1, source_target_pairs={{0,4},{1,5},{2,6},{3,7},{4,0},{5,1},{6,2},{7,3},{8,12},{9,13},{10,... | collective-permute-start | bytes 393224 | tf_op jit(solution)/shard_map/ppermute | solution.py:256
  19.5 2.4 %collective-permute-start.3 = (bf16[512,128]{1,0:T(8,128)(2,1)}, bf16[512,128]{1,0:T(8,128)(2,1)S(1)}, u32[]{:S(2)}, u32[]{:S(2)}) collective-permute-start(bf16[512,128]{1,0:T(8,128)(2,1)} %get-tuple-element.57), channel_id=1, source_target_pairs={{0,3},{1,2},{2,5},{3,4},{4,7},{5,6},{6,1},{7,0},{8,11},{9,10},{10,... | collective-permute-start | bytes 393224 | tf_op jit(solution)/shard_map/ppermute | solution.py:256
  21.9 0.5 collective-permute-start.4
  22.4 0.1 copy.8
  22.5 0.1 reshape.82
  22.7 0.2 and_reduce_fusion
  22.8 0.0 collective-permute-done.refs_1_
  22.9 2.0 %collective-permute-start.5 = (bf16[512,128]{1,0:T(8,128)(2,1)S(1)}, bf16[512,128]{1,0:T(8,128)(2,1)S(1)}, u32[]{:S(2)}, u32[]{:S(2)}) collective-permute-start(bf16[512,128]{1,0:T(8,128)(2,1)S(1)} %copy-done.5), channel_id=1, source_target_pairs={{0,5},{1,4},{2,7},{3,6},{4,1},{5,0},{6,3},{7,2},{8,13},{9,12},{10,... | collective-permute-start | bytes 393224 | tf_op jit(solution)/shard_map/ppermute | solution.py:256
  24.9 0.0 collective-permute-done.1.refs_2_
  24.9 0.1 pad_add_fusion.meta
  25.0 0.2 collective-permute-done.2.refs_3_
  25.2 3.8 %collective-permute-done.3.refs_4_ = bf16[512,128]{1,0:T(8,128)(2,1)S(1)} collective-permute-done((bf16[512,128]{1,0:T(8,128)(2,1)}, bf16[512,128]{1,0:T(8,128)(2,1)S(1)}, u32[]{:S(2)}, u32[]{:S(2)}) %collective-permute-start.3) | collective-permute-done | bytes 131104 | tf_op jit(solution)/shard_map/ppermute | solution.py:256
  28.9 0.1 collective-permute-done.4.refs_5_
  29.0 2.8 %collective-permute-done.5.refs_6_ = bf16[512,128]{1,0:T(8,128)(2,1)S(1)} collective-permute-done((bf16[512,128]{1,0:T(8,128)(2,1)S(1)}, bf16[512,128]{1,0:T(8,128)(2,1)S(1)}, u32[]{:S(2)}, u32[]{:S(2)}) %collective-permute-start.5) | collective-permute-done | bytes 131104 | tf_op jit(solution)/shard_map/ppermute | solution.py:256
  31.8 0.0 collective-permute-done.6.refs_7_
  31.8 13.0 %all-to-all-done = bf16[16,512,128]{2,1,0:T(8,128)(2,1)S(1)} async-done(((bf16[16,512,128]{2,1,0:T(8,128)(2,1)}), bf16[16,512,128]{2,1,0:T(8,128)(2,1)S(1)}, u32[]{:S(2)}, u32[]{:S(2)}) %all-to-all-start) | async-done | bytes 2097184 | tf_op jit(solution)/shard_map/all_to_all | solution.py:296
  44.8 4.4 %all-to-all-start.1 = ((bf16[16,512,128]{2,1,0:T(8,128)(2,1)}), bf16[16,512,128]{2,1,0:T(8,128)(2,1)}, u32[]{:S(2)}, u32[]{:S(2)}) async-start(bf16[16,512,128]{2,1,0:T(8,128)(2,1)} %bitcast.12), calls=%async_computation.1 | async-start | bytes 4194304 | tf_op jit(solution)/shard_map/all_to_all | solution.py:296
  49.3 0.0 copy-start.2
  49.3 0.7 pack.2
  50.0 1.7 %collective-permute-start.7 = (bf16[4,256,128]{2,1,0:T(8,128)(2,1)S(1)}, bf16[4,256,128]{2,1,0:T(8,128)(2,1)S(1)}, u32[]{:S(2)}, u32[]{:S(2)}) collective-permute-start(bf16[4,256,128]{2,1,0:T(8,128)(2,1)S(1)} %get-tuple-element.75), channel_id=1, source_target_pairs={{0,2},{1,3},{2,4},{3,5},{4,6},{5,7},{6,0},{7,1},{8,10},{9,11},{10,... | collective-permute-start | bytes 786440 | tf_op jit(solution)/shard_map/ppermute | solution.py:256
  51.7 2.2 %collective-permute-start.8 = (bf16[4,256,128]{2,1,0:T(8,128)(2,1)S(1)}, bf16[4,256,128]{2,1,0:T(8,128)(2,1)S(1)}, u32[]{:S(2)}, u32[]{:S(2)}) collective-permute-start(bf16[4,256,128]{2,1,0:T(8,128)(2,1)S(1)} %get-tuple-element.76), channel_id=1, source_target_pairs={{0,6},{1,7},{2,0},{3,1},{4,2},{5,3},{6,4},{7,5},{8,14},{9,15},{10,... | collective-permute-start | bytes 786440 | tf_op jit(solution)/shard_map/ppermute | solution.py:256
  53.9 1.2 %collective-permute-start.9 = (bf16[4,256,128]{2,1,0:T(8,128)(2,1)S(1)}, bf16[4,256,128]{2,1,0:T(8,128)(2,1)S(1)}, u32[]{:S(2)}, u32[]{:S(2)}) collective-permute-start(bf16[4,256,128]{2,1,0:T(8,128)(2,1)S(1)} %get-tuple-element.77), channel_id=1, source_target_pairs={{0,4},{1,5},{2,6},{3,7},{4,0},{5,1},{6,2},{7,3},{8,12},{9,13},{10,... | collective-permute-start | bytes 786440 | tf_op jit(solution)/shard_map/ppermute | solution.py:256
  55.1 3.6 %collective-permute-start.10 = (bf16[4,256,128]{2,1,0:T(8,128)(2,1)S(1)}, bf16[4,256,128]{2,1,0:T(8,128)(2,1)S(1)}, u32[]{:S(2)}, u32[]{:S(2)}) collective-permute-start(bf16[4,256,128]{2,1,0:T(8,128)(2,1)S(1)} %get-tuple-element.78), channel_id=1, source_target_pairs={{0,3},{1,2},{2,5},{3,4},{4,7},{5,6},{6,1},{7,0},{8,11},{9,10},{10,... | collective-permute-start | bytes 786440 | tf_op jit(solution)/shard_map/ppermute | solution.py:256
  58.7 0.0 collective-permute-start.11
  58.7 9.8 %collective-permute-start.12 = (bf16[4,256,128]{2,1,0:T(8,128)(2,1)S(1)}, bf16[4,256,128]{2,1,0:T(8,128)(2,1)S(1)}, u32[]{:S(2)}, u32[]{:S(2)}) collective-permute-start(bf16[4,256,128]{2,1,0:T(8,128)(2,1)S(1)} %get-tuple-element.80), channel_id=1, source_target_pairs={{0,5},{1,4},{2,7},{3,6},{4,1},{5,0},{6,3},{7,2},{8,13},{9,12},{10,... | collective-permute-start | bytes 786440 | tf_op jit(solution)/shard_map/ppermute | solution.py:256
  68.5 4.9 %collective-permute-done.10.refs_12_ = bf16[4,256,128]{2,1,0:T(8,128)(2,1)S(1)} collective-permute-done((bf16[4,256,128]{2,1,0:T(8,128)(2,1)S(1)}, bf16[4,256,128]{2,1,0:T(8,128)(2,1)S(1)}, u32[]{:S(2)}, u32[]{:S(2)}) %collective-permute-start.10) | collective-permute-done | bytes 262176 | tf_op jit(solution)/shard_map/ppermute | solution.py:256
  73.5 0.8 collective-permute-done.11.refs_13_
  74.3 4.1 %collective-permute-done.12.refs_14_ = bf16[4,256,128]{2,1,0:T(8,128)(2,1)S(1)} collective-permute-done((bf16[4,256,128]{2,1,0:T(8,128)(2,1)S(1)}, bf16[4,256,128]{2,1,0:T(8,128)(2,1)S(1)}, u32[]{:S(2)}, u32[]{:S(2)}) %collective-permute-start.12) | collective-permute-done | bytes 262176 | tf_op jit(solution)/shard_map/ppermute | solution.py:256
  78.4 0.0 collective-permute-done.13.refs_15_
  78.4 0.0 all-to-all-done.1
  78.4 2.3 %pack.3 = (bf16[4,256,128]{2,1,0:T(8,128)(2,1)S(1)}, bf16[4,256,128]{2,1,0:T(8,128)(2,1)S(1)}, bf16[4,256,128]{2,1,0:T(8,128)(2,1)S(1)}, bf16[4,256,128]{2,1,0:T...) custom-call(s32[33]{0:T(128)S(1)} %pad_add_fusion.meta, ...), custom_call_target="tpu_custom_call" | custom-call | tf_op jit(solution)/shard_map/pack/pallas_call | solution.py:310
  80.7 0.9 collective-permute-start.14
  81.6 1.8 %collective-permute-start.15 = (bf16[4,256,128]{2,1,0:T(8,128)(2,1)S(1)}, bf16[4,256,128]{2,1,0:T(8,128)(2,1)S(1)}, u32[]{:S(2)}, u32[]{:S(2)}) collective-permute-start(bf16[4,256,128]{2,1,0:T(8,128)(2,1)S(1)} %get-tuple-element.85), channel_id=1, source_target_pairs={{0,6},{1,7},{2,0},{3,1},{4,2},{5,3},{6,4},{7,5},{8,14},{9,15},{10,... | collective-permute-start | bytes 786440 | tf_op jit(solution)/shard_map/ppermute | solution.py:256
  83.4 0.1 collective-permute-start.16
  83.5 6.1 %collective-permute-start.17 = (bf16[4,256,128]{2,1,0:T(8,128)(2,1)S(1)}, bf16[4,256,128]{2,1,0:T(8,128)(2,1)S(1)}, u32[]{:S(2)}, u32[]{:S(2)}) collective-permute-start(bf16[4,256,128]{2,1,0:T(8,128)(2,1)S(1)} %get-tuple-element.87), channel_id=1, source_target_pairs={{0,3},{1,2},{2,5},{3,4},{4,7},{5,6},{6,1},{7,0},{8,11},{9,10},{10,... | collective-permute-start | bytes 786440 | tf_op jit(solution)/shard_map/ppermute | solution.py:256
  89.6 0.0 collective-permute-start.18
  89.6 0.0 collective-permute-done.14.refs_9_
  89.6 7.2 %collective-permute-start.19 = (bf16[4,256,128]{2,1,0:T(8,128)(2,1)S(1)}, bf16[4,256,128]{2,1,0:T(8,128)(2,1)S(1)}, u32[]{:S(2)}, u32[]{:S(2)}) collective-permute-start(bf16[4,256,128]{2,1,0:T(8,128)(2,1)S(1)} %get-tuple-element.89), channel_id=1, source_target_pairs={{0,5},{1,4},{2,7},{3,6},{4,1},{5,0},{6,3},{7,2},{8,13},{9,12},{10,... | collective-permute-start | bytes 786440 | tf_op jit(solution)/shard_map/ppermute | solution.py:256
  96.9 0.0 collective-permute-done.15.refs_10_
  96.9 0.0 collective-permute-start.20
  96.9 7.9 %chunk.2.refs_16_ = f32[128,64,512]{2,1,0:T(8,128)S(1)} custom-call(bf16[64,128]{1,0:T(8,128)(2,1)S(1)} %copy-done.2, bf16[512,128]{1,0:T(8,128)(2,1)S(1)} %copy-done, bf16[512,128]{1,0:T(8,128)(2,1)S(1)} %collective-permute-done.refs_1_, bf16[512,128]{1,0:T(8,128)(2,1)S(1)} %collective-permute-done.1.refs_2_, ...), custom_call_target="tpu_custom_call" | custom-call | flops 20000000000 | bytes 16777216 | tf_op jit(solution)/shard_map/chunk/pallas_call | solution.py:225
  104.8 2.3 %collective-permute-done.19.refs_14_ = bf16[4,256,128]{2,1,0:T(8,128)(2,1)S(1)} collective-permute-done((bf16[4,256,128]{2,1,0:T(8,128)(2,1)S(1)}, bf16[4,256,128]{2,1,0:T(8,128)(2,1)S(1)}, u32[]{:S(2)}, u32[]{:S(2)}) %collective-permute-start.19) | collective-permute-done | bytes 262176 | tf_op jit(solution)/shard_map/ppermute | solution.py:256
  107.1 9.8 %chunk.3 = bf16[4,64,16384]{2,1,0:T(8,128)(2,1)} custom-call(bf16[64,128]{1,0:T(8,128)(2,1)S(1)} %copy-done.1, bf16[512,128]{1,0:T(8,128)(2,1)S(1)} %copy-done, bf16[512,128]{1,0:T(8,128)(2,1)S(1)} %collective-permute-done.refs_1_, bf16[512,128]{1,0:T(8,128)(2,1)S(1)} %collective-permute-done.1.refs_2_, bf16[512,128]{1,0:T(8,128)(2,1)S(1)} %collective-permute-done.2.refs_3_, ...), custom_call_target="tpu_custom_call" | custom-call | flops 20000000000 | bytes 16777216 | tf_op jit(solution)/shard_map/chunk/pallas_call | solution.py:225
  (28 shorter events, 0.1 us)
Async XLA Ops:
  6.5 7.8 %copy-start.8 = (bf16[512,128]{1,0:T(8,128)(2,1)S(1)}, bf16[512,128]{1,0:T(8,128)(2,1)}, u32[]{:S(2)}) copy-start(bf16[512,128]{1,0:T(8,128)(2,1)} %get-tuple-element.54) | copy-start | bytes 393220
  6.5 9.5 %copy-start.7 = (bf16[512,128]{1,0:T(8,128)(2,1)S(1)}, bf16[512,128]{1,0:T(8,128)(2,1)}, u32[]{:S(2)}) copy-start(bf16[512,128]{1,0:T(8,128)(2,1)} %get-tuple-element.55) | copy-start | bytes 393220
  6.5 15.3 %copy-start.6 = (bf16[512,128]{1,0:T(8,128)(2,1)S(1)}, bf16[512,128]{1,0:T(8,128)(2,1)}, u32[]{:S(2)}) copy-start(bf16[512,128]{1,0:T(8,128)(2,1)} %get-tuple-element.58) | copy-start | bytes 393220
  6.5 15.9 %copy-start.3 = (s32[128,4]{0,1:T(4,128)S(1)}, s32[128,4]{0,1:T(4,128)}, u32[]{:S(2)}) copy-start(s32[128,4]{0,1:T(4,128)} %param.8) | copy-start | bytes 6148
  6.6 16.3 %copy-start.5 = (bf16[512,128]{1,0:T(8,128)(2,1)S(1)}, bf16[512,128]{1,0:T(8,128)(2,1)}, u32[]{:S(2)}) copy-start(bf16[512,128]{1,0:T(8,128)(2,1)} %get-tuple-element.59) | copy-start | bytes 393220
  6.6 18.3 %copy-start.4 = (bf16[512,128]{1,0:T(8,128)(2,1)S(1)}, bf16[512,128]{1,0:T(8,128)(2,1)}, u32[]{:S(2)}) copy-start(bf16[512,128]{1,0:T(8,128)(2,1)} %get-tuple-element.60) | copy-start | bytes 393220
  6.6 38.2 %all-to-all-start = ((bf16[16,512,128]{2,1,0:T(8,128)(2,1)}), bf16[16,512,128]{2,1,0:T(8,128)(2,1)S(1)}, u32[]{:S(2)}, u32[]{:S(2)}) async-start(bf16[16,512,128]{2,1,0:T(8,128)(2,1)} %bitcast.13), calls=%async_computation | async-start | bytes 4194304 | tf_op jit(solution)/shard_map/all_to_all | solution.py:296
  14.3 8.5 %collective-permute-start = (bf16[512,128]{1,0:T(8,128)(2,1)S(1)}, bf16[512,128]{1,0:T(8,128)(2,1)S(1)}, u32[]{:S(2)}, u32[]{:S(2)}) collective-permute-start(bf16[512,128]{1,0:T(8,128)(2,1)S(1)} %copy-done.8), channel_id=1, source_target_pairs={{0,2},{1,3},{2,4},{3,5},{4,6},{5,7},{6,0},{7,1},{8,10},{9,11},{10,... | collective-permute-start | bytes 393224 | tf_op jit(solution)/shard_map/ppermute | solution.py:256
  16.0 8.9 %collective-permute-start.1 = (bf16[512,128]{1,0:T(8,128)(2,1)S(1)}, bf16[512,128]{1,0:T(8,128)(2,1)S(1)}, u32[]{:S(2)}, u32[]{:S(2)}) collective-permute-start(bf16[512,128]{1,0:T(8,128)(2,1)S(1)} %copy-done.7), channel_id=1, source_target_pairs={{0,6},{1,7},{2,0},{3,1},{4,2},{5,3},{6,4},{7,5},{8,14},{9,15},{10,... | collective-permute-start | bytes 393224 | tf_op jit(solution)/shard_map/ppermute | solution.py:256
  18.2 6.9 %collective-permute-start.2 = (bf16[512,128]{1,0:T(8,128)(2,1)}, bf16[512,128]{1,0:T(8,128)(2,1)S(1)}, u32[]{:S(2)}, u32[]{:S(2)}) collective-permute-start(bf16[512,128]{1,0:T(8,128)(2,1)} %get-tuple-element.56), channel_id=1, source_target_pairs={{0,4},{1,5},{2,6},{3,7},{4,0},{5,1},{6,2},{7,3},{8,12},{9,13},{10,... | collective-permute-start | bytes 393224 | tf_op jit(solution)/shard_map/ppermute | solution.py:256
  19.5 9.5 %collective-permute-start.3 = (bf16[512,128]{1,0:T(8,128)(2,1)}, bf16[512,128]{1,0:T(8,128)(2,1)S(1)}, u32[]{:S(2)}, u32[]{:S(2)}) collective-permute-start(bf16[512,128]{1,0:T(8,128)(2,1)} %get-tuple-element.57), channel_id=1, source_target_pairs={{0,3},{1,2},{2,5},{3,4},{4,7},{5,6},{6,1},{7,0},{8,11},{9,10},{10,... | collective-permute-start | bytes 393224 | tf_op jit(solution)/shard_map/ppermute | solution.py:256
  21.9 7.1 %collective-permute-start.4 = (bf16[512,128]{1,0:T(8,128)(2,1)S(1)}, bf16[512,128]{1,0:T(8,128)(2,1)S(1)}, u32[]{:S(2)}, u32[]{:S(2)}) collective-permute-start(bf16[512,128]{1,0:T(8,128)(2,1)S(1)} %copy-done.6), channel_id=1, source_target_pairs={{0,7},{1,6},{2,1},{3,0},{4,3},{5,2},{6,5},{7,4},{8,15},{9,14},{10,... | collective-permute-start | bytes 393224 | tf_op jit(solution)/shard_map/ppermute | solution.py:256
  22.9 9.0 %collective-permute-start.5 = (bf16[512,128]{1,0:T(8,128)(2,1)S(1)}, bf16[512,128]{1,0:T(8,128)(2,1)S(1)}, u32[]{:S(2)}, u32[]{:S(2)}) collective-permute-start(bf16[512,128]{1,0:T(8,128)(2,1)S(1)} %copy-done.5), channel_id=1, source_target_pairs={{0,5},{1,4},{2,7},{3,6},{4,1},{5,0},{6,3},{7,2},{8,13},{9,12},{10,... | collective-permute-start | bytes 393224 | tf_op jit(solution)/shard_map/ppermute | solution.py:256
  24.9 6.9 %collective-permute-start.6 = (bf16[512,128]{1,0:T(8,128)(2,1)S(1)}, bf16[512,128]{1,0:T(8,128)(2,1)S(1)}, u32[]{:S(2)}, u32[]{:S(2)}) collective-permute-start(bf16[512,128]{1,0:T(8,128)(2,1)S(1)} %copy-done.4), channel_id=1, source_target_pairs={{0,1},{1,0},{2,3},{3,2},{4,5},{5,4},{6,7},{7,6},{8,9},{9,8},{10,11... | collective-permute-start | bytes 393224 | tf_op jit(solution)/shard_map/ppermute | solution.py:256
  44.8 33.6 %all-to-all-start.1 = ((bf16[16,512,128]{2,1,0:T(8,128)(2,1)}), bf16[16,512,128]{2,1,0:T(8,128)(2,1)}, u32[]{:S(2)}, u32[]{:S(2)}) async-start(bf16[16,512,128]{2,1,0:T(8,128)(2,1)} %bitcast.12), calls=%async_computation.1 | async-start | bytes 4194304 | tf_op jit(solution)/shard_map/all_to_all | solution.py:296
  49.3 47.6 %copy-start = (bf16[512,128]{1,0:T(8,128)(2,1)S(1)}, bf16[512,128]{1,0:T(8,128)(2,1)}, u32[]{:S(2)}) copy-start(bf16[512,128]{1,0:T(8,128)(2,1)} %get-tuple-element.61.refs_0_) | copy-start | bytes 393220
  49.3 47.6 %copy-start.2 = (bf16[64,128]{1,0:T(8,128)(2,1)S(1)}, bf16[64,128]{1,0:T(8,128)(2,1)}, u32[]{:S(2)}) copy-start(bf16[64,128]{1,0:T(8,128)(2,1)} %constant.57.clone.lag_ref) | copy-start | bytes 49156
  50.0 8.7 %collective-permute-start.7 = (bf16[4,256,128]{2,1,0:T(8,128)(2,1)S(1)}, bf16[4,256,128]{2,1,0:T(8,128)(2,1)S(1)}, u32[]{:S(2)}, u32[]{:S(2)}) collective-permute-start(bf16[4,256,128]{2,1,0:T(8,128)(2,1)S(1)} %get-tuple-element.75), channel_id=1, source_target_pairs={{0,2},{1,3},{2,4},{3,5},{4,6},{5,7},{6,0},{7,1},{8,10},{9,11},{10,... | collective-permute-start | bytes 786440 | tf_op jit(solution)/shard_map/ppermute | solution.py:256
  51.7 16.9 %collective-permute-start.8 = (bf16[4,256,128]{2,1,0:T(8,128)(2,1)S(1)}, bf16[4,256,128]{2,1,0:T(8,128)(2,1)S(1)}, u32[]{:S(2)}, u32[]{:S(2)}) collective-permute-start(bf16[4,256,128]{2,1,0:T(8,128)(2,1)S(1)} %get-tuple-element.76), channel_id=1, source_target_pairs={{0,6},{1,7},{2,0},{3,1},{4,2},{5,3},{6,4},{7,5},{8,14},{9,15},{10,... | collective-permute-start | bytes 786440 | tf_op jit(solution)/shard_map/ppermute | solution.py:256
  53.9 14.6 %collective-permute-start.9 = (bf16[4,256,128]{2,1,0:T(8,128)(2,1)S(1)}, bf16[4,256,128]{2,1,0:T(8,128)(2,1)S(1)}, u32[]{:S(2)}, u32[]{:S(2)}) collective-permute-start(bf16[4,256,128]{2,1,0:T(8,128)(2,1)S(1)} %get-tuple-element.77), channel_id=1, source_target_pairs={{0,4},{1,5},{2,6},{3,7},{4,0},{5,1},{6,2},{7,3},{8,12},{9,13},{10,... | collective-permute-start | bytes 786440 | tf_op jit(solution)/shard_map/ppermute | solution.py:256
  55.1 18.4 %collective-permute-start.10 = (bf16[4,256,128]{2,1,0:T(8,128)(2,1)S(1)}, bf16[4,256,128]{2,1,0:T(8,128)(2,1)S(1)}, u32[]{:S(2)}, u32[]{:S(2)}) collective-permute-start(bf16[4,256,128]{2,1,0:T(8,128)(2,1)S(1)} %get-tuple-element.78), channel_id=1, source_target_pairs={{0,3},{1,2},{2,5},{3,4},{4,7},{5,6},{6,1},{7,0},{8,11},{9,10},{10,... | collective-permute-start | bytes 786440 | tf_op jit(solution)/shard_map/ppermute | solution.py:256
  58.7 15.6 %collective-permute-start.11 = (bf16[4,256,128]{2,1,0:T(8,128)(2,1)S(1)}, bf16[4,256,128]{2,1,0:T(8,128)(2,1)S(1)}, u32[]{:S(2)}, u32[]{:S(2)}) collective-permute-start(bf16[4,256,128]{2,1,0:T(8,128)(2,1)S(1)} %get-tuple-element.79), channel_id=1, source_target_pairs={{0,7},{1,6},{2,1},{3,0},{4,3},{5,2},{6,5},{7,4},{8,15},{9,14},{10,... | collective-permute-start | bytes 786440 | tf_op jit(solution)/shard_map/ppermute | solution.py:256
  58.7 19.7 %collective-permute-start.12 = (bf16[4,256,128]{2,1,0:T(8,128)(2,1)S(1)}, bf16[4,256,128]{2,1,0:T(8,128)(2,1)S(1)}, u32[]{:S(2)}, u32[]{:S(2)}) collective-permute-start(bf16[4,256,128]{2,1,0:T(8,128)(2,1)S(1)} %get-tuple-element.80), channel_id=1, source_target_pairs={{0,5},{1,4},{2,7},{3,6},{4,1},{5,0},{6,3},{7,2},{8,13},{9,12},{10,... | collective-permute-start | bytes 786440 | tf_op jit(solution)/shard_map/ppermute | solution.py:256
  68.5 9.9 %collective-permute-start.13 = (bf16[4,256,128]{2,1,0:T(8,128)(2,1)S(1)}, bf16[4,256,128]{2,1,0:T(8,128)(2,1)S(1)}, u32[]{:S(2)}, u32[]{:S(2)}) collective-permute-start(bf16[4,256,128]{2,1,0:T(8,128)(2,1)S(1)} %get-tuple-element.81), channel_id=1, source_target_pairs={{0,1},{1,0},{2,3},{3,2},{4,5},{5,4},{6,7},{7,6},{8,9},{9,8},{10,11... | collective-permute-start | bytes 786440 | tf_op jit(solution)/shard_map/ppermute | solution.py:256
  80.7 8.9 %collective-permute-start.14 = (bf16[4,256,128]{2,1,0:T(8,128)(2,1)S(1)}, bf16[4,256,128]{2,1,0:T(8,128)(2,1)S(1)}, u32[]{:S(2)}, u32[]{:S(2)}) collective-permute-start(bf16[4,256,128]{2,1,0:T(8,128)(2,1)S(1)} %get-tuple-element.84), channel_id=1, source_target_pairs={{0,2},{1,3},{2,4},{3,5},{4,6},{5,7},{6,0},{7,1},{8,10},{9,11},{10,... | collective-permute-start | bytes 786440 | tf_op jit(solution)/shard_map/ppermute | solution.py:256
  81.6 15.3 %collective-permute-start.15 = (bf16[4,256,128]{2,1,0:T(8,128)(2,1)S(1)}, bf16[4,256,128]{2,1,0:T(8,128)(2,1)S(1)}, u32[]{:S(2)}, u32[]{:S(2)}) collective-permute-start(bf16[4,256,128]{2,1,0:T(8,128)(2,1)S(1)} %get-tuple-element.85), channel_id=1, source_target_pairs={{0,6},{1,7},{2,0},{3,1},{4,2},{5,3},{6,4},{7,5},{8,14},{9,15},{10,... | collective-permute-start | bytes 786440 | tf_op jit(solution)/shard_map/ppermute | solution.py:256
  83.4 21.3 %collective-permute-start.16 = (bf16[4,256,128]{2,1,0:T(8,128)(2,1)S(1)}, bf16[4,256,128]{2,1,0:T(8,128)(2,1)S(1)}, u32[]{:S(2)}, u32[]{:S(2)}) collective-permute-start(bf16[4,256,128]{2,1,0:T(8,128)(2,1)S(1)} %get-tuple-element.86), channel_id=1, source_target_pairs={{0,4},{1,5},{2,6},{3,7},{4,0},{5,1},{6,2},{7,3},{8,12},{9,13},{10,... | collective-permute-start | bytes 786440 | tf_op jit(solution)/shard_map/ppermute | solution.py:256
  83.5 21.3 %collective-permute-start.17 = (bf16[4,256,128]{2,1,0:T(8,128)(2,1)S(1)}, bf16[4,256,128]{2,1,0:T(8,128)(2,1)S(1)}, u32[]{:S(2)}, u32[]{:S(2)}) collective-permute-start(bf16[4,256,128]{2,1,0:T(8,128)(2,1)S(1)} %get-tuple-element.87), channel_id=1, source_target_pairs={{0,3},{1,2},{2,5},{3,4},{4,7},{5,6},{6,1},{7,0},{8,11},{9,10},{10,... | collective-permute-start | bytes 786440 | tf_op jit(solution)/shard_map/ppermute | solution.py:256
  89.6 15.2 %collective-permute-start.18 = (bf16[4,256,128]{2,1,0:T(8,128)(2,1)S(1)}, bf16[4,256,128]{2,1,0:T(8,128)(2,1)S(1)}, u32[]{:S(2)}, u32[]{:S(2)}) collective-permute-start(bf16[4,256,128]{2,1,0:T(8,128)(2,1)S(1)} %get-tuple-element.88), channel_id=1, source_target_pairs={{0,7},{1,6},{2,1},{3,0},{4,3},{5,2},{6,5},{7,4},{8,15},{9,14},{10,... | collective-permute-start | bytes 786440 | tf_op jit(solution)/shard_map/ppermute | solution.py:256
  89.6 17.4 %collective-permute-start.19 = (bf16[4,256,128]{2,1,0:T(8,128)(2,1)S(1)}, bf16[4,256,128]{2,1,0:T(8,128)(2,1)S(1)}, u32[]{:S(2)}, u32[]{:S(2)}) collective-permute-start(bf16[4,256,128]{2,1,0:T(8,128)(2,1)S(1)} %get-tuple-element.89), channel_id=1, source_target_pairs={{0,5},{1,4},{2,7},{3,6},{4,1},{5,0},{6,3},{7,2},{8,13},{9,12},{10,... | collective-permute-start | bytes 786440 | tf_op jit(solution)/shard_map/ppermute | solution.py:256
  96.9 10.2 %copy-start.1 = (bf16[64,128]{1,0:T(8,128)(2,1)S(1)}, bf16[64,128]{1,0:T(8,128)(2,1)}, u32[]{:S(2)}) copy-start(bf16[64,128]{1,0:T(8,128)(2,1)} %constant.58.clone.lag_ref) | copy-start | bytes 49156
  96.9 10.2 %collective-permute-start.20 = (bf16[4,256,128]{2,1,0:T(8,128)(2,1)S(1)}, bf16[4,256,128]{2,1,0:T(8,128)(2,1)S(1)}, u32[]{:S(2)}, u32[]{:S(2)}) collective-permute-start(bf16[4,256,128]{2,1,0:T(8,128)(2,1)S(1)} %get-tuple-element.90), channel_id=1, source_target_pairs={{0,1},{1,0},{2,3},{3,2},{4,5},{5,4},{6,7},{7,6},{8,9},{9,8},{10,11... | collective-permute-start | bytes 786440 | tf_op jit(solution)/shard_map/ppermute | solution.py:256
